TPU v7x, 32 devices: a whole 2x2x4 slice. The times are simulated.
32 devices in a mesh: seq: 8 (over z, x), chan: 4 (over y, core).
Axes of the slice: x: 2, y: 2, z: 4, core: 2. Of those that a mesh axis runs over, the one named last changes fastest.
Arguments:
- query: bfloat16 [2048, 4096], P('seq', 'chan'), may hold values from -6 to 6
- key_gate: bfloat16 [2048, 4096], P('seq', 'chan'), may hold values from -6 to 6
- value: bfloat16 [2048, 4096], P('seq', 'chan'), may hold values from -6 to 6
- group_order: int32 [16], replicated, may hold values from 0 to 15, each once
- emb_weight: float32 [33, 64], replicated, may hold values from -32 to 32
- emb_bias: float32 [64], replicated, may hold values from -1 to 1
- mid_weight: float32 [64, 64], replicated, may hold values from -0.75 to 0.75
- mid_bias: float32 [64], replicated, may hold values from -1 to 1
- out_filter: float32 [64, 4096], P(None, 'chan'), may hold values from -0.75 to 0.75
- decay_rate: float32 [4096], P('chan'), may hold values from 0.00014648438 to 0.0014648438
- skip_gain: float32 [4096], P('chan'), may hold values from 0.5 to 1.5
- out_weight: bfloat16 [4096, 4096], P('chan'), may hold values from -0.125 to 0.125
Outputs:
- projected: float32 [4096, 2048], P('chan', 'seq')
Inputs may be any that keep to these rules, and one draw needn't show every extreme that they name: `group_order`: a permutation of the group numbers.
All inputs are finite; a program needn't handle non-finite values.
Results may differ from a plain program's by a relative error of at most 0.011.
Values may be sent and summed in bfloat16 or wider, within the bound.
No kernel may reach another device: no remote copies, remote signals or barrier semaphores. Data moves between devices by JAX's collectives and lax.ppermute only.
A program may use at most 128 MiB of HBM per device.

v0:
```python
import math

import jax
import jax.numpy as jnp
from jax import lax
from jax.sharding import PartitionSpec as P

BLOCK = 128


sine_freq = 2.0


def transform_tables(block):
    period = 2 * block
    row_index = jnp.arange(block, dtype=jnp.int32)
    freq_index = jnp.arange(block + 1, dtype=jnp.int32)
    scale = math.pi / block
    angle_head = (freq_index[:, None] * row_index[None, :] % period).astype(jnp.float32) * scale
    fwd_head = jnp.concatenate([jnp.cos(angle_head), -jnp.sin(angle_head)], 0).astype(jnp.bfloat16)
    angle_tail = (freq_index[:, None] * (row_index[None, :] + block) % period).astype(
        jnp.float32
    ) * scale
    keep_cols = (row_index > 0).astype(jnp.float32)[None, :]
    fwd_tail = (jnp.concatenate([jnp.cos(angle_tail), -jnp.sin(angle_tail)], 0) * keep_cols).astype(
        jnp.bfloat16
    )
    weights = (
        jnp.where((freq_index == 0) | (freq_index == block), 1.0, 2.0).astype(jnp.float32) / period
    )
    angle_back = (row_index[:, None] * freq_index[None, :] % period).astype(jnp.float32) * scale
    inverse = jnp.concatenate(
        [jnp.cos(angle_back) * weights[None, :], -jnp.sin(angle_back) * weights[None, :]], 1
    ).astype(jnp.bfloat16)
    return (fwd_head, fwd_tail, inverse)


def filter_rows(
    positions, length, emb_weight, emb_bias, mid_weight, mid_bias, out_filter, decay_rate
):
    high = lax.Precision.HIGHEST
    time_float = positions.astype(jnp.float32)
    band_count = (emb_weight.shape[0] - 1) // 2
    band_index = jnp.arange(1, band_count + 1, dtype=jnp.int32)
    angles = (positions[:, None] * band_index[None, :] % length).astype(jnp.float32) * (
        2.0 * math.pi / length
    )
    embedded = jnp.concatenate([time_float[:, None] / length, jnp.cos(angles), jnp.sin(angles)], 1)
    hidden = jnp.sin(
        sine_freq * (jnp.dot(embedded, emb_weight, precision=high) + emb_bias[None, :])
    )
    hidden = jnp.sin(sine_freq * (jnp.dot(hidden, mid_weight, precision=high) + mid_bias[None, :]))
    filter_raw = jnp.dot(hidden, out_filter, precision=high)
    norm_scale = jnp.sqrt(-jnp.expm1(-2.0 * decay_rate))
    decayed = jnp.exp(-decay_rate[None, :] * time_float[:, None])
    return (filter_raw * decayed * norm_scale[None, :]).astype(jnp.bfloat16)


def local(
    query,
    key_gate,
    value,
    group_order,
    emb_weight,
    emb_bias,
    mid_weight,
    mid_bias,
    out_filter,
    decay_rate,
    skip_gain,
    out_weight,
):
    tok_rows, chan_width = query.shape
    my_groups = tok_rows // BLOCK
    seq_count = lax.axis_size("seq")
    length = tok_rows * seq_count
    total_groups = length // BLOCK
    half_rows = BLOCK + 1
    fwd_head, fwd_tail, inverse = transform_tables(BLOCK)
    seq_index = lax.axis_index("seq")
    mine = lax.dynamic_slice_in_dim(group_order, seq_index * my_groups, my_groups)
    signal = (key_gate.astype(jnp.float32) * value.astype(jnp.float32)).astype(jnp.bfloat16)
    positions = seq_index * tok_rows + jnp.arange(tok_rows, dtype=jnp.int32)
    own_rows = filter_rows(
        positions, length, emb_weight, emb_bias, mid_weight, mid_bias, out_filter, decay_rate
    )
    whole_filter = lax.all_gather(own_rows, "seq", axis=0, tiled=True)
    blocks = whole_filter.reshape(total_groups, BLOCK, chan_width)
    previous = jnp.concatenate([jnp.zeros((1, BLOCK, chan_width), jnp.bfloat16), blocks[:-1]], 0)

    def block_spectrum(blocks_pair):
        head_part = jnp.dot(fwd_head, blocks_pair[0], preferred_element_type=jnp.float32)
        tail_part = jnp.dot(fwd_tail, blocks_pair[1], preferred_element_type=jnp.float32)
        return (head_part + tail_part).astype(jnp.bfloat16)

    filter_spectrum = lax.map(block_spectrum, (blocks, previous))

    def accumulate(spectra_sum, spectrum, global_id):
        lag_index = mine - global_id
        causal = (lag_index >= 0).astype(jnp.float32)[:, None, None]
        picked = filter_spectrum[jnp.maximum(lag_index, 0)]
        filt_real = picked[:, :half_rows].astype(jnp.float32)
        filt_imag = picked[:, half_rows:].astype(jnp.float32)
        sig_real = spectrum[None, :half_rows].astype(jnp.float32)
        sig_imag = spectrum[None, half_rows:].astype(jnp.float32)
        real_part = filt_real * sig_real - filt_imag * sig_imag
        imag_part = filt_real * sig_imag + filt_imag * sig_real
        return spectra_sum + causal * jnp.concatenate([real_part, imag_part], 1)

    empty = jnp.zeros((my_groups, 2 * half_rows, chan_width), jnp.float32)

    def advance(running, element):
        spectrum = jnp.dot(fwd_head, element[0], preferred_element_type=jnp.float32).astype(
            jnp.bfloat16
        )
        return (accumulate(running, spectrum, element[1]), None)

    running, _ = lax.scan(
        advance,
        empty,
        (
            lax.all_gather(signal.reshape(my_groups, BLOCK, chan_width), "seq", axis=0, tiled=True),
            group_order,
        ),
    )
    out_spectrum = running.astype(jnp.bfloat16)
    convolved = jnp.einsum(
        "rk,nkc->nrc", inverse, out_spectrum, preferred_element_type=jnp.float32
    ).reshape(tok_rows, chan_width)
    mixed = (
        query.astype(jnp.float32) * (convolved + skip_gain[None, :] * signal.astype(jnp.float32))
    ).astype(jnp.bfloat16)
    return lax.psum_scatter(
        lax.dot_general(
            out_weight, mixed, (((0,), (1,)), ((), ())), preferred_element_type=jnp.float32
        ).astype(jnp.bfloat16),
        "chan",
        scatter_dimension=0,
        tiled=True,
    ).astype(jnp.float32)


def solution(mesh):
    return jax.shard_map(
        local,
        mesh=mesh,
        in_specs=(
            P("seq", "chan"),
            P("seq", "chan"),
            P("seq", "chan"),
            P(),
            P(),
            P(),
            P(),
            P(),
            P(None, "chan"),
            P("chan"),
            P("chan"),
            P("chan", None),
        ),
        out_specs=P("chan", "seq"),
        check_vma=False,
    )
```

profile of v0, /device:TPU:0, one launch (start us, length us, event | category | flops | bytes accessed | tf_op | source)
XLA Modules:
  0.0 414.4 jit_solution(10690862169828464235)
XLA Ops:
  14.6 74.0 %all-gather.3.cloned.1.call-done = bf16[2048,1024]{1,0:T(8,128)(2,1)} async-done(((bf16[256,1024]{1,0:T(8,128)(2,1)}), bf16[2048,1024]{1,0:T(8,128)(2,1)}) %all-gather.3.cloned.1.call-update) | async-done | bytes 4194320 | tf_op jit(solution)/shard_map/all_gather | solution.py:87
  93.2 53.1 %while.21 = (s32[]{:T(128)}, bf16[16,258,1024]{2,1,0:T(8,128)(2,1)}, bf16[16,128,1024]{2,1,0:T(8,128)(2,1)}, bf16[258,128]{1,0:T(8,128)(2,1)S(1)}, bf16[16,128,1...) while((s32[]{:T(128)}, bf16[16,258,1024]{2,1,0:T(8,128)(2,1)}, ...), condition=%wide.region_1.2_spmd, body=%wide.region_0.1_spmd.sunk | while | flops 135794688 | bytes 3312205 | solution.py:96
  146.3 16.2 %all-gather.5.cloned.1.call-done = bf16[16,128,1024]{2,1,0:T(8,128)(2,1)} async-done(((bf16[2,128,1024]{2,1,0:T(8,128)(2,1)}), bf16[16,128,1024]{2,1,0:T(8,128)(2,1)}) %all-gather.5.cloned.1.call-update) | async-done | bytes 4194320 | tf_op jit(solution)/shard_map/all_gather | solution.py:122
  162.5 203.8 %while.22 = (s32[]{:T(128)}, f32[2,258,1024]{2,1,0:T(8,128)}, s32[16]{0:T(128)S(1)}, s32[2]{0:T(128)S(1)}, bf16[16,258,1024]{2,1,0:T(8,128)(2,1)}, /*index=5*/bf...) while((s32[]{:T(128)}, f32[2,258,1024]{2,1,0:T(8,128)}, ...), condition=%wide.region_3.4_spmd.clone, body=%wide.region_2.3_spmd.clone.sunk | while | flops 72389640 | bytes 15127731 | solution.py:118
  163.7 4.1 gather_fusion
  175.8 4.1 gather_fusion
  183.3 4.0 fusion.96
  188.6 4.1 gather_fusion
  196.1 4.0 fusion.96
  201.4 4.1 gather_fusion
  214.1 4.1 gather_fusion
  226.9 4.1 gather_fusion
  239.7 4.1 gather_fusion
  252.5 4.1 gather_fusion
  265.3 4.1 gather_fusion
  278.0 4.1 gather_fusion
  290.8 4.1 gather_fusion
  303.6 4.1 gather_fusion
  316.4 4.1 gather_fusion
  329.2 4.1 gather_fusion
  341.9 4.1 gather_fusion
  354.7 4.1 gather_fusion
  368.7 7.1 %fusion.17 = bf16[4096,256]{0,1:T(8,128)(2,1)} fusion(bf16[256,1024]{1,0:T(8,128)(2,1)S(1)} %fusion.27, bf16[1024,4096]{1,0:T(8,128)(2,1)} %param.27), kind=kOutput, calls=%fused_computation.31 | convolution fusion | flops 2148532224 | bytes 11010048 | tf_op jit(solution)/shard_map/dot_general | solution.py:134
  375.8 29.8 %reduce-scatter.2.cloned.1.call-done = bf16[1024,256]{0,1:T(8,128)(2,1)} async-done(((bf16[4096,256]{0,1:T(8,128)(2,1)}), bf16[1024,256]{0,1:T(8,128)(2,1)}) %reduce-scatter.2.cloned.1.call-update) | async-done | bytes 524304 | tf_op jit(solution)/shard_map/reduce_scatter | solution.py:133
  (204 shorter events, 199.9 us)
Async XLA Ops:
  6.5 4.0 copy-start
  6.5 5.9 %copy-start.3 = (bf16[256,1024]{1,0:T(8,128)(2,1)S(1)}, bf16[256,1024]{1,0:T(8,128)(2,1)}, u32[]{:S(2)}) copy-start(bf16[256,1024]{1,0:T(8,128)(2,1)} %param.17) | copy-start | bytes 1572868
  6.5 5.9 %copy-start.2 = (bf16[256,1024]{1,0:T(8,128)(2,1)S(1)}, bf16[256,1024]{1,0:T(8,128)(2,1)}, u32[]{:S(2)}) copy-start(bf16[256,1024]{1,0:T(8,128)(2,1)} %param.18) | copy-start | bytes 1572868
  6.5 82.1 %all-gather.3.cloned.1.call-start = ((), (), s32[]{:S(2)}) async-start(), calls=%async_computation.1 | async-start | bytes 4718592 | tf_op jit(solution)/shard_map/all_gather | solution.py:87
  10.5 4.0 copy-start.6
  12.4 150.1 %all-gather.5.cloned.1.call-start = ((), (), s32[]{:S(2)}) async-start(), calls=%async_computation.2 | async-start | bytes 4718592 | tf_op jit(solution)/shard_map/all_gather | solution.py:122
  13.5 392.2 %reduce-scatter.2.cloned.1.call-start = ((), (), s32[]{:S(2)}) async-start(), calls=%async_computation.3 | async-start | bytes 2621440 | tf_op jit(solution)/shard_map/reduce_scatter | solution.py:133
  88.7 2.1 slice-start
  366.3 2.2 copy-start.1
  366.3 2.2 copy-start.4
  366.3 2.2 copy-start.5
Sparse Core Ops, SparseCore 0:
  12.5 76.0 all-gather.2
  90.8 71.6 all-gather.4
  375.9 29.6 reduce-scatter.1
where the time goes:
time: 417 us; the launch traced here: 414 us
  waiting for transfers between devices  120 us (29%)
  other arithmetic  112 us (27%)
  matrix products  87 us (21%)
  local copies, waits for them, and re-layouts  81.3 us (19%)
  between operations  13.3 us (3%)
    all_gather x1, waiting for transfers between devices, local(): whole_filter = lax.all_gather(own_rows, 'seq', axis=0, tiled=True)  74 us
    gather x16, local copies, waits for them, and re-layouts, accumulate(): picked = filter_spectrum[jnp.maximum(lag_index, 0)]  65.2 us
    add x16, other arithmetic, accumulate(): return spectra_sum + causal * jnp.concatenate([real_part, imag_part], 1)  63.5 us
    dot_general x16, matrix products, block_spectrum(): jnp.dot(fwd_tail, blocks_pair[1], preferred_element_type=jnp.float32)  33.1 us
    reduce_scatter x1, waiting for transfers between devices, local(): lax.psum_scatter(lax.dot_general(out_weight, mixed, (((0,), (1,)), ((), (...  29.8 us
    sub x16, other arithmetic, accumulate(): real_part = filt_real * sig_real - filt_imag * sig_imag  22.4 us
    dot_general x16, matrix products, advance(): jnp.dot(fwd_head, element[0], preferred_element_type=jnp.float32)  19.9 us
    dot_general x16, matrix products, block_spectrum(): jnp.dot(fwd_head, blocks_pair[0], preferred_element_type=jnp.float32)  19.9 us
  transfers between devices with their start and end apart: 3, of which 3 were waited for; matrix products, arithmetic and copies ran while one was open for 14% of the time, Pallas kernels for 0%

commit v1 on v0

v1 whole, which is shorter than its diff:
```python
import functools
import math

import jax
import jax.numpy as jnp
import numpy as np
from jax import lax
from jax.experimental import pallas as pl
from jax.experimental.pallas import tpu as pltpu
from jax.sharding import PartitionSpec as P

GROUP = 128
LANES = 128
SINE_FREQ = 2.0
F32 = jnp.float32
BF16 = jnp.bfloat16


def packed_tables(block):
    period = 2 * block
    row = np.arange(block)
    freq = np.arange(block)

    def forward(shift):
        angle = 2.0 * np.pi * (freq[:, None] * (row[None, :] + shift) % period) / period
        real, imag = np.cos(angle), -np.sin(angle)
        imag[0] = np.where((row + shift) % 2 == 0, 1.0, -1.0)
        return np.concatenate([real, imag], 0)

    head, tail = forward(0), forward(block)
    tail[:, 0] = 0.0
    weight = np.where(freq == 0, 1.0, 2.0) / period
    angle = 2.0 * np.pi * (row[:, None] * freq[None, :] % period) / period
    real, imag = np.cos(angle) * weight, -np.sin(angle) * weight
    imag[:, 0] = np.where(row % 2 == 0, 1.0, -1.0) / period
    inverse = np.concatenate([real, imag], 1)
    to_bf16 = lambda table: jnp.asarray(table.astype(np.float32)).astype(BF16)
    return to_bf16(head), to_bf16(np.concatenate([head, tail], 1)), to_bf16(inverse)


def feature_table(length, bands, rows):
    lag = np.arange(length)
    angle = 2.0 * np.pi * (np.arange(1, bands + 1)[:, None] * lag[None, :] % length) / length
    table = np.zeros((rows, length), np.float32)
    table[0] = lag / length
    table[1 : bands + 1] = np.cos(angle)
    table[bands + 1 : 2 * bands + 1] = np.sin(angle)
    table[2 * bands + 1] = 1.0
    return jnp.asarray(table)


def gated_kernel(key_ref, value_ref, out_ref):
    width = out_ref.shape[2]
    for j in range(out_ref.shape[0]):
        cols = slice(j * width, (j + 1) * width)
        out_ref[j] = (key_ref[:, cols].astype(F32) * value_ref[:, cols].astype(F32)).astype(BF16)


def contract_first(lhs, rhs):
    return lax.dot_general(
        lhs, rhs, (((0,), (0,)), ((), ())), precision=lax.Precision.HIGHEST, preferred_element_type=F32
    )


def filter_kernel(
    block, index_ref, feat_ref, emb_w_ref, emb_b_ref, mid_w_ref, mid_b_ref, out_w_ref, decay_ref, norm_ref, table_ref,
    real_ref, imag_ref, edge_ref, w1, w2, hid, filt,
):
    emb, order = emb_w_ref.shape
    length = feat_ref.shape[1]
    blocks = length // block
    w1[...] = jnp.zeros_like(w1)
    w1[0:emb, :] = emb_w_ref[...]
    w1[emb : emb + 1, :] = emb_b_ref[...]
    w2[...] = jnp.zeros_like(w2)
    w2[0:order, :] = mid_w_ref[...]
    w2[order : order + 1, :] = mid_b_ref[...]
    hid[order:, :] = jnp.ones_like(hid[order:, :])
    hid[0:order, :] = jnp.sin(SINE_FREQ * contract_first(w1[...], feat_ref[...]))
    hidden = jnp.sin(SINE_FREQ * contract_first(w2[...], hid[...]))
    raw = contract_first(hidden, out_w_ref[...])
    decay = decay_ref[...]
    within = jnp.exp(-decay * lax.broadcasted_iota(jnp.int32, (block, LANES), 0).astype(F32))
    within = within * norm_ref[...]
    filt[0:block, :] = jnp.zeros((block, LANES), BF16)
    for m in range(blocks):
        start = jnp.exp(-decay * float(m * block))
        filt[(m + 1) * block : (m + 2) * block, :] = (raw[m * block : (m + 1) * block] * (within * start)).astype(BF16)
    first_row = lax.broadcasted_iota(jnp.int32, (16, LANES), 0) == 0
    group = 2
    for m0 in range(0, blocks, group):
        stacked = jnp.concatenate(
            [
                jnp.concatenate(
                    [filt[(m + 1) * block : (m + 2) * block, :], filt[m * block : (m + 1) * block, :]], 0
                )
                for m in range(m0, m0 + group)
            ],
            1,
        )
        spectrum = jnp.dot(table_ref[...], stacked, preferred_element_type=F32)
        for i in range(group):
            m = m0 + i
            real = spectrum[:block, i * LANES : (i + 1) * LANES]
            imag = spectrum[block:, i * LANES : (i + 1) * LANES]
            real_ref[m] = real
            imag_ref[m] = imag
            edge_ref[m] = jnp.where(first_row, imag[:16], real[:16])
            imag_ref[m, 0:16, :] = jnp.where(first_row, 0.0, imag[:16])


def conv_kernel(
    block, order_ref, x_ref, real_ref, imag_ref, edge_ref, head_ref, inverse_ref, out_ref, sig, sre, sim, spec, conv
):
    slots = x_ref.shape[0]
    length = slots * GROUP
    blocks = length // block
    for p in range(slots):
        start = pl.multiple_of(order_ref[p] * GROUP, GROUP)
        sig[pl.ds(start, GROUP), :] = x_ref[p]
    group = 2
    for b0 in range(0, blocks, group):
        stacked = jnp.concatenate([sig[b * block : (b + 1) * block, :] for b in range(b0, b0 + group)], 1)
        spectrum = jnp.dot(head_ref[...], stacked, preferred_element_type=F32)
        for i in range(group):
            sre[b0 + i] = spectrum[:block, i * LANES : (i + 1) * LANES]
            sim[b0 + i] = spectrum[block:, i * LANES : (i + 1) * LANES]

    def tile(start, first):
        rows = pl.ds(start, 16)
        mirror = pl.ds(block + start, 16)
        s_real = [sre[q, rows, :] for q in range(blocks)]
        s_imag = [sim[q, rows, :] for q in range(blocks)]
        for g in range(blocks):
            acc_real = acc_imag = None
            for q in range(g + 1):
                fr, fi = real_ref[g - q, rows, :], imag_ref[g - q, rows, :]
                fe = edge_ref[g - q] if first else fr
                re = fr * s_real[q] - fi * s_imag[q]
                im = fe * s_imag[q] + fi * s_real[q]
                acc_real = re if q == 0 else acc_real + re
                acc_imag = im if q == 0 else acc_imag + im
            spec[rows, g * LANES : (g + 1) * LANES] = acc_real.astype(BF16)
            spec[mirror, g * LANES : (g + 1) * LANES] = acc_imag.astype(BF16)

    tile(0, True)

    @pl.loop(1, block // 16)
    def _(t):
        tile(pl.multiple_of(t * 16, 16), False)

    result = jnp.dot(inverse_ref[...], spec[...], preferred_element_type=F32)
    for g in range(blocks):
        conv[g * block : (g + 1) * block, :] = result[:, g * LANES : (g + 1) * LANES].astype(BF16)
    for p in range(slots):
        start = pl.multiple_of(order_ref[p] * GROUP, GROUP)
        out_ref[p] = conv[pl.ds(start, GROUP), :]


def mixed_kernel(query_ref, conv_ref, sig_ref, gain_ref, out_ref):
    width = conv_ref.shape[2]
    for j in range(conv_ref.shape[0]):
        cols = slice(j * width, (j + 1) * width)
        inner = conv_ref[j].astype(F32) + gain_ref[:, cols] * sig_ref[j].astype(F32)
        out_ref[:, cols] = (query_ref[:, cols].astype(F32) * inner).astype(BF16)


def project_kernel(index_ref, mixed_ref, weight_ref, out_ref):
    out_ref[0] = jnp.dot(mixed_ref[...], weight_ref[...], preferred_element_type=F32).astype(BF16)


def project(owners, mixed, out_weight, width):
    rows, depth = mixed.shape
    tile = min(width, 512)
    count = owners.shape[0]
    return pl.pallas_call(
        project_kernel,
        out_shape=jax.ShapeDtypeStruct((count, rows, width), BF16),
        grid_spec=pltpu.PrefetchScalarGridSpec(
            num_scalar_prefetch=1,
            grid=(count, width // tile),
            in_specs=[
                pl.BlockSpec((rows, depth), lambda j, t, o: (0, 0)),
                pl.BlockSpec((depth, tile), lambda j, t, o: (0, o[j] * (width // tile) + t)),
            ],
            out_specs=pl.BlockSpec((1, rows, tile), lambda j, t, o: (j, 0, t)),
        ),
    )(owners, mixed, out_weight)


def local(
    query, key_gate, value, group_order, emb_weight, emb_bias, mid_weight, mid_bias, out_filter, decay_rate, skip_gain,
    out_weight,
):
    rows, chan_width = query.shape
    seq_count, chan_count = lax.axis_size("seq"), lax.axis_size("chan")
    seq_index, chan_index = lax.axis_index("seq"), lax.axis_index("chan")
    length = rows * seq_count
    slots = length // GROUP
    width = chan_width // seq_count
    block = max(GROUP, length // 16)
    blocks = length // block
    emb, order = emb_weight.shape
    head, head_tail, inverse = packed_tables(block)
    feat_rows = -(-(emb + 1) // 8) * 8
    features = feature_table(length, (emb - 1) // 2, feat_rows)
    vmem = pltpu.CompilerParams(vmem_limit_bytes=48 << 20)

    signal = pl.pallas_call(
        gated_kernel,
        out_shape=jax.ShapeDtypeStruct((seq_count, rows, width), BF16),
    )(key_gate, value)
    spread = lax.all_to_all(signal, "seq", 0, 0, tiled=True).reshape(slots, GROUP, width)

    my_filter = lax.dynamic_slice_in_dim(out_filter, seq_index * width, width, 1)
    my_decay = lax.dynamic_slice_in_dim(decay_rate, seq_index * width, width)[None, :]
    norm = jnp.sqrt(-jnp.expm1(-2.0 * my_decay))
    pad = [(0, 0), (0, LANES - width)]
    if width < LANES:
        my_filter, my_decay, norm = jnp.pad(my_filter, pad), jnp.pad(my_decay, pad), jnp.pad(norm, pad)
        spread = jnp.pad(spread, [(0, 0)] + pad)
    real, imag, edge = pl.pallas_call(
        functools.partial(filter_kernel, block, None),
        out_shape=(
            jax.ShapeDtypeStruct((blocks, block, LANES), F32),
            jax.ShapeDtypeStruct((blocks, block, LANES), F32),
            jax.ShapeDtypeStruct((blocks, 16, LANES), F32),
        ),
        scratch_shapes=[
            pltpu.VMEM((feat_rows, order), F32),
            pltpu.VMEM((order + 8, order), F32),
            pltpu.VMEM((order + 8, length), F32),
            pltpu.VMEM((length + block, LANES), BF16),
        ],
        compiler_params=vmem,
    )(features, emb_weight, emb_bias[None, :], mid_weight, mid_bias[None, :], my_filter, my_decay, norm, head_tail)

    convolved = pl.pallas_call(
        functools.partial(conv_kernel, block),
        out_shape=jax.ShapeDtypeStruct((slots, GROUP, LANES), BF16),
        in_specs=[pl.BlockSpec(memory_space=pltpu.SMEM)] + [pl.BlockSpec(memory_space=pltpu.VMEM)] * 6,
        scratch_shapes=[
            pltpu.VMEM((length, LANES), BF16),
            pltpu.VMEM((blocks, block, LANES), F32),
            pltpu.VMEM((blocks, block, LANES), F32),
            pltpu.VMEM((2 * block, blocks * LANES), BF16),
            pltpu.VMEM((length, LANES), BF16),
        ],
        compiler_params=vmem,
    )(group_order, spread, real, imag, edge, head, inverse)
    if width < LANES:
        convolved = convolved[:, :, :width]
    back = lax.all_to_all(convolved.reshape(seq_count, rows, width), "seq", 0, 0, tiled=True)

    mixed = pl.pallas_call(
        mixed_kernel,
        out_shape=jax.ShapeDtypeStruct((rows, chan_width), BF16),
        compiler_params=vmem,
    )(query, back, signal, skip_gain[None, :])

    out_width = out_weight.shape[1] // chan_count
    half = chan_count // 2
    odd = chan_index ^ jnp.arange(1, chan_count, 2, dtype=jnp.int32)
    even = chan_index ^ jnp.arange(0, chan_count, 2, dtype=jnp.int32)
    away = project(odd, mixed, out_weight, out_width)
    terms = lax.ppermute(away, "chan", [(i, i ^ 1) for i in range(chan_count)])
    kept = project(even, mixed, out_weight, out_width)
    bit = 2
    total = kept.astype(F32) + terms.astype(F32)
    while bit < chan_count:
        send, keep = total[1::2].astype(BF16), total[0::2]
        total = keep + lax.ppermute(send, "chan", [(i, i ^ bit) for i in range(chan_count)]).astype(F32)
        bit *= 2
    return total[0].T


def solution(mesh):
    return jax.shard_map(
        local,
        mesh=mesh,
        in_specs=(
            P("seq", "chan"), P("seq", "chan"), P("seq", "chan"), P(), P(), P(), P(), P(), P(None, "chan"), P("chan"),
            P("chan"), P("chan", None),
        ),
        out_specs=P("chan", "seq"),
        check_vma=False,
    )
```

time: 417 us -> 80.8 us (0.19)
  other arithmetic: 112 us -> 3.58 us
  matrix products: 87 us -> 0 us
  waiting for transfers between devices: 120 us -> 34.7 us
  local copies, waits for them, and re-layouts: 81.3 us -> 4.94 us
  Pallas kernels: 0 us -> 24.2 us
  between operations: 13.3 us -> 0.14 us
  starting transfers between devices: 0.09 us -> 12.5 us
    all_gather x2 -> x0, waiting for transfers between devices: 90.2 us -> none  [the longest x1 74 us: local(): whole_filter = lax.all_gather(own_rows, 'seq', axis=0, tiled=True)]
    dot_general x53 -> x0, matrix products: 87 us -> none  [the longest x16 33.1 us: block_spectrum(): jnp.dot(fwd_tail, blocks_pair[1], preferred_element_type=jnp.float32)]
    gather x16 -> x0, local copies, waits for them, and re-layouts: 65.2 us -> none  [accumulate(): picked = filter_spectrum[jnp.maximum(lag_index, 0)]]
    add x19 -> x1, other arithmetic: 63.5 us -> 1.61 us  [local(): total = kept.astype(F32) + terms.astype(F32)]
    reduce_scatter x1 -> x0, waiting for transfers between devices: 29.8 us -> none  [local(): lax.psum_scatter(lax.dot_general(out_weight, mixed, (((0,), (1,)), ((), (...]
    pallas_call x0 -> x6, Pallas kernels: none -> 24.2 us  [the longest x2 11.3 us: project(): pl.pallas_call(project_kernel, out_shape=jax.ShapeDtypeStruct((count, row...]
    sub x16 -> x0, other arithmetic: 22.4 us -> none  [accumulate(): real_part = filt_real * sig_real - filt_imag * sig_imag]
    all_to_all x0 -> x2, waiting for transfers between devices: none -> 21.9 us  [the longest x1 14.2 us: local(): lax.all_to_all(convolved.reshape(seq_count, rows, width), 'seq', 0, 0, ti...]
  transfers between devices with their start and end apart: 3 -> 4, of which waited for: 3 -> 3; matrix products, arithmetic and copies ran while one was open for 14% -> 2% of each run, Pallas kernels for 0% -> 14%
where the time goes in v1:
time: 80.8 us; the launch traced here: 80.1 us
  waiting for transfers between devices  34.7 us (43%)
  Pallas kernels  24.2 us (30%)
  starting transfers between devices  12.5 us (15%)
  local copies, waits for them, and re-layouts  4.94 us (6%)
  other arithmetic  3.58 us (4%)
    all_to_all x1, waiting for transfers between devices, local(): lax.all_to_all(convolved.reshape(seq_count, rows, width), 'seq', 0, 0, ti...  14.2 us
    ppermute x1, waiting for transfers between devices, local(): lax.ppermute(send, 'chan', [(i, i ^ bit) for i in range(chan_count)])  12.8 us
    pallas_call x2, Pallas kernels, project(): pl.pallas_call(project_kernel, out_shape=jax.ShapeDtypeStruct((count, row...  11.3 us
    all_to_all x1, waiting for transfers between devices, local(): lax.all_to_all(signal, 'seq', 0, 0, tiled=True).reshape(slots, GROUP, width)  7.74 us
    all_to_all x1, starting transfers between devices, local(): lax.all_to_all(signal, 'seq', 0, 0, tiled=True).reshape(slots, GROUP, width)  7.26 us
    pallas_call x1, Pallas kernels, local(): pl.pallas_call(functools.partial(filter_kernel, block, None), out_shape=(...  5.89 us
    pallas_call x1, Pallas kernels, local(): pl.pallas_call(functools.partial(conv_kernel, block), out_shape=jax.Shape...  4.57 us
    all_to_all x1, starting transfers between devices, local(): lax.all_to_all(convolved.reshape(seq_count, rows, width), 'seq', 0, 0, ti...  3.64 us
  transfers between devices with their start and end apart: 4, of which 3 were waited for; matrix products, arithmetic and copies ran while one was open for 2% of the time, Pallas kernels for 14%

profile of v1, /device:TPU:0, one launch (start us, length us, event | category | flops | bytes accessed | tf_op | source)
XLA Modules:
  0.0 80.1 jit_solution(16760125742854273366)
XLA Ops:
  0.1 2.2 %shard_map.154.sig_ref = bf16[8,256,128]{2,1,0:T(8,128)(2,1)} custom-call(bf16[256,1024]{1,0:T(8,128)(2,1)} %key_ref.1, bf16[256,1024]{1,0:T(8,128)(2,1)} %value_ref.1), custom_call_target="tpu_custom_call" | custom-call | tf_op jit(solution)/shard_map/pallas_call | solution.py:209
  2.3 7.3 %all-to-all-start = ((bf16[8,256,128]{2,1,0:T(8,128)(2,1)}), bf16[8,256,128]{2,1,0:T(8,128)(2,1)S(1)}, u32[]{:S(2)}, u32[]{:S(2)}) async-start(bf16[8,256,128]{2,1,0:T(8,128)(2,1)} %shard_map.154.sig_ref), calls=%async_computation | async-start | bytes 1048576 | tf_op jit(solution)/shard_map/all_to_all | solution.py:213
  9.5 0.8 sqrt_bitcast_fusion
  10.4 5.9 %shard_map.155 = (f32[16,128,128]{2,1,0:T(8,128)S(1)}, f32[16,128,128]{2,1,0:T(8,128)S(1)}, f32[16,16,128]{2,1,0:T(8,128)S(1)}) custom-call(f32[40,2048]{1,0:T(8,128)S(1)} %copy-done.4, f32[33,64]{1,0:T(8,128)S(1)} %copy-done.9, f32[1,64]{1,0:T(1,128)S(1)} %bitcast.15, f32[64,64]{1,0:T(8,128)S(1)} %copy-done.8, f32[1,64]{1,0:T(1,128)S(1)} %bitcast.16, ...), custom_call_target="tpu_custom_call" | custom-call | tf_op jit(solution)/shard_map/pallas_call | solution.py:222
  16.3 7.7 %all-to-all-done = bf16[8,256,128]{2,1,0:T(8,128)(2,1)S(1)} async-done(((bf16[8,256,128]{2,1,0:T(8,128)(2,1)}), bf16[8,256,128]{2,1,0:T(8,128)(2,1)S(1)}, u32[]{:S(2)}, u32[]{:S(2)}) %all-to-all-start) | async-done | bytes 524320 | tf_op jit(solution)/shard_map/all_to_all | solution.py:213
  24.0 0.8 %copy-done.6 = bf16[128,256]{1,0:T(8,128)(2,1)S(1)} copy-done((bf16[128,256]{1,0:T(8,128)(2,1)S(1)}, bf16[128,256]{1,0:T(8,128)(2,1)}, u32[]{:S(2)}) %copy-start.6) | copy-done | bytes 65560
  24.9 0.8 %copy-done.7 = bf16[256,128]{1,0:T(8,128)(2,1)S(1)} copy-done((bf16[256,128]{1,0:T(8,128)(2,1)S(1)}, bf16[256,128]{1,0:T(8,128)(2,1)}, u32[]{:S(2)}) %copy-start.7) | copy-done | bytes 65560
  25.7 4.6 %shard_map.156 = bf16[16,128,128]{2,1,0:T(8,128)(2,1)} custom-call(s32[16]{0:T(128)S(1)} %copy-done.11, bf16[16,128,128]{2,1,0:T(8,128)(2,1)S(1)} %bitcast.13, f32[16,128,128]{2,1,0:T(8,128)S(1)} %get-tuple-element.8.real_ref, f32[16,128,128]{2,1,0:T(8,128)S(1)} %get-tuple-element.9.imag_ref, f32[16,16,128]{2,1,0:T(8,128)S(1)} %get-tuple-element.10.edge_ref, ...), custom_call_target="tpu_custom_call" | custom-call | tf_op jit(solution)/shard_map/pallas_call | solution.py:238
  30.3 3.6 %all-to-all-start.1 = ((bf16[8,256,128]{2,1,0:T(8,128)(2,1)}), bf16[8,256,128]{2,1,0:T(8,128)(2,1)S(1)}, u32[]{:S(2)}, u32[]{:S(2)}) async-start(bf16[8,256,128]{2,1,0:T(8,128)(2,1)} %bitcast.5), calls=%async_computation.1 | async-start | bytes 1048576 | tf_op jit(solution)/shard_map/all_to_all | solution.py:253
  33.9 0.5 add_xor_fusion.index_ref
  34.4 14.2 %all-to-all-done.1.conv_ref = bf16[8,256,128]{2,1,0:T(8,128)(2,1)S(1)} async-done(((bf16[8,256,128]{2,1,0:T(8,128)(2,1)}), bf16[8,256,128]{2,1,0:T(8,128)(2,1)S(1)}, u32[]{:S(2)}, u32[]{:S(2)}) %all-to-all-start.1) | async-done | bytes 524320 | tf_op jit(solution)/shard_map/all_to_all | solution.py:253
  48.6 1.0 %copy-done.3 = bf16[256,1024]{1,0:T(8,128)(2,1)S(1)} copy-done((bf16[256,1024]{1,0:T(8,128)(2,1)S(1)}, bf16[256,1024]{1,0:T(8,128)(2,1)}, u32[]{:S(2)}) %copy-start.3) | copy-done | bytes 524312
  49.6 0.2 shard_map.157.mixed_ref
  49.9 0.8 copy-done.1
  50.7 5.6 %shard_map.159 = bf16[2,256,1024]{2,1,0:T(8,128)(2,1)} custom-call(s32[2]{0:T(128)} %add_xor_fusion.index_ref, bf16[256,1024]{1,0:T(8,128)(2,1)} %copy-done.1, bf16[1024,4096]{1,0:T(8,128)(2,1)} %weight_ref.3), custom_call_target="tpu_custom_call" | custom-call | tf_op jit(solution)/shard_map/pallas_call | solution.py:176
  56.3 0.0 collective-permute-start
  56.3 0.5 fusion.1.index_ref
  56.8 5.7 %shard_map.158 = bf16[2,256,1024]{2,1,0:T(8,128)(2,1)} custom-call(s32[2]{0:T(128)} %fusion.1.index_ref, bf16[256,1024]{1,0:T(8,128)(2,1)} %copy-done.1, bf16[1024,4096]{1,0:T(8,128)(2,1)} %weight_ref.3), custom_call_target="tpu_custom_call" | custom-call | tf_op jit(solution)/shard_map/pallas_call | solution.py:176
  62.5 1.6 %convert_add_fusion = f32[2,256,1024]{2,1,0:T(8,128)S(1)} fusion(bf16[2,256,1024]{2,1,0:T(8,128)(2,1)S(1)} %collective-permute-done, bf16[2,256,1024]{2,1,0:T(8,128)(2,1)} %shard_map.158), kind=kLoop, calls=%fused_computation | loop fusion | flops 1572864 | bytes 4194304 | tf_op jit(solution)/shard_map/add | solution.py:269
  64.1 0.1 slice.17
  64.2 1.6 %collective-permute-start.1 = (bf16[1,256,1024]{2,1,0:T(8,128)(2,1)S(1)}, bf16[1,256,1024]{2,1,0:T(8,128)(2,1)S(1)}, u32[]{:S(2)}, u32[]{:S(2)}) collective-permute-start(bf16[1,256,1024]{2,1,0:T(8,128)(2,1)S(1)} %slice.17), channel_id=1, source_target_pairs={{0,2},{1,3},{2,0},{3,1},{4,6},{5,7},{6,4},{7,5},{8,10},{9,11},{10,... | collective-permute-start | bytes 1572872 | tf_op jit(solution)/shard_map/ppermute | solution.py:272
  65.8 12.8 %collective-permute-done.1 = bf16[1,256,1024]{2,1,0:T(8,128)(2,1)S(1)} collective-permute-done((bf16[1,256,1024]{2,1,0:T(8,128)(2,1)S(1)}, bf16[1,256,1024]{2,1,0:T(8,128)(2,1)S(1)}, u32[]{:S(2)}, u32[]{:S(2)}) %collective-permute-start.1) | collective-permute-done | bytes 524320 | tf_op jit(solution)/shard_map/ppermute | solution.py:272
  78.6 0.2 fusion
  78.8 1.3 %copy.17 = f32[1024,256]{1,0:T(8,128)} copy(f32[1024,256]{0,1:T(8,128)S(1)} %fusion) | data formatting | bytes 2097152 | tf_op jit(solution)/shard_map/transpose | solution.py:274
  (26 shorter events, 0.1 us)
Async XLA Ops:
  0.0 10.3 %copy-start = (f32[64,1024]{1,0:T(8,128)S(1)}, f32[64,1024]{1,0:T(8,128)}, u32[]{:S(2)}) copy-start(f32[64,1024]{1,0:T(8,128)} %param.24) | copy-start | bytes 786436
  0.0 10.3 %copy-start.5 = (bf16[256,256]{1,0:T(8,128)(2,1)S(1)}, bf16[256,256]{1,0:T(8,128)(2,1)}, u32[]{:S(2)}) copy-start(bf16[256,256]{1,0:T(8,128)(2,1)} %constant.33.table_ref) | copy-start | bytes 393220
  0.0 10.3 %copy-start.4 = (f32[40,2048]{1,0:T(8,128)S(1)}, f32[40,2048]{1,0:T(8,128)}, u32[]{:S(2)}) copy-start(f32[40,2048]{1,0:T(8,128)} %constant.32.clone.feat_ref) | copy-start | bytes 983044
  0.0 10.3 %copy-start.13 = (f32[64]{0:T(128)S(1)}, f32[64]{0:T(128)}, u32[]{:S(2)}) copy-start(f32[64]{0:T(128)} %param.23) | copy-start | bytes 772
  0.0 10.4 %copy-start.8 = (f32[64,64]{1,0:T(8,128)S(1)}, f32[64,64]{1,0:T(8,128)}, u32[]{:S(2)}) copy-start(f32[64,64]{1,0:T(8,128)} %mid_w_ref.1) | copy-start | bytes 49156
  0.0 10.4 %copy-start.12 = (f32[64]{0:T(128)S(1)}, f32[64]{0:T(128)}, u32[]{:S(2)}) copy-start(f32[64]{0:T(128)} %param.21) | copy-start | bytes 772
  0.0 10.4 %copy-start.9 = (f32[33,64]{1,0:T(8,128)S(1)}, f32[33,64]{1,0:T(8,128)}, u32[]{:S(2)}) copy-start(f32[33,64]{1,0:T(8,128)} %emb_w_ref.1) | copy-start | bytes 25348
  0.0 24.0 %copy-start.11 = (s32[16]{0:T(128)S(1)}, s32[16]{0:T(128)}, u32[]{:S(2)}) copy-start(s32[16]{0:T(128)} %order_ref.1) | copy-start | bytes 196
  2.3 21.7 %all-to-all-start = ((bf16[8,256,128]{2,1,0:T(8,128)(2,1)}), bf16[8,256,128]{2,1,0:T(8,128)(2,1)S(1)}, u32[]{:S(2)}, u32[]{:S(2)}) async-start(bf16[8,256,128]{2,1,0:T(8,128)(2,1)} %shard_map.154.sig_ref), calls=%async_computation | async-start | bytes 1048576 | tf_op jit(solution)/shard_map/all_to_all | solution.py:213
  24.0 0.8 %copy-start.6 = (bf16[128,256]{1,0:T(8,128)(2,1)S(1)}, bf16[128,256]{1,0:T(8,128)(2,1)}, u32[]{:S(2)}) copy-start(bf16[128,256]{1,0:T(8,128)(2,1)} %constant.35.inverse_ref) | copy-start | bytes 196612
  24.9 0.8 %copy-start.7 = (bf16[256,128]{1,0:T(8,128)(2,1)S(1)}, bf16[256,128]{1,0:T(8,128)(2,1)}, u32[]{:S(2)}) copy-start(bf16[256,128]{1,0:T(8,128)(2,1)} %constant.34.head_ref) | copy-start | bytes 196612
  25.7 22.9 %copy-start.2 = (bf16[8,256,128]{2,1,0:T(8,128)(2,1)S(1)}, bf16[8,256,128]{2,1,0:T(8,128)(2,1)}, u32[]{:S(2)}) copy-start(bf16[8,256,128]{2,1,0:T(8,128)(2,1)} %shard_map.154.sig_ref) | copy-start | bytes 1572868
  25.7 22.9 %copy-start.10 = (f32[1024]{0:T(1024)S(1)}, f32[1024]{0:T(1024)}, u32[]{:S(2)}) copy-start(f32[1024]{0:T(1024)} %param.26) | copy-start | bytes 12292
  30.3 18.3 %all-to-all-start.1 = ((bf16[8,256,128]{2,1,0:T(8,128)(2,1)}), bf16[8,256,128]{2,1,0:T(8,128)(2,1)S(1)}, u32[]{:S(2)}, u32[]{:S(2)}) async-start(bf16[8,256,128]{2,1,0:T(8,128)(2,1)} %bitcast.5), calls=%async_computation.1 | async-start | bytes 1048576 | tf_op jit(solution)/shard_map/all_to_all | solution.py:253
  48.6 1.0 %copy-start.3 = (bf16[256,1024]{1,0:T(8,128)(2,1)S(1)}, bf16[256,1024]{1,0:T(8,128)(2,1)}, u32[]{:S(2)}) copy-start(bf16[256,1024]{1,0:T(8,128)(2,1)} %query_ref.1) | copy-start | bytes 1572868
  49.9 0.8 copy-start.1
  56.3 6.2 %collective-permute-start = (bf16[2,256,1024]{2,1,0:T(8,128)(2,1)}, bf16[2,256,1024]{2,1,0:T(8,128)(2,1)S(1)}, u32[]{:S(2)}, u32[]{:S(2)}) collective-permute-start(bf16[2,256,1024]{2,1,0:T(8,128)(2,1)} %shard_map.159), channel_id=1, source_target_pairs={{0,1},{1,0},{2,3},{3,2},{4,5},{5,4},{6,7},{7,6},{8,9},{9,8},{10,11... | collective-permute-start | bytes 3145736 | tf_op jit(solution)/shard_map/ppermute | solution.py:266
  64.2 14.4 %collective-permute-start.1 = (bf16[1,256,1024]{2,1,0:T(8,128)(2,1)S(1)}, bf16[1,256,1024]{2,1,0:T(8,128)(2,1)S(1)}, u32[]{:S(2)}, u32[]{:S(2)}) collective-permute-start(bf16[1,256,1024]{2,1,0:T(8,128)(2,1)S(1)} %slice.17), channel_id=1, source_target_pairs={{0,2},{1,3},{2,0},{3,1},{4,6},{5,7},{6,4},{7,5},{8,10},{9,11},{10,... | collective-permute-start | bytes 1572872 | tf_op jit(solution)/shard_map/ppermute | solution.py:272

commit v2 on v1

--- a/solution.py
+++ b/solution.py
@@ -49,13 +49,6 @@
     return jnp.asarray(table)
 
 
-def gated_kernel(key_ref, value_ref, out_ref):
-    width = out_ref.shape[2]
-    for j in range(out_ref.shape[0]):
-        cols = slice(j * width, (j + 1) * width)
-        out_ref[j] = (key_ref[:, cols].astype(F32) * value_ref[:, cols].astype(F32)).astype(BF16)
-
-
 def contract_first(lhs, rhs):
     return lax.dot_general(
         lhs, rhs, (((0,), (0,)), ((), ())), precision=lax.Precision.HIGHEST, preferred_element_type=F32
@@ -63,9 +56,16 @@
 
 
 def filter_kernel(
-    block, index_ref, feat_ref, emb_w_ref, emb_b_ref, mid_w_ref, mid_b_ref, out_w_ref, decay_ref, norm_ref, table_ref,
-    real_ref, imag_ref, edge_ref, w1, w2, hid, filt,
+    block, out_w_ref, decay_ref, norm_ref, feat_hbm, emb_w_hbm, emb_b_hbm, mid_w_hbm, mid_b_hbm, table_hbm,
+    head_hbm, inverse_hbm, real_ref, imag_ref, edge_ref, head_ref, inverse_ref, feat_ref, emb_w_ref, emb_b_ref, mid_w_ref, mid_b_ref, table_ref, w1, w2, hid, filt, sem,
 ):
+    sources = (feat_hbm, emb_w_hbm, emb_b_hbm, mid_w_hbm, mid_b_hbm, table_hbm, head_hbm, inverse_hbm)
+    targets = (feat_ref, emb_w_ref, emb_b_ref, mid_w_ref, mid_b_ref, table_ref, head_ref, inverse_ref)
+    copies = [pltpu.make_async_copy(s, t, sem.at[i]) for i, (s, t) in enumerate(zip(sources, targets))]
+    for copy in copies:
+        copy.start()
+    for copy in copies:
+        copy.wait()
     emb, order = emb_w_ref.shape
     length = feat_ref.shape[1]
     blocks = length // block
@@ -110,8 +110,19 @@
 
 
 def conv_kernel(
-    block, order_ref, x_ref, real_ref, imag_ref, edge_ref, head_ref, inverse_ref, out_ref, sig, sre, sim, spec, conv
+    block, order_ref, index_ref, x_ref, real_ref, imag_ref, edge_ref, table_ref, inverse_ref, weight_hbm, query_hbm,
+    signal_hbm, out_ref, weight_out, query_out, signal_out, sig, sre, sim, spec, conv, weight_sem, sem,
 ):
+    owners, _, width = weight_out.shape
+    copies = [
+        pltpu.make_async_copy(query_hbm, query_out, sem.at[0]),
+        pltpu.make_async_copy(signal_hbm, signal_out, sem.at[1]),
+    ]
+    for j in range(owners):
+        cols = pl.ds(pl.multiple_of((index_ref[0] ^ j) * width, LANES), width)
+        copies.append(pltpu.make_async_copy(weight_hbm.at[:, cols], weight_out.at[j], weight_sem.at[j]))
+    for copy in copies:
+        copy.start()
     slots = x_ref.shape[0]
     length = slots * GROUP
     blocks = length // block
@@ -121,7 +132,7 @@
     group = 2
     for b0 in range(0, blocks, group):
         stacked = jnp.concatenate([sig[b * block : (b + 1) * block, :] for b in range(b0, b0 + group)], 1)
-        spectrum = jnp.dot(head_ref[...], stacked, preferred_element_type=F32)
+        spectrum = jnp.dot(table_ref[...], stacked, preferred_element_type=F32)
         for i in range(group):
             sre[b0 + i] = spectrum[:block, i * LANES : (i + 1) * LANES]
             sim[b0 + i] = spectrum[block:, i * LANES : (i + 1) * LANES]
@@ -155,37 +166,39 @@
     for p in range(slots):
         start = pl.multiple_of(order_ref[p] * GROUP, GROUP)
         out_ref[p] = conv[pl.ds(start, GROUP), :]
-
-
-def mixed_kernel(query_ref, conv_ref, sig_ref, gain_ref, out_ref):
-    width = conv_ref.shape[2]
-    for j in range(conv_ref.shape[0]):
+    for copy in copies:
+        copy.wait()
+
+
+def mix_kernel(first, step, back_ref, sig_ref, query_ref, gain_ref, weight_ref, out_ref, mixed_ref):
+    count, _, width = back_ref.shape
+    for j in range(count):
         cols = slice(j * width, (j + 1) * width)
-        inner = conv_ref[j].astype(F32) + gain_ref[:, cols] * sig_ref[j].astype(F32)
-        out_ref[:, cols] = (query_ref[:, cols].astype(F32) * inner).astype(BF16)
-
-
-def project_kernel(index_ref, mixed_ref, weight_ref, out_ref):
-    out_ref[0] = jnp.dot(mixed_ref[...], weight_ref[...], preferred_element_type=F32).astype(BF16)
-
-
-def project(owners, mixed, out_weight, width):
-    rows, depth = mixed.shape
-    tile = min(width, 512)
-    count = owners.shape[0]
-    return pl.pallas_call(
-        project_kernel,
-        out_shape=jax.ShapeDtypeStruct((count, rows, width), BF16),
-        grid_spec=pltpu.PrefetchScalarGridSpec(
-            num_scalar_prefetch=1,
-            grid=(count, width // tile),
-            in_specs=[
-                pl.BlockSpec((rows, depth), lambda j, t, o: (0, 0)),
-                pl.BlockSpec((depth, tile), lambda j, t, o: (0, o[j] * (width // tile) + t)),
-            ],
-            out_specs=pl.BlockSpec((1, rows, tile), lambda j, t, o: (j, 0, t)),
-        ),
-    )(owners, mixed, out_weight)
+        inner = back_ref[j].astype(F32) + gain_ref[:, cols] * sig_ref[j].astype(F32)
+        mixed_ref[:, cols] = (query_ref[:, cols].astype(F32) * inner).astype(BF16)
+    project_kernel(first, step, mixed_ref, weight_ref, out_ref)
+
+
+def project_kernel(first, step, mixed_ref, weight_ref, out_ref):
+    mixed = mixed_ref[...]
+    for i in range(out_ref.shape[0]):
+        terms = jnp.dot(mixed, weight_ref[first + step * i], preferred_element_type=F32)
+        out_ref[i] = terms.astype(out_ref.dtype)
+
+
+def finish_kernel(*refs):
+    *terms, out_ref = refs
+    total = terms[0][...].astype(F32)
+    for term in terms[1:]:
+        total = total + term[...].astype(F32)
+    out_ref[...] = total.T
+
+
+def gated_kernel(key_ref, value_ref, out_ref):
+    width = out_ref.shape[2]
+    for j in range(out_ref.shape[0]):
+        cols = slice(j * width, (j + 1) * width)
+        out_ref[j] = (key_ref[:, cols].astype(F32) * value_ref[:, cols].astype(F32)).astype(BF16)
 
 
 def local(
@@ -198,17 +211,20 @@
     length = rows * seq_count
     slots = length // GROUP
     width = chan_width // seq_count
-    block = max(GROUP, length // 16)
+    block = max(2 * GROUP, length // 16)
     blocks = length // block
     emb, order = emb_weight.shape
     head, head_tail, inverse = packed_tables(block)
     feat_rows = -(-(emb + 1) // 8) * 8
     features = feature_table(length, (emb - 1) // 2, feat_rows)
-    vmem = pltpu.CompilerParams(vmem_limit_bytes=48 << 20)
-
+
+    tile = GROUP // 2
     signal = pl.pallas_call(
         gated_kernel,
         out_shape=jax.ShapeDtypeStruct((seq_count, rows, width), BF16),
+        grid=(rows // tile,),
+        in_specs=[pl.BlockSpec((tile, chan_width), lambda i: (i, 0))] * 2,
+        out_specs=pl.BlockSpec((seq_count, tile, width), lambda i: (0, i, 0)),
     )(key_gate, value)
     spread = lax.all_to_all(signal, "seq", 0, 0, tiled=True).reshape(slots, GROUP, width)
 
@@ -219,59 +235,103 @@
     if width < LANES:
         my_filter, my_decay, norm = jnp.pad(my_filter, pad), jnp.pad(my_decay, pad), jnp.pad(norm, pad)
         spread = jnp.pad(spread, [(0, 0)] + pad)
-    real, imag, edge = pl.pallas_call(
-        functools.partial(filter_kernel, block, None),
+    limit = pltpu.CompilerParams(vmem_limit_bytes=20 << 20)
+    in_vmem = pl.BlockSpec(memory_space=pltpu.VMEM)
+    in_smem = pl.BlockSpec(memory_space=pltpu.SMEM)
+    in_hbm = pl.BlockSpec(memory_space=pltpu.HBM)
+    far = lambda operand: pltpu.with_memory_space_constraint(operand, pltpu.HBM)
+    out_width = out_weight.shape[1] // chan_count
+    real, imag, edge, head, inverse = pl.pallas_call(
+        functools.partial(filter_kernel, block),
         out_shape=(
             jax.ShapeDtypeStruct((blocks, block, LANES), F32),
             jax.ShapeDtypeStruct((blocks, block, LANES), F32),
             jax.ShapeDtypeStruct((blocks, 16, LANES), F32),
+            jax.ShapeDtypeStruct(head.shape, BF16),
+            jax.ShapeDtypeStruct(inverse.shape, BF16),
         ),
+        in_specs=[in_vmem] * 3 + [in_hbm] * 8,
+        out_specs=[in_vmem] * 5,
         scratch_shapes=[
+            pltpu.VMEM(features.shape, F32),
+            pltpu.VMEM((emb, order), F32),
+            pltpu.VMEM((1, order), F32),
+            pltpu.VMEM((order, order), F32),
+            pltpu.VMEM((1, order), F32),
+            pltpu.VMEM(head_tail.shape, BF16),
             pltpu.VMEM((feat_rows, order), F32),
             pltpu.VMEM((order + 8, order), F32),
             pltpu.VMEM((order + 8, length), F32),
             pltpu.VMEM((length + block, LANES), BF16),
+            pltpu.SemaphoreType.DMA((8,)),
         ],
-        compiler_params=vmem,
-    )(features, emb_weight, emb_bias[None, :], mid_weight, mid_bias[None, :], my_filter, my_decay, norm, head_tail)
-
-    convolved = pl.pallas_call(
+        compiler_params=limit,
+    )(
+        my_filter, my_decay, norm,
+        *map(far, (features, emb_weight, emb_bias[None, :], mid_weight, mid_bias[None, :], head_tail, head, inverse)),
+    )
+
+    convolved, weights, query_near, signal_near = pl.pallas_call(
         functools.partial(conv_kernel, block),
-        out_shape=jax.ShapeDtypeStruct((slots, GROUP, LANES), BF16),
-        in_specs=[pl.BlockSpec(memory_space=pltpu.SMEM)] + [pl.BlockSpec(memory_space=pltpu.VMEM)] * 6,
+        out_shape=(
+            jax.ShapeDtypeStruct((slots, GROUP, LANES), BF16),
+            jax.ShapeDtypeStruct((chan_count, chan_width, out_width), BF16),
+            jax.ShapeDtypeStruct(query.shape, BF16),
+            jax.ShapeDtypeStruct(signal.shape, BF16),
+        ),
+        in_specs=[in_smem] * 2 + [in_vmem] * 6 + [in_hbm] * 3,
+        out_specs=[in_vmem] * 4,
         scratch_shapes=[
             pltpu.VMEM((length, LANES), BF16),
             pltpu.VMEM((blocks, block, LANES), F32),
             pltpu.VMEM((blocks, block, LANES), F32),
             pltpu.VMEM((2 * block, blocks * LANES), BF16),
             pltpu.VMEM((length, LANES), BF16),
+            pltpu.SemaphoreType.DMA((chan_count,)),
+            pltpu.SemaphoreType.DMA((2,)),
         ],
-        compiler_params=vmem,
-    )(group_order, spread, real, imag, edge, head, inverse)
-    if width < LANES:
-        convolved = convolved[:, :, :width]
-    back = lax.all_to_all(convolved.reshape(seq_count, rows, width), "seq", 0, 0, tiled=True)
-
-    mixed = pl.pallas_call(
-        mixed_kernel,
-        out_shape=jax.ShapeDtypeStruct((rows, chan_width), BF16),
-        compiler_params=vmem,
-    )(query, back, signal, skip_gain[None, :])
-
-    out_width = out_weight.shape[1] // chan_count
-    half = chan_count // 2
-    odd = chan_index ^ jnp.arange(1, chan_count, 2, dtype=jnp.int32)
-    even = chan_index ^ jnp.arange(0, chan_count, 2, dtype=jnp.int32)
-    away = project(odd, mixed, out_weight, out_width)
-    terms = lax.ppermute(away, "chan", [(i, i ^ 1) for i in range(chan_count)])
-    kept = project(even, mixed, out_weight, out_width)
-    bit = 2
-    total = kept.astype(F32) + terms.astype(F32)
+        compiler_params=limit,
+    )(group_order, chan_index[None], spread, real, imag, edge, head, inverse, *map(far, (out_weight, query, signal)))
+    back = lax.all_to_all(convolved[:, :, :width].reshape(seq_count, rows, width), "seq", 0, 0, tiled=True)
+
+    def exchange(terms, bit):
+        return lax.ppermute(terms, "chan", [(d, d ^ bit) for d in range(chan_count)])
+
+    def products(first, step, count, dtype):
+        return pl.pallas_call(
+            functools.partial(project_kernel, first, step),
+            out_shape=jax.ShapeDtypeStruct((count, rows, out_width), dtype),
+            in_specs=[in_vmem] * 2,
+            out_specs=in_vmem,
+            compiler_params=limit,
+        )(mixed, weights)
+
+    quarter = chan_count // 4
+    far_away, mixed = pl.pallas_call(
+        functools.partial(mix_kernel, 3, 4),
+        out_shape=(
+            jax.ShapeDtypeStruct((quarter, rows, out_width), BF16),
+            jax.ShapeDtypeStruct((rows, chan_width), BF16),
+        ),
+        in_specs=[in_vmem] * 5,
+        out_specs=[in_vmem] * 2,
+        compiler_params=limit,
+    )(back, signal_near, query_near, skip_gain[None, :], weights)
+    far_terms = exchange(far_away, 1)
+    far_kept = products(2, 4, quarter, F32)
+    terms = [exchange((far_kept + far_terms.astype(F32)).astype(BF16), 2)]
+    near_terms = exchange(products(1, 4, quarter, BF16), 1)
+    terms += [products(0, 4, quarter, F32), near_terms]
+    bit = 4
     while bit < chan_count:
-        send, keep = total[1::2].astype(BF16), total[0::2]
-        total = keep + lax.ppermute(send, "chan", [(i, i ^ bit) for i in range(chan_count)]).astype(F32)
+        total = sum(term.astype(F32) for term in terms)
+        terms = [total[0::2], exchange(total[1::2].astype(BF16), bit)]
         bit *= 2
-    return total[0].T
+    return pl.pallas_call(
+        finish_kernel,
+        out_shape=jax.ShapeDtypeStruct((out_width, rows), F32),
+        compiler_params=limit,
+    )(*[term[0] for term in terms])
 
 
 def solution(mesh):

time: 80.8 us -> 67.1 us (0.83)
  blocking collectives: 0 us -> 18.1 us
  waiting for transfers between devices: 34.7 us -> 17.2 us
  local copies, waits for them, and re-layouts: 4.94 us -> 0.68 us
  Pallas kernels: 24.2 us -> 20.2 us
  starting transfers between devices: 12.5 us -> 9.6 us
  other arithmetic: 3.58 us -> 0.91 us
    all_to_all x0 -> x1, blocking collectives: none -> 18.1 us  [local(): lax.all_to_all(convolved[:, :, :width].reshape(seq_count, rows, width), '...]
    all_to_all x1 -> x0, waiting for transfers between devices: 14.2 us -> none  [local(): lax.all_to_all(convolved.reshape(seq_count, rows, width), 'seq', 0, 0, ti...]
    pallas_call x5 -> x7, Pallas kernels: 22 us -> 16.8 us  [the longest x1 8.14 us: local(): pl.pallas_call(functools.partial(filter_kernel, block), out_shape=(jax.Sh...]
    all_to_all x1 -> x0, starting transfers between devices: 3.64 us -> none  [local(): lax.all_to_all(convolved.reshape(seq_count, rows, width), 'seq', 0, 0, ti...]
    unnamed x28 -> x6, local copies, waits for them, and re-layouts: 3.55 us -> 0.66 us
    all_to_all x1, waiting for transfers between devices: 7.74 us -> 5.55 us  [local(): lax.all_to_all(signal, 'seq', 0, 0, tiled=True).reshape(slots, GROUP, width)]
    add x1 -> x0, other arithmetic: 1.61 us -> none  [local(): total = kept.astype(F32) + terms.astype(F32)]
    transpose x1 -> x0, local copies, waits for them, and re-layouts: 1.31 us -> none  [local(): return total[0].T]
  transfers between devices with their start and end apart: 4 -> 4, of which waited for: 3 -> 2; matrix products, arithmetic and copies ran while one was open for 2% -> 1% of each run, Pallas kernels for 14% -> 15%
where the time goes in v2:
time: 67.1 us; the launch traced here: 66.8 us
  Pallas kernels  20.2 us (30%)
  blocking collectives  18.1 us (27%)
  waiting for transfers between devices  17.2 us (26%)
  starting transfers between devices  9.6 us (14%)
  other arithmetic  0.91 us (1%)
  local copies, waits for them, and re-layouts  0.68 us (1%)
    all_to_all x1, blocking collectives, local(): lax.all_to_all(convolved[:, :, :width].reshape(seq_count, rows, width), '...  18.1 us
    ppermute x3, waiting for transfers between devices, exchange(): lax.ppermute(terms, 'chan', [(d, d ^ bit) for d in range(chan_count)])  11.6 us
    pallas_call x1, Pallas kernels, local(): pl.pallas_call(functools.partial(filter_kernel, block), out_shape=(jax.Sh...  8.14 us
    all_to_all x1, starting transfers between devices, local(): lax.all_to_all(signal, 'seq', 0, 0, tiled=True).reshape(slots, GROUP, width)  7.39 us
    all_to_all x1, waiting for transfers between devices, local(): lax.all_to_all(signal, 'seq', 0, 0, tiled=True).reshape(slots, GROUP, width)  5.55 us
    pallas_call x1, Pallas kernels, local(): pl.pallas_call(functools.partial(conv_kernel, block), out_shape=(jax.Shap...  4.44 us
    pallas_call x1, Pallas kernels, local(): pl.pallas_call(gated_kernel, out_shape=jax.ShapeDtypeStruct((seq_count, r...  3.38 us
    ppermute x3, starting transfers between devices, exchange(): lax.ppermute(terms, 'chan', [(d, d ^ bit) for d in range(chan_count)])  2.22 us
  transfers between devices with their start and end apart: 4, of which 2 were waited for; matrix products, arithmetic and copies ran while one was open for 1% of the time, Pallas kernels for 15%

profile of v2, /device:TPU:0, one launch (start us, length us, event | category | flops | bytes accessed | tf_op | source)
XLA Modules:
  0.0 66.8 jit_solution(15671012789177235161)
XLA Ops:
  0.0 0.0 copy-start
  0.0 3.4 %shard_map.154.signal_hbm = bf16[8,256,128]{2,1,0:T(8,128)(2,1)} custom-call(bf16[256,1024]{1,0:T(8,128)(2,1)} %key_ref.1, bf16[256,1024]{1,0:T(8,128)(2,1)} %value_ref.1), custom_call_target="tpu_custom_call" | custom-call | tf_op jit(solution)/shard_map/pallas_call | solution.py:222
  3.4 0.0 copy-start.1
  3.4 7.4 %all-to-all-start = ((bf16[8,256,128]{2,1,0:T(8,128)(2,1)}), bf16[8,256,128]{2,1,0:T(8,128)(2,1)S(1)}, u32[]{:S(2)}, u32[]{:S(2)}) async-start(bf16[8,256,128]{2,1,0:T(8,128)(2,1)} %shard_map.154.signal_hbm), calls=%async_computation | async-start | bytes 1048576 | tf_op jit(solution)/shard_map/all_to_all | solution.py:229
  10.8 0.8 %sqrt_bitcast_fusion = (f32[1,128]{1,0:T(1,128)S(1)}, f32[1,128]{1,0:T(1,128)S(1)}) fusion(f32[1024]{0:T(1024)} %param.25, s32[]{:T(128)S(6)} %select_n.4), kind=kLoop, calls=%fused_computation.1 | loop fusion | flops 256 | bytes 1540 | tf_op jit(solution)/shard_map/sqrt | solution.py:233
  11.5 0.0 copy-done
  11.6 8.1 %shard_map.155 = (f32[8,256,128]{2,1,0:T(8,128)S(1)}, f32[8,256,128]{2,1,0:T(8,128)S(1)}, f32[8,16,128]{2,1,0:T(8,128)S(1)}, bf16[512,256]{1,0:T(8,128)(2,1)S(1)}, bf16[256,512]{1,0:T(8,128)(2,1)S(1)}) custom-call(f32[64,128]{1,0:T(8,128)S(1)} %constant_dynamic-slice_fusion.out_w_ref, f32[1,128]{1,0:T(1,128)S(1)} %get-tuple-element.28.decay_ref, ...), custom_call_target="tpu_custom_call" | custom-call | tf_op jit(solution)/shard_map/pallas_call | solution.py:244
  19.7 5.5 %all-to-all-done = bf16[8,256,128]{2,1,0:T(8,128)(2,1)S(1)} async-done(((bf16[8,256,128]{2,1,0:T(8,128)(2,1)}), bf16[8,256,128]{2,1,0:T(8,128)(2,1)S(1)}, u32[]{:S(2)}, u32[]{:S(2)}) %all-to-all-start) | async-done | bytes 524320 | tf_op jit(solution)/shard_map/all_to_all | solution.py:229
  25.3 0.7 copy-done.2
  25.9 4.4 %shard_map.156 = (bf16[16,128,128]{2,1,0:T(8,128)(2,1)S(1)}, bf16[4,1024,1024]{2,1,0:T(8,128)(2,1)S(1)}, bf16[256,1024]{1,0:T(8,128)(2,1)S(1)}, bf16[8,256,128]{2,1,0:T(8,128)(2,1)S(1)}) custom-call(s32[16]{0:T(128)S(1)} %copy-done.2, s32[1]{0:T(128)} %bitcast.index_ref, bf16[16,128,128]{2,1,0:T(8,128)(2,1)S(1)} %bitcast.14, ...), custom_call_target="tpu_custom_call" | custom-call | tf_op jit(solution)/shard_map/pallas_call | solution.py:274
  30.4 18.1 %all_to_all.10.back_ref = bf16[8,256,128]{2,1,0:T(8,128)(2,1)S(1)} all-to-all(bf16[8,256,128]{2,1,0:T(8,128)(2,1)S(1)} %bitcast.15), channel_id=1, replica_groups=mesh['seq'=8,'chan'=4] {'seq'}, dimensions={0} | all-to-all | bytes 1048576 | tf_op jit(solution)/shard_map/all_to_all | solution.py:295
  48.5 0.0 copy-done.1
  48.5 0.8 %shard_map.157 = (bf16[1,256,1024]{2,1,0:T(8,128)(2,1)S(1)}, bf16[256,1024]{1,0:T(8,128)(2,1)S(1)}) custom-call(bf16[8,256,128]{2,1,0:T(8,128)(2,1)S(1)} %all_to_all.10.back_ref, bf16[8,256,128]{2,1,0:T(8,128)(2,1)S(1)} %get-tuple-element.22.sig_ref, bf16[256,1024]{1,0:T(8,128)(2,1)S(1)} %get-tuple-element.23.query_ref, f32[1,1024]{1,0:T(1,128)S(1)} %bitcast.18, ...), custom_call_target="tpu_custom_call" | custom-call | tf_op jit(solution)/shard_map/pallas_call | solution.py:310
  49.3 0.1 collective-permute-start
  49.4 0.7 %shard_map.160 = bf16[1,256,1024]{2,1,0:T(8,128)(2,1)S(1)} custom-call(bf16[256,1024]{1,0:T(8,128)(2,1)S(1)} %get-tuple-element.25.mixed_ref, bf16[4,1024,1024]{2,1,0:T(8,128)(2,1)S(1)} %get-tuple-element.24.weight_ref), custom_call_target="tpu_custom_call" | custom-call | tf_op jit(solution)/shard_map/pallas_call | solution.py:301
  50.1 0.7 %shard_map.158 = f32[1,256,1024]{2,1,0:T(8,128)S(1)} custom-call(bf16[256,1024]{1,0:T(8,128)(2,1)S(1)} %get-tuple-element.25.mixed_ref, bf16[4,1024,1024]{2,1,0:T(8,128)(2,1)S(1)} %get-tuple-element.24.weight_ref), custom_call_target="tpu_custom_call" | custom-call | tf_op jit(solution)/shard_map/pallas_call | solution.py:301
  50.8 0.6 collective-permute-start.2
  51.4 0.0 collective-permute-done
  51.4 0.1 add_convert_fusion
  51.5 1.6 %collective-permute-start.1 = (bf16[1,256,1024]{2,1,0:T(8,128)(2,1)S(1)}, bf16[1,256,1024]{2,1,0:T(8,128)(2,1)S(1)}, u32[]{:S(2)}, u32[]{:S(2)}) collective-permute-start(bf16[1,256,1024]{2,1,0:T(8,128)(2,1)S(1)} %add_convert_fusion), channel_id=1, source_target_pairs={{0,2},{1,3},{2,0},{3,1},{4,6},{5,7},{6,4},{7,5},{8,10},{9,11},{10,... | collective-permute-start | bytes 1572872 | tf_op jit(solution)/shard_map/ppermute | solution.py:298
  53.1 0.7 %shard_map.159 = f32[1,256,1024]{2,1,0:T(8,128)S(1)} custom-call(bf16[256,1024]{1,0:T(8,128)(2,1)S(1)} %get-tuple-element.25.mixed_ref, bf16[4,1024,1024]{2,1,0:T(8,128)(2,1)S(1)} %get-tuple-element.24.weight_ref), custom_call_target="tpu_custom_call" | custom-call | tf_op jit(solution)/shard_map/pallas_call | solution.py:301
  53.8 0.0 collective-permute-done.2
  53.8 11.6 %collective-permute-done.1 = bf16[1,256,1024]{2,1,0:T(8,128)(2,1)S(1)} collective-permute-done((bf16[1,256,1024]{2,1,0:T(8,128)(2,1)S(1)}, bf16[1,256,1024]{2,1,0:T(8,128)(2,1)S(1)}, u32[]{:S(2)}, u32[]{:S(2)}) %collective-permute-start.1) | collective-permute-done | bytes 524320 | tf_op jit(solution)/shard_map/ppermute | solution.py:298
  65.5 1.3 %shard_map.161 = f32[1024,256]{1,0:T(8,128)} custom-call(bf16[256,1024]{1,0:T(8,128)(2,1)S(1)} %bitcast.17, f32[256,1024]{1,0:T(8,128)S(1)} %bitcast.13, bf16[256,1024]{1,0:T(8,128)(2,1)S(1)} %bitcast.16), custom_call_target="tpu_custom_call" | custom-call | tf_op jit(solution)/shard_map/pallas_call | solution.py:330
  (2 shorter events, 0.0 us)
Async XLA Ops:
  0.0 11.5 %copy-start = (f32[64,1024]{1,0:T(8,128)S(1)}, f32[64,1024]{1,0:T(8,128)}, u32[]{:S(2)}) copy-start(f32[64,1024]{1,0:T(8,128)} %param.24) | copy-start | bytes 786436
  3.4 45.1 %copy-start.1 = (f32[1024]{0:T(1024)S(1)}, f32[1024]{0:T(1024)}, u32[]{:S(2)}) copy-start(f32[1024]{0:T(1024)} %param.26) | copy-start | bytes 12292
  3.4 21.9 %all-to-all-start = ((bf16[8,256,128]{2,1,0:T(8,128)(2,1)}), bf16[8,256,128]{2,1,0:T(8,128)(2,1)S(1)}, u32[]{:S(2)}, u32[]{:S(2)}) async-start(bf16[8,256,128]{2,1,0:T(8,128)(2,1)} %shard_map.154.signal_hbm), calls=%async_computation | async-start | bytes 1048576 | tf_op jit(solution)/shard_map/all_to_all | solution.py:229
  25.3 0.7 copy-start.2
  49.3 2.1 %collective-permute-start = (bf16[1,256,1024]{2,1,0:T(8,128)(2,1)S(1)}, bf16[1,256,1024]{2,1,0:T(8,128)(2,1)S(1)}, u32[]{:S(2)}, u32[]{:S(2)}) collective-permute-start(bf16[1,256,1024]{2,1,0:T(8,128)(2,1)S(1)} %get-tuple-element.26), channel_id=1, source_target_pairs={{0,1},{1,0},{2,3},{3,2},{4,5},{5,4},{6,7},{7,6},{8,9},{9,8},{10,11... | collective-permute-start | bytes 1572872 | tf_op jit(solution)/shard_map/ppermute | solution.py:298
  50.8 3.0 %collective-permute-start.2 = (bf16[1,256,1024]{2,1,0:T(8,128)(2,1)S(1)}, bf16[1,256,1024]{2,1,0:T(8,128)(2,1)S(1)}, u32[]{:S(2)}, u32[]{:S(2)}) collective-permute-start(bf16[1,256,1024]{2,1,0:T(8,128)(2,1)S(1)} %shard_map.160), channel_id=1, source_target_pairs={{0,1},{1,0},{2,3},{3,2},{4,5},{5,4},{6,7},{7,6},{8,9},{9,8},{10,11... | collective-permute-start | bytes 1572872 | tf_op jit(solution)/shard_map/ppermute | solution.py:298
  51.5 13.9 %collective-permute-start.1 = (bf16[1,256,1024]{2,1,0:T(8,128)(2,1)S(1)}, bf16[1,256,1024]{2,1,0:T(8,128)(2,1)S(1)}, u32[]{:S(2)}, u32[]{:S(2)}) collective-permute-start(bf16[1,256,1024]{2,1,0:T(8,128)(2,1)S(1)} %add_convert_fusion), channel_id=1, source_target_pairs={{0,2},{1,3},{2,0},{3,1},{4,6},{5,7},{6,4},{7,5},{8,10},{9,11},{10,... | collective-permute-start | bytes 1572872 | tf_op jit(solution)/shard_map/ppermute | solution.py:298

commit v3 on v2

--- a/solution.py
+++ b/solution.py
@@ -109,25 +109,40 @@
             imag_ref[m, 0:16, :] = jnp.where(first_row, 0.0, imag[:16])
 
 
+def weight_copies(index_ref, blocks, weight_hbm, weight_out, sem):
+    _, depth, width = weight_out.shape
+    pieces = sem.shape[1]
+    unit = depth // pieces
+    copies = []
+    for i, j in enumerate(blocks):
+        cols = pl.ds(pl.multiple_of((index_ref[0] ^ j) * width, LANES), width)
+        for k in range(pieces):
+            rows = pl.ds(pl.multiple_of((index_ref[1] ^ k) * unit, LANES), unit)
+            target = weight_out.at[i, k * unit : (k + 1) * unit]
+            copies.append(pltpu.make_async_copy(weight_hbm.at[rows, cols], target, sem.at[i, k]))
+    return copies
+
+
 def conv_kernel(
-    block, order_ref, index_ref, x_ref, real_ref, imag_ref, edge_ref, table_ref, inverse_ref, weight_hbm, query_hbm,
-    signal_hbm, out_ref, weight_out, query_out, signal_out, sig, sre, sim, spec, conv, weight_sem, sem,
+    block, far_blocks, index_ref, x_ref, real_ref, imag_ref, edge_ref, table_ref, inverse_ref, weight_hbm,
+    query_hbm, signal_hbm, *refs,
 ):
-    owners, _, width = weight_out.shape
-    copies = [
-        pltpu.make_async_copy(query_hbm, query_out, sem.at[0]),
-        pltpu.make_async_copy(signal_hbm, signal_out, sem.at[1]),
-    ]
-    for j in range(owners):
-        cols = pl.ds(pl.multiple_of((index_ref[0] ^ j) * width, LANES), width)
-        copies.append(pltpu.make_async_copy(weight_hbm.at[:, cols], weight_out.at[j], weight_sem.at[j]))
+    *out_refs, weight_out, query_out, signal_out, sig, sre, sim, spec, conv, weight_sem, query_sem, signal_sem = refs
+    pieces, _, unit = query_out.shape
+    copies = []
+    for k in range(pieces):
+        piece = index_ref[1] ^ k
+        cols = pl.ds(pl.multiple_of(piece * unit, LANES), unit)
+        copies.append(pltpu.make_async_copy(query_hbm.at[:, cols], query_out.at[k], query_sem.at[k]))
+        copies.append(pltpu.make_async_copy(signal_hbm.at[piece], signal_out.at[k], signal_sem.at[k]))
+    copies += weight_copies(index_ref, far_blocks, weight_hbm, weight_out, weight_sem)
     for copy in copies:
         copy.start()
     slots = x_ref.shape[0]
     length = slots * GROUP
     blocks = length // block
     for p in range(slots):
-        start = pl.multiple_of(order_ref[p] * GROUP, GROUP)
+        start = pl.multiple_of(index_ref[2 + p] * GROUP, GROUP)
         sig[pl.ds(start, GROUP), :] = x_ref[p]
     group = 2
     for b0 in range(0, blocks, group):
@@ -163,42 +178,77 @@
     result = jnp.dot(inverse_ref[...], spec[...], preferred_element_type=F32)
     for g in range(blocks):
         conv[g * block : (g + 1) * block, :] = result[:, g * LANES : (g + 1) * LANES].astype(BF16)
-    for p in range(slots):
-        start = pl.multiple_of(order_ref[p] * GROUP, GROUP)
-        out_ref[p] = conv[pl.ds(start, GROUP), :]
+    groups = slots // len(out_refs)
+    for k, out_ref in enumerate(out_refs):
+        for i in range(groups):
+            slot = (index_ref[1] ^ k) * groups + i
+            start = pl.multiple_of(index_ref[2 + slot] * GROUP, GROUP)
+            out_ref[i * GROUP : (i + 1) * GROUP, :] = conv[pl.ds(start, GROUP), :]
     for copy in copies:
         copy.wait()
 
 
-def mix_kernel(first, step, back_ref, sig_ref, query_ref, gain_ref, weight_ref, out_ref, mixed_ref):
-    count, _, width = back_ref.shape
-    for j in range(count):
-        cols = slice(j * width, (j + 1) * width)
-        inner = back_ref[j].astype(F32) + gain_ref[:, cols] * sig_ref[j].astype(F32)
-        mixed_ref[:, cols] = (query_ref[:, cols].astype(F32) * inner).astype(BF16)
-    project_kernel(first, step, mixed_ref, weight_ref, out_ref)
-
-
-def project_kernel(first, step, mixed_ref, weight_ref, out_ref):
+def mix_kernel(index_ref, sig_ref, query_ref, gain_ref, weight_ref, *refs):
+    *back_refs, out_ref, mixed_ref = refs
+    unit = sig_ref.shape[2]
+    for k, back_ref in enumerate(back_refs):
+        gain = gain_ref[pl.ds(index_ref[1] ^ k, 1), :]
+        inner = back_ref[...].astype(F32) + gain * sig_ref[k].astype(F32)
+        mixed_ref[:, k * unit : (k + 1) * unit] = (query_ref[k].astype(F32) * inner).astype(BF16)
+    project_kernel(0, mixed_ref, weight_ref, out_ref)
+
+
+def project_kernel(first, mixed_ref, weight_ref, out_ref):
     mixed = mixed_ref[...]
     for i in range(out_ref.shape[0]):
-        terms = jnp.dot(mixed, weight_ref[first + step * i], preferred_element_type=F32)
-        out_ref[i] = terms.astype(out_ref.dtype)
-
-
-def finish_kernel(*refs):
-    *terms, out_ref = refs
-    total = terms[0][...].astype(F32)
-    for term in terms[1:]:
+        out_ref[i] = jnp.dot(mixed, weight_ref[first + i], preferred_element_type=F32).astype(out_ref.dtype)
+
+
+def near_kernel(near_blocks, index_ref, mixed_ref, weight_hbm, away_ref, kept_ref, weight_near, sem):
+    copies = weight_copies(index_ref, near_blocks, weight_hbm, weight_near, sem)
+    for copy in copies:
+        copy.start()
+    count = away_ref.shape[0]
+    for copy in copies[: len(copies) // 2]:
+        copy.wait()
+    project_kernel(0, mixed_ref, weight_near, away_ref)
+    for copy in copies[len(copies) // 2 :]:
+        copy.wait()
+    project_kernel(count, mixed_ref, weight_near, kept_ref)
+
+
+def finish_kernel(part, count, *refs):
+    *operands, out_hbm, turned, sem = refs
+    rows = turned.shape[1]
+    total = operands[0][...].astype(F32)
+    for term in operands[1:count]:
         total = total + term[...].astype(F32)
-    out_ref[...] = total.T
-
-
-def gated_kernel(key_ref, value_ref, out_ref):
-    width = out_ref.shape[2]
-    for j in range(out_ref.shape[0]):
-        cols = slice(j * width, (j + 1) * width)
-        out_ref[j] = (key_ref[:, cols].astype(F32) * value_ref[:, cols].astype(F32)).astype(BF16)
+    turned[...] = total.T
+    copy = pltpu.make_async_copy(turned, out_hbm.at[:, part * rows : (part + 1) * rows], sem.at[0])
+    copy.start()
+    copy.wait()
+
+
+def gated_kernel(key_hbm, value_hbm, out_hbm, key_ref, value_ref, out_ref, in_sem, out_sem):
+    parts, rows, _ = key_ref.shape
+    count, _, width = out_hbm.shape
+    loads, stores = [], []
+    for i in range(parts):
+        part = slice(i * rows, (i + 1) * rows)
+        loads.append(pltpu.make_async_copy(key_hbm.at[part], key_ref.at[i], in_sem.at[0, i]))
+        loads.append(pltpu.make_async_copy(value_hbm.at[part], value_ref.at[i], in_sem.at[1, i]))
+        stores.append(pltpu.make_async_copy(out_ref.at[i], out_hbm.at[:, part], out_sem.at[i]))
+    for load in loads:
+        load.start()
+    for i in range(parts):
+        loads[2 * i].wait()
+        loads[2 * i + 1].wait()
+        for j in range(count):
+            cols = slice(j * width, (j + 1) * width)
+            out_ref[i, j] = (key_ref[i, :, cols].astype(F32) * value_ref[i, :, cols].astype(F32)).astype(BF16)
+        stores[i].start()
+    for store in stores:
+        store.wait()
 
 
 def local(
@@ -218,14 +268,26 @@
     feat_rows = -(-(emb + 1) // 8) * 8
     features = feature_table(length, (emb - 1) // 2, feat_rows)
 
-    tile = GROUP // 2
+    limit = pltpu.CompilerParams(vmem_limit_bytes=20 << 20)
+    in_vmem = pl.BlockSpec(memory_space=pltpu.VMEM)
+    in_smem = pl.BlockSpec(memory_space=pltpu.SMEM)
+    in_hbm = pl.BlockSpec(memory_space=pltpu.HBM)
+    far = lambda operand: pltpu.with_memory_space_constraint(operand, pltpu.HBM)
+    parts = 4
     signal = pl.pallas_call(
         gated_kernel,
         out_shape=jax.ShapeDtypeStruct((seq_count, rows, width), BF16),
-        grid=(rows // tile,),
-        in_specs=[pl.BlockSpec((tile, chan_width), lambda i: (i, 0))] * 2,
-        out_specs=pl.BlockSpec((seq_count, tile, width), lambda i: (0, i, 0)),
-    )(key_gate, value)
+        in_specs=[in_hbm] * 2,
+        out_specs=in_hbm,
+        scratch_shapes=[
+            pltpu.VMEM((parts, rows // parts, chan_width), BF16),
+            pltpu.VMEM((parts, rows // parts, chan_width), BF16),
+            pltpu.VMEM((parts, seq_count, rows // parts, width), BF16),
+            pltpu.SemaphoreType.DMA((2, parts)),
+            pltpu.SemaphoreType.DMA((parts,)),
+        ],
+        compiler_params=limit,
+    )(far(key_gate), far(value))
     spread = lax.all_to_all(signal, "seq", 0, 0, tiled=True).reshape(slots, GROUP, width)
 
     my_filter = lax.dynamic_slice_in_dim(out_filter, seq_index * width, width, 1)
@@ -235,11 +297,6 @@
     if width < LANES:
         my_filter, my_decay, norm = jnp.pad(my_filter, pad), jnp.pad(my_decay, pad), jnp.pad(norm, pad)
         spread = jnp.pad(spread, [(0, 0)] + pad)
-    limit = pltpu.CompilerParams(vmem_limit_bytes=20 << 20)
-    in_vmem = pl.BlockSpec(memory_space=pltpu.VMEM)
-    in_smem = pl.BlockSpec(memory_space=pltpu.SMEM)
-    in_hbm = pl.BlockSpec(memory_space=pltpu.HBM)
-    far = lambda operand: pltpu.with_memory_space_constraint(operand, pltpu.HBM)
     out_width = out_weight.shape[1] // chan_count
     real, imag, edge, head, inverse = pl.pallas_call(
         functools.partial(filter_kernel, block),
@@ -271,67 +328,106 @@
         *map(far, (features, emb_weight, emb_bias[None, :], mid_weight, mid_bias[None, :], head_tail, head, inverse)),
     )
 
-    convolved, weights, query_near, signal_near = pl.pallas_call(
-        functools.partial(conv_kernel, block),
+    unit = width if width % LANES == 0 else chan_width
+    pieces = chan_width // unit
+    if pieces == 1:
+        signal = signal.transpose(1, 0, 2).reshape(1, rows, chan_width)
+    base = seq_index if pieces > 1 else jnp.zeros_like(seq_index)
+    index = jnp.concatenate([chan_index[None], base[None], group_order])
+    quarter = chan_count // 4
+    odd = range(1, chan_count, 2)
+    far_blocks = [j for j in odd if j & 2] + [j ^ 1 for j in odd if j & 2]
+    near_blocks = [j for j in odd if not j & 2] + [j ^ 1 for j in odd if not j & 2]
+    *convolved, weights, query_near, signal_near = pl.pallas_call(
+        functools.partial(conv_kernel, block, far_blocks),
         out_shape=(
-            jax.ShapeDtypeStruct((slots, GROUP, LANES), BF16),
-            jax.ShapeDtypeStruct((chan_count, chan_width, out_width), BF16),
-            jax.ShapeDtypeStruct(query.shape, BF16),
-            jax.ShapeDtypeStruct(signal.shape, BF16),
+            *[jax.ShapeDtypeStruct((rows, LANES), BF16)] * seq_count,
+            jax.ShapeDtypeStruct((2 * quarter, chan_width, out_width), BF16),
+            jax.ShapeDtypeStruct((pieces, rows, unit), BF16),
+            jax.ShapeDtypeStruct((pieces, rows, unit), BF16),
         ),
-        in_specs=[in_smem] * 2 + [in_vmem] * 6 + [in_hbm] * 3,
-        out_specs=[in_vmem] * 4,
+        in_specs=[in_smem] + [in_vmem] * 6 + [in_hbm] * 3,
+        out_specs=[in_vmem] * (seq_count + 3),
         scratch_shapes=[
             pltpu.VMEM((length, LANES), BF16),
             pltpu.VMEM((blocks, block, LANES), F32),
             pltpu.VMEM((blocks, block, LANES), F32),
             pltpu.VMEM((2 * block, blocks * LANES), BF16),
             pltpu.VMEM((length, LANES), BF16),
-            pltpu.SemaphoreType.DMA((chan_count,)),
-            pltpu.SemaphoreType.DMA((2,)),
+            pltpu.SemaphoreType.DMA((2 * quarter, pieces)),
+            pltpu.SemaphoreType.DMA((pieces,)),
+            pltpu.SemaphoreType.DMA((pieces,)),
         ],
         compiler_params=limit,
-    )(group_order, chan_index[None], spread, real, imag, edge, head, inverse, *map(far, (out_weight, query, signal)))
-    back = lax.all_to_all(convolved[:, :, :width].reshape(seq_count, rows, width), "seq", 0, 0, tiled=True)
+    )(index, spread, real, imag, edge, head, inverse, *map(far, (out_weight, query, signal)))
+    if pieces == 1:
+        ordered = lax.all_to_all(jnp.stack([piece[:, :width] for piece in convolved]), "seq", 0, 0, tiled=True)
+        backs = [ordered.transpose(1, 0, 2).reshape(rows, chan_width)]
+    else:
+        backs = [convolved[0]]
+        for k in range(1, seq_count):
+            backs.append(lax.ppermute(convolved[k], "seq", [(d, d ^ k) for d in range(seq_count)]))
 
     def exchange(terms, bit):
         return lax.ppermute(terms, "chan", [(d, d ^ bit) for d in range(chan_count)])
 
-    def products(first, step, count, dtype):
-        return pl.pallas_call(
-            functools.partial(project_kernel, first, step),
-            out_shape=jax.ShapeDtypeStruct((count, rows, out_width), dtype),
-            in_specs=[in_vmem] * 2,
-            out_specs=in_vmem,
-            compiler_params=limit,
-        )(mixed, weights)
-
-    quarter = chan_count // 4
     far_away, mixed = pl.pallas_call(
-        functools.partial(mix_kernel, 3, 4),
+        mix_kernel,
         out_shape=(
             jax.ShapeDtypeStruct((quarter, rows, out_width), BF16),
             jax.ShapeDtypeStruct((rows, chan_width), BF16),
         ),
-        in_specs=[in_vmem] * 5,
+        in_specs=[in_smem] + [in_vmem] * (4 + pieces),
         out_specs=[in_vmem] * 2,
         compiler_params=limit,
-    )(back, signal_near, query_near, skip_gain[None, :], weights)
+    )(index, signal_near, query_near, skip_gain.reshape(pieces, unit), weights, *backs)
     far_terms = exchange(far_away, 1)
-    far_kept = products(2, 4, quarter, F32)
-    terms = [exchange((far_kept + far_terms.astype(F32)).astype(BF16), 2)]
-    near_terms = exchange(products(1, 4, quarter, BF16), 1)
-    terms += [products(0, 4, quarter, F32), near_terms]
-    bit = 4
-    while bit < chan_count:
-        total = sum(term.astype(F32) for term in terms)
-        terms = [total[0::2], exchange(total[1::2].astype(BF16), bit)]
-        bit *= 2
-    return pl.pallas_call(
-        finish_kernel,
-        out_shape=jax.ShapeDtypeStruct((out_width, rows), F32),
-        compiler_params=limit,
-    )(*[term[0] for term in terms])
+    far_kept = pl.pallas_call(
+        functools.partial(project_kernel, quarter),
+        out_shape=jax.ShapeDtypeStruct((quarter, rows, out_width), F32),
+        in_specs=[in_vmem] * 2,
+        out_specs=in_vmem,
+        compiler_params=limit,
+    )(mixed, weights)
+    send, mixed = lax.optimization_barrier(((far_kept + far_terms.astype(F32)).astype(BF16), mixed))
+    half = rows // 2
+    halves = [slice(0, half), slice(half, rows)]
+    sent = [exchange(send[:, part], 2) for part in halves]
+    near_away, near_kept = pl.pallas_call(
+        functools.partial(near_kernel, near_blocks),
+        out_shape=(
+            jax.ShapeDtypeStruct((quarter, rows, out_width), BF16),
+            jax.ShapeDtypeStruct((quarter, rows, out_width), F32),
+        ),
+        in_specs=[in_smem, in_vmem, in_hbm],
+        out_specs=[in_vmem] * 2,
+        scratch_shapes=[
+            pltpu.VMEM((2 * quarter, chan_width, out_width), BF16),
+            pltpu.SemaphoreType.DMA((2 * quarter, pieces)),
+        ],
+        compiler_params=limit,
+    )(index, mixed, far(out_weight))
+    near_terms = exchange(near_away, 1)
+    result = None
+    for i, part in enumerate(halves):
+        terms = [near_kept[:, part], near_terms[:, part], sent[i]]
+        bit = 4
+        while bit < chan_count:
+            total = sum(term.astype(F32) for term in terms)
+            terms = [total[0::2], exchange(total[1::2].astype(BF16), bit)]
+            bit *= 2
+        operands = [term[0] for term in terms]
+        extra = [] if result is None else [result]
+        result = pl.pallas_call(
+            functools.partial(finish_kernel, i, len(operands)),
+            out_shape=jax.ShapeDtypeStruct((out_width, rows), F32),
+            in_specs=[in_vmem] * len(operands) + [in_hbm] * len(extra),
+            out_specs=in_hbm,
+            scratch_shapes=[pltpu.VMEM((out_width, half), F32), pltpu.SemaphoreType.DMA((1,))],
+            input_output_aliases={len(operands): 0} if extra else {},
+            compiler_params=limit,
+        )(*operands, *extra)
+    return result
 
 
 def solution(mesh):

time: 67.1 us -> 66.5 us (level)
  blocking collectives: 18.1 us -> 0 us
  starting transfers between devices: 9.6 us -> 20.8 us
  waiting for transfers between devices: 17.2 us -> 21.8 us
  Pallas kernels: 20.2 us -> 21.7 us
  other arithmetic: 0.91 us -> 1.64 us
    all_to_all x1 -> x0, blocking collectives: 18.1 us -> none  [local(): lax.all_to_all(convolved[:, :, :width].reshape(seq_count, rows, width), '...]
    ppermute x0 -> x7, starting transfers between devices: none -> 11.2 us  [local(): lax.ppermute(convolved[k], 'seq', [(d, d ^ k) for d in range(seq_count)])]
    ppermute x0 -> x7, waiting for transfers between devices: none -> 4.78 us  [local(): lax.ppermute(convolved[k], 'seq', [(d, d ^ k) for d in range(seq_count)])]
    pallas_call x6, Pallas kernels: 8.67 us -> 11.4 us  [the longest x1 3.68 us: local(): pl.pallas_call(functools.partial(conv_kernel, block, far_blocks), out_sha...]
    pallas_call x1, Pallas kernels: 3.38 us -> 2.11 us  [local(): pl.pallas_call(gated_kernel, out_shape=jax.ShapeDtypeStruct((seq_count, r...]
    all_to_all x1, waiting for transfers between devices: 5.55 us -> 4.81 us  [local(): lax.all_to_all(signal, 'seq', 0, 0, tiled=True).reshape(slots, GROUP, width)]
    concatenate x0 -> x1, other arithmetic: none -> 0.74 us  [local(): index = jnp.concatenate([chan_index[None], base[None], group_order])]
    ppermute x3 -> x4, waiting for transfers between devices: 11.6 us -> 12.2 us  [exchange(): lax.ppermute(terms, 'chan', [(d, d ^ bit) for d in range(chan_count)])]
  transfers between devices with their start and end apart: 4 -> 12, of which waited for: 2 -> 6; matrix products, arithmetic and copies ran while one was open for 1% -> 3% of each run, Pallas kernels for 15% -> 15%
where the time goes in v3:
time: 66.5 us; the launch traced here: 66.2 us
  waiting for transfers between devices  21.8 us (33%)
  Pallas kernels  21.7 us (33%)
  starting transfers between devices  20.8 us (31%)
  other arithmetic  1.64 us (2%)
    ppermute x4, waiting for transfers between devices, exchange(): lax.ppermute(terms, 'chan', [(d, d ^ bit) for d in range(chan_count)])  12.2 us
    ppermute x7, starting transfers between devices, local(): lax.ppermute(convolved[k], 'seq', [(d, d ^ k) for d in range(seq_count)])  11.2 us
    pallas_call x1, Pallas kernels, local(): pl.pallas_call(functools.partial(filter_kernel, block), out_shape=(jax.Sh...  8.14 us
    all_to_all x1, starting transfers between devices, local(): lax.all_to_all(signal, 'seq', 0, 0, tiled=True).reshape(slots, GROUP, width)  7.26 us
    all_to_all x1, waiting for transfers between devices, local(): lax.all_to_all(signal, 'seq', 0, 0, tiled=True).reshape(slots, GROUP, width)  4.81 us
    ppermute x7, waiting for transfers between devices, local(): lax.ppermute(convolved[k], 'seq', [(d, d ^ k) for d in range(seq_count)])  4.78 us
    pallas_call x1, Pallas kernels, local(): pl.pallas_call(functools.partial(conv_kernel, block, far_blocks), out_sha...  3.68 us
    pallas_call x1, Pallas kernels, local(): pl.pallas_call(functools.partial(near_kernel, near_blocks), out_shape=(ja...  3.64 us
  transfers between devices with their start and end apart: 12, of which 6 were waited for; matrix products, arithmetic and copies ran while one was open for 3% of the time, Pallas kernels for 15%

profile of v3, /device:TPU:0, one launch (start us, length us, event | category | flops | bytes accessed | tf_op | source)
XLA Modules:
  0.0 66.2 jit_solution(17360727070530472300)
XLA Ops:
  0.0 2.1 %shard_map.154.signal_hbm = bf16[8,256,128]{2,1,0:T(8,128)(2,1)} custom-call(bf16[256,1024]{1,0:T(8,128)(2,1)} %key_hbm.1, bf16[256,1024]{1,0:T(8,128)(2,1)} %value_hbm.1), custom_call_target="tpu_custom_call" | custom-call | tf_op jit(solution)/shard_map/pallas_call | solution.py:277
  2.1 7.3 %all-to-all-start = ((bf16[8,256,128]{2,1,0:T(8,128)(2,1)}), bf16[8,256,128]{2,1,0:T(8,128)(2,1)S(1)}, u32[]{:S(2)}, u32[]{:S(2)}) async-start(bf16[8,256,128]{2,1,0:T(8,128)(2,1)} %shard_map.154.signal_hbm), calls=%async_computation | async-start | bytes 1048576 | tf_op jit(solution)/shard_map/all_to_all | solution.py:291
  9.4 0.8 %sqrt_bitcast_fusion = (f32[1,128]{1,0:T(1,128)S(1)}, f32[1,128]{1,0:T(1,128)S(1)}) fusion(f32[1024]{0:T(1024)} %param.25, s32[]{:T(128)S(6)} %select_n.4), kind=kLoop, calls=%fused_computation.6 | loop fusion | flops 256 | bytes 1540 | tf_op jit(solution)/shard_map/sqrt | solution.py:295
  10.2 8.1 %shard_map.155 = (f32[8,256,128]{2,1,0:T(8,128)S(1)}, f32[8,256,128]{2,1,0:T(8,128)S(1)}, f32[8,16,128]{2,1,0:T(8,128)S(1)}, bf16[512,256]{1,0:T(8,128)(2,1)S(1)}, bf16[256,512]{1,0:T(8,128)(2,1)S(1)}) custom-call(f32[64,128]{1,0:T(8,128)S(1)} %constant_dynamic-slice_fusion.out_w_ref, f32[1,128]{1,0:T(1,128)S(1)} %get-tuple-element.56.decay_ref, ...), custom_call_target="tpu_custom_call" | custom-call | tf_op jit(solution)/shard_map/pallas_call | solution.py:301
  18.3 0.7 %pad_add_fusion.index_ref = s32[18]{0:T(128)S(1)} fusion(s32[16]{0:T(128)} %param.19, s32[1]{0:T(128)} %bitcast.1, s32[1]{0:T(128)} %bitcast), kind=kLoop, calls=%fused_computation.5 | loop fusion | flops 36 | bytes 144 | tf_op jit(solution)/shard_map/concatenate | solution.py:336
  19.1 4.8 %all-to-all-done = bf16[8,256,128]{2,1,0:T(8,128)(2,1)S(1)} async-done(((bf16[8,256,128]{2,1,0:T(8,128)(2,1)}), bf16[8,256,128]{2,1,0:T(8,128)(2,1)S(1)}, u32[]{:S(2)}, u32[]{:S(2)}) %all-to-all-start) | async-done | bytes 524320 | tf_op jit(solution)/shard_map/all_to_all | solution.py:291
  23.9 3.7 %shard_map.156 = (bf16[256,128]{1,0:T(8,128)(2,1)S(1)}, bf16[256,128]{1,0:T(8,128)(2,1)S(1)}, bf16[256,128]{1,0:T(8,128)(2,1)S(1)}, bf16[256,128]{1,0:T(8,128)(2...) custom-call(s32[18]{0:T(128)S(1)} %pad_add_fusion.index_ref, ...), custom_call_target="tpu_custom_call" | custom-call | tf_op jit(solution)/shard_map/pallas_call | solution.py:341
  27.6 1.5 %collective-permute-start = (bf16[256,128]{1,0:T(8,128)(2,1)S(1)}, bf16[256,128]{1,0:T(8,128)(2,1)S(1)}, u32[]{:S(2)}, u32[]{:S(2)}) collective-permute-start(bf16[256,128]{1,0:T(8,128)(2,1)S(1)} %get-tuple-element.36), channel_id=1, source_target_pairs={{0,4},{4,0},{8,12},{12,8},{16,20},{20,16},{24,28},{28,24},{1,5},{5... | collective-permute-start | bytes 196616 | tf_op jit(solution)/shard_map/ppermute | solution.py:369
  29.1 2.0 %collective-permute-start.2 = (bf16[256,128]{1,0:T(8,128)(2,1)S(1)}, bf16[256,128]{1,0:T(8,128)(2,1)S(1)}, u32[]{:S(2)}, u32[]{:S(2)}) collective-permute-start(bf16[256,128]{1,0:T(8,128)(2,1)S(1)} %get-tuple-element.38), channel_id=1, source_target_pairs={{0,12},{4,8},{8,4},{12,0},{16,28},{20,24},{24,20},{28,16},{1,13},{... | collective-permute-start | bytes 196616 | tf_op jit(solution)/shard_map/ppermute | solution.py:369
  31.3 3.7 %collective-permute-start.4 = (bf16[256,128]{1,0:T(8,128)(2,1)S(1)}, bf16[256,128]{1,0:T(8,128)(2,1)S(1)}, u32[]{:S(2)}, u32[]{:S(2)}) collective-permute-start(bf16[256,128]{1,0:T(8,128)(2,1)S(1)} %get-tuple-element.40), channel_id=1, source_target_pairs={{0,20},{4,16},{8,28},{12,24},{16,4},{20,0},{24,12},{28,8},{1,21},{... | collective-permute-start | bytes 196616 | tf_op jit(solution)/shard_map/ppermute | solution.py:369
  34.9 1.5 %collective-permute-start.5 = (bf16[256,128]{1,0:T(8,128)(2,1)S(1)}, bf16[256,128]{1,0:T(8,128)(2,1)S(1)}, u32[]{:S(2)}, u32[]{:S(2)}) collective-permute-start(bf16[256,128]{1,0:T(8,128)(2,1)S(1)} %get-tuple-element.41), channel_id=1, source_target_pairs={{0,24},{4,28},{8,16},{12,20},{16,8},{20,12},{24,0},{28,4},{1,25},{... | collective-permute-start | bytes 196616 | tf_op jit(solution)/shard_map/ppermute | solution.py:369
  36.4 2.4 %collective-permute-start.6 = (bf16[256,128]{1,0:T(8,128)(2,1)S(1)}, bf16[256,128]{1,0:T(8,128)(2,1)S(1)}, u32[]{:S(2)}, u32[]{:S(2)}) collective-permute-start(bf16[256,128]{1,0:T(8,128)(2,1)S(1)} %get-tuple-element.42), channel_id=1, source_target_pairs={{0,28},{4,24},{8,20},{12,16},{16,12},{20,8},{24,4},{28,0},{1,29},{... | collective-permute-start | bytes 196616 | tf_op jit(solution)/shard_map/ppermute | solution.py:369
  38.8 2.4 %collective-permute-done.3.refs_4_ = bf16[256,128]{1,0:T(8,128)(2,1)S(1)} collective-permute-done((bf16[256,128]{1,0:T(8,128)(2,1)S(1)}, bf16[256,128]{1,0:T(8,128)(2,1)S(1)}, u32[]{:S(2)}, u32[]{:S(2)}) %collective-permute-start.3) | collective-permute-done | bytes 65568 | tf_op jit(solution)/shard_map/ppermute | solution.py:369
  41.2 2.4 %collective-permute-done.4.refs_5_ = bf16[256,128]{1,0:T(8,128)(2,1)S(1)} collective-permute-done((bf16[256,128]{1,0:T(8,128)(2,1)S(1)}, bf16[256,128]{1,0:T(8,128)(2,1)S(1)}, u32[]{:S(2)}, u32[]{:S(2)}) %collective-permute-start.4) | collective-permute-done | bytes 65568 | tf_op jit(solution)/shard_map/ppermute | solution.py:369
  43.6 1.4 %shard_map.157 = (bf16[1,256,1024]{2,1,0:T(8,128)(2,1)S(1)}, bf16[256,1024]{1,0:T(8,128)(2,1)S(1)}) custom-call(s32[18]{0:T(128)S(1)} %pad_add_fusion.index_ref, bf16[8,256,128]{2,1,0:T(8,128)(2,1)S(1)} %get-tuple-element.32.sig_ref, bf16[8,256,128]{2,1,0:T(8,128)(2,1)S(1)} %get-tuple-element.33.query_ref, f32[8,128]{1,0:T(8,128)S(1)} %bitcast.23, ...), custom_call_target="tpu_custom_call" | custom-call | tf_op jit(solution)/shard_map/pallas_call | solution.py:374
  45.0 0.7 %shard_map.158 = f32[1,256,1024]{2,1,0:T(8,128)S(1)} custom-call(bf16[256,1024]{1,0:T(8,128)(2,1)S(1)} %get-tuple-element.45.mixed_ref, bf16[2,1024,1024]{2,1,0:T(8,128)(2,1)S(1)} %get-tuple-element.34.weight_ref), custom_call_target="tpu_custom_call" | custom-call | tf_op jit(solution)/shard_map/pallas_call | solution.py:385
  45.7 1.2 %collective-permute-done.7 = bf16[1,256,1024]{2,1,0:T(8,128)(2,1)S(1)} collective-permute-done((bf16[1,256,1024]{2,1,0:T(8,128)(2,1)S(1)}, bf16[1,256,1024]{2,1,0:T(8,128)(2,1)S(1)}, u32[]{:S(2)}, u32[]{:S(2)}) %collective-permute-start.7) | collective-permute-done | bytes 524320 | tf_op jit(solution)/shard_map/ppermute | solution.py:372
  47.1 3.6 %shard_map.159 = (bf16[1,256,1024]{2,1,0:T(8,128)(2,1)S(1)}, f32[1,256,1024]{2,1,0:T(8,128)S(1)}) custom-call(s32[18]{0:T(128)S(1)} %pad_add_fusion.index_ref, bf16[256,1024]{1,0:T(8,128)(2,1)S(1)} %get-tuple-element.45.mixed_ref, bf16[1024,4096]{1,0:T(8,128)(2,1)} %weight_hbm.3), custom_call_target="tpu_custom_call" | custom-call | tf_op jit(solution)/shard_map/pallas_call | solution.py:396
  50.9 1.6 %collective-permute-start.10 = (bf16[1,128,1024]{2,1,0:T(8,128)(2,1)S(1)}, bf16[1,128,1024]{2,1,0:T(8,128)(2,1)S(1)}, u32[]{:S(2)}, u32[]{:S(2)}) collective-permute-start(bf16[1,128,1024]{2,1,0:T(8,128)(2,1)S(1)} %get-tuple-element.51), channel_id=1, source_target_pairs={{0,2},{1,3},{2,0},{3,1},{4,6},{5,7},{6,4},{7,5},{8,10},{9,11},{10,... | collective-permute-start | bytes 786440 | tf_op jit(solution)/shard_map/ppermute | solution.py:372
  52.5 0.5 collective-permute-start.9
  53.2 6.9 %collective-permute-done.10 = bf16[1,128,1024]{2,1,0:T(8,128)(2,1)S(1)} collective-permute-done((bf16[1,128,1024]{2,1,0:T(8,128)(2,1)S(1)}, bf16[1,128,1024]{2,1,0:T(8,128)(2,1)S(1)}, u32[]{:S(2)}, u32[]{:S(2)}) %collective-permute-start.10) | collective-permute-done | bytes 262176 | tf_op jit(solution)/shard_map/ppermute | solution.py:372
  60.1 1.0 %shard_map.160.refs_3_ = f32[1024,256]{1,0:T(8,128)} custom-call(f32[128,1024]{1,0:T(8,128)S(1)} %get-tuple-element.49.refs_0_, bf16[128,1024]{1,0:T(8,128)(2,1)S(1)} %get-tuple-element.53.refs_1_, bf16[128,1024]{1,0:T(8,128)(2,1)S(1)} %bitcast.22), custom_call_target="tpu_custom_call" | custom-call | tf_op jit(solution)/shard_map/pallas_call | solution.py:421
  61.2 4.1 %collective-permute-done.9 = bf16[1,128,1024]{2,1,0:T(8,128)(2,1)S(1)} collective-permute-done((bf16[1,128,1024]{2,1,0:T(8,128)(2,1)S(1)}, bf16[1,128,1024]{2,1,0:T(8,128)(2,1)S(1)}, u32[]{:S(2)}, u32[]{:S(2)}) %collective-permute-start.9) | collective-permute-done | bytes 262176 | tf_op jit(solution)/shard_map/ppermute | solution.py:372
  65.2 1.0 %shard_map.161 = f32[1024,256]{1,0:T(8,128)} custom-call(f32[128,1024]{1,0:T(8,128)S(1)} %get-tuple-element.50.refs_0_, bf16[128,1024]{1,0:T(8,128)(2,1)S(1)} %get-tuple-element.54.refs_1_, bf16[128,1024]{1,0:T(8,128)(2,1)S(1)} %bitcast.21, f32[1024,256]{1,0:T(8,128)} %shard_map.160.refs_3_), custom_call_target="tpu_custom_call", output_to_operand_aliasing={{}: (3, {})} | custom-call | tf_op jit(solution)/shard_map/pallas_call | solution.py:421
  (19 shorter events, 0.8 us)
Async XLA Ops:
  0.0 10.2 %copy-start = (f32[64,1024]{1,0:T(8,128)S(1)}, f32[64,1024]{1,0:T(8,128)}, u32[]{:S(2)}) copy-start(f32[64,1024]{1,0:T(8,128)} %param.24) | copy-start | bytes 786436
  0.0 43.6 %copy-start.1 = (f32[1024]{0:T(1024)S(1)}, f32[1024]{0:T(1024)}, u32[]{:S(2)}) copy-start(f32[1024]{0:T(1024)} %param.26) | copy-start | bytes 12292
  2.1 21.8 %all-to-all-start = ((bf16[8,256,128]{2,1,0:T(8,128)(2,1)}), bf16[8,256,128]{2,1,0:T(8,128)(2,1)S(1)}, u32[]{:S(2)}, u32[]{:S(2)}) async-start(bf16[8,256,128]{2,1,0:T(8,128)(2,1)} %shard_map.154.signal_hbm), calls=%async_computation | async-start | bytes 1048576 | tf_op jit(solution)/shard_map/all_to_all | solution.py:291
  27.6 7.4 %collective-permute-start = (bf16[256,128]{1,0:T(8,128)(2,1)S(1)}, bf16[256,128]{1,0:T(8,128)(2,1)S(1)}, u32[]{:S(2)}, u32[]{:S(2)}) collective-permute-start(bf16[256,128]{1,0:T(8,128)(2,1)S(1)} %get-tuple-element.36), channel_id=1, source_target_pairs={{0,4},{4,0},{8,12},{12,8},{16,20},{20,16},{24,28},{28,24},{1,5},{5... | collective-permute-start | bytes 196616 | tf_op jit(solution)/shard_map/ppermute | solution.py:369
  29.1 7.3 %collective-permute-start.1 = (bf16[256,128]{1,0:T(8,128)(2,1)S(1)}, bf16[256,128]{1,0:T(8,128)(2,1)S(1)}, u32[]{:S(2)}, u32[]{:S(2)}) collective-permute-start(bf16[256,128]{1,0:T(8,128)(2,1)S(1)} %get-tuple-element.37), channel_id=1, source_target_pairs={{0,8},{4,12},{8,0},{12,4},{16,24},{20,28},{24,16},{28,20},{1,9},{5... | collective-permute-start | bytes 196616 | tf_op jit(solution)/shard_map/ppermute | solution.py:369
  29.1 9.7 %collective-permute-start.2 = (bf16[256,128]{1,0:T(8,128)(2,1)S(1)}, bf16[256,128]{1,0:T(8,128)(2,1)S(1)}, u32[]{:S(2)}, u32[]{:S(2)}) collective-permute-start(bf16[256,128]{1,0:T(8,128)(2,1)S(1)} %get-tuple-element.38), channel_id=1, source_target_pairs={{0,12},{4,8},{8,4},{12,0},{16,28},{20,24},{24,20},{28,16},{1,13},{... | collective-permute-start | bytes 196616 | tf_op jit(solution)/shard_map/ppermute | solution.py:369
  31.1 10.1 %collective-permute-start.3 = (bf16[256,128]{1,0:T(8,128)(2,1)S(1)}, bf16[256,128]{1,0:T(8,128)(2,1)S(1)}, u32[]{:S(2)}, u32[]{:S(2)}) collective-permute-start(bf16[256,128]{1,0:T(8,128)(2,1)S(1)} %get-tuple-element.39), channel_id=1, source_target_pairs={{0,16},{4,20},{8,24},{12,28},{16,0},{20,4},{24,8},{28,12},{1,17},{... | collective-permute-start | bytes 196616 | tf_op jit(solution)/shard_map/ppermute | solution.py:369
  31.3 12.3 %collective-permute-start.4 = (bf16[256,128]{1,0:T(8,128)(2,1)S(1)}, bf16[256,128]{1,0:T(8,128)(2,1)S(1)}, u32[]{:S(2)}, u32[]{:S(2)}) collective-permute-start(bf16[256,128]{1,0:T(8,128)(2,1)S(1)} %get-tuple-element.40), channel_id=1, source_target_pairs={{0,20},{4,16},{8,28},{12,24},{16,4},{20,0},{24,12},{28,8},{1,21},{... | collective-permute-start | bytes 196616 | tf_op jit(solution)/shard_map/ppermute | solution.py:369
  34.9 8.6 %collective-permute-start.5 = (bf16[256,128]{1,0:T(8,128)(2,1)S(1)}, bf16[256,128]{1,0:T(8,128)(2,1)S(1)}, u32[]{:S(2)}, u32[]{:S(2)}) collective-permute-start(bf16[256,128]{1,0:T(8,128)(2,1)S(1)} %get-tuple-element.41), channel_id=1, source_target_pairs={{0,24},{4,28},{8,16},{12,20},{16,8},{20,12},{24,0},{28,4},{1,25},{... | collective-permute-start | bytes 196616 | tf_op jit(solution)/shard_map/ppermute | solution.py:369
  36.4 7.1 %collective-permute-start.6 = (bf16[256,128]{1,0:T(8,128)(2,1)S(1)}, bf16[256,128]{1,0:T(8,128)(2,1)S(1)}, u32[]{:S(2)}, u32[]{:S(2)}) collective-permute-start(bf16[256,128]{1,0:T(8,128)(2,1)S(1)} %get-tuple-element.42), channel_id=1, source_target_pairs={{0,28},{4,24},{8,20},{12,16},{16,12},{20,8},{24,4},{28,0},{1,29},{... | collective-permute-start | bytes 196616 | tf_op jit(solution)/shard_map/ppermute | solution.py:369
  44.9 2.0 %collective-permute-start.7 = (bf16[1,256,1024]{2,1,0:T(8,128)(2,1)S(1)}, bf16[1,256,1024]{2,1,0:T(8,128)(2,1)S(1)}, u32[]{:S(2)}, u32[]{:S(2)}) collective-permute-start(bf16[1,256,1024]{2,1,0:T(8,128)(2,1)S(1)} %get-tuple-element.44), channel_id=1, source_target_pairs={{0,1},{1,0},{2,3},{3,2},{4,5},{5,4},{6,7},{7,6},{8,9},{9,8},{10,11... | collective-permute-start | bytes 1572872 | tf_op jit(solution)/shard_map/ppermute | solution.py:372
  50.7 2.5 %collective-permute-start.8 = (bf16[1,256,1024]{2,1,0:T(8,128)(2,1)S(1)}, bf16[1,256,1024]{2,1,0:T(8,128)(2,1)S(1)}, u32[]{:S(2)}, u32[]{:S(2)}) collective-permute-start(bf16[1,256,1024]{2,1,0:T(8,128)(2,1)S(1)} %get-tuple-element.47), channel_id=1, source_target_pairs={{0,1},{1,0},{2,3},{3,2},{4,5},{5,4},{6,7},{7,6},{8,9},{9,8},{10,11... | collective-permute-start | bytes 1572872 | tf_op jit(solution)/shard_map/ppermute | solution.py:372
  50.9 9.2 %collective-permute-start.10 = (bf16[1,128,1024]{2,1,0:T(8,128)(2,1)S(1)}, bf16[1,128,1024]{2,1,0:T(8,128)(2,1)S(1)}, u32[]{:S(2)}, u32[]{:S(2)}) collective-permute-start(bf16[1,128,1024]{2,1,0:T(8,128)(2,1)S(1)} %get-tuple-element.51), channel_id=1, source_target_pairs={{0,2},{1,3},{2,0},{3,1},{4,6},{5,7},{6,4},{7,5},{8,10},{9,11},{10,... | collective-permute-start | bytes 786440 | tf_op jit(solution)/shard_map/ppermute | solution.py:372
  52.5 12.7 %collective-permute-start.9 = (bf16[1,128,1024]{2,1,0:T(8,128)(2,1)S(1)}, bf16[1,128,1024]{2,1,0:T(8,128)(2,1)S(1)}, u32[]{:S(2)}, u32[]{:S(2)}) collective-permute-start(bf16[1,128,1024]{2,1,0:T(8,128)(2,1)S(1)} %get-tuple-element.52), channel_id=1, source_target_pairs={{0,2},{1,3},{2,0},{3,1},{4,6},{5,7},{6,4},{7,5},{8,10},{9,11},{10,... | collective-permute-start | bytes 786440 | tf_op jit(solution)/shard_map/ppermute | solution.py:372

commit v4 on v3

--- a/solution.py
+++ b/solution.py
@@ -124,10 +124,10 @@
 
 
 def conv_kernel(
-    block, far_blocks, index_ref, x_ref, real_ref, imag_ref, edge_ref, table_ref, inverse_ref, weight_hbm,
-    query_hbm, signal_hbm, *refs,
+    block, first_blocks, index_ref, x_ref, real_ref, imag_ref, edge_ref, table_ref, inverse_ref, gain_ref,
+    weight_hbm, query_hbm, signal_hbm, *refs,
 ):
-    *out_refs, weight_out, query_out, signal_out, sig, sre, sim, spec, conv, weight_sem, query_sem, signal_sem = refs
+    *out_refs, weight_out, query_out, signal_out, gain_out, sig, sre, sim, spec, conv, weight_sem, query_sem, signal_sem = refs
     pieces, _, unit = query_out.shape
     copies = []
     for k in range(pieces):
@@ -135,7 +135,8 @@
         cols = pl.ds(pl.multiple_of(piece * unit, LANES), unit)
         copies.append(pltpu.make_async_copy(query_hbm.at[:, cols], query_out.at[k], query_sem.at[k]))
         copies.append(pltpu.make_async_copy(signal_hbm.at[piece], signal_out.at[k], signal_sem.at[k]))
-    copies += weight_copies(index_ref, far_blocks, weight_hbm, weight_out, weight_sem)
+        gain_out[k : k + 1, :] = gain_ref[pl.ds(piece, 1), :]
+    copies += weight_copies(index_ref, first_blocks, weight_hbm, weight_out, weight_sem)
     for copy in copies:
         copy.start()
     slots = x_ref.shape[0]
@@ -188,12 +189,11 @@
         copy.wait()
 
 
-def mix_kernel(index_ref, sig_ref, query_ref, gain_ref, weight_ref, *refs):
+def mix_kernel(sig_ref, query_ref, gain_ref, weight_ref, *refs):
     *back_refs, out_ref, mixed_ref = refs
     unit = sig_ref.shape[2]
     for k, back_ref in enumerate(back_refs):
-        gain = gain_ref[pl.ds(index_ref[1] ^ k, 1), :]
-        inner = back_ref[...].astype(F32) + gain * sig_ref[k].astype(F32)
+        inner = back_ref[...].astype(F32) + gain_ref[k : k + 1, :] * sig_ref[k].astype(F32)
         mixed_ref[:, k * unit : (k + 1) * unit] = (query_ref[k].astype(F32) * inner).astype(BF16)
     project_kernel(0, mixed_ref, weight_ref, out_ref)
 
@@ -204,27 +204,30 @@
         out_ref[i] = jnp.dot(mixed, weight_ref[first + i], preferred_element_type=F32).astype(out_ref.dtype)
 
 
-def near_kernel(near_blocks, index_ref, mixed_ref, weight_hbm, away_ref, kept_ref, weight_near, sem):
-    copies = weight_copies(index_ref, near_blocks, weight_hbm, weight_near, sem)
+def last_kernel(last_blocks, index_ref, mixed_ref, weight_hbm, out_ref, weight_near, sem):
+    copies = weight_copies(index_ref, last_blocks, weight_hbm, weight_near, sem)
     for copy in copies:
         copy.start()
-    count = away_ref.shape[0]
-    for copy in copies[: len(copies) // 2]:
+    for copy in copies:
         copy.wait()
-    project_kernel(0, mixed_ref, weight_near, away_ref)
-    for copy in copies[len(copies) // 2 :]:
-        copy.wait()
-    project_kernel(count, mixed_ref, weight_near, kept_ref)
-
-
-def finish_kernel(part, count, *refs):
-    *operands, out_hbm, turned, sem = refs
+    project_kernel(0, mixed_ref, weight_near, out_ref)
+
+
+def finish_kernel(part, spans, count, *refs):
+    operands, (out_hbm, turned, sem) = refs[: count + len(spans)], refs[-3:]
     rows = turned.shape[1]
-    total = operands[0][...].astype(F32)
-    for term in operands[1:count]:
-        total = total + term[...].astype(F32)
+    first, last = part * rows, (part + 1) * rows
+    total = jnp.concatenate(
+        [
+            ref[max(first, start) - start : min(last, stop) - start, :].astype(F32)
+            for ref, (start, stop) in zip(operands[count:], spans)
+        ],
+        0,
+    )
+    for ref in operands[:count]:
+        total = total + ref[first:last, :].astype(F32)
     turned[...] = total.T
-    copy = pltpu.make_async_copy(turned, out_hbm.at[:, part * rows : (part + 1) * rows], sem.at[0])
+    copy = pltpu.make_async_copy(turned, out_hbm.at[:, first:last], sem.at[0])
     copy.start()
     copy.wait()
 
@@ -336,30 +339,34 @@
     index = jnp.concatenate([chan_index[None], base[None], group_order])
     quarter = chan_count // 4
     odd = range(1, chan_count, 2)
-    far_blocks = [j for j in odd if j & 2] + [j ^ 1 for j in odd if j & 2]
-    near_blocks = [j for j in odd if not j & 2] + [j ^ 1 for j in odd if not j & 2]
-    *convolved, weights, query_near, signal_near = pl.pallas_call(
-        functools.partial(conv_kernel, block, far_blocks),
+    first_blocks = [j for j in odd if j & 2] + [j ^ 1 for j in odd if j & 2] + [j for j in odd if not j & 2]
+    last_blocks = [j ^ 1 for j in odd if not j & 2]
+    *convolved, weights, query_near, signal_near, gain_near = pl.pallas_call(
+        functools.partial(conv_kernel, block, first_blocks),
         out_shape=(
             *[jax.ShapeDtypeStruct((rows, LANES), BF16)] * seq_count,
-            jax.ShapeDtypeStruct((2 * quarter, chan_width, out_width), BF16),
+            jax.ShapeDtypeStruct((3 * quarter, chan_width, out_width), BF16),
             jax.ShapeDtypeStruct((pieces, rows, unit), BF16),
             jax.ShapeDtypeStruct((pieces, rows, unit), BF16),
+            jax.ShapeDtypeStruct((pieces, unit), F32),
         ),
-        in_specs=[in_smem] + [in_vmem] * 6 + [in_hbm] * 3,
-        out_specs=[in_vmem] * (seq_count + 3),
+        in_specs=[in_smem] + [in_vmem] * 7 + [in_hbm] * 3,
+        out_specs=[in_vmem] * (seq_count + 4),
         scratch_shapes=[
             pltpu.VMEM((length, LANES), BF16),
             pltpu.VMEM((blocks, block, LANES), F32),
             pltpu.VMEM((blocks, block, LANES), F32),
             pltpu.VMEM((2 * block, blocks * LANES), BF16),
             pltpu.VMEM((length, LANES), BF16),
-            pltpu.SemaphoreType.DMA((2 * quarter, pieces)),
+            pltpu.SemaphoreType.DMA((3 * quarter, pieces)),
             pltpu.SemaphoreType.DMA((pieces,)),
             pltpu.SemaphoreType.DMA((pieces,)),
         ],
         compiler_params=limit,
-    )(index, spread, real, imag, edge, head, inverse, *map(far, (out_weight, query, signal)))
+    )(
+        index, spread, real, imag, edge, head, inverse, skip_gain.reshape(pieces, unit),
+        *map(far, (out_weight, query, signal)),
+    )
     if pieces == 1:
         ordered = lax.all_to_all(jnp.stack([piece[:, :width] for piece in convolved]), "seq", 0, 0, tiled=True)
         backs = [ordered.transpose(1, 0, 2).reshape(rows, chan_width)]
@@ -377,53 +384,57 @@
             jax.ShapeDtypeStruct((quarter, rows, out_width), BF16),
             jax.ShapeDtypeStruct((rows, chan_width), BF16),
         ),
-        in_specs=[in_smem] + [in_vmem] * (4 + pieces),
+        in_specs=[in_vmem] * (4 + pieces),
         out_specs=[in_vmem] * 2,
         compiler_params=limit,
-    )(index, signal_near, query_near, skip_gain.reshape(pieces, unit), weights, *backs)
+    )(signal_near, query_near, gain_near, weights, *backs)
     far_terms = exchange(far_away, 1)
-    far_kept = pl.pallas_call(
-        functools.partial(project_kernel, quarter),
+
+    def products(first, dtype):
+        return pl.pallas_call(
+            functools.partial(project_kernel, first),
+            out_shape=jax.ShapeDtypeStruct((quarter, rows, out_width), dtype),
+            in_specs=[in_vmem] * 2,
+            out_specs=in_vmem,
+            compiler_params=limit,
+        )(mixed, weights)
+
+    far_kept, near_away = products(quarter, F32), products(2 * quarter, BF16)
+    cuts = [0, rows // 2, rows]
+    spans = list(zip(cuts, cuts[1:]))
+    send = [(far_kept[:, a:b] + far_terms[:, a:b].astype(F32)).astype(BF16) for a, b in spans]
+    send, near_away, mixed = lax.optimization_barrier((send, near_away, mixed))
+    sent = [exchange(piece, 2) for piece in send]
+    near_terms = exchange(near_away, 1)
+    near_kept = pl.pallas_call(
+        functools.partial(last_kernel, last_blocks),
         out_shape=jax.ShapeDtypeStruct((quarter, rows, out_width), F32),
-        in_specs=[in_vmem] * 2,
+        in_specs=[in_smem, in_vmem, in_hbm],
         out_specs=in_vmem,
-        compiler_params=limit,
-    )(mixed, weights)
-    send, mixed = lax.optimization_barrier(((far_kept + far_terms.astype(F32)).astype(BF16), mixed))
-    half = rows // 2
-    halves = [slice(0, half), slice(half, rows)]
-    sent = [exchange(send[:, part], 2) for part in halves]
-    near_away, near_kept = pl.pallas_call(
-        functools.partial(near_kernel, near_blocks),
-        out_shape=(
-            jax.ShapeDtypeStruct((quarter, rows, out_width), BF16),
-            jax.ShapeDtypeStruct((quarter, rows, out_width), F32),
-        ),
-        in_specs=[in_smem, in_vmem, in_hbm],
-        out_specs=[in_vmem] * 2,
         scratch_shapes=[
-            pltpu.VMEM((2 * quarter, chan_width, out_width), BF16),
-            pltpu.SemaphoreType.DMA((2 * quarter, pieces)),
+            pltpu.VMEM((quarter, chan_width, out_width), BF16),
+            pltpu.SemaphoreType.DMA((quarter, pieces)),
         ],
         compiler_params=limit,
     )(index, mixed, far(out_weight))
-    near_terms = exchange(near_away, 1)
+    terms = [near_kept, near_terms]
+    bit = 4
+    while bit < chan_count:
+        total = terms[0] + terms[1].astype(F32) + jnp.concatenate(sent, 1).astype(F32)
+        sent, spans = [exchange(total[1::2].astype(BF16), bit)], [(0, rows)]
+        terms = [total[0::2], jnp.zeros_like(total[0::2])]
+        bit *= 2
     result = None
-    for i, part in enumerate(halves):
-        terms = [near_kept[:, part], near_terms[:, part], sent[i]]
-        bit = 4
-        while bit < chan_count:
-            total = sum(term.astype(F32) for term in terms)
-            terms = [total[0::2], exchange(total[1::2].astype(BF16), bit)]
-            bit *= 2
-        operands = [term[0] for term in terms]
+    for i in range(rows // GROUP):
+        held = [j for j, (a, b) in enumerate(spans) if a < (i + 1) * GROUP and b > i * GROUP]
+        operands = [term[0] for term in terms] + [sent[j][0] for j in held]
         extra = [] if result is None else [result]
         result = pl.pallas_call(
-            functools.partial(finish_kernel, i, len(operands)),
+            functools.partial(finish_kernel, i, [spans[j] for j in held], len(terms)),
             out_shape=jax.ShapeDtypeStruct((out_width, rows), F32),
             in_specs=[in_vmem] * len(operands) + [in_hbm] * len(extra),
             out_specs=in_hbm,
-            scratch_shapes=[pltpu.VMEM((out_width, half), F32), pltpu.SemaphoreType.DMA((1,))],
+            scratch_shapes=[pltpu.VMEM((out_width, GROUP), F32), pltpu.SemaphoreType.DMA((1,))],
             input_output_aliases={len(operands): 0} if extra else {},
             compiler_params=limit,
         )(*operands, *extra)

time: 66.5 us -> 63.7 us (0.958)
  waiting for transfers between devices: 21.8 us -> 18.4 us
    ppermute x4, waiting for transfers between devices: 12.2 us -> 8.75 us  [exchange(): lax.ppermute(terms, 'chan', [(d, d ^ bit) for d in range(chan_count)])]
    unnamed x4, local copies, waits for them, and re-layouts: 0.01 us -> 0.69 us
    pallas_call x5 -> x6, Pallas kernels: 10 us -> 10.7 us  [the longest x1 4.37 us: local(): pl.pallas_call(functools.partial(conv_kernel, block, first_blocks), out_s...]
  transfers between devices with their start and end apart: 12 -> 12, of which waited for: 6 -> 6; matrix products, arithmetic and copies ran while one was open for 3% -> 2% of each run, Pallas kernels for 15% -> 21%
where the time goes in v4:
time: 63.7 us; the launch traced here: 63.3 us
  Pallas kernels  21.7 us (34%)
  starting transfers between devices  20.8 us (33%)
  waiting for transfers between devices  18.4 us (29%)
  other arithmetic  1.67 us (3%)
  local copies, waits for them, and re-layouts  0.71 us (1%)
    ppermute x7, starting transfers between devices, local(): lax.ppermute(convolved[k], 'seq', [(d, d ^ k) for d in range(seq_count)])  11.2 us
    ppermute x4, waiting for transfers between devices, exchange(): lax.ppermute(terms, 'chan', [(d, d ^ bit) for d in range(chan_count)])  8.75 us
    pallas_call x1, Pallas kernels, local(): pl.pallas_call(functools.partial(filter_kernel, block), out_shape=(jax.Sh...  8.13 us
    all_to_all x1, starting transfers between devices, local(): lax.all_to_all(signal, 'seq', 0, 0, tiled=True).reshape(slots, GROUP, width)  7.26 us
    all_to_all x1, waiting for transfers between devices, local(): lax.all_to_all(signal, 'seq', 0, 0, tiled=True).reshape(slots, GROUP, width)  4.82 us
    ppermute x7, waiting for transfers between devices, local(): lax.ppermute(convolved[k], 'seq', [(d, d ^ k) for d in range(seq_count)])  4.79 us
    pallas_call x1, Pallas kernels, local(): pl.pallas_call(functools.partial(conv_kernel, block, first_blocks), out_s...  4.37 us
    pallas_call x1, Pallas kernels, local(): pl.pallas_call(functools.partial(last_kernel, last_blocks), out_shape=jax...  2.84 us
  transfers between devices with their start and end apart: 12, of which 6 were waited for; matrix products, arithmetic and copies ran while one was open for 2% of the time, Pallas kernels for 21%

profile of v4, /device:TPU:0, one launch (start us, length us, event | category | flops | bytes accessed | tf_op | source)
XLA Modules:
  0.0 63.3 jit_solution(7042887769290144643)
XLA Ops:
  0.0 2.1 %shard_map.154.signal_hbm = bf16[8,256,128]{2,1,0:T(8,128)(2,1)} custom-call(bf16[256,1024]{1,0:T(8,128)(2,1)} %key_hbm.1, bf16[256,1024]{1,0:T(8,128)(2,1)} %value_hbm.1), custom_call_target="tpu_custom_call" | custom-call | tf_op jit(solution)/shard_map/pallas_call | solution.py:280
  2.1 7.3 %all-to-all-start = ((bf16[8,256,128]{2,1,0:T(8,128)(2,1)}), bf16[8,256,128]{2,1,0:T(8,128)(2,1)S(1)}, u32[]{:S(2)}, u32[]{:S(2)}) async-start(bf16[8,256,128]{2,1,0:T(8,128)(2,1)} %shard_map.154.signal_hbm), calls=%async_computation | async-start | bytes 1048576 | tf_op jit(solution)/shard_map/all_to_all | solution.py:294
  9.4 0.8 %sqrt_bitcast_fusion = (f32[1,128]{1,0:T(1,128)S(1)}, f32[1,128]{1,0:T(1,128)S(1)}) fusion(f32[1024]{0:T(1024)} %param.25, s32[]{:T(128)S(6)} %select_n.4), kind=kLoop, calls=%fused_computation.5 | loop fusion | flops 256 | bytes 1540 | tf_op jit(solution)/shard_map/sqrt | solution.py:298
  10.2 8.1 %shard_map.155 = (f32[8,256,128]{2,1,0:T(8,128)S(1)}, f32[8,256,128]{2,1,0:T(8,128)S(1)}, f32[8,16,128]{2,1,0:T(8,128)S(1)}, bf16[512,256]{1,0:T(8,128)(2,1)S(1)}, bf16[256,512]{1,0:T(8,128)(2,1)S(1)}) custom-call(f32[64,128]{1,0:T(8,128)S(1)} %constant_dynamic-slice_fusion.out_w_ref, f32[1,128]{1,0:T(1,128)S(1)} %get-tuple-element.54.decay_ref, ...), custom_call_target="tpu_custom_call" | custom-call | tf_op jit(solution)/shard_map/pallas_call | solution.py:304
  18.3 0.7 %pad_add_fusion.index_ref = s32[18]{0:T(128)S(1)} fusion(s32[16]{0:T(128)} %param.19, s32[1]{0:T(128)} %bitcast.1, s32[1]{0:T(128)} %bitcast), kind=kLoop, calls=%fused_computation.4 | loop fusion | flops 36 | bytes 144 | tf_op jit(solution)/shard_map/concatenate | solution.py:339
  19.1 4.8 %all-to-all-done = bf16[8,256,128]{2,1,0:T(8,128)(2,1)S(1)} async-done(((bf16[8,256,128]{2,1,0:T(8,128)(2,1)}), bf16[8,256,128]{2,1,0:T(8,128)(2,1)S(1)}, u32[]{:S(2)}, u32[]{:S(2)}) %all-to-all-start) | async-done | bytes 524320 | tf_op jit(solution)/shard_map/all_to_all | solution.py:294
  23.9 0.7 %copy-done.1 = f32[1024]{0:T(1024)S(1)} copy-done((f32[1024]{0:T(1024)S(1)}, f32[1024]{0:T(1024)}, u32[]{:S(2)}) %copy-start.1) | copy-done | bytes 4120
  24.6 4.4 %shard_map.156 = (bf16[256,128]{1,0:T(8,128)(2,1)S(1)}, bf16[256,128]{1,0:T(8,128)(2,1)S(1)}, bf16[256,128]{1,0:T(8,128)(2,1)S(1)}, bf16[256,128]{1,0:T(8,128)(2...) custom-call(s32[18]{0:T(128)S(1)} %pad_add_fusion.index_ref, ...), custom_call_target="tpu_custom_call" | custom-call | tf_op jit(solution)/shard_map/pallas_call | solution.py:344
  28.9 1.5 %collective-permute-start = (bf16[256,128]{1,0:T(8,128)(2,1)S(1)}, bf16[256,128]{1,0:T(8,128)(2,1)S(1)}, u32[]{:S(2)}, u32[]{:S(2)}) collective-permute-start(bf16[256,128]{1,0:T(8,128)(2,1)S(1)} %get-tuple-element.38), channel_id=1, source_target_pairs={{0,4},{4,0},{8,12},{12,8},{16,20},{20,16},{24,28},{28,24},{1,5},{5... | collective-permute-start | bytes 196616 | tf_op jit(solution)/shard_map/ppermute | solution.py:376
  30.5 2.0 %collective-permute-start.2 = (bf16[256,128]{1,0:T(8,128)(2,1)S(1)}, bf16[256,128]{1,0:T(8,128)(2,1)S(1)}, u32[]{:S(2)}, u32[]{:S(2)}) collective-permute-start(bf16[256,128]{1,0:T(8,128)(2,1)S(1)} %get-tuple-element.40), channel_id=1, source_target_pairs={{0,12},{4,8},{8,4},{12,0},{16,28},{20,24},{24,20},{28,16},{1,13},{... | collective-permute-start | bytes 196616 | tf_op jit(solution)/shard_map/ppermute | solution.py:376
  32.6 3.7 %collective-permute-start.4 = (bf16[256,128]{1,0:T(8,128)(2,1)S(1)}, bf16[256,128]{1,0:T(8,128)(2,1)S(1)}, u32[]{:S(2)}, u32[]{:S(2)}) collective-permute-start(bf16[256,128]{1,0:T(8,128)(2,1)S(1)} %get-tuple-element.42), channel_id=1, source_target_pairs={{0,20},{4,16},{8,28},{12,24},{16,4},{20,0},{24,12},{28,8},{1,21},{... | collective-permute-start | bytes 196616 | tf_op jit(solution)/shard_map/ppermute | solution.py:376
  36.3 1.5 %collective-permute-start.5 = (bf16[256,128]{1,0:T(8,128)(2,1)S(1)}, bf16[256,128]{1,0:T(8,128)(2,1)S(1)}, u32[]{:S(2)}, u32[]{:S(2)}) collective-permute-start(bf16[256,128]{1,0:T(8,128)(2,1)S(1)} %get-tuple-element.43), channel_id=1, source_target_pairs={{0,24},{4,28},{8,16},{12,20},{16,8},{20,12},{24,0},{28,4},{1,25},{... | collective-permute-start | bytes 196616 | tf_op jit(solution)/shard_map/ppermute | solution.py:376
  37.8 2.4 %collective-permute-start.6 = (bf16[256,128]{1,0:T(8,128)(2,1)S(1)}, bf16[256,128]{1,0:T(8,128)(2,1)S(1)}, u32[]{:S(2)}, u32[]{:S(2)}) collective-permute-start(bf16[256,128]{1,0:T(8,128)(2,1)S(1)} %get-tuple-element.44), channel_id=1, source_target_pairs={{0,28},{4,24},{8,20},{12,16},{16,12},{20,8},{24,4},{28,0},{1,29},{... | collective-permute-start | bytes 196616 | tf_op jit(solution)/shard_map/ppermute | solution.py:376
  40.2 2.4 %collective-permute-done.3.refs_4_ = bf16[256,128]{1,0:T(8,128)(2,1)S(1)} collective-permute-done((bf16[256,128]{1,0:T(8,128)(2,1)S(1)}, bf16[256,128]{1,0:T(8,128)(2,1)S(1)}, u32[]{:S(2)}, u32[]{:S(2)}) %collective-permute-start.3) | collective-permute-done | bytes 65568 | tf_op jit(solution)/shard_map/ppermute | solution.py:376
  42.6 2.4 %collective-permute-done.4.refs_5_ = bf16[256,128]{1,0:T(8,128)(2,1)S(1)} collective-permute-done((bf16[256,128]{1,0:T(8,128)(2,1)S(1)}, bf16[256,128]{1,0:T(8,128)(2,1)S(1)}, u32[]{:S(2)}, u32[]{:S(2)}) %collective-permute-start.4) | collective-permute-done | bytes 65568 | tf_op jit(solution)/shard_map/ppermute | solution.py:376
  44.9 0.8 %shard_map.157 = (bf16[1,256,1024]{2,1,0:T(8,128)(2,1)S(1)}, bf16[256,1024]{1,0:T(8,128)(2,1)S(1)}) custom-call(bf16[8,256,128]{2,1,0:T(8,128)(2,1)S(1)} %get-tuple-element.33.sig_ref, bf16[8,256,128]{2,1,0:T(8,128)(2,1)S(1)} %get-tuple-element.34.query_ref, f32[8,128]{1,0:T(8,128)S(1)} %get-tuple-element.35.gain_ref, ...), custom_call_target="tpu_custom_call" | custom-call | tf_op jit(solution)/shard_map/pallas_call | solution.py:381
  45.8 0.7 %shard_map.159 = bf16[1,256,1024]{2,1,0:T(8,128)(2,1)S(1)} custom-call(bf16[256,1024]{1,0:T(8,128)(2,1)S(1)} %get-tuple-element.47.mixed_ref, bf16[3,1024,1024]{2,1,0:T(8,128)(2,1)S(1)} %get-tuple-element.36.weight_ref), custom_call_target="tpu_custom_call" | custom-call | tf_op jit(solution)/shard_map/pallas_call | solution.py:394
  46.6 0.7 %shard_map.158 = f32[1,256,1024]{2,1,0:T(8,128)S(1)} custom-call(bf16[256,1024]{1,0:T(8,128)(2,1)S(1)} %get-tuple-element.47.mixed_ref, bf16[3,1024,1024]{2,1,0:T(8,128)(2,1)S(1)} %get-tuple-element.36.weight_ref), custom_call_target="tpu_custom_call" | custom-call | tf_op jit(solution)/shard_map/pallas_call | solution.py:394
  48.1 1.5 %collective-permute-start.10 = (bf16[1,128,1024]{2,1,0:T(8,128)(2,1)S(1)}, bf16[1,128,1024]{2,1,0:T(8,128)(2,1)S(1)}, u32[]{:S(2)}, u32[]{:S(2)}) collective-permute-start(bf16[1,128,1024]{2,1,0:T(8,128)(2,1)S(1)} %get-tuple-element.50), channel_id=1, source_target_pairs={{0,2},{1,3},{2,0},{3,1},{4,6},{5,7},{6,4},{7,5},{8,10},{9,11},{10,... | collective-permute-start | bytes 786440 | tf_op jit(solution)/shard_map/ppermute | solution.py:379
  50.2 2.8 %shard_map.160 = f32[1,256,1024]{2,1,0:T(8,128)S(1)} custom-call(s32[18]{0:T(128)S(1)} %pad_add_fusion.index_ref, bf16[256,1024]{1,0:T(8,128)(2,1)S(1)} %get-tuple-element.47.mixed_ref, bf16[1024,4096]{1,0:T(8,128)(2,1)} %weight_hbm.3), custom_call_target="tpu_custom_call" | custom-call | tf_op jit(solution)/shard_map/pallas_call | solution.py:409
  53.0 4.3 %collective-permute-done.10 = bf16[1,128,1024]{2,1,0:T(8,128)(2,1)S(1)} collective-permute-done((bf16[1,128,1024]{2,1,0:T(8,128)(2,1)S(1)}, bf16[1,128,1024]{2,1,0:T(8,128)(2,1)S(1)}, u32[]{:S(2)}, u32[]{:S(2)}) %collective-permute-start.10) | collective-permute-done | bytes 262176 | tf_op jit(solution)/shard_map/ppermute | solution.py:379
  57.3 1.0 %shard_map.161.refs_3_ = f32[1024,256]{1,0:T(8,128)} custom-call(f32[256,1024]{1,0:T(8,128)S(1)} %bitcast.14, bf16[256,1024]{1,0:T(8,128)(2,1)S(1)} %bitcast.17, bf16[128,1024]{1,0:T(8,128)(2,1)S(1)} %bitcast.19), custom_call_target="tpu_custom_call" | custom-call | tf_op jit(solution)/shard_map/pallas_call | solution.py:432
  58.3 4.0 %collective-permute-done.9 = bf16[1,128,1024]{2,1,0:T(8,128)(2,1)S(1)} collective-permute-done((bf16[1,128,1024]{2,1,0:T(8,128)(2,1)S(1)}, bf16[1,128,1024]{2,1,0:T(8,128)(2,1)S(1)}, u32[]{:S(2)}, u32[]{:S(2)}) %collective-permute-start.9) | collective-permute-done | bytes 262176 | tf_op jit(solution)/shard_map/ppermute | solution.py:379
  62.3 1.0 %shard_map.162 = f32[1024,256]{1,0:T(8,128)} custom-call(f32[256,1024]{1,0:T(8,128)S(1)} %bitcast.15, bf16[256,1024]{1,0:T(8,128)(2,1)S(1)} %bitcast.18, bf16[128,1024]{1,0:T(8,128)(2,1)S(1)} %bitcast.20, f32[1024,256]{1,0:T(8,128)} %shard_map.161.refs_3_), custom_call_target="tpu_custom_call", output_to_operand_aliasing={{}: (3, {})} | custom-call | tf_op jit(solution)/shard_map/pallas_call | solution.py:432
  (17 shorter events, 1.6 us)
Async XLA Ops:
  0.0 10.2 %copy-start = (f32[64,1024]{1,0:T(8,128)S(1)}, f32[64,1024]{1,0:T(8,128)}, u32[]{:S(2)}) copy-start(f32[64,1024]{1,0:T(8,128)} %param.24) | copy-start | bytes 786436
  2.1 21.8 %all-to-all-start = ((bf16[8,256,128]{2,1,0:T(8,128)(2,1)}), bf16[8,256,128]{2,1,0:T(8,128)(2,1)S(1)}, u32[]{:S(2)}, u32[]{:S(2)}) async-start(bf16[8,256,128]{2,1,0:T(8,128)(2,1)} %shard_map.154.signal_hbm), calls=%async_computation | async-start | bytes 1048576 | tf_op jit(solution)/shard_map/all_to_all | solution.py:294
  23.9 0.7 %copy-start.1 = (f32[1024]{0:T(1024)S(1)}, f32[1024]{0:T(1024)}, u32[]{:S(2)}) copy-start(f32[1024]{0:T(1024)} %param.26) | copy-start | bytes 12292
  28.9 7.4 %collective-permute-start = (bf16[256,128]{1,0:T(8,128)(2,1)S(1)}, bf16[256,128]{1,0:T(8,128)(2,1)S(1)}, u32[]{:S(2)}, u32[]{:S(2)}) collective-permute-start(bf16[256,128]{1,0:T(8,128)(2,1)S(1)} %get-tuple-element.38), channel_id=1, source_target_pairs={{0,4},{4,0},{8,12},{12,8},{16,20},{20,16},{24,28},{28,24},{1,5},{5... | collective-permute-start | bytes 196616 | tf_op jit(solution)/shard_map/ppermute | solution.py:376
  30.5 7.3 %collective-permute-start.1 = (bf16[256,128]{1,0:T(8,128)(2,1)S(1)}, bf16[256,128]{1,0:T(8,128)(2,1)S(1)}, u32[]{:S(2)}, u32[]{:S(2)}) collective-permute-start(bf16[256,128]{1,0:T(8,128)(2,1)S(1)} %get-tuple-element.39), channel_id=1, source_target_pairs={{0,8},{4,12},{8,0},{12,4},{16,24},{20,28},{24,16},{28,20},{1,9},{5... | collective-permute-start | bytes 196616 | tf_op jit(solution)/shard_map/ppermute | solution.py:376
  30.5 9.7 %collective-permute-start.2 = (bf16[256,128]{1,0:T(8,128)(2,1)S(1)}, bf16[256,128]{1,0:T(8,128)(2,1)S(1)}, u32[]{:S(2)}, u32[]{:S(2)}) collective-permute-start(bf16[256,128]{1,0:T(8,128)(2,1)S(1)} %get-tuple-element.40), channel_id=1, source_target_pairs={{0,12},{4,8},{8,4},{12,0},{16,28},{20,24},{24,20},{28,16},{1,13},{... | collective-permute-start | bytes 196616 | tf_op jit(solution)/shard_map/ppermute | solution.py:376
  32.5 10.1 %collective-permute-start.3 = (bf16[256,128]{1,0:T(8,128)(2,1)S(1)}, bf16[256,128]{1,0:T(8,128)(2,1)S(1)}, u32[]{:S(2)}, u32[]{:S(2)}) collective-permute-start(bf16[256,128]{1,0:T(8,128)(2,1)S(1)} %get-tuple-element.41), channel_id=1, source_target_pairs={{0,16},{4,20},{8,24},{12,28},{16,0},{20,4},{24,8},{28,12},{1,17},{... | collective-permute-start | bytes 196616 | tf_op jit(solution)/shard_map/ppermute | solution.py:376
  32.6 12.3 %collective-permute-start.4 = (bf16[256,128]{1,0:T(8,128)(2,1)S(1)}, bf16[256,128]{1,0:T(8,128)(2,1)S(1)}, u32[]{:S(2)}, u32[]{:S(2)}) collective-permute-start(bf16[256,128]{1,0:T(8,128)(2,1)S(1)} %get-tuple-element.42), channel_id=1, source_target_pairs={{0,20},{4,16},{8,28},{12,24},{16,4},{20,0},{24,12},{28,8},{1,21},{... | collective-permute-start | bytes 196616 | tf_op jit(solution)/shard_map/ppermute | solution.py:376
  36.3 8.6 %collective-permute-start.5 = (bf16[256,128]{1,0:T(8,128)(2,1)S(1)}, bf16[256,128]{1,0:T(8,128)(2,1)S(1)}, u32[]{:S(2)}, u32[]{:S(2)}) collective-permute-start(bf16[256,128]{1,0:T(8,128)(2,1)S(1)} %get-tuple-element.43), channel_id=1, source_target_pairs={{0,24},{4,28},{8,16},{12,20},{16,8},{20,12},{24,0},{28,4},{1,25},{... | collective-permute-start | bytes 196616 | tf_op jit(solution)/shard_map/ppermute | solution.py:376
  37.8 7.1 %collective-permute-start.6 = (bf16[256,128]{1,0:T(8,128)(2,1)S(1)}, bf16[256,128]{1,0:T(8,128)(2,1)S(1)}, u32[]{:S(2)}, u32[]{:S(2)}) collective-permute-start(bf16[256,128]{1,0:T(8,128)(2,1)S(1)} %get-tuple-element.44), channel_id=1, source_target_pairs={{0,28},{4,24},{8,20},{12,16},{16,12},{20,8},{24,4},{28,0},{1,29},{... | collective-permute-start | bytes 196616 | tf_op jit(solution)/shard_map/ppermute | solution.py:376
  45.8 2.0 %collective-permute-start.7 = (bf16[1,256,1024]{2,1,0:T(8,128)(2,1)S(1)}, bf16[1,256,1024]{2,1,0:T(8,128)(2,1)S(1)}, u32[]{:S(2)}, u32[]{:S(2)}) collective-permute-start(bf16[1,256,1024]{2,1,0:T(8,128)(2,1)S(1)} %get-tuple-element.46), channel_id=1, source_target_pairs={{0,1},{1,0},{2,3},{3,2},{4,5},{5,4},{6,7},{7,6},{8,9},{9,8},{10,11... | collective-permute-start | bytes 1572872 | tf_op jit(solution)/shard_map/ppermute | solution.py:379
  47.9 9.3 %collective-permute-start.8 = (bf16[1,256,1024]{2,1,0:T(8,128)(2,1)S(1)}, bf16[1,256,1024]{2,1,0:T(8,128)(2,1)S(1)}, u32[]{:S(2)}, u32[]{:S(2)}) collective-permute-start(bf16[1,256,1024]{2,1,0:T(8,128)(2,1)S(1)} %shard_map.159), channel_id=1, source_target_pairs={{0,1},{1,0},{2,3},{3,2},{4,5},{5,4},{6,7},{7,6},{8,9},{9,8},{10,11... | collective-permute-start | bytes 1572872 | tf_op jit(solution)/shard_map/ppermute | solution.py:379
  48.1 9.1 %collective-permute-start.10 = (bf16[1,128,1024]{2,1,0:T(8,128)(2,1)S(1)}, bf16[1,128,1024]{2,1,0:T(8,128)(2,1)S(1)}, u32[]{:S(2)}, u32[]{:S(2)}) collective-permute-start(bf16[1,128,1024]{2,1,0:T(8,128)(2,1)S(1)} %get-tuple-element.50), channel_id=1, source_target_pairs={{0,2},{1,3},{2,0},{3,1},{4,6},{5,7},{6,4},{7,5},{8,10},{9,11},{10,... | collective-permute-start | bytes 786440 | tf_op jit(solution)/shard_map/ppermute | solution.py:379
  49.6 12.7 %collective-permute-start.9 = (bf16[1,128,1024]{2,1,0:T(8,128)(2,1)S(1)}, bf16[1,128,1024]{2,1,0:T(8,128)(2,1)S(1)}, u32[]{:S(2)}, u32[]{:S(2)}) collective-permute-start(bf16[1,128,1024]{2,1,0:T(8,128)(2,1)S(1)} %get-tuple-element.49), channel_id=1, source_target_pairs={{0,2},{1,3},{2,0},{3,1},{4,6},{5,7},{6,4},{7,5},{8,10},{9,11},{10,... | collective-permute-start | bytes 786440 | tf_op jit(solution)/shard_map/ppermute | solution.py:379

commit v5 on v4

v5 whole, which is shorter than its diff:
```python
import functools
import math

import jax
import jax.numpy as jnp
import numpy as np
from jax import lax
from jax.experimental import pallas as pl
from jax.experimental.pallas import tpu as pltpu
from jax.sharding import PartitionSpec as P

GROUP = 128
LANES = 128
SINE_FREQ = 2.0
F32 = jnp.float32
BF16 = jnp.bfloat16


def packed_tables(block):
    period = 2 * block
    row = np.arange(block)
    freq = np.arange(block)

    def forward(shift):
        angle = 2.0 * np.pi * (freq[:, None] * (row[None, :] + shift) % period) / period
        real, imag = np.cos(angle), -np.sin(angle)
        imag[0] = np.where((row + shift) % 2 == 0, 1.0, -1.0)
        return np.concatenate([real, imag], 0)

    head, tail = forward(0), forward(block)
    tail[:, 0] = 0.0
    weight = np.where(freq == 0, 1.0, 2.0) / period
    angle = 2.0 * np.pi * (row[:, None] * freq[None, :] % period) / period
    real, imag = np.cos(angle) * weight, -np.sin(angle) * weight
    imag[:, 0] = np.where(row % 2 == 0, 1.0, -1.0) / period
    inverse = np.concatenate([real, imag], 1)
    to_bf16 = lambda table: jnp.asarray(table.astype(np.float32)).astype(BF16)
    return to_bf16(head), to_bf16(np.concatenate([head, tail], 1)), to_bf16(inverse)


def feature_table(length, bands, rows):
    lag = np.arange(length)
    angle = 2.0 * np.pi * (np.arange(1, bands + 1)[:, None] * lag[None, :] % length) / length
    table = np.zeros((rows, length), np.float32)
    table[0] = lag / length
    table[1 : bands + 1] = np.cos(angle)
    table[bands + 1 : 2 * bands + 1] = np.sin(angle)
    table[2 * bands + 1] = 1.0
    return jnp.asarray(table)


def sine(x):
    n = jnp.round(x * (1.0 / math.pi))
    r = x - n * 3.140625
    r = r - n * 9.67502593994140625e-4
    r = r - n * 1.509957990978376432e-7
    square = r * r
    series = jnp.full_like(r, -2.5052108e-8)
    for term in (2.7557319e-6, -1.9841270e-4, 8.3333333e-3, -1.6666667e-1):
        series = series * square + term
    odd = n * 0.5 - jnp.floor(n * 0.5)
    return (r + r * square * series) * (1.0 - 4.0 * odd)


def contract_first(lhs, rhs):
    return lax.dot_general(
        lhs, rhs, (((0,), (0,)), ((), ())), precision=lax.Precision.HIGHEST, preferred_element_type=F32
    )


def first_piece(pieces):
    return lax.axis_index("seq") if pieces > 1 else 0


def filter_kernel(
    block, order_of_blocks, out_w_ref, decay_ref, norm_ref, *refs,
):
    smalls, refs = refs[:7], refs[7:]
    weight_hbm, query_hbm, real_ref, imag_ref, edge_ref, weight_out, query_out, gain_out, *refs = refs
    near, (w1, w2, hid, filt, near_sem, weight_sem, query_sem) = refs[:7], refs[7:]
    feat_ref, emb_w_ref, emb_b_ref, mid_w_ref, mid_b_ref, gain_ref, table_ref = near
    fetches = [pltpu.make_async_copy(s, t, near_sem.at[i]) for i, (s, t) in enumerate(zip(smalls, near))]
    for fetch in fetches:
        fetch.start()
    pieces, _, unit = query_out.shape
    width = weight_out.shape[2]
    chan_index, first = lax.axis_index("chan"), first_piece(pieces)
    copies = []
    for k in range(pieces):
        rows = pl.ds(pl.multiple_of((first ^ k) * unit, LANES), unit)
        copies.append(pltpu.make_async_copy(query_hbm.at[:, rows], query_out.at[k], query_sem.at[k]))
        for i, j in enumerate(order_of_blocks):
            cols = pl.ds(pl.multiple_of((chan_index ^ j) * width, LANES), width)
            target = weight_out.at[i, k * unit : (k + 1) * unit]
            copies.append(pltpu.make_async_copy(weight_hbm.at[rows, cols], target, weight_sem.at[i, k]))
    for copy in copies:
        copy.start()
    for fetch in fetches[:-1]:
        fetch.wait()
    for k in range(pieces):
        gain_out[k : k + 1, :] = gain_ref[pl.ds(first ^ k, 1), :]
    emb, order = emb_w_ref.shape
    length = feat_ref.shape[1]
    blocks = length // block
    w1[...] = jnp.zeros_like(w1)
    w1[0:emb, :] = emb_w_ref[...]
    w1[emb : emb + 1, :] = emb_b_ref[...]
    w2[...] = jnp.zeros_like(w2)
    w2[0:order, :] = mid_w_ref[...]
    w2[order : order + 1, :] = mid_b_ref[...]
    hid[order:, :] = jnp.ones_like(hid[order:, :])
    hid[0:order, :] = sine(SINE_FREQ * contract_first(w1[...], feat_ref[...]))
    hidden = sine(SINE_FREQ * contract_first(w2[...], hid[...]))
    raw = contract_first(hidden, out_w_ref[...])
    decay = decay_ref[...]
    within = jnp.exp(-decay * lax.broadcasted_iota(jnp.int32, (block, LANES), 0).astype(F32))
    within = within * norm_ref[...]
    filt[0:block, :] = jnp.zeros((block, LANES), BF16)
    for m in range(blocks):
        start = jnp.exp(-decay * float(m * block))
        filt[(m + 1) * block : (m + 2) * block, :] = (raw[m * block : (m + 1) * block] * (within * start)).astype(BF16)
    fetches[-1].wait()
    first_row = lax.broadcasted_iota(jnp.int32, (16, LANES), 0) == 0
    group = 2
    for m0 in range(0, blocks, group):
        stacked = jnp.concatenate(
            [
                jnp.concatenate(
                    [filt[(m + 1) * block : (m + 2) * block, :], filt[m * block : (m + 1) * block, :]], 0
                )
                for m in range(m0, m0 + group)
            ],
            1,
        )
        spectrum = jnp.dot(table_ref[...], stacked, preferred_element_type=F32)
        for i in range(group):
            m = m0 + i
            real = spectrum[:block, i * LANES : (i + 1) * LANES]
            imag = spectrum[block:, i * LANES : (i + 1) * LANES]
            real_ref[m] = real
            imag_ref[m] = imag
            edge_ref[m] = jnp.where(first_row, imag[:16], real[:16])
            imag_ref[m, 0:16, :] = jnp.where(first_row, 0.0, imag[:16])
    for copy in copies:
        copy.wait()


def conv_kernel(block, relative, order_ref, real_ref, imag_ref, edge_ref, table_ref, inverse_ref, *refs):
    *refs, sig, sre, sim, spec, conv = refs
    count = len(refs) // 2
    x_refs, out_refs = refs[:count], refs[count:]
    first = first_piece(count if relative else 1)
    groups = x_refs[0].shape[0] // GROUP
    length = sig.shape[0]
    blocks = length // block

    def place(k, i):
        return pl.multiple_of(order_ref[(first ^ k) * groups + i] * GROUP, GROUP)

    for k, x_ref in enumerate(x_refs):
        for i in range(groups):
            sig[pl.ds(place(k, i), GROUP), :] = x_ref[i * GROUP : (i + 1) * GROUP, :]
    group = 2
    for b0 in range(0, blocks, group):
        stacked = jnp.concatenate([sig[b * block : (b + 1) * block, :] for b in range(b0, b0 + group)], 1)
        spectrum = jnp.dot(table_ref[...], stacked, preferred_element_type=F32)
        for i in range(group):
            sre[b0 + i] = spectrum[:block, i * LANES : (i + 1) * LANES]
            sim[b0 + i] = spectrum[block:, i * LANES : (i + 1) * LANES]

    def tile(start, first):
        rows = pl.ds(start, 16)
        mirror = pl.ds(block + start, 16)
        s_real = [sre[q, rows, :] for q in range(blocks)]
        s_imag = [sim[q, rows, :] for q in range(blocks)]
        for g in range(blocks):
            acc_real = acc_imag = None
            for q in range(g + 1):
                fr, fi = real_ref[g - q, rows, :], imag_ref[g - q, rows, :]
                fe = edge_ref[g - q] if first else fr
                re = fr * s_real[q] - fi * s_imag[q]
                im = fe * s_imag[q] + fi * s_real[q]
                acc_real = re if q == 0 else acc_real + re
                acc_imag = im if q == 0 else acc_imag + im
            spec[rows, g * LANES : (g + 1) * LANES] = acc_real.astype(BF16)
            spec[mirror, g * LANES : (g + 1) * LANES] = acc_imag.astype(BF16)

    tile(0, True)

    @pl.loop(1, block // 16)
    def _(t):
        tile(pl.multiple_of(t * 16, 16), False)

    result = jnp.dot(inverse_ref[...], spec[...], preferred_element_type=F32)
    for g in range(blocks):
        conv[g * block : (g + 1) * block, :] = result[:, g * LANES : (g + 1) * LANES].astype(BF16)
    for k, out_ref in enumerate(out_refs):
        for i in range(groups):
            out_ref[i * GROUP : (i + 1) * GROUP, :] = conv[pl.ds(place(k, i), GROUP), :]


def mix_kernel(query_ref, gain_ref, weight_ref, *refs):
    *refs, out_ref, mixed_ref = refs
    count = len(refs) // 2
    unit = query_ref.shape[2]
    for k, (back_ref, sig_ref) in enumerate(zip(refs[:count], refs[count:])):
        inner = back_ref[...].astype(F32) + gain_ref[k : k + 1, :] * sig_ref[...].astype(F32)
        mixed_ref[:, k * unit : (k + 1) * unit] = (query_ref[k].astype(F32) * inner).astype(BF16)
    project_kernel(0, mixed_ref, weight_ref, out_ref)


def project_kernel(first, mixed_ref, weight_ref, out_ref):
    mixed = mixed_ref[...]
    for i in range(out_ref.shape[0]):
        out_ref[i] = jnp.dot(mixed, weight_ref[first + i], preferred_element_type=F32).astype(out_ref.dtype)


def finish_kernel(part, spans, count, *refs):
    operands, (out_hbm, turned, sem) = refs[: count + len(spans)], refs[-3:]
    rows = turned.shape[1]
    first, last = part * rows, (part + 1) * rows
    total = jnp.concatenate(
        [
            ref[max(first, start) - start : min(last, stop) - start, :].astype(F32)
            for ref, (start, stop) in zip(operands[count:], spans)
        ],
        0,
    )
    for ref in operands[:count]:
        total = total + ref[first:last, :].astype(F32)
    turned[...] = total.T
    copy = pltpu.make_async_copy(turned, out_hbm.at[:, first:last], sem.at[0])
    copy.start()
    copy.wait()


def gated_kernel(key_hbm, value_hbm, *refs):
    *out_refs, key_ref, value_ref, sem = refs
    pieces = len(out_refs)
    unit = out_refs[0].shape[1]
    copies = []
    for k in range(pieces):
        cols = pl.ds(pl.multiple_of((first_piece(pieces) ^ k) * unit, LANES), unit)
        copies.append(pltpu.make_async_copy(key_hbm.at[:, cols], key_ref.at[k], sem.at[0, k]))
        copies.append(pltpu.make_async_copy(value_hbm.at[:, cols], value_ref.at[k], sem.at[1, k]))
    for copy in copies:
        copy.start()
    for k, out_ref in enumerate(out_refs):
        copies[2 * k].wait()
        copies[2 * k + 1].wait()
        out_ref[...] = (key_ref[k].astype(F32) * value_ref[k].astype(F32)).astype(BF16)


def local(
    query, key_gate, value, group_order, emb_weight, emb_bias, mid_weight, mid_bias, out_filter, decay_rate, skip_gain,
    out_weight,
):
    rows, chan_width = query.shape
    seq_count, chan_count = lax.axis_size("seq"), lax.axis_size("chan")
    seq_index, chan_index = lax.axis_index("seq"), lax.axis_index("chan")
    length = rows * seq_count
    slots = length // GROUP
    width = chan_width // seq_count
    block = max(2 * GROUP, length // 16)
    blocks = length // block
    emb, order = emb_weight.shape
    head, head_tail, inverse = packed_tables(block)
    feat_rows = -(-(emb + 1) // 8) * 8
    features = feature_table(length, (emb - 1) // 2, feat_rows)

    limit = pltpu.CompilerParams(vmem_limit_bytes=20 << 20)
    in_vmem = pl.BlockSpec(memory_space=pltpu.VMEM)
    in_smem = pl.BlockSpec(memory_space=pltpu.SMEM)
    in_hbm = pl.BlockSpec(memory_space=pltpu.HBM)
    far = lambda operand: pltpu.with_memory_space_constraint(operand, pltpu.HBM)
    unit = width if width % LANES == 0 else chan_width
    pieces = chan_width // unit

    def swap(arrays):
        return [arrays[0]] + [
            lax.ppermute(arrays[k], "seq", [(d, d ^ k) for d in range(seq_count)]) for k in range(1, seq_count)
        ]

    signal = pl.pallas_call(
        gated_kernel,
        out_shape=[jax.ShapeDtypeStruct((rows, unit), BF16)] * pieces,
        in_specs=[in_hbm] * 2,
        out_specs=[in_vmem] * pieces,
        scratch_shapes=[
            pltpu.VMEM((pieces, rows, unit), BF16),
            pltpu.VMEM((pieces, rows, unit), BF16),
            pltpu.SemaphoreType.DMA((2, pieces)),
        ],
        compiler_params=limit,
    )(far(key_gate), far(value))
    if pieces > 1:
        spread = swap(signal)
    else:
        in_order = signal[0].reshape(rows, seq_count, width).transpose(1, 0, 2)
        in_order = lax.all_to_all(in_order, "seq", 0, 0, tiled=True)
        spread = list(jnp.pad(in_order, [(0, 0), (0, 0), (0, LANES - width)]))

    my_filter = lax.dynamic_slice_in_dim(out_filter, seq_index * width, width, 1)
    my_decay = lax.dynamic_slice_in_dim(decay_rate, seq_index * width, width)[None, :]
    norm = jnp.sqrt(-jnp.expm1(-2.0 * my_decay))
    pad = [(0, 0), (0, LANES - width)]
    if width < LANES:
        my_filter, my_decay, norm = jnp.pad(my_filter, pad), jnp.pad(my_decay, pad), jnp.pad(norm, pad)
    out_width = out_weight.shape[1] // chan_count
    quarter = chan_count // 4
    odd = range(1, chan_count, 2)
    far_odd, near_odd = [j for j in odd if j & 2], [j for j in odd if not j & 2]
    order_of_blocks = far_odd + [j ^ 1 for j in far_odd] + near_odd + [j ^ 1 for j in near_odd]
    smalls = (
        features, emb_weight, emb_bias[None, :], mid_weight, mid_bias[None, :], skip_gain.reshape(pieces, unit), head_tail
    )
    real, imag, edge, weights, query_near, gain_near = pl.pallas_call(
        functools.partial(filter_kernel, block, order_of_blocks),
        out_shape=(
            jax.ShapeDtypeStruct((blocks, block, LANES), F32),
            jax.ShapeDtypeStruct((blocks, block, LANES), F32),
            jax.ShapeDtypeStruct((blocks, 16, LANES), F32),
            jax.ShapeDtypeStruct((chan_count, chan_width, out_width), BF16),
            jax.ShapeDtypeStruct((pieces, rows, unit), BF16),
            jax.ShapeDtypeStruct((pieces, unit), F32),
        ),
        in_specs=[in_vmem] * 3 + [in_hbm] * 9,
        out_specs=[in_vmem] * 6,
        scratch_shapes=[
            *[pltpu.VMEM(small.shape, small.dtype) for small in smalls],
            pltpu.VMEM((feat_rows, order), F32),
            pltpu.VMEM((order + 8, order), F32),
            pltpu.VMEM((order + 8, length), F32),
            pltpu.VMEM((length + block, LANES), BF16),
            pltpu.SemaphoreType.DMA((len(smalls),)),
            pltpu.SemaphoreType.DMA((chan_count, pieces)),
            pltpu.SemaphoreType.DMA((pieces,)),
        ],
        compiler_params=limit,
    )(my_filter, my_decay, norm, *map(far, (*smalls, out_weight, query)))

    convolved = pl.pallas_call(
        functools.partial(conv_kernel, block, pieces > 1),
        out_shape=[jax.ShapeDtypeStruct((rows, LANES), BF16)] * seq_count,
        in_specs=[in_smem] + [in_vmem] * (5 + seq_count),
        out_specs=[in_vmem] * seq_count,
        scratch_shapes=[
            pltpu.VMEM((length, LANES), BF16),
            pltpu.VMEM((blocks, block, LANES), F32),
            pltpu.VMEM((blocks, block, LANES), F32),
            pltpu.VMEM((2 * block, blocks * LANES), BF16),
            pltpu.VMEM((length, LANES), BF16),
        ],
        compiler_params=limit,
    )(group_order, real, imag, edge, head, inverse, *spread)
    if pieces > 1:
        backs = swap(convolved)
    else:
        in_order = lax.all_to_all(jnp.stack([piece[:, :width] for piece in convolved]), "seq", 0, 0, tiled=True)
        backs = [in_order.transpose(1, 0, 2).reshape(rows, chan_width)]

    def exchange(terms, bit):
        return lax.ppermute(terms, "chan", [(d, d ^ bit) for d in range(chan_count)])

    far_away, mixed = pl.pallas_call(
        mix_kernel,
        out_shape=(
            jax.ShapeDtypeStruct((quarter, rows, out_width), BF16),
            jax.ShapeDtypeStruct((rows, chan_width), BF16),
        ),
        in_specs=[in_vmem] * (3 + 2 * pieces),
        out_specs=[in_vmem] * 2,
        compiler_params=limit,
    )(query_near, gain_near, weights, *backs, *signal)
    far_terms = exchange(far_away, 1)

    def products(first, mixed, dtype):
        return pl.pallas_call(
            functools.partial(project_kernel, first),
            out_shape=jax.ShapeDtypeStruct((quarter, rows, out_width), dtype),
            in_specs=[in_vmem] * 2,
            out_specs=in_vmem,
            compiler_params=limit,
        )(mixed, weights)

    far_kept, near_away = products(quarter, mixed, F32), products(2 * quarter, mixed, BF16)
    cuts = [0, rows // 2, rows]
    spans = list(zip(cuts, cuts[1:]))
    send = [(far_kept[:, a:b] + far_terms[:, a:b].astype(F32)).astype(BF16) for a, b in spans]
    send, near_away, mixed = lax.optimization_barrier((send, near_away, mixed))
    sent = [exchange(piece, 2) for piece in send]
    near_terms = exchange(near_away, 1)
    near_kept = products(3 * quarter, mixed, F32)
    terms = [near_kept, near_terms]
    bit = 4
    while bit < chan_count:
        total = terms[0] + terms[1].astype(F32) + jnp.concatenate(sent, 1).astype(F32)
        sent, spans = [exchange(total[1::2].astype(BF16), bit)], [(0, rows)]
        terms = [total[0::2], jnp.zeros_like(total[0::2])]
        bit *= 2
    result = None
    for i in range(rows // GROUP):
        held = [j for j, (a, b) in enumerate(spans) if a < (i + 1) * GROUP and b > i * GROUP]
        operands = [term[0] for term in terms] + [sent[j][0] for j in held]
        extra = [] if result is None else [result]
        result = pl.pallas_call(
            functools.partial(finish_kernel, i, [spans[j] for j in held], len(terms)),
            out_shape=jax.ShapeDtypeStruct((out_width, rows), F32),
            in_specs=[in_vmem] * len(operands) + [in_hbm] * len(extra),
            out_specs=in_hbm,
            scratch_shapes=[pltpu.VMEM((out_width, GROUP), F32), pltpu.SemaphoreType.DMA((1,))],
            input_output_aliases={len(operands): 0} if extra else {},
            compiler_params=limit,
        )(*operands, *extra)
    return result


def solution(mesh):
    return jax.shard_map(
        local,
        mesh=mesh,
        in_specs=(
            P("seq", "chan"), P("seq", "chan"), P("seq", "chan"), P(), P(), P(), P(), P(), P(None, "chan"), P("chan"),
            P("chan"), P("chan", None),
        ),
        out_specs=P("chan", "seq"),
        check_vma=False,
    )
```

time: 63.7 us -> 62.6 us (0.983)
  starting transfers between devices: 20.8 us -> 26.1 us
  Pallas kernels: 21.7 us -> 17.4 us
  other arithmetic: 1.67 us -> 0.93 us
  local copies, waits for them, and re-layouts: 0.71 us -> 0.02 us
    ppermute x7 -> x14, starting transfers between devices: 11.2 us -> 23.8 us  [swap(): lax.ppermute(arrays[k], 'seq', [(d, d ^ k) for d in range(seq_count)])]
    all_to_all x1 -> x0, starting transfers between devices: 7.26 us -> none  [local(): lax.all_to_all(signal, 'seq', 0, 0, tiled=True).reshape(slots, GROUP, width)]
    pallas_call x4 -> x3, Pallas kernels: 17.4 us -> 12.4 us  [the longest x1 8.09 us: local(): pl.pallas_call(functools.partial(filter_kernel, block, order_of_blocks),...]
    all_to_all x1 -> x0, waiting for transfers between devices: 4.82 us -> none  [local(): lax.all_to_all(signal, 'seq', 0, 0, tiled=True).reshape(slots, GROUP, width)]
    ppermute x4, waiting for transfers between devices: 8.75 us -> 10.9 us  [exchange(): lax.ppermute(terms, 'chan', [(d, d ^ bit) for d in range(chan_count)])]
    ppermute x7 -> x14, waiting for transfers between devices: 4.79 us -> 6.93 us  [swap(): lax.ppermute(arrays[k], 'seq', [(d, d ^ k) for d in range(seq_count)])]
    concatenate x1 -> x0, other arithmetic: 0.74 us -> none  [local(): index = jnp.concatenate([chan_index[None], base[None], group_order])]
    pallas_call x2 -> x3, Pallas kernels: 1.42 us -> 2.12 us  [products(): pl.pallas_call(functools.partial(project_kernel, first), out_shape=jax.Sh...]
  transfers between devices with their start and end apart: 12 -> 18, of which waited for: 6 -> 6; matrix products, arithmetic and copies ran while one was open for 2% -> 1% of each run, Pallas kernels for 21% -> 18%
where the time goes in v5:
time: 62.6 us; the launch traced here: 62.4 us
  starting transfers between devices  26.1 us (42%)
  waiting for transfers between devices  17.8 us (28%)
  Pallas kernels  17.4 us (28%)
  other arithmetic  0.93 us (1%)
    ppermute x14, starting transfers between devices, swap(): lax.ppermute(arrays[k], 'seq', [(d, d ^ k) for d in range(seq_count)])  23.8 us
    ppermute x4, waiting for transfers between devices, exchange(): lax.ppermute(terms, 'chan', [(d, d ^ bit) for d in range(chan_count)])  10.9 us
    pallas_call x1, Pallas kernels, local(): pl.pallas_call(functools.partial(filter_kernel, block, order_of_blocks),...  8.09 us
    ppermute x14, waiting for transfers between devices, swap(): lax.ppermute(arrays[k], 'seq', [(d, d ^ k) for d in range(seq_count)])  6.93 us
    pallas_call x1, Pallas kernels, local(): pl.pallas_call(functools.partial(conv_kernel, block, pieces > 1), out_sha...  2.82 us
    ppermute x4, starting transfers between devices, exchange(): lax.ppermute(terms, 'chan', [(d, d ^ bit) for d in range(chan_count)])  2.31 us
    pallas_call x3, Pallas kernels, products(): pl.pallas_call(functools.partial(project_kernel, first), out_shape=jax.Sh...  2.12 us
    pallas_call x2, Pallas kernels, local(): pl.pallas_call(functools.partial(finish_kernel, i, [spans[j] for j in hel...  2.01 us
  transfers between devices with their start and end apart: 18, of which 6 were waited for; matrix products, arithmetic and copies ran while one was open for 1% of the time, Pallas kernels for 18%

profile of v5, /device:TPU:0, one launch (start us, length us, event | category | flops | bytes accessed | tf_op | source)
XLA Modules:
  0.0 62.4 jit_solution(7507591445532995682)
XLA Ops:
  0.0 1.5 %shard_map.155 = (bf16[256,128]{1,0:T(8,128)(2,1)S(1)}, bf16[256,128]{1,0:T(8,128)(2,1)S(1)}, bf16[256,128]{1,0:T(8,128)(2,1)S(1)}, bf16[256,128]{1,0:T(8,128)(2...) custom-call(bf16[256,1024]{1,0:T(8,128)(2,1)} %key_hbm.1, ...), custom_call_target="tpu_custom_call" | custom-call | tf_op jit(solution)/shard_map/pallas_call | solution.py:284
  1.5 3.0 %collective-permute-start = (bf16[256,128]{1,0:T(8,128)(2,1)S(1)}, bf16[256,128]{1,0:T(8,128)(2,1)S(1)}, u32[]{:S(2)}, u32[]{:S(2)}) collective-permute-start(bf16[256,128]{1,0:T(8,128)(2,1)S(1)} %get-tuple-element.40.refs_9_), channel_id=1, source_target_pairs={{0,4},{4,0},{8,12},{12,8},{16,20},{20,16},{24,28},{28,24},{1,5},{5... | collective-permute-start | bytes 196616 | tf_op jit(solution)/shard_map/ppermute | solution.py:281
  4.5 1.6 %collective-permute-start.1 = (bf16[256,128]{1,0:T(8,128)(2,1)S(1)}, bf16[256,128]{1,0:T(8,128)(2,1)S(1)}, u32[]{:S(2)}, u32[]{:S(2)}) collective-permute-start(bf16[256,128]{1,0:T(8,128)(2,1)S(1)} %get-tuple-element.41.refs_10_), channel_id=1, source_target_pairs={{0,8},{4,12},{8,0},{12,4},{16,24},{20,28},{24,16},{28,20},{1,9},{5... | collective-permute-start | bytes 196616 | tf_op jit(solution)/shard_map/ppermute | solution.py:281
  6.1 3.0 %collective-permute-start.3 = (bf16[256,128]{1,0:T(8,128)(2,1)S(1)}, bf16[256,128]{1,0:T(8,128)(2,1)S(1)}, u32[]{:S(2)}, u32[]{:S(2)}) collective-permute-start(bf16[256,128]{1,0:T(8,128)(2,1)S(1)} %get-tuple-element.43.refs_12_), channel_id=1, source_target_pairs={{0,16},{4,20},{8,24},{12,28},{16,0},{20,4},{24,8},{28,12},{1,17},{... | collective-permute-start | bytes 196616 | tf_op jit(solution)/shard_map/ppermute | solution.py:281
  9.1 1.3 %collective-permute-start.4 = (bf16[256,128]{1,0:T(8,128)(2,1)S(1)}, bf16[256,128]{1,0:T(8,128)(2,1)S(1)}, u32[]{:S(2)}, u32[]{:S(2)}) collective-permute-start(bf16[256,128]{1,0:T(8,128)(2,1)S(1)} %get-tuple-element.44.refs_13_), channel_id=1, source_target_pairs={{0,20},{4,16},{8,28},{12,24},{16,4},{20,0},{24,12},{28,8},{1,21},{... | collective-permute-start | bytes 196616 | tf_op jit(solution)/shard_map/ppermute | solution.py:281
  10.4 3.7 %collective-permute-start.5 = (bf16[256,128]{1,0:T(8,128)(2,1)S(1)}, bf16[256,128]{1,0:T(8,128)(2,1)S(1)}, u32[]{:S(2)}, u32[]{:S(2)}) collective-permute-start(bf16[256,128]{1,0:T(8,128)(2,1)S(1)} %get-tuple-element.45.refs_14_), channel_id=1, source_target_pairs={{0,24},{4,28},{8,16},{12,20},{16,8},{20,12},{24,0},{28,4},{1,25},{... | collective-permute-start | bytes 196616 | tf_op jit(solution)/shard_map/ppermute | solution.py:281
  14.1 0.8 %sqrt_bitcast_fusion = (f32[1,128]{1,0:T(1,128)S(1)}, f32[1,128]{1,0:T(1,128)S(1)}) fusion(f32[1024]{0:T(1024)} %param.25, s32[]{:T(128)S(6)} %select_n.4), kind=kLoop, calls=%fused_computation.4 | loop fusion | flops 256 | bytes 1540 | tf_op jit(solution)/shard_map/sqrt | solution.py:305
  14.9 8.1 %shard_map.154 = (f32[8,256,128]{2,1,0:T(8,128)S(1)}, f32[8,256,128]{2,1,0:T(8,128)S(1)}, f32[8,16,128]{2,1,0:T(8,128)S(1)}, bf16[4,1024,1024]{2,1,0:T(8,128)(2,...) custom-call(f32[64,128]{1,0:T(8,128)S(1)} %constant_dynamic-slice_fusion.out_w_ref, ...), custom_call_target="tpu_custom_call" | custom-call | tf_op jit(solution)/shard_map/pallas_call | solution.py:317
  23.1 2.8 %shard_map.156 = (bf16[256,128]{1,0:T(8,128)(2,1)S(1)}, bf16[256,128]{1,0:T(8,128)(2,1)S(1)}, bf16[256,128]{1,0:T(8,128)(2,1)S(1)}, bf16[256,128]{1,0:T(8,128)(2...) custom-call(s32[16]{0:T(128)S(1)} %copy-done.3, ...), custom_call_target="tpu_custom_call" | custom-call | tf_op jit(solution)/shard_map/pallas_call | solution.py:342
  25.9 1.7 %collective-permute-start.7 = (bf16[256,128]{1,0:T(8,128)(2,1)S(1)}, bf16[256,128]{1,0:T(8,128)(2,1)S(1)}, u32[]{:S(2)}, u32[]{:S(2)}) collective-permute-start(bf16[256,128]{1,0:T(8,128)(2,1)S(1)} %get-tuple-element.48), channel_id=1, source_target_pairs={{0,4},{4,0},{8,12},{12,8},{16,20},{20,16},{24,28},{28,24},{1,5},{5... | collective-permute-start | bytes 196616 | tf_op jit(solution)/shard_map/ppermute | solution.py:281
  27.6 1.9 %collective-permute-start.9 = (bf16[256,128]{1,0:T(8,128)(2,1)S(1)}, bf16[256,128]{1,0:T(8,128)(2,1)S(1)}, u32[]{:S(2)}, u32[]{:S(2)}) collective-permute-start(bf16[256,128]{1,0:T(8,128)(2,1)S(1)} %get-tuple-element.50), channel_id=1, source_target_pairs={{0,12},{4,8},{8,4},{12,0},{16,28},{20,24},{24,20},{28,16},{1,13},{... | collective-permute-start | bytes 196616 | tf_op jit(solution)/shard_map/ppermute | solution.py:281
  29.5 2.3 %collective-permute-start.10 = (bf16[256,128]{1,0:T(8,128)(2,1)S(1)}, bf16[256,128]{1,0:T(8,128)(2,1)S(1)}, u32[]{:S(2)}, u32[]{:S(2)}) collective-permute-start(bf16[256,128]{1,0:T(8,128)(2,1)S(1)} %get-tuple-element.51), channel_id=1, source_target_pairs={{0,16},{4,20},{8,24},{12,28},{16,0},{20,4},{24,8},{28,12},{1,17},{... | collective-permute-start | bytes 196616 | tf_op jit(solution)/shard_map/ppermute | solution.py:281
  31.8 1.7 %collective-permute-start.11 = (bf16[256,128]{1,0:T(8,128)(2,1)S(1)}, bf16[256,128]{1,0:T(8,128)(2,1)S(1)}, u32[]{:S(2)}, u32[]{:S(2)}) collective-permute-start(bf16[256,128]{1,0:T(8,128)(2,1)S(1)} %get-tuple-element.52), channel_id=1, source_target_pairs={{0,20},{4,16},{8,28},{12,24},{16,4},{20,0},{24,12},{28,8},{1,21},{... | collective-permute-start | bytes 196616 | tf_op jit(solution)/shard_map/ppermute | solution.py:281
  33.4 3.6 %collective-permute-start.12 = (bf16[256,128]{1,0:T(8,128)(2,1)S(1)}, bf16[256,128]{1,0:T(8,128)(2,1)S(1)}, u32[]{:S(2)}, u32[]{:S(2)}) collective-permute-start(bf16[256,128]{1,0:T(8,128)(2,1)S(1)} %get-tuple-element.53), channel_id=1, source_target_pairs={{0,24},{4,28},{8,16},{12,20},{16,8},{20,12},{24,0},{28,4},{1,25},{... | collective-permute-start | bytes 196616 | tf_op jit(solution)/shard_map/ppermute | solution.py:281
  37.4 4.0 %collective-permute-done.11.refs_5_ = bf16[256,128]{1,0:T(8,128)(2,1)S(1)} collective-permute-done((bf16[256,128]{1,0:T(8,128)(2,1)S(1)}, bf16[256,128]{1,0:T(8,128)(2,1)S(1)}, u32[]{:S(2)}, u32[]{:S(2)}) %collective-permute-start.11) | collective-permute-done | bytes 65568 | tf_op jit(solution)/shard_map/ppermute | solution.py:281
  41.4 2.6 %collective-permute-done.13.refs_7_ = bf16[256,128]{1,0:T(8,128)(2,1)S(1)} collective-permute-done((bf16[256,128]{1,0:T(8,128)(2,1)S(1)}, bf16[256,128]{1,0:T(8,128)(2,1)S(1)}, u32[]{:S(2)}, u32[]{:S(2)}) %collective-permute-start.13) | collective-permute-done | bytes 65568 | tf_op jit(solution)/shard_map/ppermute | solution.py:281
  44.0 0.8 %shard_map.157 = (bf16[1,256,1024]{2,1,0:T(8,128)(2,1)S(1)}, bf16[256,1024]{1,0:T(8,128)(2,1)S(1)}) custom-call(bf16[8,256,128]{2,1,0:T(8,128)(2,1)S(1)} %get-tuple-element.33.query_ref, f32[8,128]{1,0:T(8,128)S(1)} %get-tuple-element.34.gain_ref, bf16[4,1024,1024]{2,1,0:T(8,128)(2,1)S(1)} %get-tuple-element.35.weight_ref, ...), custom_call_target="tpu_custom_call" | custom-call | tf_op jit(solution)/shard_map/pallas_call | solution.py:365
  44.9 0.7 %shard_map.159 = bf16[1,256,1024]{2,1,0:T(8,128)(2,1)S(1)} custom-call(bf16[256,1024]{1,0:T(8,128)(2,1)S(1)} %get-tuple-element.57.mixed_ref, bf16[4,1024,1024]{2,1,0:T(8,128)(2,1)S(1)} %get-tuple-element.35.weight_ref), custom_call_target="tpu_custom_call" | custom-call | tf_op jit(solution)/shard_map/pallas_call | solution.py:378
  45.7 0.7 %shard_map.158 = f32[1,256,1024]{2,1,0:T(8,128)S(1)} custom-call(bf16[256,1024]{1,0:T(8,128)(2,1)S(1)} %get-tuple-element.57.mixed_ref, bf16[4,1024,1024]{2,1,0:T(8,128)(2,1)S(1)} %get-tuple-element.35.weight_ref), custom_call_target="tpu_custom_call" | custom-call | tf_op jit(solution)/shard_map/pallas_call | solution.py:378
  47.2 1.5 %collective-permute-start.17 = (bf16[1,128,1024]{2,1,0:T(8,128)(2,1)S(1)}, bf16[1,128,1024]{2,1,0:T(8,128)(2,1)S(1)}, u32[]{:S(2)}, u32[]{:S(2)}) collective-permute-start(bf16[1,128,1024]{2,1,0:T(8,128)(2,1)S(1)} %get-tuple-element.60), channel_id=1, source_target_pairs={{0,2},{1,3},{2,0},{3,1},{4,6},{5,7},{6,4},{7,5},{8,10},{9,11},{10,... | collective-permute-start | bytes 786440 | tf_op jit(solution)/shard_map/ppermute | solution.py:363
  50.0 6.4 %collective-permute-done.17 = bf16[1,128,1024]{2,1,0:T(8,128)(2,1)S(1)} collective-permute-done((bf16[1,128,1024]{2,1,0:T(8,128)(2,1)S(1)}, bf16[1,128,1024]{2,1,0:T(8,128)(2,1)S(1)}, u32[]{:S(2)}, u32[]{:S(2)}) %collective-permute-start.17) | collective-permute-done | bytes 262176 | tf_op jit(solution)/shard_map/ppermute | solution.py:363
  56.4 1.0 %shard_map.161.refs_3_ = f32[1024,256]{1,0:T(8,128)} custom-call(f32[256,1024]{1,0:T(8,128)S(1)} %bitcast.11, bf16[256,1024]{1,0:T(8,128)(2,1)S(1)} %bitcast.13, bf16[128,1024]{1,0:T(8,128)(2,1)S(1)} %bitcast.15), custom_call_target="tpu_custom_call" | custom-call | tf_op jit(solution)/shard_map/pallas_call | solution.py:406
  57.4 4.0 %collective-permute-done.16 = bf16[1,128,1024]{2,1,0:T(8,128)(2,1)S(1)} collective-permute-done((bf16[1,128,1024]{2,1,0:T(8,128)(2,1)S(1)}, bf16[1,128,1024]{2,1,0:T(8,128)(2,1)S(1)}, u32[]{:S(2)}, u32[]{:S(2)}) %collective-permute-start.16) | collective-permute-done | bytes 262176 | tf_op jit(solution)/shard_map/ppermute | solution.py:363
  61.4 1.0 %shard_map.162 = f32[1024,256]{1,0:T(8,128)} custom-call(f32[256,1024]{1,0:T(8,128)S(1)} %bitcast.12, bf16[256,1024]{1,0:T(8,128)(2,1)S(1)} %bitcast.14, bf16[128,1024]{1,0:T(8,128)(2,1)S(1)} %bitcast.16, f32[1024,256]{1,0:T(8,128)} %shard_map.161.refs_3_), custom_call_target="tpu_custom_call", output_to_operand_aliasing={{}: (3, {})} | custom-call | tf_op jit(solution)/shard_map/pallas_call | solution.py:406
  (32 shorter events, 2.5 us)
Async XLA Ops:
  0.0 10.4 %copy-start = (f32[64,1024]{1,0:T(8,128)S(1)}, f32[64,1024]{1,0:T(8,128)}, u32[]{:S(2)}) copy-start(f32[64,1024]{1,0:T(8,128)} %param.24) | copy-start | bytes 786436
  0.0 23.0 %copy-start.1 = (bf16[256,512]{1,0:T(8,128)(2,1)S(1)}, bf16[256,512]{1,0:T(8,128)(2,1)}, u32[]{:S(2)}) copy-start(bf16[256,512]{1,0:T(8,128)(2,1)} %constant.28.inverse_ref) | copy-start | bytes 786436
  0.0 23.1 %copy-start.2 = (bf16[512,256]{1,0:T(8,128)(2,1)S(1)}, bf16[512,256]{1,0:T(8,128)(2,1)}, u32[]{:S(2)}) copy-start(bf16[512,256]{1,0:T(8,128)(2,1)} %constant.27.table_ref) | copy-start | bytes 786436
  0.0 23.1 %copy-start.3 = (s32[16]{0:T(128)S(1)}, s32[16]{0:T(128)}, u32[]{:S(2)}) copy-start(s32[16]{0:T(128)} %order_ref.1) | copy-start | bytes 196
  1.5 8.9 %collective-permute-start = (bf16[256,128]{1,0:T(8,128)(2,1)S(1)}, bf16[256,128]{1,0:T(8,128)(2,1)S(1)}, u32[]{:S(2)}, u32[]{:S(2)}) collective-permute-start(bf16[256,128]{1,0:T(8,128)(2,1)S(1)} %get-tuple-element.40.refs_9_), channel_id=1, source_target_pairs={{0,4},{4,0},{8,12},{12,8},{16,20},{20,16},{24,28},{28,24},{1,5},{5... | collective-permute-start | bytes 196616 | tf_op jit(solution)/shard_map/ppermute | solution.py:281
  4.5 9.5 %collective-permute-start.1 = (bf16[256,128]{1,0:T(8,128)(2,1)S(1)}, bf16[256,128]{1,0:T(8,128)(2,1)S(1)}, u32[]{:S(2)}, u32[]{:S(2)}) collective-permute-start(bf16[256,128]{1,0:T(8,128)(2,1)S(1)} %get-tuple-element.41.refs_10_), channel_id=1, source_target_pairs={{0,8},{4,12},{8,0},{12,4},{16,24},{20,28},{24,16},{28,20},{1,9},{5... | collective-permute-start | bytes 196616 | tf_op jit(solution)/shard_map/ppermute | solution.py:281
  6.1 16.9 %collective-permute-start.2 = (bf16[256,128]{1,0:T(8,128)(2,1)S(1)}, bf16[256,128]{1,0:T(8,128)(2,1)S(1)}, u32[]{:S(2)}, u32[]{:S(2)}) collective-permute-start(bf16[256,128]{1,0:T(8,128)(2,1)S(1)} %get-tuple-element.42.refs_11_), channel_id=1, source_target_pairs={{0,12},{4,8},{8,4},{12,0},{16,28},{20,24},{24,20},{28,16},{1,13},{... | collective-permute-start | bytes 196616 | tf_op jit(solution)/shard_map/ppermute | solution.py:281
  6.1 16.9 %collective-permute-start.3 = (bf16[256,128]{1,0:T(8,128)(2,1)S(1)}, bf16[256,128]{1,0:T(8,128)(2,1)S(1)}, u32[]{:S(2)}, u32[]{:S(2)}) collective-permute-start(bf16[256,128]{1,0:T(8,128)(2,1)S(1)} %get-tuple-element.43.refs_12_), channel_id=1, source_target_pairs={{0,16},{4,20},{8,24},{12,28},{16,0},{20,4},{24,8},{28,12},{1,17},{... | collective-permute-start | bytes 196616 | tf_op jit(solution)/shard_map/ppermute | solution.py:281
  9.1 13.9 %collective-permute-start.4 = (bf16[256,128]{1,0:T(8,128)(2,1)S(1)}, bf16[256,128]{1,0:T(8,128)(2,1)S(1)}, u32[]{:S(2)}, u32[]{:S(2)}) collective-permute-start(bf16[256,128]{1,0:T(8,128)(2,1)S(1)} %get-tuple-element.44.refs_13_), channel_id=1, source_target_pairs={{0,20},{4,16},{8,28},{12,24},{16,4},{20,0},{24,12},{28,8},{1,21},{... | collective-permute-start | bytes 196616 | tf_op jit(solution)/shard_map/ppermute | solution.py:281
  10.4 12.6 %collective-permute-start.5 = (bf16[256,128]{1,0:T(8,128)(2,1)S(1)}, bf16[256,128]{1,0:T(8,128)(2,1)S(1)}, u32[]{:S(2)}, u32[]{:S(2)}) collective-permute-start(bf16[256,128]{1,0:T(8,128)(2,1)S(1)} %get-tuple-element.45.refs_14_), channel_id=1, source_target_pairs={{0,24},{4,28},{8,16},{12,20},{16,8},{20,12},{24,0},{28,4},{1,25},{... | collective-permute-start | bytes 196616 | tf_op jit(solution)/shard_map/ppermute | solution.py:281
  14.1 9.0 %collective-permute-start.6 = (bf16[256,128]{1,0:T(8,128)(2,1)S(1)}, bf16[256,128]{1,0:T(8,128)(2,1)S(1)}, u32[]{:S(2)}, u32[]{:S(2)}) collective-permute-start(bf16[256,128]{1,0:T(8,128)(2,1)S(1)} %get-tuple-element.46.refs_15_), channel_id=1, source_target_pairs={{0,28},{4,24},{8,20},{12,16},{16,12},{20,8},{24,4},{28,0},{1,29},{... | collective-permute-start | bytes 196616 | tf_op jit(solution)/shard_map/ppermute | solution.py:281
  25.9 7.5 %collective-permute-start.7 = (bf16[256,128]{1,0:T(8,128)(2,1)S(1)}, bf16[256,128]{1,0:T(8,128)(2,1)S(1)}, u32[]{:S(2)}, u32[]{:S(2)}) collective-permute-start(bf16[256,128]{1,0:T(8,128)(2,1)S(1)} %get-tuple-element.48), channel_id=1, source_target_pairs={{0,4},{4,0},{8,12},{12,8},{16,20},{20,16},{24,28},{28,24},{1,5},{5... | collective-permute-start | bytes 196616 | tf_op jit(solution)/shard_map/ppermute | solution.py:281
  27.6 9.5 %collective-permute-start.8 = (bf16[256,128]{1,0:T(8,128)(2,1)S(1)}, bf16[256,128]{1,0:T(8,128)(2,1)S(1)}, u32[]{:S(2)}, u32[]{:S(2)}) collective-permute-start(bf16[256,128]{1,0:T(8,128)(2,1)S(1)} %get-tuple-element.49), channel_id=1, source_target_pairs={{0,8},{4,12},{8,0},{12,4},{16,24},{20,28},{24,16},{28,20},{1,9},{5... | collective-permute-start | bytes 196616 | tf_op jit(solution)/shard_map/ppermute | solution.py:281
  27.6 9.5 %collective-permute-start.9 = (bf16[256,128]{1,0:T(8,128)(2,1)S(1)}, bf16[256,128]{1,0:T(8,128)(2,1)S(1)}, u32[]{:S(2)}, u32[]{:S(2)}) collective-permute-start(bf16[256,128]{1,0:T(8,128)(2,1)S(1)} %get-tuple-element.50), channel_id=1, source_target_pairs={{0,12},{4,8},{8,4},{12,0},{16,28},{20,24},{24,20},{28,16},{1,13},{... | collective-permute-start | bytes 196616 | tf_op jit(solution)/shard_map/ppermute | solution.py:281
  29.5 7.9 %collective-permute-start.10 = (bf16[256,128]{1,0:T(8,128)(2,1)S(1)}, bf16[256,128]{1,0:T(8,128)(2,1)S(1)}, u32[]{:S(2)}, u32[]{:S(2)}) collective-permute-start(bf16[256,128]{1,0:T(8,128)(2,1)S(1)} %get-tuple-element.51), channel_id=1, source_target_pairs={{0,16},{4,20},{8,24},{12,28},{16,0},{20,4},{24,8},{28,12},{1,17},{... | collective-permute-start | bytes 196616 | tf_op jit(solution)/shard_map/ppermute | solution.py:281
  31.8 9.6 %collective-permute-start.11 = (bf16[256,128]{1,0:T(8,128)(2,1)S(1)}, bf16[256,128]{1,0:T(8,128)(2,1)S(1)}, u32[]{:S(2)}, u32[]{:S(2)}) collective-permute-start(bf16[256,128]{1,0:T(8,128)(2,1)S(1)} %get-tuple-element.52), channel_id=1, source_target_pairs={{0,20},{4,16},{8,28},{12,24},{16,4},{20,0},{24,12},{28,8},{1,21},{... | collective-permute-start | bytes 196616 | tf_op jit(solution)/shard_map/ppermute | solution.py:281
  33.4 8.0 %collective-permute-start.12 = (bf16[256,128]{1,0:T(8,128)(2,1)S(1)}, bf16[256,128]{1,0:T(8,128)(2,1)S(1)}, u32[]{:S(2)}, u32[]{:S(2)}) collective-permute-start(bf16[256,128]{1,0:T(8,128)(2,1)S(1)} %get-tuple-element.53), channel_id=1, source_target_pairs={{0,24},{4,28},{8,16},{12,20},{16,8},{20,12},{24,0},{28,4},{1,25},{... | collective-permute-start | bytes 196616 | tf_op jit(solution)/shard_map/ppermute | solution.py:281
  37.1 7.0 %collective-permute-start.13 = (bf16[256,128]{1,0:T(8,128)(2,1)S(1)}, bf16[256,128]{1,0:T(8,128)(2,1)S(1)}, u32[]{:S(2)}, u32[]{:S(2)}) collective-permute-start(bf16[256,128]{1,0:T(8,128)(2,1)S(1)} %get-tuple-element.54), channel_id=1, source_target_pairs={{0,28},{4,24},{8,20},{12,16},{16,12},{20,8},{24,4},{28,0},{1,29},{... | collective-permute-start | bytes 196616 | tf_op jit(solution)/shard_map/ppermute | solution.py:281
  44.9 2.0 %collective-permute-start.14 = (bf16[1,256,1024]{2,1,0:T(8,128)(2,1)S(1)}, bf16[1,256,1024]{2,1,0:T(8,128)(2,1)S(1)}, u32[]{:S(2)}, u32[]{:S(2)}) collective-permute-start(bf16[1,256,1024]{2,1,0:T(8,128)(2,1)S(1)} %get-tuple-element.56), channel_id=1, source_target_pairs={{0,1},{1,0},{2,3},{3,2},{4,5},{5,4},{6,7},{7,6},{8,9},{9,8},{10,11... | collective-permute-start | bytes 1572872 | tf_op jit(solution)/shard_map/ppermute | solution.py:363
  47.0 9.3 %collective-permute-start.15 = (bf16[1,256,1024]{2,1,0:T(8,128)(2,1)S(1)}, bf16[1,256,1024]{2,1,0:T(8,128)(2,1)S(1)}, u32[]{:S(2)}, u32[]{:S(2)}) collective-permute-start(bf16[1,256,1024]{2,1,0:T(8,128)(2,1)S(1)} %shard_map.159), channel_id=1, source_target_pairs={{0,1},{1,0},{2,3},{3,2},{4,5},{5,4},{6,7},{7,6},{8,9},{9,8},{10,11... | collective-permute-start | bytes 1572872 | tf_op jit(solution)/shard_map/ppermute | solution.py:363
  47.2 9.1 %collective-permute-start.17 = (bf16[1,128,1024]{2,1,0:T(8,128)(2,1)S(1)}, bf16[1,128,1024]{2,1,0:T(8,128)(2,1)S(1)}, u32[]{:S(2)}, u32[]{:S(2)}) collective-permute-start(bf16[1,128,1024]{2,1,0:T(8,128)(2,1)S(1)} %get-tuple-element.60), channel_id=1, source_target_pairs={{0,2},{1,3},{2,0},{3,1},{4,6},{5,7},{6,4},{7,5},{8,10},{9,11},{10,... | collective-permute-start | bytes 786440 | tf_op jit(solution)/shard_map/ppermute | solution.py:363
  48.8 12.7 %collective-permute-start.16 = (bf16[1,128,1024]{2,1,0:T(8,128)(2,1)S(1)}, bf16[1,128,1024]{2,1,0:T(8,128)(2,1)S(1)}, u32[]{:S(2)}, u32[]{:S(2)}) collective-permute-start(bf16[1,128,1024]{2,1,0:T(8,128)(2,1)S(1)} %get-tuple-element.59), channel_id=1, source_target_pairs={{0,2},{1,3},{2,0},{3,1},{4,6},{5,7},{6,4},{7,5},{8,10},{9,11},{10,... | collective-permute-start | bytes 786440 | tf_op jit(solution)/shard_map/ppermute | solution.py:363

commit v6 on v5

--- a/solution.py
+++ b/solution.py
@@ -72,31 +72,44 @@
     return lax.axis_index("seq") if pieces > 1 else 0
 
 
-def filter_kernel(
-    block, order_of_blocks, out_w_ref, decay_ref, norm_ref, *refs,
-):
-    smalls, refs = refs[:7], refs[7:]
-    weight_hbm, query_hbm, real_ref, imag_ref, edge_ref, weight_out, query_out, gain_out, *refs = refs
-    near, (w1, w2, hid, filt, near_sem, weight_sem, query_sem) = refs[:7], refs[7:]
-    feat_ref, emb_w_ref, emb_b_ref, mid_w_ref, mid_b_ref, gain_ref, table_ref = near
+def weight_copies(blocks, pieces, weight_hbm, weight_out, sem):
+    _, depth, width = weight_out.shape
+    unit = depth // pieces
+    copies = []
+    for i, j in enumerate(blocks):
+        cols = pl.ds(pl.multiple_of((lax.axis_index("chan") ^ j) * width, LANES), width)
+        for k in range(pieces):
+            rows = pl.ds(pl.multiple_of((first_piece(pieces) ^ k) * unit, LANES), unit)
+            target = weight_out.at[i, k * unit : (k + 1) * unit]
+            copies.append(pltpu.make_async_copy(weight_hbm.at[rows, cols], target, sem.at[i, k]))
+    return copies
+
+
+def one_minus_exp(y):
+    series = jnp.full_like(y, -1.0 / 40320)
+    for term in (5040, -720, 120, -24, 6, -2, 1):
+        series = series * y + 1.0 / term
+    return jnp.where(y < 0.5, y * series, 1.0 - jnp.exp(-y))
+
+
+def filter_kernel(block, blocks_first, out_w_ref, *refs):
+    smalls, (weight_hbm, query_hbm), refs = refs[:8], refs[8:10], refs[10:]
+    (real_ref, imag_ref, edge_ref, weight_out, query_out, gain_out), refs = refs[:6], refs[6:]
+    near, (w1, w2, hid, filt, near_sem, weight_sem, query_sem) = refs[:8], refs[8:]
+    feat_ref, emb_w_ref, emb_b_ref, mid_w_ref, mid_b_ref, gain_ref, decay_all, table_ref = near
     fetches = [pltpu.make_async_copy(s, t, near_sem.at[i]) for i, (s, t) in enumerate(zip(smalls, near))]
     for fetch in fetches:
         fetch.start()
     pieces, _, unit = query_out.shape
-    width = weight_out.shape[2]
-    chan_index, first = lax.axis_index("chan"), first_piece(pieces)
-    copies = []
+    first = first_piece(pieces)
+    copies = weight_copies(blocks_first, pieces, weight_hbm, weight_out, weight_sem)
     for k in range(pieces):
-        rows = pl.ds(pl.multiple_of((first ^ k) * unit, LANES), unit)
-        copies.append(pltpu.make_async_copy(query_hbm.at[:, rows], query_out.at[k], query_sem.at[k]))
-        for i, j in enumerate(order_of_blocks):
-            cols = pl.ds(pl.multiple_of((chan_index ^ j) * width, LANES), width)
-            target = weight_out.at[i, k * unit : (k + 1) * unit]
-            copies.append(pltpu.make_async_copy(weight_hbm.at[rows, cols], target, weight_sem.at[i, k]))
+        cols = pl.ds(pl.multiple_of((first ^ k) * unit, LANES), unit)
+        copies.append(pltpu.make_async_copy(query_hbm.at[:, cols], query_out.at[k], query_sem.at[k]))
+    for fetch in fetches:
+        fetch.wait()
     for copy in copies:
         copy.start()
-    for fetch in fetches[:-1]:
-        fetch.wait()
     for k in range(pieces):
         gain_out[k : k + 1, :] = gain_ref[pl.ds(first ^ k, 1), :]
     emb, order = emb_w_ref.shape
@@ -112,14 +125,13 @@
     hid[0:order, :] = sine(SINE_FREQ * contract_first(w1[...], feat_ref[...]))
     hidden = sine(SINE_FREQ * contract_first(w2[...], hid[...]))
     raw = contract_first(hidden, out_w_ref[...])
-    decay = decay_ref[...]
+    decay = decay_all[pl.ds(first, 1), :]
     within = jnp.exp(-decay * lax.broadcasted_iota(jnp.int32, (block, LANES), 0).astype(F32))
-    within = within * norm_ref[...]
+    within = within * jnp.sqrt(one_minus_exp(2.0 * decay))
     filt[0:block, :] = jnp.zeros((block, LANES), BF16)
     for m in range(blocks):
         start = jnp.exp(-decay * float(m * block))
         filt[(m + 1) * block : (m + 2) * block, :] = (raw[m * block : (m + 1) * block] * (within * start)).astype(BF16)
-    fetches[-1].wait()
     first_row = lax.broadcasted_iota(jnp.int32, (16, LANES), 0) == 0
     group = 2
     for m0 in range(0, blocks, group):
@@ -145,11 +157,17 @@
         copy.wait()
 
 
-def conv_kernel(block, relative, order_ref, real_ref, imag_ref, edge_ref, table_ref, inverse_ref, *refs):
-    *refs, sig, sre, sim, spec, conv = refs
+def conv_kernel(
+    block, blocks_next, relative, order_ref, real_ref, imag_ref, edge_ref, table_ref, inverse_ref, weight_hbm, *refs
+):
+    *refs, weight_out, sig, sre, sim, spec, conv, weight_sem = refs
     count = len(refs) // 2
     x_refs, out_refs = refs[:count], refs[count:]
-    first = first_piece(count if relative else 1)
+    pieces = count if relative else 1
+    first = first_piece(pieces)
+    copies = weight_copies(blocks_next, pieces, weight_hbm, weight_out, weight_sem)
+    for copy in copies:
+        copy.start()
     groups = x_refs[0].shape[0] // GROUP
     length = sig.shape[0]
     blocks = length // block
@@ -197,6 +215,8 @@
     for k, out_ref in enumerate(out_refs):
         for i in range(groups):
             out_ref[i * GROUP : (i + 1) * GROUP, :] = conv[pl.ds(place(k, i), GROUP), :]
+    for copy in copies:
+        copy.wait()
 
 
 def mix_kernel(query_ref, gain_ref, weight_ref, *refs):
@@ -213,6 +233,15 @@
     mixed = mixed_ref[...]
     for i in range(out_ref.shape[0]):
         out_ref[i] = jnp.dot(mixed, weight_ref[first + i], preferred_element_type=F32).astype(out_ref.dtype)
+
+
+def last_kernel(blocks_last, pieces, mixed_ref, weight_hbm, out_ref, weight_near, sem):
+    copies = weight_copies(blocks_last, pieces, weight_hbm, weight_near, sem)
+    for copy in copies:
+        copy.start()
+    for copy in copies:
+        copy.wait()
+    project_kernel(0, mixed_ref, weight_near, out_ref)
 
 
 def finish_kernel(part, spans, count, *refs):
@@ -301,30 +330,31 @@
         spread = list(jnp.pad(in_order, [(0, 0), (0, 0), (0, LANES - width)]))
 
     my_filter = lax.dynamic_slice_in_dim(out_filter, seq_index * width, width, 1)
-    my_decay = lax.dynamic_slice_in_dim(decay_rate, seq_index * width, width)[None, :]
-    norm = jnp.sqrt(-jnp.expm1(-2.0 * my_decay))
-    pad = [(0, 0), (0, LANES - width)]
-    if width < LANES:
-        my_filter, my_decay, norm = jnp.pad(my_filter, pad), jnp.pad(my_decay, pad), jnp.pad(norm, pad)
+    decay = decay_rate.reshape(seq_count, width)
+    if pieces == 1:
+        pad = [(0, 0), (0, LANES - width)]
+        my_filter = jnp.pad(my_filter, pad)
+        decay = jnp.pad(lax.dynamic_slice_in_dim(decay, seq_index, 1), pad)
     out_width = out_weight.shape[1] // chan_count
     quarter = chan_count // 4
     odd = range(1, chan_count, 2)
     far_odd, near_odd = [j for j in odd if j & 2], [j for j in odd if not j & 2]
-    order_of_blocks = far_odd + [j ^ 1 for j in far_odd] + near_odd + [j ^ 1 for j in near_odd]
+    blocks_first, blocks_next, blocks_last = far_odd + [j ^ 1 for j in far_odd], near_odd, [j ^ 1 for j in near_odd]
     smalls = (
-        features, emb_weight, emb_bias[None, :], mid_weight, mid_bias[None, :], skip_gain.reshape(pieces, unit), head_tail
+        features, emb_weight, emb_bias[None, :], mid_weight, mid_bias[None, :], skip_gain.reshape(pieces, unit), decay,
+        head_tail,
     )
-    real, imag, edge, weights, query_near, gain_near = pl.pallas_call(
-        functools.partial(filter_kernel, block, order_of_blocks),
+    real, imag, edge, weights_first, query_near, gain_near = pl.pallas_call(
+        functools.partial(filter_kernel, block, blocks_first),
         out_shape=(
             jax.ShapeDtypeStruct((blocks, block, LANES), F32),
             jax.ShapeDtypeStruct((blocks, block, LANES), F32),
             jax.ShapeDtypeStruct((blocks, 16, LANES), F32),
-            jax.ShapeDtypeStruct((chan_count, chan_width, out_width), BF16),
+            jax.ShapeDtypeStruct((2 * quarter, chan_width, out_width), BF16),
             jax.ShapeDtypeStruct((pieces, rows, unit), BF16),
             jax.ShapeDtypeStruct((pieces, unit), F32),
         ),
-        in_specs=[in_vmem] * 3 + [in_hbm] * 9,
+        in_specs=[in_vmem] + [in_hbm] * 10,
         out_specs=[in_vmem] * 6,
         scratch_shapes=[
             *[pltpu.VMEM(small.shape, small.dtype) for small in smalls],
@@ -333,26 +363,30 @@
             pltpu.VMEM((order + 8, length), F32),
             pltpu.VMEM((length + block, LANES), BF16),
             pltpu.SemaphoreType.DMA((len(smalls),)),
-            pltpu.SemaphoreType.DMA((chan_count, pieces)),
+            pltpu.SemaphoreType.DMA((2 * quarter, pieces)),
             pltpu.SemaphoreType.DMA((pieces,)),
         ],
         compiler_params=limit,
-    )(my_filter, my_decay, norm, *map(far, (*smalls, out_weight, query)))
-
-    convolved = pl.pallas_call(
-        functools.partial(conv_kernel, block, pieces > 1),
-        out_shape=[jax.ShapeDtypeStruct((rows, LANES), BF16)] * seq_count,
-        in_specs=[in_smem] + [in_vmem] * (5 + seq_count),
-        out_specs=[in_vmem] * seq_count,
+    )(my_filter, *map(far, (*smalls, out_weight, query)))
+
+    *convolved, weights_next = pl.pallas_call(
+        functools.partial(conv_kernel, block, blocks_next, pieces > 1),
+        out_shape=[
+            *[jax.ShapeDtypeStruct((rows, LANES), BF16)] * seq_count,
+            jax.ShapeDtypeStruct((quarter, chan_width, out_width), BF16),
+        ],
+        in_specs=[in_smem] + [in_vmem] * 5 + [in_hbm] + [in_vmem] * seq_count,
+        out_specs=[in_vmem] * (seq_count + 1),
         scratch_shapes=[
             pltpu.VMEM((length, LANES), BF16),
             pltpu.VMEM((blocks, block, LANES), F32),
             pltpu.VMEM((blocks, block, LANES), F32),
             pltpu.VMEM((2 * block, blocks * LANES), BF16),
             pltpu.VMEM((length, LANES), BF16),
+            pltpu.SemaphoreType.DMA((quarter, pieces)),
         ],
         compiler_params=limit,
-    )(group_order, real, imag, edge, head, inverse, *spread)
+    )(group_order, real, imag, edge, head, inverse, far(out_weight), *spread)
     if pieces > 1:
         backs = swap(convolved)
     else:
@@ -371,10 +405,10 @@
         in_specs=[in_vmem] * (3 + 2 * pieces),
         out_specs=[in_vmem] * 2,
         compiler_params=limit,
-    )(query_near, gain_near, weights, *backs, *signal)
+    )(query_near, gain_near, weights_first, *backs, *signal)
     far_terms = exchange(far_away, 1)
 
-    def products(first, mixed, dtype):
+    def products(first, weights, dtype):
         return pl.pallas_call(
             functools.partial(project_kernel, first),
             out_shape=jax.ShapeDtypeStruct((quarter, rows, out_width), dtype),
@@ -383,14 +417,24 @@
             compiler_params=limit,
         )(mixed, weights)
 
-    far_kept, near_away = products(quarter, mixed, F32), products(2 * quarter, mixed, BF16)
+    far_kept, near_away = products(quarter, weights_first, F32), products(0, weights_next, BF16)
     cuts = [0, rows // 2, rows]
     spans = list(zip(cuts, cuts[1:]))
     send = [(far_kept[:, a:b] + far_terms[:, a:b].astype(F32)).astype(BF16) for a, b in spans]
     send, near_away, mixed = lax.optimization_barrier((send, near_away, mixed))
     sent = [exchange(piece, 2) for piece in send]
     near_terms = exchange(near_away, 1)
-    near_kept = products(3 * quarter, mixed, F32)
+    near_kept = pl.pallas_call(
+        functools.partial(last_kernel, blocks_last, pieces),
+        out_shape=jax.ShapeDtypeStruct((quarter, rows, out_width), F32),
+        in_specs=[in_vmem, in_hbm],
+        out_specs=in_vmem,
+        scratch_shapes=[
+            pltpu.VMEM((quarter, chan_width, out_width), BF16),
+            pltpu.SemaphoreType.DMA((quarter, pieces)),
+        ],
+        compiler_params=limit,
+    )(mixed, far(out_weight))
     terms = [near_kept, near_terms]
     bit = 4
     while bit < chan_count:

time: 62.6 us -> 61.6 us (0.984)
  waiting for transfers between devices: 17.8 us -> 16.3 us
  Pallas kernels: 17.4 us -> 18.8 us
  other arithmetic: 0.93 us -> 0.14 us
    pallas_call x2 -> x3, Pallas kernels: 10.9 us -> 13.1 us  [the longest x1 7.88 us: local(): pl.pallas_call(functools.partial(filter_kernel, block, blocks_first), out...]
    ppermute x4, waiting for transfers between devices: 10.9 us -> 9.32 us  [exchange(): lax.ppermute(terms, 'chan', [(d, d ^ bit) for d in range(chan_count)])]
    sqrt x1 -> x0, other arithmetic: 0.77 us -> none  [local(): norm = jnp.sqrt(-jnp.expm1(-2.0 * my_decay))]
    pallas_call x3 -> x2, Pallas kernels: 2.12 us -> 1.41 us  [products(): pl.pallas_call(functools.partial(project_kernel, first), out_shape=jax.Sh...]
  transfers between devices with their start and end apart: 18 -> 18, of which waited for: 6 -> 6; matrix products, arithmetic and copies ran while one was open for 1% -> 0% of each run, Pallas kernels for 18% -> 20%
where the time goes in v6:
time: 61.6 us; the launch traced here: 61.4 us
  starting transfers between devices  26 us (42%)
  Pallas kernels  18.8 us (31%)
  waiting for transfers between devices  16.3 us (26%)
    ppermute x14, starting transfers between devices, swap(): lax.ppermute(arrays[k], 'seq', [(d, d ^ k) for d in range(seq_count)])  23.7 us
    ppermute x4, waiting for transfers between devices, exchange(): lax.ppermute(terms, 'chan', [(d, d ^ bit) for d in range(chan_count)])  9.32 us
    pallas_call x1, Pallas kernels, local(): pl.pallas_call(functools.partial(filter_kernel, block, blocks_first), out...  7.88 us
    ppermute x14, waiting for transfers between devices, swap(): lax.ppermute(arrays[k], 'seq', [(d, d ^ k) for d in range(seq_count)])  6.94 us
    pallas_call x1, Pallas kernels, local(): pl.pallas_call(functools.partial(conv_kernel, block, blocks_next, pieces...  2.92 us
    ppermute x4, starting transfers between devices, exchange(): lax.ppermute(terms, 'chan', [(d, d ^ bit) for d in range(chan_count)])  2.31 us
    pallas_call x1, Pallas kernels, local(): pl.pallas_call(functools.partial(last_kernel, blocks_last, pieces), out_s...  2.29 us
    pallas_call x2, Pallas kernels, local(): pl.pallas_call(functools.partial(finish_kernel, i, [spans[j] for j in hel...  2.01 us
  transfers between devices with their start and end apart: 18, of which 6 were waited for; matrix products, arithmetic and copies ran while one was open for 0% of the time, Pallas kernels for 20%

profile of v6, /device:TPU:0, one launch (start us, length us, event | category | flops | bytes accessed | tf_op | source)
XLA Modules:
  0.0 61.4 jit_solution(4744875792625965576)
XLA Ops:
  0.0 1.5 %shard_map.155 = (bf16[256,128]{1,0:T(8,128)(2,1)S(1)}, bf16[256,128]{1,0:T(8,128)(2,1)S(1)}, bf16[256,128]{1,0:T(8,128)(2,1)S(1)}, bf16[256,128]{1,0:T(8,128)(2...) custom-call(bf16[256,1024]{1,0:T(8,128)(2,1)} %key_hbm.1, ...), custom_call_target="tpu_custom_call" | custom-call | tf_op jit(solution)/shard_map/pallas_call | solution.py:313
  1.5 3.0 %collective-permute-start = (bf16[256,128]{1,0:T(8,128)(2,1)S(1)}, bf16[256,128]{1,0:T(8,128)(2,1)S(1)}, u32[]{:S(2)}, u32[]{:S(2)}) collective-permute-start(bf16[256,128]{1,0:T(8,128)(2,1)S(1)} %get-tuple-element.41.refs_9_), channel_id=1, source_target_pairs={{0,4},{4,0},{8,12},{12,8},{16,20},{20,16},{24,28},{28,24},{1,5},{5... | collective-permute-start | bytes 196616 | tf_op jit(solution)/shard_map/ppermute | solution.py:310
  4.5 1.6 %collective-permute-start.1 = (bf16[256,128]{1,0:T(8,128)(2,1)S(1)}, bf16[256,128]{1,0:T(8,128)(2,1)S(1)}, u32[]{:S(2)}, u32[]{:S(2)}) collective-permute-start(bf16[256,128]{1,0:T(8,128)(2,1)S(1)} %get-tuple-element.42.refs_10_), channel_id=1, source_target_pairs={{0,8},{4,12},{8,0},{12,4},{16,24},{20,28},{24,16},{28,20},{1,9},{5... | collective-permute-start | bytes 196616 | tf_op jit(solution)/shard_map/ppermute | solution.py:310
  6.1 3.0 %collective-permute-start.3 = (bf16[256,128]{1,0:T(8,128)(2,1)S(1)}, bf16[256,128]{1,0:T(8,128)(2,1)S(1)}, u32[]{:S(2)}, u32[]{:S(2)}) collective-permute-start(bf16[256,128]{1,0:T(8,128)(2,1)S(1)} %get-tuple-element.44.refs_12_), channel_id=1, source_target_pairs={{0,16},{4,20},{8,24},{12,28},{16,0},{20,4},{24,8},{28,12},{1,17},{... | collective-permute-start | bytes 196616 | tf_op jit(solution)/shard_map/ppermute | solution.py:310
  9.1 1.3 %collective-permute-start.4 = (bf16[256,128]{1,0:T(8,128)(2,1)S(1)}, bf16[256,128]{1,0:T(8,128)(2,1)S(1)}, u32[]{:S(2)}, u32[]{:S(2)}) collective-permute-start(bf16[256,128]{1,0:T(8,128)(2,1)S(1)} %get-tuple-element.45.refs_13_), channel_id=1, source_target_pairs={{0,20},{4,16},{8,28},{12,24},{16,4},{20,0},{24,12},{28,8},{1,21},{... | collective-permute-start | bytes 196616 | tf_op jit(solution)/shard_map/ppermute | solution.py:310
  10.3 3.6 %collective-permute-start.5 = (bf16[256,128]{1,0:T(8,128)(2,1)S(1)}, bf16[256,128]{1,0:T(8,128)(2,1)S(1)}, u32[]{:S(2)}, u32[]{:S(2)}) collective-permute-start(bf16[256,128]{1,0:T(8,128)(2,1)S(1)} %get-tuple-element.46.refs_14_), channel_id=1, source_target_pairs={{0,24},{4,28},{8,16},{12,20},{16,8},{20,12},{24,0},{28,4},{1,25},{... | collective-permute-start | bytes 196616 | tf_op jit(solution)/shard_map/ppermute | solution.py:310
  14.0 7.9 %shard_map.154 = (f32[8,256,128]{2,1,0:T(8,128)S(1)}, f32[8,256,128]{2,1,0:T(8,128)S(1)}, f32[8,16,128]{2,1,0:T(8,128)S(1)}, bf16[2,1024,1024]{2,1,0:T(8,128)(2,...) custom-call(f32[64,128]{1,0:T(8,128)S(1)} %constant_dynamic-slice_fusion.out_w_ref, ...), custom_call_target="tpu_custom_call" | custom-call | tf_op jit(solution)/shard_map/pallas_call | solution.py:347
  22.0 2.9 %shard_map.156 = (bf16[256,128]{1,0:T(8,128)(2,1)S(1)}, bf16[256,128]{1,0:T(8,128)(2,1)S(1)}, bf16[256,128]{1,0:T(8,128)(2,1)S(1)}, bf16[256,128]{1,0:T(8,128)(2...) custom-call(s32[16]{0:T(128)S(1)} %copy-done.3, ...), custom_call_target="tpu_custom_call" | custom-call | tf_op jit(solution)/shard_map/pallas_call | solution.py:372
  24.9 1.7 %collective-permute-start.7 = (bf16[256,128]{1,0:T(8,128)(2,1)S(1)}, bf16[256,128]{1,0:T(8,128)(2,1)S(1)}, u32[]{:S(2)}, u32[]{:S(2)}) collective-permute-start(bf16[256,128]{1,0:T(8,128)(2,1)S(1)} %get-tuple-element.49), channel_id=1, source_target_pairs={{0,4},{4,0},{8,12},{12,8},{16,20},{20,16},{24,28},{28,24},{1,5},{5... | collective-permute-start | bytes 196616 | tf_op jit(solution)/shard_map/ppermute | solution.py:310
  26.6 1.8 %collective-permute-start.9 = (bf16[256,128]{1,0:T(8,128)(2,1)S(1)}, bf16[256,128]{1,0:T(8,128)(2,1)S(1)}, u32[]{:S(2)}, u32[]{:S(2)}) collective-permute-start(bf16[256,128]{1,0:T(8,128)(2,1)S(1)} %get-tuple-element.51), channel_id=1, source_target_pairs={{0,12},{4,8},{8,4},{12,0},{16,28},{20,24},{24,20},{28,16},{1,13},{... | collective-permute-start | bytes 196616 | tf_op jit(solution)/shard_map/ppermute | solution.py:310
  28.5 2.3 %collective-permute-start.10 = (bf16[256,128]{1,0:T(8,128)(2,1)S(1)}, bf16[256,128]{1,0:T(8,128)(2,1)S(1)}, u32[]{:S(2)}, u32[]{:S(2)}) collective-permute-start(bf16[256,128]{1,0:T(8,128)(2,1)S(1)} %get-tuple-element.52), channel_id=1, source_target_pairs={{0,16},{4,20},{8,24},{12,28},{16,0},{20,4},{24,8},{28,12},{1,17},{... | collective-permute-start | bytes 196616 | tf_op jit(solution)/shard_map/ppermute | solution.py:310
  30.8 1.7 %collective-permute-start.11 = (bf16[256,128]{1,0:T(8,128)(2,1)S(1)}, bf16[256,128]{1,0:T(8,128)(2,1)S(1)}, u32[]{:S(2)}, u32[]{:S(2)}) collective-permute-start(bf16[256,128]{1,0:T(8,128)(2,1)S(1)} %get-tuple-element.53), channel_id=1, source_target_pairs={{0,20},{4,16},{8,28},{12,24},{16,4},{20,0},{24,12},{28,8},{1,21},{... | collective-permute-start | bytes 196616 | tf_op jit(solution)/shard_map/ppermute | solution.py:310
  32.5 3.6 %collective-permute-start.12 = (bf16[256,128]{1,0:T(8,128)(2,1)S(1)}, bf16[256,128]{1,0:T(8,128)(2,1)S(1)}, u32[]{:S(2)}, u32[]{:S(2)}) collective-permute-start(bf16[256,128]{1,0:T(8,128)(2,1)S(1)} %get-tuple-element.54), channel_id=1, source_target_pairs={{0,24},{4,28},{8,16},{12,20},{16,8},{20,12},{24,0},{28,4},{1,25},{... | collective-permute-start | bytes 196616 | tf_op jit(solution)/shard_map/ppermute | solution.py:310
  36.4 4.0 %collective-permute-done.11.refs_5_ = bf16[256,128]{1,0:T(8,128)(2,1)S(1)} collective-permute-done((bf16[256,128]{1,0:T(8,128)(2,1)S(1)}, bf16[256,128]{1,0:T(8,128)(2,1)S(1)}, u32[]{:S(2)}, u32[]{:S(2)}) %collective-permute-start.11) | collective-permute-done | bytes 65568 | tf_op jit(solution)/shard_map/ppermute | solution.py:310
  40.4 2.7 %collective-permute-done.13.refs_7_ = bf16[256,128]{1,0:T(8,128)(2,1)S(1)} collective-permute-done((bf16[256,128]{1,0:T(8,128)(2,1)S(1)}, bf16[256,128]{1,0:T(8,128)(2,1)S(1)}, u32[]{:S(2)}, u32[]{:S(2)}) %collective-permute-start.13) | collective-permute-done | bytes 65568 | tf_op jit(solution)/shard_map/ppermute | solution.py:310
  43.0 0.8 %shard_map.157 = (bf16[1,256,1024]{2,1,0:T(8,128)(2,1)S(1)}, bf16[256,1024]{1,0:T(8,128)(2,1)S(1)}) custom-call(bf16[8,256,128]{2,1,0:T(8,128)(2,1)S(1)} %get-tuple-element.34.query_ref, f32[8,128]{1,0:T(8,128)S(1)} %get-tuple-element.35.gain_ref, bf16[2,1024,1024]{2,1,0:T(8,128)(2,1)S(1)} %get-tuple-element.36.weight_ref, ...), custom_call_target="tpu_custom_call" | custom-call | tf_op jit(solution)/shard_map/pallas_call | solution.py:399
  44.0 0.7 %shard_map.158 = f32[1,256,1024]{2,1,0:T(8,128)S(1)} custom-call(bf16[256,1024]{1,0:T(8,128)(2,1)S(1)} %get-tuple-element.59.mixed_ref, bf16[2,1024,1024]{2,1,0:T(8,128)(2,1)S(1)} %get-tuple-element.36.weight_ref), custom_call_target="tpu_custom_call" | custom-call | tf_op jit(solution)/shard_map/pallas_call | solution.py:412
  44.7 0.7 %shard_map.159 = bf16[1,256,1024]{2,1,0:T(8,128)(2,1)S(1)} custom-call(bf16[256,1024]{1,0:T(8,128)(2,1)S(1)} %get-tuple-element.59.mixed_ref, bf16[1,1024,1024]{2,1,0:T(8,128)(2,1)S(1)} %get-tuple-element.58.weight_ref), custom_call_target="tpu_custom_call" | custom-call | tf_op jit(solution)/shard_map/pallas_call | solution.py:412
  46.2 1.5 %collective-permute-start.17 = (bf16[1,128,1024]{2,1,0:T(8,128)(2,1)S(1)}, bf16[1,128,1024]{2,1,0:T(8,128)(2,1)S(1)}, u32[]{:S(2)}, u32[]{:S(2)}) collective-permute-start(bf16[1,128,1024]{2,1,0:T(8,128)(2,1)S(1)} %get-tuple-element.62), channel_id=1, source_target_pairs={{0,2},{1,3},{2,0},{3,1},{4,6},{5,7},{6,4},{7,5},{8,10},{9,11},{10,... | collective-permute-start | bytes 786440 | tf_op jit(solution)/shard_map/ppermute | solution.py:397
  48.3 2.3 %shard_map.160 = f32[1,256,1024]{2,1,0:T(8,128)S(1)} custom-call(bf16[256,1024]{1,0:T(8,128)(2,1)S(1)} %get-tuple-element.59.mixed_ref, bf16[1024,4096]{1,0:T(8,128)(2,1)} %weight_hbm.3), custom_call_target="tpu_custom_call" | custom-call | tf_op jit(solution)/shard_map/pallas_call | solution.py:427
  50.6 4.8 %collective-permute-done.17 = bf16[1,128,1024]{2,1,0:T(8,128)(2,1)S(1)} collective-permute-done((bf16[1,128,1024]{2,1,0:T(8,128)(2,1)S(1)}, bf16[1,128,1024]{2,1,0:T(8,128)(2,1)S(1)}, u32[]{:S(2)}, u32[]{:S(2)}) %collective-permute-start.17) | collective-permute-done | bytes 262176 | tf_op jit(solution)/shard_map/ppermute | solution.py:397
  55.4 1.0 %shard_map.161.refs_3_ = f32[1024,256]{1,0:T(8,128)} custom-call(f32[256,1024]{1,0:T(8,128)S(1)} %bitcast.8, bf16[256,1024]{1,0:T(8,128)(2,1)S(1)} %bitcast.10, bf16[128,1024]{1,0:T(8,128)(2,1)S(1)} %bitcast.12), custom_call_target="tpu_custom_call" | custom-call | tf_op jit(solution)/shard_map/pallas_call | solution.py:450
  56.4 4.0 %collective-permute-done.16 = bf16[1,128,1024]{2,1,0:T(8,128)(2,1)S(1)} collective-permute-done((bf16[1,128,1024]{2,1,0:T(8,128)(2,1)S(1)}, bf16[1,128,1024]{2,1,0:T(8,128)(2,1)S(1)}, u32[]{:S(2)}, u32[]{:S(2)}) %collective-permute-start.16) | collective-permute-done | bytes 262176 | tf_op jit(solution)/shard_map/ppermute | solution.py:397
  60.4 1.0 %shard_map.162 = f32[1024,256]{1,0:T(8,128)} custom-call(f32[256,1024]{1,0:T(8,128)S(1)} %bitcast.9, bf16[256,1024]{1,0:T(8,128)(2,1)S(1)} %bitcast.11, bf16[128,1024]{1,0:T(8,128)(2,1)S(1)} %bitcast.13, f32[1024,256]{1,0:T(8,128)} %shard_map.161.refs_3_), custom_call_target="tpu_custom_call", output_to_operand_aliasing={{}: (3, {})} | custom-call | tf_op jit(solution)/shard_map/pallas_call | solution.py:450
  (31 shorter events, 1.8 us)
Async XLA Ops:
  0.0 14.0 %copy-start = (f32[64,1024]{1,0:T(8,128)S(1)}, f32[64,1024]{1,0:T(8,128)}, u32[]{:S(2)}) copy-start(f32[64,1024]{1,0:T(8,128)} %param.24) | copy-start | bytes 786436
  1.5 8.9 %collective-permute-start = (bf16[256,128]{1,0:T(8,128)(2,1)S(1)}, bf16[256,128]{1,0:T(8,128)(2,1)S(1)}, u32[]{:S(2)}, u32[]{:S(2)}) collective-permute-start(bf16[256,128]{1,0:T(8,128)(2,1)S(1)} %get-tuple-element.41.refs_9_), channel_id=1, source_target_pairs={{0,4},{4,0},{8,12},{12,8},{16,20},{20,16},{24,28},{28,24},{1,5},{5... | collective-permute-start | bytes 196616 | tf_op jit(solution)/shard_map/ppermute | solution.py:310
  4.5 9.5 %collective-permute-start.1 = (bf16[256,128]{1,0:T(8,128)(2,1)S(1)}, bf16[256,128]{1,0:T(8,128)(2,1)S(1)}, u32[]{:S(2)}, u32[]{:S(2)}) collective-permute-start(bf16[256,128]{1,0:T(8,128)(2,1)S(1)} %get-tuple-element.42.refs_10_), channel_id=1, source_target_pairs={{0,8},{4,12},{8,0},{12,4},{16,24},{20,28},{24,16},{28,20},{1,9},{5... | collective-permute-start | bytes 196616 | tf_op jit(solution)/shard_map/ppermute | solution.py:310
  6.1 15.9 %collective-permute-start.2 = (bf16[256,128]{1,0:T(8,128)(2,1)S(1)}, bf16[256,128]{1,0:T(8,128)(2,1)S(1)}, u32[]{:S(2)}, u32[]{:S(2)}) collective-permute-start(bf16[256,128]{1,0:T(8,128)(2,1)S(1)} %get-tuple-element.43.refs_11_), channel_id=1, source_target_pairs={{0,12},{4,8},{8,4},{12,0},{16,28},{20,24},{24,20},{28,16},{1,13},{... | collective-permute-start | bytes 196616 | tf_op jit(solution)/shard_map/ppermute | solution.py:310
  6.1 15.9 %collective-permute-start.3 = (bf16[256,128]{1,0:T(8,128)(2,1)S(1)}, bf16[256,128]{1,0:T(8,128)(2,1)S(1)}, u32[]{:S(2)}, u32[]{:S(2)}) collective-permute-start(bf16[256,128]{1,0:T(8,128)(2,1)S(1)} %get-tuple-element.44.refs_12_), channel_id=1, source_target_pairs={{0,16},{4,20},{8,24},{12,28},{16,0},{20,4},{24,8},{28,12},{1,17},{... | collective-permute-start | bytes 196616 | tf_op jit(solution)/shard_map/ppermute | solution.py:310
  9.1 12.9 %collective-permute-start.4 = (bf16[256,128]{1,0:T(8,128)(2,1)S(1)}, bf16[256,128]{1,0:T(8,128)(2,1)S(1)}, u32[]{:S(2)}, u32[]{:S(2)}) collective-permute-start(bf16[256,128]{1,0:T(8,128)(2,1)S(1)} %get-tuple-element.45.refs_13_), channel_id=1, source_target_pairs={{0,20},{4,16},{8,28},{12,24},{16,4},{20,0},{24,12},{28,8},{1,21},{... | collective-permute-start | bytes 196616 | tf_op jit(solution)/shard_map/ppermute | solution.py:310
  10.3 11.6 %collective-permute-start.5 = (bf16[256,128]{1,0:T(8,128)(2,1)S(1)}, bf16[256,128]{1,0:T(8,128)(2,1)S(1)}, u32[]{:S(2)}, u32[]{:S(2)}) collective-permute-start(bf16[256,128]{1,0:T(8,128)(2,1)S(1)} %get-tuple-element.46.refs_14_), channel_id=1, source_target_pairs={{0,24},{4,28},{8,16},{12,20},{16,8},{20,12},{24,0},{28,4},{1,25},{... | collective-permute-start | bytes 196616 | tf_op jit(solution)/shard_map/ppermute | solution.py:310
  13.9 8.0 %collective-permute-start.6 = (bf16[256,128]{1,0:T(8,128)(2,1)S(1)}, bf16[256,128]{1,0:T(8,128)(2,1)S(1)}, u32[]{:S(2)}, u32[]{:S(2)}) collective-permute-start(bf16[256,128]{1,0:T(8,128)(2,1)S(1)} %get-tuple-element.47.refs_15_), channel_id=1, source_target_pairs={{0,28},{4,24},{8,20},{12,16},{16,12},{20,8},{24,4},{28,0},{1,29},{... | collective-permute-start | bytes 196616 | tf_op jit(solution)/shard_map/ppermute | solution.py:310
  14.0 8.0 %copy-start.1 = (bf16[256,512]{1,0:T(8,128)(2,1)S(1)}, bf16[256,512]{1,0:T(8,128)(2,1)}, u32[]{:S(2)}) copy-start(bf16[256,512]{1,0:T(8,128)(2,1)} %constant.26.inverse_ref) | copy-start | bytes 786436
  14.0 8.0 %copy-start.2 = (bf16[512,256]{1,0:T(8,128)(2,1)S(1)}, bf16[512,256]{1,0:T(8,128)(2,1)}, u32[]{:S(2)}) copy-start(bf16[512,256]{1,0:T(8,128)(2,1)} %constant.25.table_ref) | copy-start | bytes 786436
  14.0 8.0 %copy-start.3 = (s32[16]{0:T(128)S(1)}, s32[16]{0:T(128)}, u32[]{:S(2)}) copy-start(s32[16]{0:T(128)} %order_ref.1) | copy-start | bytes 196
  24.9 7.6 %collective-permute-start.7 = (bf16[256,128]{1,0:T(8,128)(2,1)S(1)}, bf16[256,128]{1,0:T(8,128)(2,1)S(1)}, u32[]{:S(2)}, u32[]{:S(2)}) collective-permute-start(bf16[256,128]{1,0:T(8,128)(2,1)S(1)} %get-tuple-element.49), channel_id=1, source_target_pairs={{0,4},{4,0},{8,12},{12,8},{16,20},{20,16},{24,28},{28,24},{1,5},{5... | collective-permute-start | bytes 196616 | tf_op jit(solution)/shard_map/ppermute | solution.py:310
  26.6 9.5 %collective-permute-start.8 = (bf16[256,128]{1,0:T(8,128)(2,1)S(1)}, bf16[256,128]{1,0:T(8,128)(2,1)S(1)}, u32[]{:S(2)}, u32[]{:S(2)}) collective-permute-start(bf16[256,128]{1,0:T(8,128)(2,1)S(1)} %get-tuple-element.50), channel_id=1, source_target_pairs={{0,8},{4,12},{8,0},{12,4},{16,24},{20,28},{24,16},{28,20},{1,9},{5... | collective-permute-start | bytes 196616 | tf_op jit(solution)/shard_map/ppermute | solution.py:310
  26.6 9.5 %collective-permute-start.9 = (bf16[256,128]{1,0:T(8,128)(2,1)S(1)}, bf16[256,128]{1,0:T(8,128)(2,1)S(1)}, u32[]{:S(2)}, u32[]{:S(2)}) collective-permute-start(bf16[256,128]{1,0:T(8,128)(2,1)S(1)} %get-tuple-element.51), channel_id=1, source_target_pairs={{0,12},{4,8},{8,4},{12,0},{16,28},{20,24},{24,20},{28,16},{1,13},{... | collective-permute-start | bytes 196616 | tf_op jit(solution)/shard_map/ppermute | solution.py:310
  28.5 7.9 %collective-permute-start.10 = (bf16[256,128]{1,0:T(8,128)(2,1)S(1)}, bf16[256,128]{1,0:T(8,128)(2,1)S(1)}, u32[]{:S(2)}, u32[]{:S(2)}) collective-permute-start(bf16[256,128]{1,0:T(8,128)(2,1)S(1)} %get-tuple-element.52), channel_id=1, source_target_pairs={{0,16},{4,20},{8,24},{12,28},{16,0},{20,4},{24,8},{28,12},{1,17},{... | collective-permute-start | bytes 196616 | tf_op jit(solution)/shard_map/ppermute | solution.py:310
  30.8 9.6 %collective-permute-start.11 = (bf16[256,128]{1,0:T(8,128)(2,1)S(1)}, bf16[256,128]{1,0:T(8,128)(2,1)S(1)}, u32[]{:S(2)}, u32[]{:S(2)}) collective-permute-start(bf16[256,128]{1,0:T(8,128)(2,1)S(1)} %get-tuple-element.53), channel_id=1, source_target_pairs={{0,20},{4,16},{8,28},{12,24},{16,4},{20,0},{24,12},{28,8},{1,21},{... | collective-permute-start | bytes 196616 | tf_op jit(solution)/shard_map/ppermute | solution.py:310
  32.5 7.9 %collective-permute-start.12 = (bf16[256,128]{1,0:T(8,128)(2,1)S(1)}, bf16[256,128]{1,0:T(8,128)(2,1)S(1)}, u32[]{:S(2)}, u32[]{:S(2)}) collective-permute-start(bf16[256,128]{1,0:T(8,128)(2,1)S(1)} %get-tuple-element.54), channel_id=1, source_target_pairs={{0,24},{4,28},{8,16},{12,20},{16,8},{20,12},{24,0},{28,4},{1,25},{... | collective-permute-start | bytes 196616 | tf_op jit(solution)/shard_map/ppermute | solution.py:310
  36.1 7.0 %collective-permute-start.13 = (bf16[256,128]{1,0:T(8,128)(2,1)S(1)}, bf16[256,128]{1,0:T(8,128)(2,1)S(1)}, u32[]{:S(2)}, u32[]{:S(2)}) collective-permute-start(bf16[256,128]{1,0:T(8,128)(2,1)S(1)} %get-tuple-element.55), channel_id=1, source_target_pairs={{0,28},{4,24},{8,20},{12,16},{16,12},{20,8},{24,4},{28,0},{1,29},{... | collective-permute-start | bytes 196616 | tf_op jit(solution)/shard_map/ppermute | solution.py:310
  43.9 2.0 %collective-permute-start.14 = (bf16[1,256,1024]{2,1,0:T(8,128)(2,1)S(1)}, bf16[1,256,1024]{2,1,0:T(8,128)(2,1)S(1)}, u32[]{:S(2)}, u32[]{:S(2)}) collective-permute-start(bf16[1,256,1024]{2,1,0:T(8,128)(2,1)S(1)} %get-tuple-element.57), channel_id=1, source_target_pairs={{0,1},{1,0},{2,3},{3,2},{4,5},{5,4},{6,7},{7,6},{8,9},{9,8},{10,11... | collective-permute-start | bytes 1572872 | tf_op jit(solution)/shard_map/ppermute | solution.py:397
  46.0 9.3 %collective-permute-start.15 = (bf16[1,256,1024]{2,1,0:T(8,128)(2,1)S(1)}, bf16[1,256,1024]{2,1,0:T(8,128)(2,1)S(1)}, u32[]{:S(2)}, u32[]{:S(2)}) collective-permute-start(bf16[1,256,1024]{2,1,0:T(8,128)(2,1)S(1)} %shard_map.159), channel_id=1, source_target_pairs={{0,1},{1,0},{2,3},{3,2},{4,5},{5,4},{6,7},{7,6},{8,9},{9,8},{10,11... | collective-permute-start | bytes 1572872 | tf_op jit(solution)/shard_map/ppermute | solution.py:397
  46.2 9.1 %collective-permute-start.17 = (bf16[1,128,1024]{2,1,0:T(8,128)(2,1)S(1)}, bf16[1,128,1024]{2,1,0:T(8,128)(2,1)S(1)}, u32[]{:S(2)}, u32[]{:S(2)}) collective-permute-start(bf16[1,128,1024]{2,1,0:T(8,128)(2,1)S(1)} %get-tuple-element.62), channel_id=1, source_target_pairs={{0,2},{1,3},{2,0},{3,1},{4,6},{5,7},{6,4},{7,5},{8,10},{9,11},{10,... | collective-permute-start | bytes 786440 | tf_op jit(solution)/shard_map/ppermute | solution.py:397
  47.8 12.7 %collective-permute-start.16 = (bf16[1,128,1024]{2,1,0:T(8,128)(2,1)S(1)}, bf16[1,128,1024]{2,1,0:T(8,128)(2,1)S(1)}, u32[]{:S(2)}, u32[]{:S(2)}) collective-permute-start(bf16[1,128,1024]{2,1,0:T(8,128)(2,1)S(1)} %get-tuple-element.61), channel_id=1, source_target_pairs={{0,2},{1,3},{2,0},{3,1},{4,6},{5,7},{6,4},{7,5},{8,10},{9,11},{10,... | collective-permute-start | bytes 786440 | tf_op jit(solution)/shard_map/ppermute | solution.py:397

commit v7 on v6

--- a/solution.py
+++ b/solution.py
@@ -72,16 +72,12 @@
     return lax.axis_index("seq") if pieces > 1 else 0
 
 
-def weight_copies(blocks, pieces, weight_hbm, weight_out, sem):
-    _, depth, width = weight_out.shape
-    unit = depth // pieces
+def weight_copies(blocks, weight_hbm, weight_out, sem):
+    width = weight_out.shape[2]
     copies = []
     for i, j in enumerate(blocks):
         cols = pl.ds(pl.multiple_of((lax.axis_index("chan") ^ j) * width, LANES), width)
-        for k in range(pieces):
-            rows = pl.ds(pl.multiple_of((first_piece(pieces) ^ k) * unit, LANES), unit)
-            target = weight_out.at[i, k * unit : (k + 1) * unit]
-            copies.append(pltpu.make_async_copy(weight_hbm.at[rows, cols], target, sem.at[i, k]))
+        copies.append(pltpu.make_async_copy(weight_hbm.at[:, cols], weight_out.at[i], sem.at[i]))
     return copies
 
 
@@ -92,26 +88,20 @@
     return jnp.where(y < 0.5, y * series, 1.0 - jnp.exp(-y))
 
 
-def filter_kernel(block, blocks_first, out_w_ref, *refs):
-    smalls, (weight_hbm, query_hbm), refs = refs[:8], refs[8:10], refs[10:]
-    (real_ref, imag_ref, edge_ref, weight_out, query_out, gain_out), refs = refs[:6], refs[6:]
-    near, (w1, w2, hid, filt, near_sem, weight_sem, query_sem) = refs[:8], refs[8:]
-    feat_ref, emb_w_ref, emb_b_ref, mid_w_ref, mid_b_ref, gain_ref, decay_all, table_ref = near
+def filter_kernel(block, blocks_first, relative, out_w_ref, *refs):
+    smalls, (weight_hbm, query_hbm), refs = refs[:7], refs[7:9], refs[9:]
+    (real_ref, imag_ref, edge_ref, weight_out, query_out), refs = refs[:5], refs[5:]
+    near, (w1, w2, hid, filt, near_sem, weight_sem, query_sem) = refs[:7], refs[7:]
+    feat_ref, emb_w_ref, emb_b_ref, mid_w_ref, mid_b_ref, decay_all, table_ref = near
     fetches = [pltpu.make_async_copy(s, t, near_sem.at[i]) for i, (s, t) in enumerate(zip(smalls, near))]
     for fetch in fetches:
         fetch.start()
-    pieces, _, unit = query_out.shape
-    first = first_piece(pieces)
-    copies = weight_copies(blocks_first, pieces, weight_hbm, weight_out, weight_sem)
-    for k in range(pieces):
-        cols = pl.ds(pl.multiple_of((first ^ k) * unit, LANES), unit)
-        copies.append(pltpu.make_async_copy(query_hbm.at[:, cols], query_out.at[k], query_sem.at[k]))
-    for fetch in fetches:
+    for fetch in fetches[:-1]:
         fetch.wait()
+    copies = weight_copies(blocks_first, weight_hbm, weight_out, weight_sem)
+    copies.append(pltpu.make_async_copy(query_hbm, query_out, query_sem.at[0]))
     for copy in copies:
         copy.start()
-    for k in range(pieces):
-        gain_out[k : k + 1, :] = gain_ref[pl.ds(first ^ k, 1), :]
     emb, order = emb_w_ref.shape
     length = feat_ref.shape[1]
     blocks = length // block
@@ -124,8 +114,8 @@
     hid[order:, :] = jnp.ones_like(hid[order:, :])
     hid[0:order, :] = sine(SINE_FREQ * contract_first(w1[...], feat_ref[...]))
     hidden = sine(SINE_FREQ * contract_first(w2[...], hid[...]))
-    raw = contract_first(hidden, out_w_ref[...])
-    decay = decay_all[pl.ds(first, 1), :]
+    raw = contract_first(out_w_ref[...], hidden).T
+    decay = decay_all[pl.ds(lax.axis_index("seq") if relative else 0, 1), :]
     within = jnp.exp(-decay * lax.broadcasted_iota(jnp.int32, (block, LANES), 0).astype(F32))
     within = within * jnp.sqrt(one_minus_exp(2.0 * decay))
     filt[0:block, :] = jnp.zeros((block, LANES), BF16)
@@ -133,6 +123,7 @@
         start = jnp.exp(-decay * float(m * block))
         filt[(m + 1) * block : (m + 2) * block, :] = (raw[m * block : (m + 1) * block] * (within * start)).astype(BF16)
     first_row = lax.broadcasted_iota(jnp.int32, (16, LANES), 0) == 0
+    fetches[-1].wait()
     group = 2
     for m0 in range(0, blocks, group):
         stacked = jnp.concatenate(
@@ -163,9 +154,8 @@
     *refs, weight_out, sig, sre, sim, spec, conv, weight_sem = refs
     count = len(refs) // 2
     x_refs, out_refs = refs[:count], refs[count:]
-    pieces = count if relative else 1
-    first = first_piece(pieces)
-    copies = weight_copies(blocks_next, pieces, weight_hbm, weight_out, weight_sem)
+    first = first_piece(count if relative else 1)
+    copies = weight_copies(blocks_next, weight_hbm, weight_out, weight_sem)
     for copy in copies:
         copy.start()
     groups = x_refs[0].shape[0] // GROUP
@@ -221,11 +211,12 @@
 
 def mix_kernel(query_ref, gain_ref, weight_ref, *refs):
     *refs, out_ref, mixed_ref = refs
-    count = len(refs) // 2
-    unit = query_ref.shape[2]
-    for k, (back_ref, sig_ref) in enumerate(zip(refs[:count], refs[count:])):
-        inner = back_ref[...].astype(F32) + gain_ref[k : k + 1, :] * sig_ref[...].astype(F32)
-        mixed_ref[:, k * unit : (k + 1) * unit] = (query_ref[k].astype(F32) * inner).astype(BF16)
+    pieces = len(refs) // 2
+    unit = refs[0].shape[1]
+    for k, (back_ref, sig_ref) in enumerate(zip(refs[:pieces], refs[pieces:])):
+        cols = pl.ds(pl.multiple_of((first_piece(pieces) ^ k) * unit, LANES), unit)
+        inner = back_ref[...].astype(F32) + gain_ref[:, cols] * sig_ref[...].astype(F32)
+        mixed_ref[:, cols] = (query_ref[:, cols].astype(F32) * inner).astype(BF16)
     project_kernel(0, mixed_ref, weight_ref, out_ref)
 
 
@@ -235,8 +226,8 @@
         out_ref[i] = jnp.dot(mixed, weight_ref[first + i], preferred_element_type=F32).astype(out_ref.dtype)
 
 
-def last_kernel(blocks_last, pieces, mixed_ref, weight_hbm, out_ref, weight_near, sem):
-    copies = weight_copies(blocks_last, pieces, weight_hbm, weight_near, sem)
+def last_kernel(blocks_last, mixed_ref, weight_hbm, out_ref, weight_near, sem):
+    copies = weight_copies(blocks_last, weight_hbm, weight_near, sem)
     for copy in copies:
         copy.start()
     for copy in copies:
@@ -244,21 +235,14 @@
     project_kernel(0, mixed_ref, weight_near, out_ref)
 
 
-def finish_kernel(part, spans, count, *refs):
-    operands, (out_hbm, turned, sem) = refs[: count + len(spans)], refs[-3:]
-    rows = turned.shape[1]
-    first, last = part * rows, (part + 1) * rows
-    total = jnp.concatenate(
-        [
-            ref[max(first, start) - start : min(last, stop) - start, :].astype(F32)
-            for ref, (start, stop) in zip(operands[count:], spans)
-        ],
-        0,
-    )
-    for ref in operands[:count]:
-        total = total + ref[first:last, :].astype(F32)
+def finish_kernel(span, count, *refs):
+    (*held, arrived), (out_hbm, turned, sem) = refs[: count + 1], refs[-3:]
+    first, last = span
+    total = arrived[...].astype(F32)
+    for ref in held:
+        total = total + ref[:, first:last].astype(F32)
     turned[...] = total.T
-    copy = pltpu.make_async_copy(turned, out_hbm.at[:, first:last], sem.at[0])
+    copy = pltpu.make_async_copy(turned, out_hbm.at[first:last], sem.at[0])
     copy.start()
     copy.wait()
 
@@ -341,21 +325,19 @@
     far_odd, near_odd = [j for j in odd if j & 2], [j for j in odd if not j & 2]
     blocks_first, blocks_next, blocks_last = far_odd + [j ^ 1 for j in far_odd], near_odd, [j ^ 1 for j in near_odd]
     smalls = (
-        features, emb_weight, emb_bias[None, :], mid_weight, mid_bias[None, :], skip_gain.reshape(pieces, unit), decay,
-        head_tail,
+        features, emb_weight, emb_bias[None, :], mid_weight, mid_bias[None, :], decay, head_tail,
     )
-    real, imag, edge, weights_first, query_near, gain_near = pl.pallas_call(
-        functools.partial(filter_kernel, block, blocks_first),
+    real, imag, edge, weights_first, query_near = pl.pallas_call(
+        functools.partial(filter_kernel, block, blocks_first, pieces > 1),
         out_shape=(
             jax.ShapeDtypeStruct((blocks, block, LANES), F32),
             jax.ShapeDtypeStruct((blocks, block, LANES), F32),
             jax.ShapeDtypeStruct((blocks, 16, LANES), F32),
             jax.ShapeDtypeStruct((2 * quarter, chan_width, out_width), BF16),
-            jax.ShapeDtypeStruct((pieces, rows, unit), BF16),
-            jax.ShapeDtypeStruct((pieces, unit), F32),
+            jax.ShapeDtypeStruct(query.shape, BF16),
         ),
-        in_specs=[in_vmem] + [in_hbm] * 10,
-        out_specs=[in_vmem] * 6,
+        in_specs=[in_vmem] + [in_hbm] * 9,
+        out_specs=[in_vmem] * 5,
         scratch_shapes=[
             *[pltpu.VMEM(small.shape, small.dtype) for small in smalls],
             pltpu.VMEM((feat_rows, order), F32),
@@ -363,8 +345,8 @@
             pltpu.VMEM((order + 8, length), F32),
             pltpu.VMEM((length + block, LANES), BF16),
             pltpu.SemaphoreType.DMA((len(smalls),)),
-            pltpu.SemaphoreType.DMA((2 * quarter, pieces)),
-            pltpu.SemaphoreType.DMA((pieces,)),
+            pltpu.SemaphoreType.DMA((2 * quarter,)),
+            pltpu.SemaphoreType.DMA((1,)),
         ],
         compiler_params=limit,
     )(my_filter, *map(far, (*smalls, out_weight, query)))
@@ -383,7 +365,7 @@
             pltpu.VMEM((blocks, block, LANES), F32),
             pltpu.VMEM((2 * block, blocks * LANES), BF16),
             pltpu.VMEM((length, LANES), BF16),
-            pltpu.SemaphoreType.DMA((quarter, pieces)),
+            pltpu.SemaphoreType.DMA((quarter,)),
         ],
         compiler_params=limit,
     )(group_order, real, imag, edge, head, inverse, far(out_weight), *spread)
@@ -405,7 +387,7 @@
         in_specs=[in_vmem] * (3 + 2 * pieces),
         out_specs=[in_vmem] * 2,
         compiler_params=limit,
-    )(query_near, gain_near, weights_first, *backs, *signal)
+    )(query_near, skip_gain[None, :], weights_first, *backs, *signal)
     far_terms = exchange(far_away, 1)
 
     def products(first, weights, dtype):
@@ -418,45 +400,44 @@
         )(mixed, weights)
 
     far_kept, near_away = products(quarter, weights_first, F32), products(0, weights_next, BF16)
-    cuts = [0, rows // 2, rows]
+    cuts = sorted({0, out_width // 2, max(out_width // 2, out_width * 7 // 8 // LANES * LANES), out_width})
     spans = list(zip(cuts, cuts[1:]))
-    send = [(far_kept[:, a:b] + far_terms[:, a:b].astype(F32)).astype(BF16) for a, b in spans]
+    send = [(far_kept[:, :, a:b] + far_terms[:, :, a:b].astype(F32)).astype(BF16) for a, b in spans]
     send, near_away, mixed = lax.optimization_barrier((send, near_away, mixed))
     sent = [exchange(piece, 2) for piece in send]
     near_terms = exchange(near_away, 1)
     near_kept = pl.pallas_call(
-        functools.partial(last_kernel, blocks_last, pieces),
+        functools.partial(last_kernel, blocks_last),
         out_shape=jax.ShapeDtypeStruct((quarter, rows, out_width), F32),
         in_specs=[in_vmem, in_hbm],
         out_specs=in_vmem,
         scratch_shapes=[
             pltpu.VMEM((quarter, chan_width, out_width), BF16),
-            pltpu.SemaphoreType.DMA((quarter, pieces)),
+            pltpu.SemaphoreType.DMA((quarter,)),
         ],
         compiler_params=limit,
     )(mixed, far(out_weight))
     terms = [near_kept, near_terms]
     bit = 4
     while bit < chan_count:
-        total = terms[0] + terms[1].astype(F32) + jnp.concatenate(sent, 1).astype(F32)
-        sent, spans = [exchange(total[1::2].astype(BF16), bit)], [(0, rows)]
-        terms = [total[0::2], jnp.zeros_like(total[0::2])]
+        total = sum(term.astype(F32) for term in (*terms, jnp.concatenate(sent, 2)))
+        terms, sent, spans = [total[0::2]], [exchange(total[1::2].astype(BF16), bit)], [(0, out_width)]
         bit *= 2
-    result = None
-    for i in range(rows // GROUP):
-        held = [j for j, (a, b) in enumerate(spans) if a < (i + 1) * GROUP and b > i * GROUP]
-        operands = [term[0] for term in terms] + [sent[j][0] for j in held]
-        extra = [] if result is None else [result]
-        result = pl.pallas_call(
-            functools.partial(finish_kernel, i, [spans[j] for j in held], len(terms)),
-            out_shape=jax.ShapeDtypeStruct((out_width, rows), F32),
-            in_specs=[in_vmem] * len(operands) + [in_hbm] * len(extra),
-            out_specs=in_hbm,
-            scratch_shapes=[pltpu.VMEM((out_width, GROUP), F32), pltpu.SemaphoreType.DMA((1,))],
-            input_output_aliases={len(operands): 0} if extra else {},
-            compiler_params=limit,
-        )(*operands, *extra)
-    return result
+    result = []
+    for span, piece in zip(spans, sent):
+        operands = [*[term[0] for term in terms], piece[0]]
+        result = [
+            pl.pallas_call(
+                functools.partial(finish_kernel, span, len(terms)),
+                out_shape=jax.ShapeDtypeStruct((out_width, rows), F32),
+                in_specs=[in_vmem] * len(operands) + [in_hbm] * len(result),
+                out_specs=in_hbm,
+                scratch_shapes=[pltpu.VMEM((span[1] - span[0], rows), F32), pltpu.SemaphoreType.DMA((1,))],
+                input_output_aliases={len(operands): 0} if result else {},
+                compiler_params=limit,
+            )(*operands, *result)
+        ]
+    return result[0]
 
 
 def solution(mesh):

time: 61.6 us -> 58.5 us (0.950)
  Pallas kernels: 18.8 us -> 16.4 us
  waiting for transfers between devices: 16.3 us -> 14 us
  starting transfers between devices: 26 us -> 27.5 us
    pallas_call x4 -> x5, Pallas kernels: 12.2 us -> 9.64 us  [the longest x1 4.63 us: local(): pl.pallas_call(functools.partial(filter_kernel, block, blocks_first, piec...]
    ppermute x4 -> x5, waiting for transfers between devices: 9.32 us -> 6.94 us  [exchange(): lax.ppermute(terms, 'chan', [(d, d ^ bit) for d in range(chan_count)])]
    ppermute x4 -> x5, starting transfers between devices: 2.31 us -> 3.83 us  [exchange(): lax.ppermute(terms, 'chan', [(d, d ^ bit) for d in range(chan_count)])]
  transfers between devices with their start and end apart: 18 -> 19, of which waited for: 6 -> 8; matrix products, arithmetic and copies ran while one was open for 0% -> 0% of each run, Pallas kernels for 20% -> 18%
where the time goes in v7:
time: 58.5 us; the launch traced here: 58.3 us
  starting transfers between devices  27.5 us (47%)
  Pallas kernels  16.4 us (28%)
  waiting for transfers between devices  14 us (24%)
    ppermute x14, starting transfers between devices, swap(): lax.ppermute(arrays[k], 'seq', [(d, d ^ k) for d in range(seq_count)])  23.7 us
    ppermute x14, waiting for transfers between devices, swap(): lax.ppermute(arrays[k], 'seq', [(d, d ^ k) for d in range(seq_count)])  7.09 us
    ppermute x5, waiting for transfers between devices, exchange(): lax.ppermute(terms, 'chan', [(d, d ^ bit) for d in range(chan_count)])  6.94 us
    pallas_call x1, Pallas kernels, local(): pl.pallas_call(functools.partial(filter_kernel, block, blocks_first, piec...  4.63 us
    ppermute x5, starting transfers between devices, exchange(): lax.ppermute(terms, 'chan', [(d, d ^ bit) for d in range(chan_count)])  3.83 us
    pallas_call x1, Pallas kernels, local(): pl.pallas_call(functools.partial(conv_kernel, block, blocks_next, pieces...  2.85 us
    pallas_call x3, Pallas kernels, local(): pl.pallas_call(functools.partial(finish_kernel, span, len(terms)), out_sh...  2.7 us
    pallas_call x1, Pallas kernels, local(): pl.pallas_call(functools.partial(last_kernel, blocks_last), out_shape=jax...  2.31 us
  transfers between devices with their start and end apart: 19, of which 8 were waited for; matrix products, arithmetic and copies ran while one was open for 0% of the time, Pallas kernels for 18%

profile of v7, /device:TPU:0, one launch (start us, length us, event | category | flops | bytes accessed | tf_op | source)
XLA Modules:
  0.0 58.3 jit_solution(14944088394705807816)
XLA Ops:
  0.0 1.5 %shard_map.155 = (bf16[256,128]{1,0:T(8,128)(2,1)S(1)}, bf16[256,128]{1,0:T(8,128)(2,1)S(1)}, bf16[256,128]{1,0:T(8,128)(2,1)S(1)}, bf16[256,128]{1,0:T(8,128)(2...) custom-call(bf16[256,1024]{1,0:T(8,128)(2,1)} %key_hbm.1, ...), custom_call_target="tpu_custom_call" | custom-call | tf_op jit(solution)/shard_map/pallas_call | solution.py:297
  1.5 3.0 %collective-permute-start = (bf16[256,128]{1,0:T(8,128)(2,1)S(1)}, bf16[256,128]{1,0:T(8,128)(2,1)S(1)}, u32[]{:S(2)}, u32[]{:S(2)}) collective-permute-start(bf16[256,128]{1,0:T(8,128)(2,1)S(1)} %get-tuple-element.40.refs_9_), channel_id=1, source_target_pairs={{0,4},{4,0},{8,12},{12,8},{16,20},{20,16},{24,28},{28,24},{1,5},{5... | collective-permute-start | bytes 196616 | tf_op jit(solution)/shard_map/ppermute | solution.py:294
  4.5 1.6 %collective-permute-start.1 = (bf16[256,128]{1,0:T(8,128)(2,1)S(1)}, bf16[256,128]{1,0:T(8,128)(2,1)S(1)}, u32[]{:S(2)}, u32[]{:S(2)}) collective-permute-start(bf16[256,128]{1,0:T(8,128)(2,1)S(1)} %get-tuple-element.41.refs_10_), channel_id=1, source_target_pairs={{0,8},{4,12},{8,0},{12,4},{16,24},{20,28},{24,16},{28,20},{1,9},{5... | collective-permute-start | bytes 196616 | tf_op jit(solution)/shard_map/ppermute | solution.py:294
  6.1 3.0 %collective-permute-start.3 = (bf16[256,128]{1,0:T(8,128)(2,1)S(1)}, bf16[256,128]{1,0:T(8,128)(2,1)S(1)}, u32[]{:S(2)}, u32[]{:S(2)}) collective-permute-start(bf16[256,128]{1,0:T(8,128)(2,1)S(1)} %get-tuple-element.43.refs_12_), channel_id=1, source_target_pairs={{0,16},{4,20},{8,24},{12,28},{16,0},{20,4},{24,8},{28,12},{1,17},{... | collective-permute-start | bytes 196616 | tf_op jit(solution)/shard_map/ppermute | solution.py:294
  9.1 1.3 %collective-permute-start.4 = (bf16[256,128]{1,0:T(8,128)(2,1)S(1)}, bf16[256,128]{1,0:T(8,128)(2,1)S(1)}, u32[]{:S(2)}, u32[]{:S(2)}) collective-permute-start(bf16[256,128]{1,0:T(8,128)(2,1)S(1)} %get-tuple-element.44.refs_13_), channel_id=1, source_target_pairs={{0,20},{4,16},{8,28},{12,24},{16,4},{20,0},{24,12},{28,8},{1,21},{... | collective-permute-start | bytes 196616 | tf_op jit(solution)/shard_map/ppermute | solution.py:294
  10.3 3.6 %collective-permute-start.5 = (bf16[256,128]{1,0:T(8,128)(2,1)S(1)}, bf16[256,128]{1,0:T(8,128)(2,1)S(1)}, u32[]{:S(2)}, u32[]{:S(2)}) collective-permute-start(bf16[256,128]{1,0:T(8,128)(2,1)S(1)} %get-tuple-element.45.refs_14_), channel_id=1, source_target_pairs={{0,24},{4,28},{8,16},{12,20},{16,8},{20,12},{24,0},{28,4},{1,25},{... | collective-permute-start | bytes 196616 | tf_op jit(solution)/shard_map/ppermute | solution.py:294
  14.0 4.6 %shard_map.154 = (f32[8,256,128]{2,1,0:T(8,128)S(1)}, f32[8,256,128]{2,1,0:T(8,128)S(1)}, f32[8,16,128]{2,1,0:T(8,128)S(1)}, bf16[2,1024,1024]{2,1,0:T(8,128)(2,1)S(1)}, bf16[256,1024]{1,0:T(8,128)(2,1)S(1)}) custom-call(f32[64,128]{1,0:T(8,128)S(1)} %constant_dynamic-slice_fusion.out_w_ref, f32[40,2048]{1,0:T(8,128)} %constant.23.clone.refs_0_, ...), custom_call_target="tpu_custom_call" | custom-call | tf_op jit(solution)/shard_map/pallas_call | solution.py:330
  19.2 1.8 %collective-permute-done.6.refs_7_ = bf16[256,128]{1,0:T(8,128)(2,1)S(1)} collective-permute-done((bf16[256,128]{1,0:T(8,128)(2,1)S(1)}, bf16[256,128]{1,0:T(8,128)(2,1)S(1)}, u32[]{:S(2)}, u32[]{:S(2)}) %collective-permute-start.6) | collective-permute-done | bytes 65568 | tf_op jit(solution)/shard_map/ppermute | solution.py:294
  21.0 2.9 %shard_map.156 = (bf16[256,128]{1,0:T(8,128)(2,1)S(1)}, bf16[256,128]{1,0:T(8,128)(2,1)S(1)}, bf16[256,128]{1,0:T(8,128)(2,1)S(1)}, bf16[256,128]{1,0:T(8,128)(2...) custom-call(s32[16]{0:T(128)S(1)} %copy-done.4, ...), custom_call_target="tpu_custom_call" | custom-call | tf_op jit(solution)/shard_map/pallas_call | solution.py:354
  24.5 1.9 %collective-permute-start.8 = (bf16[256,128]{1,0:T(8,128)(2,1)S(1)}, bf16[256,128]{1,0:T(8,128)(2,1)S(1)}, u32[]{:S(2)}, u32[]{:S(2)}) collective-permute-start(bf16[256,128]{1,0:T(8,128)(2,1)S(1)} %get-tuple-element.49), channel_id=1, source_target_pairs={{0,8},{4,12},{8,0},{12,4},{16,24},{20,28},{24,16},{28,20},{1,9},{5... | collective-permute-start | bytes 196616 | tf_op jit(solution)/shard_map/ppermute | solution.py:294
  26.4 1.1 %collective-permute-start.9 = (bf16[256,128]{1,0:T(8,128)(2,1)S(1)}, bf16[256,128]{1,0:T(8,128)(2,1)S(1)}, u32[]{:S(2)}, u32[]{:S(2)}) collective-permute-start(bf16[256,128]{1,0:T(8,128)(2,1)S(1)} %get-tuple-element.50), channel_id=1, source_target_pairs={{0,12},{4,8},{8,4},{12,0},{16,28},{20,24},{24,20},{28,16},{1,13},{... | collective-permute-start | bytes 196616 | tf_op jit(solution)/shard_map/ppermute | solution.py:294
  27.4 2.7 %collective-permute-start.10 = (bf16[256,128]{1,0:T(8,128)(2,1)S(1)}, bf16[256,128]{1,0:T(8,128)(2,1)S(1)}, u32[]{:S(2)}, u32[]{:S(2)}) collective-permute-start(bf16[256,128]{1,0:T(8,128)(2,1)S(1)} %get-tuple-element.51), channel_id=1, source_target_pairs={{0,16},{4,20},{8,24},{12,28},{16,0},{20,4},{24,8},{28,12},{1,17},{... | collective-permute-start | bytes 196616 | tf_op jit(solution)/shard_map/ppermute | solution.py:294
  30.3 2.4 %collective-permute-start.12 = (bf16[256,128]{1,0:T(8,128)(2,1)S(1)}, bf16[256,128]{1,0:T(8,128)(2,1)S(1)}, u32[]{:S(2)}, u32[]{:S(2)}) collective-permute-start(bf16[256,128]{1,0:T(8,128)(2,1)S(1)} %get-tuple-element.53), channel_id=1, source_target_pairs={{0,24},{4,28},{8,16},{12,20},{16,8},{20,12},{24,0},{28,4},{1,25},{... | collective-permute-start | bytes 196616 | tf_op jit(solution)/shard_map/ppermute | solution.py:294
  32.8 2.3 %collective-permute-start.13 = (bf16[256,128]{1,0:T(8,128)(2,1)S(1)}, bf16[256,128]{1,0:T(8,128)(2,1)S(1)}, u32[]{:S(2)}, u32[]{:S(2)}) collective-permute-start(bf16[256,128]{1,0:T(8,128)(2,1)S(1)} %get-tuple-element.54), channel_id=1, source_target_pairs={{0,28},{4,24},{8,20},{12,16},{16,12},{20,8},{24,4},{28,0},{1,29},{... | collective-permute-start | bytes 196616 | tf_op jit(solution)/shard_map/ppermute | solution.py:294
  35.1 2.3 %collective-permute-done.10.refs_4_ = bf16[256,128]{1,0:T(8,128)(2,1)S(1)} collective-permute-done((bf16[256,128]{1,0:T(8,128)(2,1)S(1)}, bf16[256,128]{1,0:T(8,128)(2,1)S(1)}, u32[]{:S(2)}, u32[]{:S(2)}) %collective-permute-start.10) | collective-permute-done | bytes 65568 | tf_op jit(solution)/shard_map/ppermute | solution.py:294
  37.4 1.3 %collective-permute-done.11.refs_5_ = bf16[256,128]{1,0:T(8,128)(2,1)S(1)} collective-permute-done((bf16[256,128]{1,0:T(8,128)(2,1)S(1)}, bf16[256,128]{1,0:T(8,128)(2,1)S(1)}, u32[]{:S(2)}, u32[]{:S(2)}) %collective-permute-start.11) | collective-permute-done | bytes 65568 | tf_op jit(solution)/shard_map/ppermute | solution.py:294
  38.7 1.1 %collective-permute-done.13.refs_7_ = bf16[256,128]{1,0:T(8,128)(2,1)S(1)} collective-permute-done((bf16[256,128]{1,0:T(8,128)(2,1)S(1)}, bf16[256,128]{1,0:T(8,128)(2,1)S(1)}, u32[]{:S(2)}, u32[]{:S(2)}) %collective-permute-start.13) | collective-permute-done | bytes 65568 | tf_op jit(solution)/shard_map/ppermute | solution.py:294
  39.9 1.0 %shard_map.157 = (bf16[1,256,1024]{2,1,0:T(8,128)(2,1)S(1)}, bf16[256,1024]{1,0:T(8,128)(2,1)S(1)}) custom-call(bf16[256,1024]{1,0:T(8,128)(2,1)S(1)} %get-tuple-element.34.query_ref, f32[1,1024]{1,0:T(1,128)S(1)} %bitcast.18, bf16[2,1024,1024]{2,1,0:T(8,128)(2,1)S(1)} %get-tuple-element.35.weight_ref, bf16[256,128]{1,0:T(8,128)(2,1)S(1)} %get-tuple-element.47.refs_0_, ...), custom_call_target="tpu_custom_call" | custom-call | tf_op jit(solution)/shard_map/pallas_call | solution.py:381
  43.3 1.5 %collective-permute-start.18 = (bf16[1,256,512]{2,1,0:T(8,128)(2,1)S(1)}, bf16[1,256,512]{2,1,0:T(8,128)(2,1)S(1)}, u32[]{:S(2)}, u32[]{:S(2)}) collective-permute-start(bf16[1,256,512]{2,1,0:T(8,128)(2,1)S(1)} %fusion), channel_id=1, source_target_pairs={{0,2},{1,3},{2,0},{3,1},{4,6},{5,7},{6,4},{7,5},{8,10},{9,11},{10,... | collective-permute-start | bytes 786440 | tf_op jit(solution)/shard_map/ppermute | solution.py:379
  45.3 1.5 %collective-permute-start.16 = (bf16[1,256,128]{2,1,0:T(8,128)(2,1)S(1)}, bf16[1,256,128]{2,1,0:T(8,128)(2,1)S(1)}, u32[]{:S(2)}, u32[]{:S(2)}) collective-permute-start(bf16[1,256,128]{2,1,0:T(8,128)(2,1)S(1)} %fusion.2), channel_id=1, source_target_pairs={{0,2},{1,3},{2,0},{3,1},{4,6},{5,7},{6,4},{7,5},{8,10},{9,11},{10,... | collective-permute-start | bytes 196616 | tf_op jit(solution)/shard_map/ppermute | solution.py:379
  46.8 2.3 %shard_map.160 = f32[1,256,1024]{2,1,0:T(8,128)S(1)} custom-call(bf16[256,1024]{1,0:T(8,128)(2,1)S(1)} %get-tuple-element.58.mixed_ref, bf16[1024,4096]{1,0:T(8,128)(2,1)} %weight_hbm.3), custom_call_target="tpu_custom_call" | custom-call | tf_op jit(solution)/shard_map/pallas_call | solution.py:409
  49.1 3.3 %collective-permute-done.18 = bf16[1,256,512]{2,1,0:T(8,128)(2,1)S(1)} collective-permute-done((bf16[1,256,512]{2,1,0:T(8,128)(2,1)S(1)}, bf16[1,256,512]{2,1,0:T(8,128)(2,1)S(1)}, u32[]{:S(2)}, u32[]{:S(2)}) %collective-permute-start.18) | collective-permute-done | bytes 262176 | tf_op jit(solution)/shard_map/ppermute | solution.py:379
  52.4 1.0 %shard_map.161.refs_3_ = f32[1024,256]{1,0:T(8,128)} custom-call(f32[256,1024]{1,0:T(8,128)S(1)} %bitcast.9, bf16[256,1024]{1,0:T(8,128)(2,1)S(1)} %bitcast.12, bf16[256,512]{1,0:T(8,128)(2,1)S(1)} %bitcast.15), custom_call_target="tpu_custom_call" | custom-call | tf_op jit(solution)/shard_map/pallas_call | solution.py:430
  53.4 3.2 %collective-permute-done.17 = bf16[1,256,384]{2,1,0:T(8,128)(2,1)S(1)} collective-permute-done((bf16[1,256,384]{2,1,0:T(8,128)(2,1)S(1)}, bf16[1,256,384]{2,1,0:T(8,128)(2,1)S(1)}, u32[]{:S(2)}, u32[]{:S(2)}) %collective-permute-start.17) | collective-permute-done | bytes 196640 | tf_op jit(solution)/shard_map/ppermute | solution.py:379
  (38 shorter events, 6.0 us)
Async XLA Ops:
  0.0 14.0 %copy-start = (f32[64,1024]{1,0:T(8,128)S(1)}, f32[64,1024]{1,0:T(8,128)}, u32[]{:S(2)}) copy-start(f32[64,1024]{1,0:T(8,128)} %param.24) | copy-start | bytes 786436
  1.5 8.9 %collective-permute-start = (bf16[256,128]{1,0:T(8,128)(2,1)S(1)}, bf16[256,128]{1,0:T(8,128)(2,1)S(1)}, u32[]{:S(2)}, u32[]{:S(2)}) collective-permute-start(bf16[256,128]{1,0:T(8,128)(2,1)S(1)} %get-tuple-element.40.refs_9_), channel_id=1, source_target_pairs={{0,4},{4,0},{8,12},{12,8},{16,20},{20,16},{24,28},{28,24},{1,5},{5... | collective-permute-start | bytes 196616 | tf_op jit(solution)/shard_map/ppermute | solution.py:294
  4.5 9.5 %collective-permute-start.1 = (bf16[256,128]{1,0:T(8,128)(2,1)S(1)}, bf16[256,128]{1,0:T(8,128)(2,1)S(1)}, u32[]{:S(2)}, u32[]{:S(2)}) collective-permute-start(bf16[256,128]{1,0:T(8,128)(2,1)S(1)} %get-tuple-element.41.refs_10_), channel_id=1, source_target_pairs={{0,8},{4,12},{8,0},{12,4},{16,24},{20,28},{24,16},{28,20},{1,9},{5... | collective-permute-start | bytes 196616 | tf_op jit(solution)/shard_map/ppermute | solution.py:294
  6.1 12.6 %collective-permute-start.2 = (bf16[256,128]{1,0:T(8,128)(2,1)S(1)}, bf16[256,128]{1,0:T(8,128)(2,1)S(1)}, u32[]{:S(2)}, u32[]{:S(2)}) collective-permute-start(bf16[256,128]{1,0:T(8,128)(2,1)S(1)} %get-tuple-element.42.refs_11_), channel_id=1, source_target_pairs={{0,12},{4,8},{8,4},{12,0},{16,28},{20,24},{24,20},{28,16},{1,13},{... | collective-permute-start | bytes 196616 | tf_op jit(solution)/shard_map/ppermute | solution.py:294
  6.1 12.6 %collective-permute-start.3 = (bf16[256,128]{1,0:T(8,128)(2,1)S(1)}, bf16[256,128]{1,0:T(8,128)(2,1)S(1)}, u32[]{:S(2)}, u32[]{:S(2)}) collective-permute-start(bf16[256,128]{1,0:T(8,128)(2,1)S(1)} %get-tuple-element.43.refs_12_), channel_id=1, source_target_pairs={{0,16},{4,20},{8,24},{12,28},{16,0},{20,4},{24,8},{28,12},{1,17},{... | collective-permute-start | bytes 196616 | tf_op jit(solution)/shard_map/ppermute | solution.py:294
  9.1 10.2 %collective-permute-start.4 = (bf16[256,128]{1,0:T(8,128)(2,1)S(1)}, bf16[256,128]{1,0:T(8,128)(2,1)S(1)}, u32[]{:S(2)}, u32[]{:S(2)}) collective-permute-start(bf16[256,128]{1,0:T(8,128)(2,1)S(1)} %get-tuple-element.44.refs_13_), channel_id=1, source_target_pairs={{0,20},{4,16},{8,28},{12,24},{16,4},{20,0},{24,12},{28,8},{1,21},{... | collective-permute-start | bytes 196616 | tf_op jit(solution)/shard_map/ppermute | solution.py:294
  10.3 8.9 %collective-permute-start.5 = (bf16[256,128]{1,0:T(8,128)(2,1)S(1)}, bf16[256,128]{1,0:T(8,128)(2,1)S(1)}, u32[]{:S(2)}, u32[]{:S(2)}) collective-permute-start(bf16[256,128]{1,0:T(8,128)(2,1)S(1)} %get-tuple-element.45.refs_14_), channel_id=1, source_target_pairs={{0,24},{4,28},{8,16},{12,20},{16,8},{20,12},{24,0},{28,4},{1,25},{... | collective-permute-start | bytes 196616 | tf_op jit(solution)/shard_map/ppermute | solution.py:294
  13.9 7.1 %collective-permute-start.6 = (bf16[256,128]{1,0:T(8,128)(2,1)S(1)}, bf16[256,128]{1,0:T(8,128)(2,1)S(1)}, u32[]{:S(2)}, u32[]{:S(2)}) collective-permute-start(bf16[256,128]{1,0:T(8,128)(2,1)S(1)} %get-tuple-element.46.refs_15_), channel_id=1, source_target_pairs={{0,28},{4,24},{8,20},{12,16},{16,12},{20,8},{24,4},{28,0},{1,29},{... | collective-permute-start | bytes 196616 | tf_op jit(solution)/shard_map/ppermute | solution.py:294
  14.0 7.0 %copy-start.1 = (bf16[256,512]{1,0:T(8,128)(2,1)S(1)}, bf16[256,512]{1,0:T(8,128)(2,1)}, u32[]{:S(2)}) copy-start(bf16[256,512]{1,0:T(8,128)(2,1)} %constant.26.inverse_ref) | copy-start | bytes 786436
  14.0 7.0 %copy-start.2 = (bf16[512,256]{1,0:T(8,128)(2,1)S(1)}, bf16[512,256]{1,0:T(8,128)(2,1)}, u32[]{:S(2)}) copy-start(bf16[512,256]{1,0:T(8,128)(2,1)} %constant.25.table_ref) | copy-start | bytes 786436
  14.0 7.0 %copy-start.4 = (s32[16]{0:T(128)S(1)}, s32[16]{0:T(128)}, u32[]{:S(2)}) copy-start(s32[16]{0:T(128)} %order_ref.1) | copy-start | bytes 196
  21.0 18.8 %copy-start.3 = (f32[1024]{0:T(1024)S(1)}, f32[1024]{0:T(1024)}, u32[]{:S(2)}) copy-start(f32[1024]{0:T(1024)} %param.26) | copy-start | bytes 12292
  23.9 6.5 %collective-permute-start.7 = (bf16[256,128]{1,0:T(8,128)(2,1)S(1)}, bf16[256,128]{1,0:T(8,128)(2,1)S(1)}, u32[]{:S(2)}, u32[]{:S(2)}) collective-permute-start(bf16[256,128]{1,0:T(8,128)(2,1)S(1)} %get-tuple-element.48), channel_id=1, source_target_pairs={{0,4},{4,0},{8,12},{12,8},{16,20},{20,16},{24,28},{28,24},{1,5},{5... | collective-permute-start | bytes 196616 | tf_op jit(solution)/shard_map/ppermute | solution.py:294
  24.5 8.3 %collective-permute-start.8 = (bf16[256,128]{1,0:T(8,128)(2,1)S(1)}, bf16[256,128]{1,0:T(8,128)(2,1)S(1)}, u32[]{:S(2)}, u32[]{:S(2)}) collective-permute-start(bf16[256,128]{1,0:T(8,128)(2,1)S(1)} %get-tuple-element.49), channel_id=1, source_target_pairs={{0,8},{4,12},{8,0},{12,4},{16,24},{20,28},{24,16},{28,20},{1,9},{5... | collective-permute-start | bytes 196616 | tf_op jit(solution)/shard_map/ppermute | solution.py:294
  26.4 8.7 %collective-permute-start.9 = (bf16[256,128]{1,0:T(8,128)(2,1)S(1)}, bf16[256,128]{1,0:T(8,128)(2,1)S(1)}, u32[]{:S(2)}, u32[]{:S(2)}) collective-permute-start(bf16[256,128]{1,0:T(8,128)(2,1)S(1)} %get-tuple-element.50), channel_id=1, source_target_pairs={{0,12},{4,8},{8,4},{12,0},{16,28},{20,24},{24,20},{28,16},{1,13},{... | collective-permute-start | bytes 196616 | tf_op jit(solution)/shard_map/ppermute | solution.py:294
  27.4 10.0 %collective-permute-start.10 = (bf16[256,128]{1,0:T(8,128)(2,1)S(1)}, bf16[256,128]{1,0:T(8,128)(2,1)S(1)}, u32[]{:S(2)}, u32[]{:S(2)}) collective-permute-start(bf16[256,128]{1,0:T(8,128)(2,1)S(1)} %get-tuple-element.51), channel_id=1, source_target_pairs={{0,16},{4,20},{8,24},{12,28},{16,0},{20,4},{24,8},{28,12},{1,17},{... | collective-permute-start | bytes 196616 | tf_op jit(solution)/shard_map/ppermute | solution.py:294
  30.2 8.5 %collective-permute-start.11 = (bf16[256,128]{1,0:T(8,128)(2,1)S(1)}, bf16[256,128]{1,0:T(8,128)(2,1)S(1)}, u32[]{:S(2)}, u32[]{:S(2)}) collective-permute-start(bf16[256,128]{1,0:T(8,128)(2,1)S(1)} %get-tuple-element.52), channel_id=1, source_target_pairs={{0,20},{4,16},{8,28},{12,24},{16,4},{20,0},{24,12},{28,8},{1,21},{... | collective-permute-start | bytes 196616 | tf_op jit(solution)/shard_map/ppermute | solution.py:294
  30.3 8.4 %collective-permute-start.12 = (bf16[256,128]{1,0:T(8,128)(2,1)S(1)}, bf16[256,128]{1,0:T(8,128)(2,1)S(1)}, u32[]{:S(2)}, u32[]{:S(2)}) collective-permute-start(bf16[256,128]{1,0:T(8,128)(2,1)S(1)} %get-tuple-element.53), channel_id=1, source_target_pairs={{0,24},{4,28},{8,16},{12,20},{16,8},{20,12},{24,0},{28,4},{1,25},{... | collective-permute-start | bytes 196616 | tf_op jit(solution)/shard_map/ppermute | solution.py:294
  32.8 7.1 %collective-permute-start.13 = (bf16[256,128]{1,0:T(8,128)(2,1)S(1)}, bf16[256,128]{1,0:T(8,128)(2,1)S(1)}, u32[]{:S(2)}, u32[]{:S(2)}) collective-permute-start(bf16[256,128]{1,0:T(8,128)(2,1)S(1)} %get-tuple-element.54), channel_id=1, source_target_pairs={{0,28},{4,24},{8,20},{12,16},{16,12},{20,8},{24,4},{28,0},{1,29},{... | collective-permute-start | bytes 196616 | tf_op jit(solution)/shard_map/ppermute | solution.py:294
  40.9 2.0 %collective-permute-start.14 = (bf16[1,256,1024]{2,1,0:T(8,128)(2,1)S(1)}, bf16[1,256,1024]{2,1,0:T(8,128)(2,1)S(1)}, u32[]{:S(2)}, u32[]{:S(2)}) collective-permute-start(bf16[1,256,1024]{2,1,0:T(8,128)(2,1)S(1)} %get-tuple-element.56), channel_id=1, source_target_pairs={{0,1},{1,0},{2,3},{3,2},{4,5},{5,4},{6,7},{7,6},{8,9},{9,8},{10,11... | collective-permute-start | bytes 1572872 | tf_op jit(solution)/shard_map/ppermute | solution.py:379
  43.1 9.3 %collective-permute-start.15 = (bf16[1,256,1024]{2,1,0:T(8,128)(2,1)S(1)}, bf16[1,256,1024]{2,1,0:T(8,128)(2,1)S(1)}, u32[]{:S(2)}, u32[]{:S(2)}) collective-permute-start(bf16[1,256,1024]{2,1,0:T(8,128)(2,1)S(1)} %shard_map.159), channel_id=1, source_target_pairs={{0,1},{1,0},{2,3},{3,2},{4,5},{5,4},{6,7},{7,6},{8,9},{9,8},{10,11... | collective-permute-start | bytes 1572872 | tf_op jit(solution)/shard_map/ppermute | solution.py:379
  43.3 9.1 %collective-permute-start.18 = (bf16[1,256,512]{2,1,0:T(8,128)(2,1)S(1)}, bf16[1,256,512]{2,1,0:T(8,128)(2,1)S(1)}, u32[]{:S(2)}, u32[]{:S(2)}) collective-permute-start(bf16[1,256,512]{2,1,0:T(8,128)(2,1)S(1)} %fusion), channel_id=1, source_target_pairs={{0,2},{1,3},{2,0},{3,1},{4,6},{5,7},{6,4},{7,5},{8,10},{9,11},{10,... | collective-permute-start | bytes 786440 | tf_op jit(solution)/shard_map/ppermute | solution.py:379
  44.8 11.8 %collective-permute-start.17 = (bf16[1,256,384]{2,1,0:T(8,128)(2,1)S(1)}, bf16[1,256,384]{2,1,0:T(8,128)(2,1)S(1)}, u32[]{:S(2)}, u32[]{:S(2)}) collective-permute-start(bf16[1,256,384]{2,1,0:T(8,128)(2,1)S(1)} %fusion.1), channel_id=1, source_target_pairs={{0,2},{1,3},{2,0},{3,1},{4,6},{5,7},{6,4},{7,5},{8,10},{9,11},{10,... | collective-permute-start | bytes 589832 | tf_op jit(solution)/shard_map/ppermute | solution.py:379
  45.3 12.2 %collective-permute-start.16 = (bf16[1,256,128]{2,1,0:T(8,128)(2,1)S(1)}, bf16[1,256,128]{2,1,0:T(8,128)(2,1)S(1)}, u32[]{:S(2)}, u32[]{:S(2)}) collective-permute-start(bf16[1,256,128]{2,1,0:T(8,128)(2,1)S(1)} %fusion.2), channel_id=1, source_target_pairs={{0,2},{1,3},{2,0},{3,1},{4,6},{5,7},{6,4},{7,5},{8,10},{9,11},{10,... | collective-permute-start | bytes 196616 | tf_op jit(solution)/shard_map/ppermute | solution.py:379

commit v8 on v7

--- a/solution.py
+++ b/solution.py
@@ -209,7 +209,7 @@
         copy.wait()
 
 
-def mix_kernel(query_ref, gain_ref, weight_ref, *refs):
+def mix_kernel(span, query_ref, gain_ref, weight_ref, *refs):
     *refs, out_ref, mixed_ref = refs
     pieces = len(refs) // 2
     unit = refs[0].shape[1]
@@ -217,13 +217,14 @@
         cols = pl.ds(pl.multiple_of((first_piece(pieces) ^ k) * unit, LANES), unit)
         inner = back_ref[...].astype(F32) + gain_ref[:, cols] * sig_ref[...].astype(F32)
         mixed_ref[:, cols] = (query_ref[:, cols].astype(F32) * inner).astype(BF16)
-    project_kernel(0, mixed_ref, weight_ref, out_ref)
-
-
-def project_kernel(first, mixed_ref, weight_ref, out_ref):
+    project_kernel(0, span, mixed_ref, weight_ref, out_ref)
+
+
+def project_kernel(first, span, mixed_ref, weight_ref, out_ref):
     mixed = mixed_ref[...]
     for i in range(out_ref.shape[0]):
-        out_ref[i] = jnp.dot(mixed, weight_ref[first + i], preferred_element_type=F32).astype(out_ref.dtype)
+        weight = weight_ref[first + i, :, slice(*span)]
+        out_ref[i] = jnp.dot(mixed, weight, preferred_element_type=F32).astype(out_ref.dtype)
 
 
 def last_kernel(blocks_last, mixed_ref, weight_hbm, out_ref, weight_near, sem):
@@ -232,7 +233,7 @@
         copy.start()
     for copy in copies:
         copy.wait()
-    project_kernel(0, mixed_ref, weight_near, out_ref)
+    project_kernel(0, (0, out_ref.shape[2]), mixed_ref, weight_near, out_ref)
 
 
 def finish_kernel(span, count, *refs):
@@ -290,9 +291,10 @@
     pieces = chan_width // unit
 
     def swap(arrays):
-        return [arrays[0]] + [
-            lax.ppermute(arrays[k], "seq", [(d, d ^ k) for d in range(seq_count)]) for k in range(1, seq_count)
-        ]
+        swapped = list(arrays)
+        for k in sorted(range(1, seq_count), key=lambda k: (k & 1, k)):
+            swapped[k] = lax.ppermute(arrays[k], "seq", [(d, d ^ k) for d in range(seq_count)])
+        return swapped
 
     signal = pl.pallas_call(
         gated_kernel,
@@ -378,34 +380,35 @@
     def exchange(terms, bit):
         return lax.ppermute(terms, "chan", [(d, d ^ bit) for d in range(chan_count)])
 
+    def products(mixed, first, span, weights, dtype):
+        return pl.pallas_call(
+            functools.partial(project_kernel, first, span),
+            out_shape=jax.ShapeDtypeStruct((quarter, rows, span[1] - span[0]), dtype),
+            in_specs=[in_vmem] * 2,
+            out_specs=in_vmem,
+            compiler_params=limit,
+        )(mixed, weights)
+
+    spans = [(0, out_width // 2), (out_width // 2, out_width)]
     far_away, mixed = pl.pallas_call(
-        mix_kernel,
+        functools.partial(mix_kernel, spans[0]),
         out_shape=(
-            jax.ShapeDtypeStruct((quarter, rows, out_width), BF16),
+            jax.ShapeDtypeStruct((quarter, rows, spans[0][1]), BF16),
             jax.ShapeDtypeStruct((rows, chan_width), BF16),
         ),
         in_specs=[in_vmem] * (3 + 2 * pieces),
         out_specs=[in_vmem] * 2,
         compiler_params=limit,
     )(query_near, skip_gain[None, :], weights_first, *backs, *signal)
-    far_terms = exchange(far_away, 1)
-
-    def products(first, weights, dtype):
-        return pl.pallas_call(
-            functools.partial(project_kernel, first),
-            out_shape=jax.ShapeDtypeStruct((quarter, rows, out_width), dtype),
-            in_specs=[in_vmem] * 2,
-            out_specs=in_vmem,
-            compiler_params=limit,
-        )(mixed, weights)
-
-    far_kept, near_away = products(quarter, weights_first, F32), products(0, weights_next, BF16)
-    cuts = sorted({0, out_width // 2, max(out_width // 2, out_width * 7 // 8 // LANES * LANES), out_width})
-    spans = list(zip(cuts, cuts[1:]))
-    send = [(far_kept[:, :, a:b] + far_terms[:, :, a:b].astype(F32)).astype(BF16) for a, b in spans]
-    send, near_away, mixed = lax.optimization_barrier((send, near_away, mixed))
-    sent = [exchange(piece, 2) for piece in send]
+    far_terms = [exchange(far_away, 1), exchange(products(mixed, 0, spans[1], weights_first, BF16), 1)]
+    sent = []
+    for span, terms in zip(spans, far_terms):
+        far_kept = products(mixed, quarter, span, weights_first, F32)
+        send = (far_kept + terms.astype(F32)).astype(BF16)
+        sent.append(exchange(send, 2))
+    near_away = products(mixed, 0, (0, out_width), weights_next, BF16)
     near_terms = exchange(near_away, 1)
+    sent[0], mixed = lax.optimization_barrier((sent[0], mixed))
     near_kept = pl.pallas_call(
         functools.partial(last_kernel, blocks_last),
         out_shape=jax.ShapeDtypeStruct((quarter, rows, out_width), F32),

time: 58.5 us -> 59.1 us (1.010)
  waiting for transfers between devices: 14 us -> 15.9 us
  starting transfers between devices: 27.5 us -> 26.6 us
    ppermute x5, waiting for transfers between devices: 6.94 us -> 8.81 us  [exchange(): lax.ppermute(terms, 'chan', [(d, d ^ bit) for d in range(chan_count)])]
    ppermute x5, starting transfers between devices: 3.83 us -> 2.86 us  [exchange(): lax.ppermute(terms, 'chan', [(d, d ^ bit) for d in range(chan_count)])]
    pallas_call x3 -> x2, Pallas kernels: 2.7 us -> 2.01 us  [local(): pl.pallas_call(functools.partial(finish_kernel, span, len(terms)), out_sh...]
    pallas_call x3 -> x5, Pallas kernels: 2.44 us -> 2.78 us  [the longest x4 2.01 us: products(): pl.pallas_call(functools.partial(project_kernel, first, span), out_shape=...]
  transfers between devices with their start and end apart: 19 -> 19, of which waited for: 8 -> 7; matrix products, arithmetic and copies ran while one was open for 0% -> 0% of each run, Pallas kernels for 18% -> 17%
where the time goes in v8:
time: 59.1 us; the launch traced here: 58.9 us
  starting transfers between devices  26.6 us (45%)
  Pallas kernels  16 us (27%)
  waiting for transfers between devices  15.9 us (27%)
    ppermute x14, starting transfers between devices, swap(): lax.ppermute(arrays[k], 'seq', [(d, d ^ k) for d in range(seq_count)])  23.7 us
    ppermute x5, waiting for transfers between devices, exchange(): lax.ppermute(terms, 'chan', [(d, d ^ bit) for d in range(chan_count)])  8.81 us
    ppermute x14, waiting for transfers between devices, swap(): lax.ppermute(arrays[k], 'seq', [(d, d ^ k) for d in range(seq_count)])  7.1 us
    pallas_call x1, Pallas kernels, local(): pl.pallas_call(functools.partial(filter_kernel, block, blocks_first, piec...  4.63 us
    ppermute x5, starting transfers between devices, exchange(): lax.ppermute(terms, 'chan', [(d, d ^ bit) for d in range(chan_count)])  2.86 us
    pallas_call x1, Pallas kernels, local(): pl.pallas_call(functools.partial(conv_kernel, block, blocks_next, pieces...  2.85 us
    pallas_call x1, Pallas kernels, local(): pl.pallas_call(functools.partial(last_kernel, blocks_last), out_shape=jax...  2.31 us
    pallas_call x2, Pallas kernels, local(): pl.pallas_call(functools.partial(finish_kernel, span, len(terms)), out_sh...  2.01 us
  transfers between devices with their start and end apart: 19, of which 7 were waited for; matrix products, arithmetic and copies ran while one was open for 0% of the time, Pallas kernels for 17%

profile of v8, /device:TPU:0, one launch (start us, length us, event | category | flops | bytes accessed | tf_op | source)
XLA Modules:
  0.0 58.9 jit_solution(16665183366616907326)
XLA Ops:
  0.0 1.5 %shard_map.155 = (bf16[256,128]{1,0:T(8,128)(2,1)S(1)}, bf16[256,128]{1,0:T(8,128)(2,1)S(1)}, bf16[256,128]{1,0:T(8,128)(2,1)S(1)}, bf16[256,128]{1,0:T(8,128)(2...) custom-call(bf16[256,1024]{1,0:T(8,128)(2,1)} %key_hbm.1, ...), custom_call_target="tpu_custom_call" | custom-call | tf_op jit(solution)/shard_map/pallas_call | solution.py:299
  1.5 3.0 %collective-permute-start = (bf16[256,128]{1,0:T(8,128)(2,1)S(1)}, bf16[256,128]{1,0:T(8,128)(2,1)S(1)}, u32[]{:S(2)}, u32[]{:S(2)}) collective-permute-start(bf16[256,128]{1,0:T(8,128)(2,1)S(1)} %get-tuple-element.37.refs_9_), channel_id=1, source_target_pairs={{0,4},{4,0},{8,12},{12,8},{16,20},{20,16},{24,28},{28,24},{1,5},{5... | collective-permute-start | bytes 196616 | tf_op jit(solution)/shard_map/ppermute | solution.py:296
  4.5 1.6 %collective-permute-start.1 = (bf16[256,128]{1,0:T(8,128)(2,1)S(1)}, bf16[256,128]{1,0:T(8,128)(2,1)S(1)}, u32[]{:S(2)}, u32[]{:S(2)}) collective-permute-start(bf16[256,128]{1,0:T(8,128)(2,1)S(1)} %get-tuple-element.38.refs_10_), channel_id=1, source_target_pairs={{0,8},{4,12},{8,0},{12,4},{16,24},{20,28},{24,16},{28,20},{1,9},{5... | collective-permute-start | bytes 196616 | tf_op jit(solution)/shard_map/ppermute | solution.py:296
  6.1 3.0 %collective-permute-start.3 = (bf16[256,128]{1,0:T(8,128)(2,1)S(1)}, bf16[256,128]{1,0:T(8,128)(2,1)S(1)}, u32[]{:S(2)}, u32[]{:S(2)}) collective-permute-start(bf16[256,128]{1,0:T(8,128)(2,1)S(1)} %get-tuple-element.40.refs_12_), channel_id=1, source_target_pairs={{0,16},{4,20},{8,24},{12,28},{16,0},{20,4},{24,8},{28,12},{1,17},{... | collective-permute-start | bytes 196616 | tf_op jit(solution)/shard_map/ppermute | solution.py:296
  9.1 1.3 %collective-permute-start.4 = (bf16[256,128]{1,0:T(8,128)(2,1)S(1)}, bf16[256,128]{1,0:T(8,128)(2,1)S(1)}, u32[]{:S(2)}, u32[]{:S(2)}) collective-permute-start(bf16[256,128]{1,0:T(8,128)(2,1)S(1)} %get-tuple-element.41.refs_13_), channel_id=1, source_target_pairs={{0,20},{4,16},{8,28},{12,24},{16,4},{20,0},{24,12},{28,8},{1,21},{... | collective-permute-start | bytes 196616 | tf_op jit(solution)/shard_map/ppermute | solution.py:296
  10.3 3.6 %collective-permute-start.5 = (bf16[256,128]{1,0:T(8,128)(2,1)S(1)}, bf16[256,128]{1,0:T(8,128)(2,1)S(1)}, u32[]{:S(2)}, u32[]{:S(2)}) collective-permute-start(bf16[256,128]{1,0:T(8,128)(2,1)S(1)} %get-tuple-element.42.refs_14_), channel_id=1, source_target_pairs={{0,24},{4,28},{8,16},{12,20},{16,8},{20,12},{24,0},{28,4},{1,25},{... | collective-permute-start | bytes 196616 | tf_op jit(solution)/shard_map/ppermute | solution.py:296
  14.0 4.6 %shard_map.154 = (f32[8,256,128]{2,1,0:T(8,128)S(1)}, f32[8,256,128]{2,1,0:T(8,128)S(1)}, f32[8,16,128]{2,1,0:T(8,128)S(1)}, bf16[2,1024,1024]{2,1,0:T(8,128)(2,1)S(1)}, bf16[256,1024]{1,0:T(8,128)(2,1)S(1)}) custom-call(f32[64,128]{1,0:T(8,128)S(1)} %constant_dynamic-slice_fusion.out_w_ref, f32[40,2048]{1,0:T(8,128)} %constant.23.clone.refs_0_, ...), custom_call_target="tpu_custom_call" | custom-call | tf_op jit(solution)/shard_map/pallas_call | solution.py:332
  19.2 1.8 %collective-permute-done.6.refs_7_ = bf16[256,128]{1,0:T(8,128)(2,1)S(1)} collective-permute-done((bf16[256,128]{1,0:T(8,128)(2,1)S(1)}, bf16[256,128]{1,0:T(8,128)(2,1)S(1)}, u32[]{:S(2)}, u32[]{:S(2)}) %collective-permute-start.6) | collective-permute-done | bytes 65568 | tf_op jit(solution)/shard_map/ppermute | solution.py:296
  21.0 2.9 %shard_map.156 = (bf16[256,128]{1,0:T(8,128)(2,1)S(1)}, bf16[256,128]{1,0:T(8,128)(2,1)S(1)}, bf16[256,128]{1,0:T(8,128)(2,1)S(1)}, bf16[256,128]{1,0:T(8,128)(2...) custom-call(s32[16]{0:T(128)S(1)} %copy-done.4, ...), custom_call_target="tpu_custom_call" | custom-call | tf_op jit(solution)/shard_map/pallas_call | solution.py:356
  24.5 1.9 %collective-permute-start.8 = (bf16[256,128]{1,0:T(8,128)(2,1)S(1)}, bf16[256,128]{1,0:T(8,128)(2,1)S(1)}, u32[]{:S(2)}, u32[]{:S(2)}) collective-permute-start(bf16[256,128]{1,0:T(8,128)(2,1)S(1)} %get-tuple-element.46), channel_id=1, source_target_pairs={{0,8},{4,12},{8,0},{12,4},{16,24},{20,28},{24,16},{28,20},{1,9},{5... | collective-permute-start | bytes 196616 | tf_op jit(solution)/shard_map/ppermute | solution.py:296
  26.4 1.1 %collective-permute-start.9 = (bf16[256,128]{1,0:T(8,128)(2,1)S(1)}, bf16[256,128]{1,0:T(8,128)(2,1)S(1)}, u32[]{:S(2)}, u32[]{:S(2)}) collective-permute-start(bf16[256,128]{1,0:T(8,128)(2,1)S(1)} %get-tuple-element.47), channel_id=1, source_target_pairs={{0,12},{4,8},{8,4},{12,0},{16,28},{20,24},{24,20},{28,16},{1,13},{... | collective-permute-start | bytes 196616 | tf_op jit(solution)/shard_map/ppermute | solution.py:296
  27.4 2.7 %collective-permute-start.10 = (bf16[256,128]{1,0:T(8,128)(2,1)S(1)}, bf16[256,128]{1,0:T(8,128)(2,1)S(1)}, u32[]{:S(2)}, u32[]{:S(2)}) collective-permute-start(bf16[256,128]{1,0:T(8,128)(2,1)S(1)} %get-tuple-element.48), channel_id=1, source_target_pairs={{0,16},{4,20},{8,24},{12,28},{16,0},{20,4},{24,8},{28,12},{1,17},{... | collective-permute-start | bytes 196616 | tf_op jit(solution)/shard_map/ppermute | solution.py:296
  30.3 2.4 %collective-permute-start.12 = (bf16[256,128]{1,0:T(8,128)(2,1)S(1)}, bf16[256,128]{1,0:T(8,128)(2,1)S(1)}, u32[]{:S(2)}, u32[]{:S(2)}) collective-permute-start(bf16[256,128]{1,0:T(8,128)(2,1)S(1)} %get-tuple-element.50), channel_id=1, source_target_pairs={{0,24},{4,28},{8,16},{12,20},{16,8},{20,12},{24,0},{28,4},{1,25},{... | collective-permute-start | bytes 196616 | tf_op jit(solution)/shard_map/ppermute | solution.py:296
  32.8 2.3 %collective-permute-start.13 = (bf16[256,128]{1,0:T(8,128)(2,1)S(1)}, bf16[256,128]{1,0:T(8,128)(2,1)S(1)}, u32[]{:S(2)}, u32[]{:S(2)}) collective-permute-start(bf16[256,128]{1,0:T(8,128)(2,1)S(1)} %get-tuple-element.51), channel_id=1, source_target_pairs={{0,28},{4,24},{8,20},{12,16},{16,12},{20,8},{24,4},{28,0},{1,29},{... | collective-permute-start | bytes 196616 | tf_op jit(solution)/shard_map/ppermute | solution.py:296
  35.1 2.3 %collective-permute-done.10.refs_4_ = bf16[256,128]{1,0:T(8,128)(2,1)S(1)} collective-permute-done((bf16[256,128]{1,0:T(8,128)(2,1)S(1)}, bf16[256,128]{1,0:T(8,128)(2,1)S(1)}, u32[]{:S(2)}, u32[]{:S(2)}) %collective-permute-start.10) | collective-permute-done | bytes 65568 | tf_op jit(solution)/shard_map/ppermute | solution.py:296
  37.4 1.3 %collective-permute-done.11.refs_5_ = bf16[256,128]{1,0:T(8,128)(2,1)S(1)} collective-permute-done((bf16[256,128]{1,0:T(8,128)(2,1)S(1)}, bf16[256,128]{1,0:T(8,128)(2,1)S(1)}, u32[]{:S(2)}, u32[]{:S(2)}) %collective-permute-start.11) | collective-permute-done | bytes 65568 | tf_op jit(solution)/shard_map/ppermute | solution.py:296
  38.7 1.1 %collective-permute-done.13.refs_7_ = bf16[256,128]{1,0:T(8,128)(2,1)S(1)} collective-permute-done((bf16[256,128]{1,0:T(8,128)(2,1)S(1)}, bf16[256,128]{1,0:T(8,128)(2,1)S(1)}, u32[]{:S(2)}, u32[]{:S(2)}) %collective-permute-start.13) | collective-permute-done | bytes 65568 | tf_op jit(solution)/shard_map/ppermute | solution.py:296
  39.9 0.8 %shard_map.157 = (bf16[1,256,512]{2,1,0:T(8,128)(2,1)S(1)}, bf16[256,1024]{1,0:T(8,128)(2,1)S(1)}) custom-call(bf16[256,1024]{1,0:T(8,128)(2,1)S(1)} %get-tuple-element.31.query_ref, f32[1,1024]{1,0:T(1,128)S(1)} %bitcast.14, bf16[2,1024,1024]{2,1,0:T(8,128)(2,1)S(1)} %get-tuple-element.32.weight_ref, bf16[256,128]{1,0:T(8,128)(2,1)S(1)} %get-tuple-element.44.refs_0_, ...), custom_call_target="tpu_custom_call" | custom-call | tf_op jit(solution)/shard_map/pallas_call | solution.py:393
  43.5 1.6 %collective-permute-start.15 = (bf16[1,256,512]{2,1,0:T(8,128)(2,1)S(1)}, bf16[1,256,512]{2,1,0:T(8,128)(2,1)S(1)}, u32[]{:S(2)}, u32[]{:S(2)}) collective-permute-start(bf16[1,256,512]{2,1,0:T(8,128)(2,1)S(1)} %add_convert_fusion.1), channel_id=1, source_target_pairs={{0,2},{1,3},{2,0},{3,1},{4,6},{5,7},{6,4},{7,5},{8,10},{9,11},{10,... | collective-permute-start | bytes 786440 | tf_op jit(solution)/shard_map/ppermute | solution.py:381
  45.7 6.9 %collective-permute-done.15 = bf16[1,256,512]{2,1,0:T(8,128)(2,1)S(1)} collective-permute-done((bf16[1,256,512]{2,1,0:T(8,128)(2,1)S(1)}, bf16[1,256,512]{2,1,0:T(8,128)(2,1)S(1)}, u32[]{:S(2)}, u32[]{:S(2)}) %collective-permute-start.15) | collective-permute-done | bytes 262176 | tf_op jit(solution)/shard_map/ppermute | solution.py:381
  52.7 2.3 %shard_map.159 = f32[1,256,1024]{2,1,0:T(8,128)S(1)} custom-call(bf16[256,1024]{1,0:T(8,128)(2,1)S(1)} %get-tuple-element.54.mixed_ref, bf16[1024,4096]{1,0:T(8,128)(2,1)} %weight_hbm.3), custom_call_target="tpu_custom_call" | custom-call | tf_op jit(solution)/shard_map/pallas_call | solution.py:412
  55.0 1.0 %shard_map.163.refs_3_ = f32[1024,256]{1,0:T(8,128)} custom-call(f32[256,1024]{1,0:T(8,128)S(1)} %bitcast.8, bf16[256,1024]{1,0:T(8,128)(2,1)S(1)} %bitcast.10, bf16[256,512]{1,0:T(8,128)(2,1)S(1)} %bitcast.12), custom_call_target="tpu_custom_call" | custom-call | tf_op jit(solution)/shard_map/pallas_call | solution.py:433
  56.0 1.9 %collective-permute-done.18 = bf16[1,256,512]{2,1,0:T(8,128)(2,1)S(1)} collective-permute-done((bf16[1,256,512]{2,1,0:T(8,128)(2,1)S(1)}, bf16[1,256,512]{2,1,0:T(8,128)(2,1)S(1)}, u32[]{:S(2)}, u32[]{:S(2)}) %collective-permute-start.18) | collective-permute-done | bytes 262176 | tf_op jit(solution)/shard_map/ppermute | solution.py:381
  57.9 1.0 %shard_map.164 = f32[1024,256]{1,0:T(8,128)} custom-call(f32[256,1024]{1,0:T(8,128)S(1)} %bitcast.9, bf16[256,1024]{1,0:T(8,128)(2,1)S(1)} %bitcast.11, bf16[256,512]{1,0:T(8,128)(2,1)S(1)} %bitcast.13, f32[1024,256]{1,0:T(8,128)} %shard_map.163.refs_3_), custom_call_target="tpu_custom_call", output_to_operand_aliasing={{}: (3, {})} | custom-call | tf_op jit(solution)/shard_map/pallas_call | solution.py:433
  (38 shorter events, 4.8 us)
Async XLA Ops:
  0.0 14.0 %copy-start = (f32[64,1024]{1,0:T(8,128)S(1)}, f32[64,1024]{1,0:T(8,128)}, u32[]{:S(2)}) copy-start(f32[64,1024]{1,0:T(8,128)} %param.24) | copy-start | bytes 786436
  1.5 8.9 %collective-permute-start = (bf16[256,128]{1,0:T(8,128)(2,1)S(1)}, bf16[256,128]{1,0:T(8,128)(2,1)S(1)}, u32[]{:S(2)}, u32[]{:S(2)}) collective-permute-start(bf16[256,128]{1,0:T(8,128)(2,1)S(1)} %get-tuple-element.37.refs_9_), channel_id=1, source_target_pairs={{0,4},{4,0},{8,12},{12,8},{16,20},{20,16},{24,28},{28,24},{1,5},{5... | collective-permute-start | bytes 196616 | tf_op jit(solution)/shard_map/ppermute | solution.py:296
  4.5 9.5 %collective-permute-start.1 = (bf16[256,128]{1,0:T(8,128)(2,1)S(1)}, bf16[256,128]{1,0:T(8,128)(2,1)S(1)}, u32[]{:S(2)}, u32[]{:S(2)}) collective-permute-start(bf16[256,128]{1,0:T(8,128)(2,1)S(1)} %get-tuple-element.38.refs_10_), channel_id=1, source_target_pairs={{0,8},{4,12},{8,0},{12,4},{16,24},{20,28},{24,16},{28,20},{1,9},{5... | collective-permute-start | bytes 196616 | tf_op jit(solution)/shard_map/ppermute | solution.py:296
  6.1 12.6 %collective-permute-start.2 = (bf16[256,128]{1,0:T(8,128)(2,1)S(1)}, bf16[256,128]{1,0:T(8,128)(2,1)S(1)}, u32[]{:S(2)}, u32[]{:S(2)}) collective-permute-start(bf16[256,128]{1,0:T(8,128)(2,1)S(1)} %get-tuple-element.39.refs_11_), channel_id=1, source_target_pairs={{0,12},{4,8},{8,4},{12,0},{16,28},{20,24},{24,20},{28,16},{1,13},{... | collective-permute-start | bytes 196616 | tf_op jit(solution)/shard_map/ppermute | solution.py:296
  6.1 12.6 %collective-permute-start.3 = (bf16[256,128]{1,0:T(8,128)(2,1)S(1)}, bf16[256,128]{1,0:T(8,128)(2,1)S(1)}, u32[]{:S(2)}, u32[]{:S(2)}) collective-permute-start(bf16[256,128]{1,0:T(8,128)(2,1)S(1)} %get-tuple-element.40.refs_12_), channel_id=1, source_target_pairs={{0,16},{4,20},{8,24},{12,28},{16,0},{20,4},{24,8},{28,12},{1,17},{... | collective-permute-start | bytes 196616 | tf_op jit(solution)/shard_map/ppermute | solution.py:296
  9.1 10.2 %collective-permute-start.4 = (bf16[256,128]{1,0:T(8,128)(2,1)S(1)}, bf16[256,128]{1,0:T(8,128)(2,1)S(1)}, u32[]{:S(2)}, u32[]{:S(2)}) collective-permute-start(bf16[256,128]{1,0:T(8,128)(2,1)S(1)} %get-tuple-element.41.refs_13_), channel_id=1, source_target_pairs={{0,20},{4,16},{8,28},{12,24},{16,4},{20,0},{24,12},{28,8},{1,21},{... | collective-permute-start | bytes 196616 | tf_op jit(solution)/shard_map/ppermute | solution.py:296
  10.3 8.9 %collective-permute-start.5 = (bf16[256,128]{1,0:T(8,128)(2,1)S(1)}, bf16[256,128]{1,0:T(8,128)(2,1)S(1)}, u32[]{:S(2)}, u32[]{:S(2)}) collective-permute-start(bf16[256,128]{1,0:T(8,128)(2,1)S(1)} %get-tuple-element.42.refs_14_), channel_id=1, source_target_pairs={{0,24},{4,28},{8,16},{12,20},{16,8},{20,12},{24,0},{28,4},{1,25},{... | collective-permute-start | bytes 196616 | tf_op jit(solution)/shard_map/ppermute | solution.py:296
  13.9 7.1 %collective-permute-start.6 = (bf16[256,128]{1,0:T(8,128)(2,1)S(1)}, bf16[256,128]{1,0:T(8,128)(2,1)S(1)}, u32[]{:S(2)}, u32[]{:S(2)}) collective-permute-start(bf16[256,128]{1,0:T(8,128)(2,1)S(1)} %get-tuple-element.43.refs_15_), channel_id=1, source_target_pairs={{0,28},{4,24},{8,20},{12,16},{16,12},{20,8},{24,4},{28,0},{1,29},{... | collective-permute-start | bytes 196616 | tf_op jit(solution)/shard_map/ppermute | solution.py:296
  14.0 7.0 %copy-start.1 = (bf16[256,512]{1,0:T(8,128)(2,1)S(1)}, bf16[256,512]{1,0:T(8,128)(2,1)}, u32[]{:S(2)}) copy-start(bf16[256,512]{1,0:T(8,128)(2,1)} %constant.26.inverse_ref) | copy-start | bytes 786436
  14.0 7.0 %copy-start.2 = (bf16[512,256]{1,0:T(8,128)(2,1)S(1)}, bf16[512,256]{1,0:T(8,128)(2,1)}, u32[]{:S(2)}) copy-start(bf16[512,256]{1,0:T(8,128)(2,1)} %constant.25.table_ref) | copy-start | bytes 786436
  14.0 7.0 %copy-start.4 = (s32[16]{0:T(128)S(1)}, s32[16]{0:T(128)}, u32[]{:S(2)}) copy-start(s32[16]{0:T(128)} %order_ref.1) | copy-start | bytes 196
  21.0 18.9 %copy-start.3 = (f32[1024]{0:T(1024)S(1)}, f32[1024]{0:T(1024)}, u32[]{:S(2)}) copy-start(f32[1024]{0:T(1024)} %param.26) | copy-start | bytes 12292
  23.9 6.5 %collective-permute-start.7 = (bf16[256,128]{1,0:T(8,128)(2,1)S(1)}, bf16[256,128]{1,0:T(8,128)(2,1)S(1)}, u32[]{:S(2)}, u32[]{:S(2)}) collective-permute-start(bf16[256,128]{1,0:T(8,128)(2,1)S(1)} %get-tuple-element.45), channel_id=1, source_target_pairs={{0,4},{4,0},{8,12},{12,8},{16,20},{20,16},{24,28},{28,24},{1,5},{5... | collective-permute-start | bytes 196616 | tf_op jit(solution)/shard_map/ppermute | solution.py:296
  24.5 8.3 %collective-permute-start.8 = (bf16[256,128]{1,0:T(8,128)(2,1)S(1)}, bf16[256,128]{1,0:T(8,128)(2,1)S(1)}, u32[]{:S(2)}, u32[]{:S(2)}) collective-permute-start(bf16[256,128]{1,0:T(8,128)(2,1)S(1)} %get-tuple-element.46), channel_id=1, source_target_pairs={{0,8},{4,12},{8,0},{12,4},{16,24},{20,28},{24,16},{28,20},{1,9},{5... | collective-permute-start | bytes 196616 | tf_op jit(solution)/shard_map/ppermute | solution.py:296
  26.4 8.7 %collective-permute-start.9 = (bf16[256,128]{1,0:T(8,128)(2,1)S(1)}, bf16[256,128]{1,0:T(8,128)(2,1)S(1)}, u32[]{:S(2)}, u32[]{:S(2)}) collective-permute-start(bf16[256,128]{1,0:T(8,128)(2,1)S(1)} %get-tuple-element.47), channel_id=1, source_target_pairs={{0,12},{4,8},{8,4},{12,0},{16,28},{20,24},{24,20},{28,16},{1,13},{... | collective-permute-start | bytes 196616 | tf_op jit(solution)/shard_map/ppermute | solution.py:296
  27.4 10.0 %collective-permute-start.10 = (bf16[256,128]{1,0:T(8,128)(2,1)S(1)}, bf16[256,128]{1,0:T(8,128)(2,1)S(1)}, u32[]{:S(2)}, u32[]{:S(2)}) collective-permute-start(bf16[256,128]{1,0:T(8,128)(2,1)S(1)} %get-tuple-element.48), channel_id=1, source_target_pairs={{0,16},{4,20},{8,24},{12,28},{16,0},{20,4},{24,8},{28,12},{1,17},{... | collective-permute-start | bytes 196616 | tf_op jit(solution)/shard_map/ppermute | solution.py:296
  30.2 8.5 %collective-permute-start.11 = (bf16[256,128]{1,0:T(8,128)(2,1)S(1)}, bf16[256,128]{1,0:T(8,128)(2,1)S(1)}, u32[]{:S(2)}, u32[]{:S(2)}) collective-permute-start(bf16[256,128]{1,0:T(8,128)(2,1)S(1)} %get-tuple-element.49), channel_id=1, source_target_pairs={{0,20},{4,16},{8,28},{12,24},{16,4},{20,0},{24,12},{28,8},{1,21},{... | collective-permute-start | bytes 196616 | tf_op jit(solution)/shard_map/ppermute | solution.py:296
  30.3 8.4 %collective-permute-start.12 = (bf16[256,128]{1,0:T(8,128)(2,1)S(1)}, bf16[256,128]{1,0:T(8,128)(2,1)S(1)}, u32[]{:S(2)}, u32[]{:S(2)}) collective-permute-start(bf16[256,128]{1,0:T(8,128)(2,1)S(1)} %get-tuple-element.50), channel_id=1, source_target_pairs={{0,24},{4,28},{8,16},{12,20},{16,8},{20,12},{24,0},{28,4},{1,25},{... | collective-permute-start | bytes 196616 | tf_op jit(solution)/shard_map/ppermute | solution.py:296
  32.8 7.1 %collective-permute-start.13 = (bf16[256,128]{1,0:T(8,128)(2,1)S(1)}, bf16[256,128]{1,0:T(8,128)(2,1)S(1)}, u32[]{:S(2)}, u32[]{:S(2)}) collective-permute-start(bf16[256,128]{1,0:T(8,128)(2,1)S(1)} %get-tuple-element.51), channel_id=1, source_target_pairs={{0,28},{4,24},{8,20},{12,16},{16,12},{20,8},{24,4},{28,0},{1,29},{... | collective-permute-start | bytes 196616 | tf_op jit(solution)/shard_map/ppermute | solution.py:296
  40.6 2.8 %collective-permute-start.14 = (bf16[1,256,512]{2,1,0:T(8,128)(2,1)S(1)}, bf16[1,256,512]{2,1,0:T(8,128)(2,1)S(1)}, u32[]{:S(2)}, u32[]{:S(2)}) collective-permute-start(bf16[1,256,512]{2,1,0:T(8,128)(2,1)S(1)} %get-tuple-element.53), channel_id=1, source_target_pairs={{0,1},{1,0},{2,3},{3,2},{4,5},{5,4},{6,7},{7,6},{8,9},{9,8},{10,11... | collective-permute-start | bytes 786440 | tf_op jit(solution)/shard_map/ppermute | solution.py:381
  41.2 3.9 %collective-permute-start.17 = (bf16[1,256,512]{2,1,0:T(8,128)(2,1)S(1)}, bf16[1,256,512]{2,1,0:T(8,128)(2,1)S(1)}, u32[]{:S(2)}, u32[]{:S(2)}) collective-permute-start(bf16[1,256,512]{2,1,0:T(8,128)(2,1)S(1)} %shard_map.162), channel_id=1, source_target_pairs={{0,1},{1,0},{2,3},{3,2},{4,5},{5,4},{6,7},{7,6},{8,9},{9,8},{10,11... | collective-permute-start | bytes 786440 | tf_op jit(solution)/shard_map/ppermute | solution.py:381
  43.3 11.7 %collective-permute-start.16 = (bf16[1,256,1024]{2,1,0:T(8,128)(2,1)S(1)}, bf16[1,256,1024]{2,1,0:T(8,128)(2,1)S(1)}, u32[]{:S(2)}, u32[]{:S(2)}) collective-permute-start(bf16[1,256,1024]{2,1,0:T(8,128)(2,1)S(1)} %shard_map.160), channel_id=1, source_target_pairs={{0,1},{1,0},{2,3},{3,2},{4,5},{5,4},{6,7},{7,6},{8,9},{9,8},{10,11... | collective-permute-start | bytes 1572872 | tf_op jit(solution)/shard_map/ppermute | solution.py:381
  43.5 9.2 %collective-permute-start.15 = (bf16[1,256,512]{2,1,0:T(8,128)(2,1)S(1)}, bf16[1,256,512]{2,1,0:T(8,128)(2,1)S(1)}, u32[]{:S(2)}, u32[]{:S(2)}) collective-permute-start(bf16[1,256,512]{2,1,0:T(8,128)(2,1)S(1)} %add_convert_fusion.1), channel_id=1, source_target_pairs={{0,2},{1,3},{2,0},{3,1},{4,6},{5,7},{6,4},{7,5},{8,10},{9,11},{10,... | collective-permute-start | bytes 786440 | tf_op jit(solution)/shard_map/ppermute | solution.py:381
  45.2 12.7 %collective-permute-start.18 = (bf16[1,256,512]{2,1,0:T(8,128)(2,1)S(1)}, bf16[1,256,512]{2,1,0:T(8,128)(2,1)S(1)}, u32[]{:S(2)}, u32[]{:S(2)}) collective-permute-start(bf16[1,256,512]{2,1,0:T(8,128)(2,1)S(1)} %add_convert_fusion), channel_id=1, source_target_pairs={{0,2},{1,3},{2,0},{3,1},{4,6},{5,7},{6,4},{7,5},{8,10},{9,11},{10,... | collective-permute-start | bytes 786440 | tf_op jit(solution)/shard_map/ppermute | solution.py:381

commit v9 on v7

--- a/solution.py
+++ b/solution.py
@@ -149,7 +149,7 @@
 
 
 def conv_kernel(
-    block, blocks_next, relative, order_ref, real_ref, imag_ref, edge_ref, table_ref, inverse_ref, weight_hbm, *refs
+    block, blocks_next, arrival, relative, order_ref, real_ref, imag_ref, edge_ref, table_ref, inverse_ref, weight_hbm, *refs
 ):
     *refs, weight_out, sig, sre, sim, spec, conv, weight_sem = refs
     count = len(refs) // 2
@@ -165,7 +165,7 @@
     def place(k, i):
         return pl.multiple_of(order_ref[(first ^ k) * groups + i] * GROUP, GROUP)
 
-    for k, x_ref in enumerate(x_refs):
+    for k, x_ref in zip(arrival, x_refs):
         for i in range(groups):
             sig[pl.ds(place(k, i), GROUP), :] = x_ref[i * GROUP : (i + 1) * GROUP, :]
     group = 2
@@ -209,11 +209,11 @@
         copy.wait()
 
 
-def mix_kernel(query_ref, gain_ref, weight_ref, *refs):
+def mix_kernel(arrival, query_ref, gain_ref, weight_ref, *refs):
     *refs, out_ref, mixed_ref = refs
     pieces = len(refs) // 2
     unit = refs[0].shape[1]
-    for k, (back_ref, sig_ref) in enumerate(zip(refs[:pieces], refs[pieces:])):
+    for k, back_ref, sig_ref in zip(arrival, refs[:pieces], refs[pieces:]):
         cols = pl.ds(pl.multiple_of((first_piece(pieces) ^ k) * unit, LANES), unit)
         inner = back_ref[...].astype(F32) + gain_ref[:, cols] * sig_ref[...].astype(F32)
         mixed_ref[:, cols] = (query_ref[:, cols].astype(F32) * inner).astype(BF16)
@@ -238,13 +238,18 @@
 def finish_kernel(span, count, *refs):
     (*held, arrived), (out_hbm, turned, sem) = refs[: count + 1], refs[-3:]
     first, last = span
-    total = arrived[...].astype(F32)
-    for ref in held:
-        total = total + ref[:, first:last].astype(F32)
-    turned[...] = total.T
-    copy = pltpu.make_async_copy(turned, out_hbm.at[first:last], sem.at[0])
-    copy.start()
-    copy.wait()
+    step = min(LANES, last - first)
+    copies = []
+    for i, start in enumerate(range(0, last - first, step)):
+        cols = slice(start, start + step)
+        total = arrived[:, cols].astype(F32)
+        for ref in held:
+            total = total + ref[:, first + start : first + start + step].astype(F32)
+        turned[cols] = total.T
+        copies.append(pltpu.make_async_copy(turned.at[cols], out_hbm.at[first + start : first + start + step], sem.at[i]))
+        copies[-1].start()
+    for copy in copies:
+        copy.wait()
 
 
 def gated_kernel(key_hbm, value_hbm, *refs):
@@ -288,6 +293,8 @@
     far = lambda operand: pltpu.with_memory_space_constraint(operand, pltpu.HBM)
     unit = width if width % LANES == 0 else chan_width
     pieces = chan_width // unit
+
+    arrival = sorted(range(seq_count), key=lambda k: (k & 1, k))
 
     def swap(arrays):
         return [arrays[0]] + [
@@ -352,7 +359,7 @@
     )(my_filter, *map(far, (*smalls, out_weight, query)))
 
     *convolved, weights_next = pl.pallas_call(
-        functools.partial(conv_kernel, block, blocks_next, pieces > 1),
+        functools.partial(conv_kernel, block, blocks_next, arrival, pieces > 1),
         out_shape=[
             *[jax.ShapeDtypeStruct((rows, LANES), BF16)] * seq_count,
             jax.ShapeDtypeStruct((quarter, chan_width, out_width), BF16),
@@ -368,7 +375,7 @@
             pltpu.SemaphoreType.DMA((quarter,)),
         ],
         compiler_params=limit,
-    )(group_order, real, imag, edge, head, inverse, far(out_weight), *spread)
+    )(group_order, real, imag, edge, head, inverse, far(out_weight), *[spread[k] for k in arrival])
     if pieces > 1:
         backs = swap(convolved)
     else:
@@ -379,7 +386,7 @@
         return lax.ppermute(terms, "chan", [(d, d ^ bit) for d in range(chan_count)])
 
     far_away, mixed = pl.pallas_call(
-        mix_kernel,
+        functools.partial(mix_kernel, arrival if pieces > 1 else [0]),
         out_shape=(
             jax.ShapeDtypeStruct((quarter, rows, out_width), BF16),
             jax.ShapeDtypeStruct((rows, chan_width), BF16),
@@ -387,7 +394,7 @@
         in_specs=[in_vmem] * (3 + 2 * pieces),
         out_specs=[in_vmem] * 2,
         compiler_params=limit,
-    )(query_near, skip_gain[None, :], weights_first, *backs, *signal)
+    )(query_near, skip_gain[None, :], weights_first, *[array[k] for array in (backs, signal) for k in (arrival if pieces > 1 else [0])])
     far_terms = exchange(far_away, 1)
 
     def products(first, weights, dtype):
@@ -400,8 +407,7 @@
         )(mixed, weights)
 
     far_kept, near_away = products(quarter, weights_first, F32), products(0, weights_next, BF16)
-    cuts = sorted({0, out_width // 2, max(out_width // 2, out_width * 7 // 8 // LANES * LANES), out_width})
-    spans = list(zip(cuts, cuts[1:]))
+    spans = [(0, out_width // 2), (out_width // 2, out_width)]
     send = [(far_kept[:, :, a:b] + far_terms[:, :, a:b].astype(F32)).astype(BF16) for a, b in spans]
     send, near_away, mixed = lax.optimization_barrier((send, near_away, mixed))
     sent = [exchange(piece, 2) for piece in send]
@@ -432,7 +438,10 @@
                 out_shape=jax.ShapeDtypeStruct((out_width, rows), F32),
                 in_specs=[in_vmem] * len(operands) + [in_hbm] * len(result),
                 out_specs=in_hbm,
-                scratch_shapes=[pltpu.VMEM((span[1] - span[0], rows), F32), pltpu.SemaphoreType.DMA((1,))],
+                scratch_shapes=[
+                    pltpu.VMEM((span[1] - span[0], rows), F32),
+                    pltpu.SemaphoreType.DMA((max(1, (span[1] - span[0]) // LANES),)),
+                ],
                 input_output_aliases={len(operands): 0} if result else {},
                 compiler_params=limit,
             )(*operands, *result)

time: 58.5 us -> 58.5 us (level)
  waiting for transfers between devices: 14 us -> 15.4 us
  Pallas kernels: 16.4 us -> 15.6 us
  starting transfers between devices: 27.5 us -> 26.9 us
    ppermute x5 -> x4, waiting for transfers between devices: 6.94 us -> 9.36 us  [exchange(): lax.ppermute(terms, 'chan', [(d, d ^ bit) for d in range(chan_count)])]
    ppermute x5 -> x4, starting transfers between devices: 3.83 us -> 2.31 us  [exchange(): lax.ppermute(terms, 'chan', [(d, d ^ bit) for d in range(chan_count)])]
    ppermute x14, waiting for transfers between devices: 7.09 us -> 6.05 us  [swap(): lax.ppermute(arrays[k], 'seq', [(d, d ^ k) for d in range(seq_count)])]
    ppermute x14, starting transfers between devices: 23.7 us -> 24.6 us  [swap(): lax.ppermute(arrays[k], 'seq', [(d, d ^ k) for d in range(seq_count)])]
    pallas_call x3 -> x2, Pallas kernels: 2.7 us -> 1.87 us  [local(): pl.pallas_call(functools.partial(finish_kernel, span, len(terms)), out_sh...]
  transfers between devices with their start and end apart: 19 -> 18, of which waited for: 8 -> 6; matrix products, arithmetic and copies ran while one was open for 0% -> 0% of each run, Pallas kernels for 18% -> 16%
where the time goes in v9:
time: 58.5 us; the launch traced here: 58.3 us
  starting transfers between devices  26.9 us (46%)
  Pallas kernels  15.6 us (27%)
  waiting for transfers between devices  15.4 us (26%)
    ppermute x14, starting transfers between devices, swap(): lax.ppermute(arrays[k], 'seq', [(d, d ^ k) for d in range(seq_count)])  24.6 us
    ppermute x4, waiting for transfers between devices, exchange(): lax.ppermute(terms, 'chan', [(d, d ^ bit) for d in range(chan_count)])  9.36 us
    ppermute x14, waiting for transfers between devices, swap(): lax.ppermute(arrays[k], 'seq', [(d, d ^ k) for d in range(seq_count)])  6.05 us
    pallas_call x1, Pallas kernels, local(): pl.pallas_call(functools.partial(filter_kernel, block, blocks_first, piec...  4.63 us
    pallas_call x1, Pallas kernels, local(): pl.pallas_call(functools.partial(conv_kernel, block, blocks_next, arrival...  2.85 us
    ppermute x4, starting transfers between devices, exchange(): lax.ppermute(terms, 'chan', [(d, d ^ bit) for d in range(chan_count)])  2.31 us
    pallas_call x1, Pallas kernels, local(): pl.pallas_call(functools.partial(last_kernel, blocks_last), out_shape=jax...  2.31 us
    pallas_call x2, Pallas kernels, local(): pl.pallas_call(functools.partial(finish_kernel, span, len(terms)), out_sh...  1.87 us
  transfers between devices with their start and end apart: 18, of which 6 were waited for; matrix products, arithmetic and copies ran while one was open for 0% of the time, Pallas kernels for 16%

profile of v9, /device:TPU:0, one launch (start us, length us, event | category | flops | bytes accessed | tf_op | source)
XLA Modules:
  0.0 58.3 jit_solution(5345931527568113939)
XLA Ops:
  0.0 1.5 %shard_map.155 = (bf16[256,128]{1,0:T(8,128)(2,1)S(1)}, bf16[256,128]{1,0:T(8,128)(2,1)S(1)}, bf16[256,128]{1,0:T(8,128)(2,1)S(1)}, bf16[256,128]{1,0:T(8,128)(2...) custom-call(bf16[256,1024]{1,0:T(8,128)(2,1)} %key_hbm.1, ...), custom_call_target="tpu_custom_call" | custom-call | tf_op jit(solution)/shard_map/pallas_call | solution.py:304
  1.5 3.1 %collective-permute-start = (bf16[256,128]{1,0:T(8,128)(2,1)S(1)}, bf16[256,128]{1,0:T(8,128)(2,1)S(1)}, u32[]{:S(2)}, u32[]{:S(2)}) collective-permute-start(bf16[256,128]{1,0:T(8,128)(2,1)S(1)} %get-tuple-element.39.refs_9_), channel_id=1, source_target_pairs={{0,8},{4,12},{8,0},{12,4},{16,24},{20,28},{24,16},{28,20},{1,9},{5... | collective-permute-start | bytes 196616 | tf_op jit(solution)/shard_map/ppermute | solution.py:301
  4.6 2.6 %collective-permute-start.1 = (bf16[256,128]{1,0:T(8,128)(2,1)S(1)}, bf16[256,128]{1,0:T(8,128)(2,1)S(1)}, u32[]{:S(2)}, u32[]{:S(2)}) collective-permute-start(bf16[256,128]{1,0:T(8,128)(2,1)S(1)} %get-tuple-element.40.refs_10_), channel_id=1, source_target_pairs={{0,16},{4,20},{8,24},{12,28},{16,0},{20,4},{24,8},{28,12},{1,17},{... | collective-permute-start | bytes 196616 | tf_op jit(solution)/shard_map/ppermute | solution.py:301
  7.2 1.7 %collective-permute-start.3 = (bf16[256,128]{1,0:T(8,128)(2,1)S(1)}, bf16[256,128]{1,0:T(8,128)(2,1)S(1)}, u32[]{:S(2)}, u32[]{:S(2)}) collective-permute-start(bf16[256,128]{1,0:T(8,128)(2,1)S(1)} %get-tuple-element.42.refs_12_), channel_id=1, source_target_pairs={{0,4},{4,0},{8,12},{12,8},{16,20},{20,16},{24,28},{28,24},{1,5},{5... | collective-permute-start | bytes 196616 | tf_op jit(solution)/shard_map/ppermute | solution.py:301
  9.5 4.4 %collective-permute-start.5 = (bf16[256,128]{1,0:T(8,128)(2,1)S(1)}, bf16[256,128]{1,0:T(8,128)(2,1)S(1)}, u32[]{:S(2)}, u32[]{:S(2)}) collective-permute-start(bf16[256,128]{1,0:T(8,128)(2,1)S(1)} %get-tuple-element.44.refs_14_), channel_id=1, source_target_pairs={{0,20},{4,16},{8,28},{12,24},{16,4},{20,0},{24,12},{28,8},{1,21},{... | collective-permute-start | bytes 196616 | tf_op jit(solution)/shard_map/ppermute | solution.py:301
  13.9 2.4 %collective-permute-start.6 = (bf16[256,128]{1,0:T(8,128)(2,1)S(1)}, bf16[256,128]{1,0:T(8,128)(2,1)S(1)}, u32[]{:S(2)}, u32[]{:S(2)}) collective-permute-start(bf16[256,128]{1,0:T(8,128)(2,1)S(1)} %get-tuple-element.45.refs_15_), channel_id=1, source_target_pairs={{0,28},{4,24},{8,20},{12,16},{16,12},{20,8},{24,4},{28,0},{1,29},{... | collective-permute-start | bytes 196616 | tf_op jit(solution)/shard_map/ppermute | solution.py:301
  16.4 4.6 %shard_map.154 = (f32[8,256,128]{2,1,0:T(8,128)S(1)}, f32[8,256,128]{2,1,0:T(8,128)S(1)}, f32[8,16,128]{2,1,0:T(8,128)S(1)}, bf16[2,1024,1024]{2,1,0:T(8,128)(2,1)S(1)}, bf16[256,1024]{1,0:T(8,128)(2,1)S(1)}) custom-call(f32[64,128]{1,0:T(8,128)S(1)} %constant_dynamic-slice_fusion.out_w_ref, f32[40,2048]{1,0:T(8,128)} %constant.23.clone.refs_0_, ...), custom_call_target="tpu_custom_call" | custom-call | tf_op jit(solution)/shard_map/pallas_call | solution.py:337
  21.1 2.9 %shard_map.156 = (bf16[256,128]{1,0:T(8,128)(2,1)S(1)}, bf16[256,128]{1,0:T(8,128)(2,1)S(1)}, bf16[256,128]{1,0:T(8,128)(2,1)S(1)}, bf16[256,128]{1,0:T(8,128)(2...) custom-call(s32[16]{0:T(128)S(1)} %copy-done.4, ...), custom_call_target="tpu_custom_call" | custom-call | tf_op jit(solution)/shard_map/pallas_call | solution.py:361
  24.0 2.0 %collective-permute-start.8 = (bf16[256,128]{1,0:T(8,128)(2,1)S(1)}, bf16[256,128]{1,0:T(8,128)(2,1)S(1)}, u32[]{:S(2)}, u32[]{:S(2)}) collective-permute-start(bf16[256,128]{1,0:T(8,128)(2,1)S(1)} %get-tuple-element.48), channel_id=1, source_target_pairs={{0,16},{4,20},{8,24},{12,28},{16,0},{20,4},{24,8},{28,12},{1,17},{... | collective-permute-start | bytes 196616 | tf_op jit(solution)/shard_map/ppermute | solution.py:301
  26.0 2.4 %collective-permute-start.9 = (bf16[256,128]{1,0:T(8,128)(2,1)S(1)}, bf16[256,128]{1,0:T(8,128)(2,1)S(1)}, u32[]{:S(2)}, u32[]{:S(2)}) collective-permute-start(bf16[256,128]{1,0:T(8,128)(2,1)S(1)} %get-tuple-element.49), channel_id=1, source_target_pairs={{0,24},{4,28},{8,16},{12,20},{16,8},{20,12},{24,0},{28,4},{1,25},{... | collective-permute-start | bytes 196616 | tf_op jit(solution)/shard_map/ppermute | solution.py:301
  29.0 1.4 %collective-permute-done.7.refs_1_ = bf16[256,128]{1,0:T(8,128)(2,1)S(1)} collective-permute-done((bf16[256,128]{1,0:T(8,128)(2,1)S(1)}, bf16[256,128]{1,0:T(8,128)(2,1)S(1)}, u32[]{:S(2)}, u32[]{:S(2)}) %collective-permute-start.7) | collective-permute-done | bytes 65568 | tf_op jit(solution)/shard_map/ppermute | solution.py:301
  30.5 2.3 %collective-permute-start.12 = (bf16[256,128]{1,0:T(8,128)(2,1)S(1)}, bf16[256,128]{1,0:T(8,128)(2,1)S(1)}, u32[]{:S(2)}, u32[]{:S(2)}) collective-permute-start(bf16[256,128]{1,0:T(8,128)(2,1)S(1)} %get-tuple-element.52), channel_id=1, source_target_pairs={{0,20},{4,16},{8,28},{12,24},{16,4},{20,0},{24,12},{28,8},{1,21},{... | collective-permute-start | bytes 196616 | tf_op jit(solution)/shard_map/ppermute | solution.py:301
  32.8 2.4 %collective-permute-start.13 = (bf16[256,128]{1,0:T(8,128)(2,1)S(1)}, bf16[256,128]{1,0:T(8,128)(2,1)S(1)}, u32[]{:S(2)}, u32[]{:S(2)}) collective-permute-start(bf16[256,128]{1,0:T(8,128)(2,1)S(1)} %get-tuple-element.53), channel_id=1, source_target_pairs={{0,28},{4,24},{8,20},{12,16},{16,12},{20,8},{24,4},{28,0},{1,29},{... | collective-permute-start | bytes 196616 | tf_op jit(solution)/shard_map/ppermute | solution.py:301
  35.2 1.4 %collective-permute-done.12.refs_6_ = bf16[256,128]{1,0:T(8,128)(2,1)S(1)} collective-permute-done((bf16[256,128]{1,0:T(8,128)(2,1)S(1)}, bf16[256,128]{1,0:T(8,128)(2,1)S(1)}, u32[]{:S(2)}, u32[]{:S(2)}) %collective-permute-start.12) | collective-permute-done | bytes 65568 | tf_op jit(solution)/shard_map/ppermute | solution.py:301
  36.5 3.2 %collective-permute-done.13.refs_7_ = bf16[256,128]{1,0:T(8,128)(2,1)S(1)} collective-permute-done((bf16[256,128]{1,0:T(8,128)(2,1)S(1)}, bf16[256,128]{1,0:T(8,128)(2,1)S(1)}, u32[]{:S(2)}, u32[]{:S(2)}) %collective-permute-start.13) | collective-permute-done | bytes 65568 | tf_op jit(solution)/shard_map/ppermute | solution.py:301
  39.7 1.0 %shard_map.157 = (bf16[1,256,1024]{2,1,0:T(8,128)(2,1)S(1)}, bf16[256,1024]{1,0:T(8,128)(2,1)S(1)}) custom-call(bf16[256,1024]{1,0:T(8,128)(2,1)S(1)} %get-tuple-element.33.query_ref, f32[1,1024]{1,0:T(1,128)S(1)} %bitcast.14, bf16[2,1024,1024]{2,1,0:T(8,128)(2,1)S(1)} %get-tuple-element.34.weight_ref, bf16[256,128]{1,0:T(8,128)(2,1)S(1)} %get-tuple-element.46.refs_0_, ...), custom_call_target="tpu_custom_call" | custom-call | tf_op jit(solution)/shard_map/pallas_call | solution.py:388
  40.9 0.7 %shard_map.158 = f32[1,256,1024]{2,1,0:T(8,128)S(1)} custom-call(bf16[256,1024]{1,0:T(8,128)(2,1)S(1)} %get-tuple-element.57.mixed_ref, bf16[2,1024,1024]{2,1,0:T(8,128)(2,1)S(1)} %get-tuple-element.34.weight_ref), custom_call_target="tpu_custom_call" | custom-call | tf_op jit(solution)/shard_map/pallas_call | solution.py:401
  41.6 0.7 %shard_map.159 = bf16[1,256,1024]{2,1,0:T(8,128)(2,1)S(1)} custom-call(bf16[256,1024]{1,0:T(8,128)(2,1)S(1)} %get-tuple-element.57.mixed_ref, bf16[1,1024,1024]{2,1,0:T(8,128)(2,1)S(1)} %get-tuple-element.56.weight_ref), custom_call_target="tpu_custom_call" | custom-call | tf_op jit(solution)/shard_map/pallas_call | solution.py:401
  43.1 1.5 %collective-permute-start.17 = (bf16[1,256,512]{2,1,0:T(8,128)(2,1)S(1)}, bf16[1,256,512]{2,1,0:T(8,128)(2,1)S(1)}, u32[]{:S(2)}, u32[]{:S(2)}) collective-permute-start(bf16[1,256,512]{2,1,0:T(8,128)(2,1)S(1)} %get-tuple-element.60), channel_id=1, source_target_pairs={{0,2},{1,3},{2,0},{3,1},{4,6},{5,7},{6,4},{7,5},{8,10},{9,11},{10,... | collective-permute-start | bytes 786440 | tf_op jit(solution)/shard_map/ppermute | solution.py:386
  45.2 2.3 %shard_map.160 = f32[1,256,1024]{2,1,0:T(8,128)S(1)} custom-call(bf16[256,1024]{1,0:T(8,128)(2,1)S(1)} %get-tuple-element.57.mixed_ref, bf16[1024,4096]{1,0:T(8,128)(2,1)} %weight_hbm.3), custom_call_target="tpu_custom_call" | custom-call | tf_op jit(solution)/shard_map/pallas_call | solution.py:415
  47.5 4.8 %collective-permute-done.17 = bf16[1,256,512]{2,1,0:T(8,128)(2,1)S(1)} collective-permute-done((bf16[1,256,512]{2,1,0:T(8,128)(2,1)S(1)}, bf16[1,256,512]{2,1,0:T(8,128)(2,1)S(1)}, u32[]{:S(2)}, u32[]{:S(2)}) %collective-permute-start.17) | collective-permute-done | bytes 262176 | tf_op jit(solution)/shard_map/ppermute | solution.py:386
  52.3 0.9 %shard_map.161.refs_3_ = f32[1024,256]{1,0:T(8,128)} custom-call(f32[256,1024]{1,0:T(8,128)S(1)} %bitcast.8, bf16[256,1024]{1,0:T(8,128)(2,1)S(1)} %bitcast.10, bf16[256,512]{1,0:T(8,128)(2,1)S(1)} %bitcast.12), custom_call_target="tpu_custom_call" | custom-call | tf_op jit(solution)/shard_map/pallas_call | solution.py:436
  53.2 4.1 %collective-permute-done.16 = bf16[1,256,512]{2,1,0:T(8,128)(2,1)S(1)} collective-permute-done((bf16[1,256,512]{2,1,0:T(8,128)(2,1)S(1)}, bf16[1,256,512]{2,1,0:T(8,128)(2,1)S(1)}, u32[]{:S(2)}, u32[]{:S(2)}) %collective-permute-start.16) | collective-permute-done | bytes 262176 | tf_op jit(solution)/shard_map/ppermute | solution.py:386
  57.3 0.9 %shard_map.162 = f32[1024,256]{1,0:T(8,128)} custom-call(f32[256,1024]{1,0:T(8,128)S(1)} %bitcast.9, bf16[256,1024]{1,0:T(8,128)(2,1)S(1)} %bitcast.11, bf16[256,512]{1,0:T(8,128)(2,1)S(1)} %bitcast.13, f32[1024,256]{1,0:T(8,128)} %shard_map.161.refs_3_), custom_call_target="tpu_custom_call", output_to_operand_aliasing={{}: (3, {})} | custom-call | tf_op jit(solution)/shard_map/pallas_call | solution.py:436
  (33 shorter events, 2.8 us)
Async XLA Ops:
  0.0 16.3 %copy-start = (f32[64,1024]{1,0:T(8,128)S(1)}, f32[64,1024]{1,0:T(8,128)}, u32[]{:S(2)}) copy-start(f32[64,1024]{1,0:T(8,128)} %param.24) | copy-start | bytes 786436
  1.5 8.0 %collective-permute-start = (bf16[256,128]{1,0:T(8,128)(2,1)S(1)}, bf16[256,128]{1,0:T(8,128)(2,1)S(1)}, u32[]{:S(2)}, u32[]{:S(2)}) collective-permute-start(bf16[256,128]{1,0:T(8,128)(2,1)S(1)} %get-tuple-element.39.refs_9_), channel_id=1, source_target_pairs={{0,8},{4,12},{8,0},{12,4},{16,24},{20,28},{24,16},{28,20},{1,9},{5... | collective-permute-start | bytes 196616 | tf_op jit(solution)/shard_map/ppermute | solution.py:301
  4.6 9.4 %collective-permute-start.1 = (bf16[256,128]{1,0:T(8,128)(2,1)S(1)}, bf16[256,128]{1,0:T(8,128)(2,1)S(1)}, u32[]{:S(2)}, u32[]{:S(2)}) collective-permute-start(bf16[256,128]{1,0:T(8,128)(2,1)S(1)} %get-tuple-element.40.refs_10_), channel_id=1, source_target_pairs={{0,16},{4,20},{8,24},{12,28},{16,0},{20,4},{24,8},{28,12},{1,17},{... | collective-permute-start | bytes 196616 | tf_op jit(solution)/shard_map/ppermute | solution.py:301
  7.1 13.8 %collective-permute-start.2 = (bf16[256,128]{1,0:T(8,128)(2,1)S(1)}, bf16[256,128]{1,0:T(8,128)(2,1)S(1)}, u32[]{:S(2)}, u32[]{:S(2)}) collective-permute-start(bf16[256,128]{1,0:T(8,128)(2,1)S(1)} %get-tuple-element.41.refs_11_), channel_id=1, source_target_pairs={{0,24},{4,28},{8,16},{12,20},{16,8},{20,12},{24,0},{28,4},{1,25},{... | collective-permute-start | bytes 196616 | tf_op jit(solution)/shard_map/ppermute | solution.py:301
  7.2 13.9 %collective-permute-start.3 = (bf16[256,128]{1,0:T(8,128)(2,1)S(1)}, bf16[256,128]{1,0:T(8,128)(2,1)S(1)}, u32[]{:S(2)}, u32[]{:S(2)}) collective-permute-start(bf16[256,128]{1,0:T(8,128)(2,1)S(1)} %get-tuple-element.42.refs_12_), channel_id=1, source_target_pairs={{0,4},{4,0},{8,12},{12,8},{16,20},{20,16},{24,28},{28,24},{1,5},{5... | collective-permute-start | bytes 196616 | tf_op jit(solution)/shard_map/ppermute | solution.py:301
  8.9 12.2 %collective-permute-start.4 = (bf16[256,128]{1,0:T(8,128)(2,1)S(1)}, bf16[256,128]{1,0:T(8,128)(2,1)S(1)}, u32[]{:S(2)}, u32[]{:S(2)}) collective-permute-start(bf16[256,128]{1,0:T(8,128)(2,1)S(1)} %get-tuple-element.43.refs_13_), channel_id=1, source_target_pairs={{0,12},{4,8},{8,4},{12,0},{16,28},{20,24},{24,20},{28,16},{1,13},{... | collective-permute-start | bytes 196616 | tf_op jit(solution)/shard_map/ppermute | solution.py:301
  9.5 11.5 %collective-permute-start.5 = (bf16[256,128]{1,0:T(8,128)(2,1)S(1)}, bf16[256,128]{1,0:T(8,128)(2,1)S(1)}, u32[]{:S(2)}, u32[]{:S(2)}) collective-permute-start(bf16[256,128]{1,0:T(8,128)(2,1)S(1)} %get-tuple-element.44.refs_14_), channel_id=1, source_target_pairs={{0,20},{4,16},{8,28},{12,24},{16,4},{20,0},{24,12},{28,8},{1,21},{... | collective-permute-start | bytes 196616 | tf_op jit(solution)/shard_map/ppermute | solution.py:301
  13.9 7.1 %collective-permute-start.6 = (bf16[256,128]{1,0:T(8,128)(2,1)S(1)}, bf16[256,128]{1,0:T(8,128)(2,1)S(1)}, u32[]{:S(2)}, u32[]{:S(2)}) collective-permute-start(bf16[256,128]{1,0:T(8,128)(2,1)S(1)} %get-tuple-element.45.refs_15_), channel_id=1, source_target_pairs={{0,28},{4,24},{8,20},{12,16},{16,12},{20,8},{24,4},{28,0},{1,29},{... | collective-permute-start | bytes 196616 | tf_op jit(solution)/shard_map/ppermute | solution.py:301
  16.3 4.7 %copy-start.1 = (bf16[256,512]{1,0:T(8,128)(2,1)S(1)}, bf16[256,512]{1,0:T(8,128)(2,1)}, u32[]{:S(2)}) copy-start(bf16[256,512]{1,0:T(8,128)(2,1)} %constant.26.inverse_ref) | copy-start | bytes 786436
  16.3 4.7 %copy-start.2 = (bf16[512,256]{1,0:T(8,128)(2,1)S(1)}, bf16[512,256]{1,0:T(8,128)(2,1)}, u32[]{:S(2)}) copy-start(bf16[512,256]{1,0:T(8,128)(2,1)} %constant.25.table_ref) | copy-start | bytes 786436
  16.3 4.7 %copy-start.4 = (s32[16]{0:T(128)S(1)}, s32[16]{0:T(128)}, u32[]{:S(2)}) copy-start(s32[16]{0:T(128)} %order_ref.1) | copy-start | bytes 196
  21.1 18.7 %copy-start.3 = (f32[1024]{0:T(1024)S(1)}, f32[1024]{0:T(1024)}, u32[]{:S(2)}) copy-start(f32[1024]{0:T(1024)} %param.26) | copy-start | bytes 12292
  23.9 6.5 %collective-permute-start.7 = (bf16[256,128]{1,0:T(8,128)(2,1)S(1)}, bf16[256,128]{1,0:T(8,128)(2,1)S(1)}, u32[]{:S(2)}, u32[]{:S(2)}) collective-permute-start(bf16[256,128]{1,0:T(8,128)(2,1)S(1)} %get-tuple-element.47), channel_id=1, source_target_pairs={{0,8},{4,12},{8,0},{12,4},{16,24},{20,28},{24,16},{28,20},{1,9},{5... | collective-permute-start | bytes 196616 | tf_op jit(solution)/shard_map/ppermute | solution.py:301
  24.0 8.8 %collective-permute-start.8 = (bf16[256,128]{1,0:T(8,128)(2,1)S(1)}, bf16[256,128]{1,0:T(8,128)(2,1)S(1)}, u32[]{:S(2)}, u32[]{:S(2)}) collective-permute-start(bf16[256,128]{1,0:T(8,128)(2,1)S(1)} %get-tuple-element.48), channel_id=1, source_target_pairs={{0,16},{4,20},{8,24},{12,28},{16,0},{20,4},{24,8},{28,12},{1,17},{... | collective-permute-start | bytes 196616 | tf_op jit(solution)/shard_map/ppermute | solution.py:301
  26.0 9.2 %collective-permute-start.9 = (bf16[256,128]{1,0:T(8,128)(2,1)S(1)}, bf16[256,128]{1,0:T(8,128)(2,1)S(1)}, u32[]{:S(2)}, u32[]{:S(2)}) collective-permute-start(bf16[256,128]{1,0:T(8,128)(2,1)S(1)} %get-tuple-element.49), channel_id=1, source_target_pairs={{0,24},{4,28},{8,16},{12,20},{16,8},{20,12},{24,0},{28,4},{1,25},{... | collective-permute-start | bytes 196616 | tf_op jit(solution)/shard_map/ppermute | solution.py:301
  28.4 6.8 %collective-permute-start.10 = (bf16[256,128]{1,0:T(8,128)(2,1)S(1)}, bf16[256,128]{1,0:T(8,128)(2,1)S(1)}, u32[]{:S(2)}, u32[]{:S(2)}) collective-permute-start(bf16[256,128]{1,0:T(8,128)(2,1)S(1)} %get-tuple-element.50), channel_id=1, source_target_pairs={{0,4},{4,0},{8,12},{12,8},{16,20},{20,16},{24,28},{28,24},{1,5},{5... | collective-permute-start | bytes 196616 | tf_op jit(solution)/shard_map/ppermute | solution.py:301
  28.8 6.4 %collective-permute-start.11 = (bf16[256,128]{1,0:T(8,128)(2,1)S(1)}, bf16[256,128]{1,0:T(8,128)(2,1)S(1)}, u32[]{:S(2)}, u32[]{:S(2)}) collective-permute-start(bf16[256,128]{1,0:T(8,128)(2,1)S(1)} %get-tuple-element.51), channel_id=1, source_target_pairs={{0,12},{4,8},{8,4},{12,0},{16,28},{20,24},{24,20},{28,16},{1,13},{... | collective-permute-start | bytes 196616 | tf_op jit(solution)/shard_map/ppermute | solution.py:301
  30.5 6.1 %collective-permute-start.12 = (bf16[256,128]{1,0:T(8,128)(2,1)S(1)}, bf16[256,128]{1,0:T(8,128)(2,1)S(1)}, u32[]{:S(2)}, u32[]{:S(2)}) collective-permute-start(bf16[256,128]{1,0:T(8,128)(2,1)S(1)} %get-tuple-element.52), channel_id=1, source_target_pairs={{0,20},{4,16},{8,28},{12,24},{16,4},{20,0},{24,12},{28,8},{1,21},{... | collective-permute-start | bytes 196616 | tf_op jit(solution)/shard_map/ppermute | solution.py:301
  32.8 7.0 %collective-permute-start.13 = (bf16[256,128]{1,0:T(8,128)(2,1)S(1)}, bf16[256,128]{1,0:T(8,128)(2,1)S(1)}, u32[]{:S(2)}, u32[]{:S(2)}) collective-permute-start(bf16[256,128]{1,0:T(8,128)(2,1)S(1)} %get-tuple-element.53), channel_id=1, source_target_pairs={{0,28},{4,24},{8,20},{12,16},{16,12},{20,8},{24,4},{28,0},{1,29},{... | collective-permute-start | bytes 196616 | tf_op jit(solution)/shard_map/ppermute | solution.py:301
  40.8 2.0 %collective-permute-start.14 = (bf16[1,256,1024]{2,1,0:T(8,128)(2,1)S(1)}, bf16[1,256,1024]{2,1,0:T(8,128)(2,1)S(1)}, u32[]{:S(2)}, u32[]{:S(2)}) collective-permute-start(bf16[1,256,1024]{2,1,0:T(8,128)(2,1)S(1)} %get-tuple-element.55), channel_id=1, source_target_pairs={{0,1},{1,0},{2,3},{3,2},{4,5},{5,4},{6,7},{7,6},{8,9},{9,8},{10,11... | collective-permute-start | bytes 1572872 | tf_op jit(solution)/shard_map/ppermute | solution.py:386
  42.9 9.3 %collective-permute-start.15 = (bf16[1,256,1024]{2,1,0:T(8,128)(2,1)S(1)}, bf16[1,256,1024]{2,1,0:T(8,128)(2,1)S(1)}, u32[]{:S(2)}, u32[]{:S(2)}) collective-permute-start(bf16[1,256,1024]{2,1,0:T(8,128)(2,1)S(1)} %shard_map.159), channel_id=1, source_target_pairs={{0,1},{1,0},{2,3},{3,2},{4,5},{5,4},{6,7},{7,6},{8,9},{9,8},{10,11... | collective-permute-start | bytes 1572872 | tf_op jit(solution)/shard_map/ppermute | solution.py:386
  43.1 9.1 %collective-permute-start.17 = (bf16[1,256,512]{2,1,0:T(8,128)(2,1)S(1)}, bf16[1,256,512]{2,1,0:T(8,128)(2,1)S(1)}, u32[]{:S(2)}, u32[]{:S(2)}) collective-permute-start(bf16[1,256,512]{2,1,0:T(8,128)(2,1)S(1)} %get-tuple-element.60), channel_id=1, source_target_pairs={{0,2},{1,3},{2,0},{3,1},{4,6},{5,7},{6,4},{7,5},{8,10},{9,11},{10,... | collective-permute-start | bytes 786440 | tf_op jit(solution)/shard_map/ppermute | solution.py:386
  44.7 12.7 %collective-permute-start.16 = (bf16[1,256,512]{2,1,0:T(8,128)(2,1)S(1)}, bf16[1,256,512]{2,1,0:T(8,128)(2,1)S(1)}, u32[]{:S(2)}, u32[]{:S(2)}) collective-permute-start(bf16[1,256,512]{2,1,0:T(8,128)(2,1)S(1)} %get-tuple-element.59), channel_id=1, source_target_pairs={{0,2},{1,3},{2,0},{3,1},{4,6},{5,7},{6,4},{7,5},{8,10},{9,11},{10,... | collective-permute-start | bytes 786440 | tf_op jit(solution)/shard_map/ppermute | solution.py:386

commit v10 on v9

--- a/solution.py
+++ b/solution.py
@@ -88,16 +88,10 @@
     return jnp.where(y < 0.5, y * series, 1.0 - jnp.exp(-y))
 
 
-def filter_kernel(block, blocks_first, relative, out_w_ref, *refs):
-    smalls, (weight_hbm, query_hbm), refs = refs[:7], refs[7:9], refs[9:]
-    (real_ref, imag_ref, edge_ref, weight_out, query_out), refs = refs[:5], refs[5:]
-    near, (w1, w2, hid, filt, near_sem, weight_sem, query_sem) = refs[:7], refs[7:]
-    feat_ref, emb_w_ref, emb_b_ref, mid_w_ref, mid_b_ref, decay_all, table_ref = near
-    fetches = [pltpu.make_async_copy(s, t, near_sem.at[i]) for i, (s, t) in enumerate(zip(smalls, near))]
-    for fetch in fetches:
-        fetch.start()
-    for fetch in fetches[:-1]:
-        fetch.wait()
+def filter_kernel(
+    block, blocks_first, relative, out_w_ref, feat_ref, emb_w_ref, emb_b_ref, mid_w_ref, mid_b_ref, decay_all, table_ref,
+    weight_hbm, query_hbm, real_ref, imag_ref, edge_ref, weight_out, query_out, w1, w2, hid, filt, weight_sem, query_sem,
+):
     copies = weight_copies(blocks_first, weight_hbm, weight_out, weight_sem)
     copies.append(pltpu.make_async_copy(query_hbm, query_out, query_sem.at[0]))
     for copy in copies:
@@ -123,7 +117,6 @@
         start = jnp.exp(-decay * float(m * block))
         filt[(m + 1) * block : (m + 2) * block, :] = (raw[m * block : (m + 1) * block] * (within * start)).astype(BF16)
     first_row = lax.broadcasted_iota(jnp.int32, (16, LANES), 0) == 0
-    fetches[-1].wait()
     group = 2
     for m0 in range(0, blocks, group):
         stacked = jnp.concatenate(
@@ -252,8 +245,9 @@
         copy.wait()
 
 
-def gated_kernel(key_hbm, value_hbm, *refs):
-    *out_refs, key_ref, value_ref, sem = refs
+def gated_kernel(smalls, key_hbm, value_hbm, *refs):
+    small_hbms, (*out_refs, key_ref, value_ref, sem, small_sem) = refs[:smalls], refs[smalls:]
+    out_refs, small_refs = out_refs[:-smalls], out_refs[-smalls:]
     pieces = len(out_refs)
     unit = out_refs[0].shape[1]
     copies = []
@@ -261,12 +255,15 @@
         cols = pl.ds(pl.multiple_of((first_piece(pieces) ^ k) * unit, LANES), unit)
         copies.append(pltpu.make_async_copy(key_hbm.at[:, cols], key_ref.at[k], sem.at[0, k]))
         copies.append(pltpu.make_async_copy(value_hbm.at[:, cols], value_ref.at[k], sem.at[1, k]))
-    for copy in copies:
+    fetches = [pltpu.make_async_copy(s, t, small_sem.at[i]) for i, (s, t) in enumerate(zip(small_hbms, small_refs))]
+    for copy in copies + fetches:
         copy.start()
     for k, out_ref in enumerate(out_refs):
         copies[2 * k].wait()
         copies[2 * k + 1].wait()
         out_ref[...] = (key_ref[k].astype(F32) * value_ref[k].astype(F32)).astype(BF16)
+    for fetch in fetches:
+        fetch.wait()
 
 
 def local(
@@ -301,18 +298,28 @@
             lax.ppermute(arrays[k], "seq", [(d, d ^ k) for d in range(seq_count)]) for k in range(1, seq_count)
         ]
 
-    signal = pl.pallas_call(
-        gated_kernel,
-        out_shape=[jax.ShapeDtypeStruct((rows, unit), BF16)] * pieces,
-        in_specs=[in_hbm] * 2,
-        out_specs=[in_vmem] * pieces,
+    decay = decay_rate.reshape(seq_count, width)
+    if pieces == 1:
+        pad = [(0, 0), (0, LANES - width)]
+        decay = jnp.pad(lax.dynamic_slice_in_dim(decay, seq_index, 1), pad)
+    smalls = (features, emb_weight, emb_bias[None, :], mid_weight, mid_bias[None, :], decay, head_tail)
+    near = pl.pallas_call(
+        functools.partial(gated_kernel, len(smalls)),
+        out_shape=[
+            *[jax.ShapeDtypeStruct((rows, unit), BF16)] * pieces,
+            *[jax.ShapeDtypeStruct(small.shape, small.dtype) for small in smalls],
+        ],
+        in_specs=[in_hbm] * (2 + len(smalls)),
+        out_specs=[in_vmem] * (pieces + len(smalls)),
         scratch_shapes=[
             pltpu.VMEM((pieces, rows, unit), BF16),
             pltpu.VMEM((pieces, rows, unit), BF16),
             pltpu.SemaphoreType.DMA((2, pieces)),
+            pltpu.SemaphoreType.DMA((len(smalls),)),
         ],
         compiler_params=limit,
-    )(far(key_gate), far(value))
+    )(*map(far, (key_gate, value, *smalls)))
+    signal, smalls = near[:pieces], near[pieces:]
     if pieces > 1:
         spread = swap(signal)
     else:
@@ -321,19 +328,13 @@
         spread = list(jnp.pad(in_order, [(0, 0), (0, 0), (0, LANES - width)]))
 
     my_filter = lax.dynamic_slice_in_dim(out_filter, seq_index * width, width, 1)
-    decay = decay_rate.reshape(seq_count, width)
     if pieces == 1:
-        pad = [(0, 0), (0, LANES - width)]
         my_filter = jnp.pad(my_filter, pad)
-        decay = jnp.pad(lax.dynamic_slice_in_dim(decay, seq_index, 1), pad)
     out_width = out_weight.shape[1] // chan_count
     quarter = chan_count // 4
     odd = range(1, chan_count, 2)
     far_odd, near_odd = [j for j in odd if j & 2], [j for j in odd if not j & 2]
     blocks_first, blocks_next, blocks_last = far_odd + [j ^ 1 for j in far_odd], near_odd, [j ^ 1 for j in near_odd]
-    smalls = (
-        features, emb_weight, emb_bias[None, :], mid_weight, mid_bias[None, :], decay, head_tail,
-    )
     real, imag, edge, weights_first, query_near = pl.pallas_call(
         functools.partial(filter_kernel, block, blocks_first, pieces > 1),
         out_shape=(
@@ -343,20 +344,18 @@
             jax.ShapeDtypeStruct((2 * quarter, chan_width, out_width), BF16),
             jax.ShapeDtypeStruct(query.shape, BF16),
         ),
-        in_specs=[in_vmem] + [in_hbm] * 9,
+        in_specs=[in_vmem] * 8 + [in_hbm] * 2,
         out_specs=[in_vmem] * 5,
         scratch_shapes=[
-            *[pltpu.VMEM(small.shape, small.dtype) for small in smalls],
             pltpu.VMEM((feat_rows, order), F32),
             pltpu.VMEM((order + 8, order), F32),
             pltpu.VMEM((order + 8, length), F32),
             pltpu.VMEM((length + block, LANES), BF16),
-            pltpu.SemaphoreType.DMA((len(smalls),)),
             pltpu.SemaphoreType.DMA((2 * quarter,)),
             pltpu.SemaphoreType.DMA((1,)),
         ],
         compiler_params=limit,
-    )(my_filter, *map(far, (*smalls, out_weight, query)))
+    )(my_filter, *smalls, far(out_weight), far(query))
 
     *convolved, weights_next = pl.pallas_call(
         functools.partial(conv_kernel, block, blocks_next, arrival, pieces > 1),

time: 58.5 us -> 59.3 us (1.014)
  Pallas kernels: 15.6 us -> 16.4 us
where the time goes in v10:
time: 59.3 us; the launch traced here: 59.2 us
  starting transfers between devices  26.8 us (45%)
  Pallas kernels  16.4 us (28%)
  waiting for transfers between devices  15.5 us (26%)
    ppermute x14, starting transfers between devices, swap(): lax.ppermute(arrays[k], 'seq', [(d, d ^ k) for d in range(seq_count)])  24.5 us
    ppermute x4, waiting for transfers between devices, exchange(): lax.ppermute(terms, 'chan', [(d, d ^ bit) for d in range(chan_count)])  9.36 us
    ppermute x14, waiting for transfers between devices, swap(): lax.ppermute(arrays[k], 'seq', [(d, d ^ k) for d in range(seq_count)])  6.15 us
    pallas_call x1, Pallas kernels, local(): pl.pallas_call(functools.partial(filter_kernel, block, blocks_first, piec...  5.05 us
    pallas_call x1, Pallas kernels, local(): pl.pallas_call(functools.partial(conv_kernel, block, blocks_next, arrival...  2.85 us
    ppermute x4, starting transfers between devices, exchange(): lax.ppermute(terms, 'chan', [(d, d ^ bit) for d in range(chan_count)])  2.31 us
    pallas_call x1, Pallas kernels, local(): pl.pallas_call(functools.partial(last_kernel, blocks_last), out_shape=jax...  2.31 us
    pallas_call x2, Pallas kernels, local(): pl.pallas_call(functools.partial(finish_kernel, span, len(terms)), out_sh...  1.87 us
  transfers between devices with their start and end apart: 18, of which 6 were waited for; matrix products, arithmetic and copies ran while one was open for 0% of the time, Pallas kernels for 16%

profile of v10, /device:TPU:0, one launch (start us, length us, event | category | flops | bytes accessed | tf_op | source)
XLA Modules:
  0.0 59.2 jit_solution(17144738534403439147)
XLA Ops:
  0.0 1.9 %shard_map.154 = (bf16[256,128]{1,0:T(8,128)(2,1)S(1)}, bf16[256,128]{1,0:T(8,128)(2,1)S(1)}, bf16[256,128]{1,0:T(8,128)(2,1)S(1)}, bf16[256,128]{1,0:T(8,128)(2...) custom-call(bf16[256,1024]{1,0:T(8,128)(2,1)} %key_hbm.1, ...), custom_call_target="tpu_custom_call" | custom-call | tf_op jit(solution)/shard_map/pallas_call | solution.py:306
  1.9 3.1 %collective-permute-start = (bf16[256,128]{1,0:T(8,128)(2,1)S(1)}, bf16[256,128]{1,0:T(8,128)(2,1)S(1)}, u32[]{:S(2)}, u32[]{:S(2)}) collective-permute-start(bf16[256,128]{1,0:T(8,128)(2,1)S(1)} %get-tuple-element.53.refs_9_), channel_id=1, source_target_pairs={{0,8},{4,12},{8,0},{12,4},{16,24},{20,28},{24,16},{28,20},{1,9},{5... | collective-permute-start | bytes 196616 | tf_op jit(solution)/shard_map/ppermute | solution.py:298
  5.0 2.6 %collective-permute-start.1 = (bf16[256,128]{1,0:T(8,128)(2,1)S(1)}, bf16[256,128]{1,0:T(8,128)(2,1)S(1)}, u32[]{:S(2)}, u32[]{:S(2)}) collective-permute-start(bf16[256,128]{1,0:T(8,128)(2,1)S(1)} %get-tuple-element.54.refs_10_), channel_id=1, source_target_pairs={{0,16},{4,20},{8,24},{12,28},{16,0},{20,4},{24,8},{28,12},{1,17},{... | collective-permute-start | bytes 196616 | tf_op jit(solution)/shard_map/ppermute | solution.py:298
  7.6 1.7 %collective-permute-start.3 = (bf16[256,128]{1,0:T(8,128)(2,1)S(1)}, bf16[256,128]{1,0:T(8,128)(2,1)S(1)}, u32[]{:S(2)}, u32[]{:S(2)}) collective-permute-start(bf16[256,128]{1,0:T(8,128)(2,1)S(1)} %get-tuple-element.56.refs_12_), channel_id=1, source_target_pairs={{0,4},{4,0},{8,12},{12,8},{16,20},{20,16},{24,28},{28,24},{1,5},{5... | collective-permute-start | bytes 196616 | tf_op jit(solution)/shard_map/ppermute | solution.py:298
  9.9 4.4 %collective-permute-start.5 = (bf16[256,128]{1,0:T(8,128)(2,1)S(1)}, bf16[256,128]{1,0:T(8,128)(2,1)S(1)}, u32[]{:S(2)}, u32[]{:S(2)}) collective-permute-start(bf16[256,128]{1,0:T(8,128)(2,1)S(1)} %get-tuple-element.58.refs_14_), channel_id=1, source_target_pairs={{0,20},{4,16},{8,28},{12,24},{16,4},{20,0},{24,12},{28,8},{1,21},{... | collective-permute-start | bytes 196616 | tf_op jit(solution)/shard_map/ppermute | solution.py:298
  14.3 2.4 %collective-permute-start.6 = (bf16[256,128]{1,0:T(8,128)(2,1)S(1)}, bf16[256,128]{1,0:T(8,128)(2,1)S(1)}, u32[]{:S(2)}, u32[]{:S(2)}) collective-permute-start(bf16[256,128]{1,0:T(8,128)(2,1)S(1)} %get-tuple-element.59.refs_15_), channel_id=1, source_target_pairs={{0,28},{4,24},{8,20},{12,16},{16,12},{20,8},{24,4},{28,0},{1,29},{... | collective-permute-start | bytes 196616 | tf_op jit(solution)/shard_map/ppermute | solution.py:298
  16.8 5.1 %shard_map.155 = (f32[8,256,128]{2,1,0:T(8,128)S(1)}, f32[8,256,128]{2,1,0:T(8,128)S(1)}, f32[8,16,128]{2,1,0:T(8,128)S(1)}, bf16[2,1024,1024]{2,1,0:T(8,128)(2,1)S(1)}, bf16[256,1024]{1,0:T(8,128)(2,1)S(1)}) custom-call(f32[64,128]{1,0:T(8,128)S(1)} %constant_dynamic-slice_fusion.out_w_ref, f32[40,2048]{1,0:T(8,128)S(1)} %get-tuple-element.40.feat_ref, ...), custom_call_target="tpu_custom_call" | custom-call | tf_op jit(solution)/shard_map/pallas_call | solution.py:338
  21.9 2.8 %shard_map.156 = (bf16[256,128]{1,0:T(8,128)(2,1)S(1)}, bf16[256,128]{1,0:T(8,128)(2,1)S(1)}, bf16[256,128]{1,0:T(8,128)(2,1)S(1)}, bf16[256,128]{1,0:T(8,128)(2...) custom-call(s32[16]{0:T(128)S(1)} %copy-done.4, ...), custom_call_target="tpu_custom_call" | custom-call | tf_op jit(solution)/shard_map/pallas_call | solution.py:360
  24.8 2.0 %collective-permute-start.8 = (bf16[256,128]{1,0:T(8,128)(2,1)S(1)}, bf16[256,128]{1,0:T(8,128)(2,1)S(1)}, u32[]{:S(2)}, u32[]{:S(2)}) collective-permute-start(bf16[256,128]{1,0:T(8,128)(2,1)S(1)} %get-tuple-element.62), channel_id=1, source_target_pairs={{0,16},{4,20},{8,24},{12,28},{16,0},{20,4},{24,8},{28,12},{1,17},{... | collective-permute-start | bytes 196616 | tf_op jit(solution)/shard_map/ppermute | solution.py:298
  26.8 2.4 %collective-permute-start.9 = (bf16[256,128]{1,0:T(8,128)(2,1)S(1)}, bf16[256,128]{1,0:T(8,128)(2,1)S(1)}, u32[]{:S(2)}, u32[]{:S(2)}) collective-permute-start(bf16[256,128]{1,0:T(8,128)(2,1)S(1)} %get-tuple-element.63), channel_id=1, source_target_pairs={{0,24},{4,28},{8,16},{12,20},{16,8},{20,12},{24,0},{28,4},{1,25},{... | collective-permute-start | bytes 196616 | tf_op jit(solution)/shard_map/ppermute | solution.py:298
  29.9 1.5 %collective-permute-done.7.refs_1_ = bf16[256,128]{1,0:T(8,128)(2,1)S(1)} collective-permute-done((bf16[256,128]{1,0:T(8,128)(2,1)S(1)}, bf16[256,128]{1,0:T(8,128)(2,1)S(1)}, u32[]{:S(2)}, u32[]{:S(2)}) %collective-permute-start.7) | collective-permute-done | bytes 65568 | tf_op jit(solution)/shard_map/ppermute | solution.py:298
  31.4 2.2 %collective-permute-start.12 = (bf16[256,128]{1,0:T(8,128)(2,1)S(1)}, bf16[256,128]{1,0:T(8,128)(2,1)S(1)}, u32[]{:S(2)}, u32[]{:S(2)}) collective-permute-start(bf16[256,128]{1,0:T(8,128)(2,1)S(1)} %get-tuple-element.66), channel_id=1, source_target_pairs={{0,20},{4,16},{8,28},{12,24},{16,4},{20,0},{24,12},{28,8},{1,21},{... | collective-permute-start | bytes 196616 | tf_op jit(solution)/shard_map/ppermute | solution.py:298
  33.6 2.3 %collective-permute-start.13 = (bf16[256,128]{1,0:T(8,128)(2,1)S(1)}, bf16[256,128]{1,0:T(8,128)(2,1)S(1)}, u32[]{:S(2)}, u32[]{:S(2)}) collective-permute-start(bf16[256,128]{1,0:T(8,128)(2,1)S(1)} %get-tuple-element.67), channel_id=1, source_target_pairs={{0,28},{4,24},{8,20},{12,16},{16,12},{20,8},{24,4},{28,0},{1,29},{... | collective-permute-start | bytes 196616 | tf_op jit(solution)/shard_map/ppermute | solution.py:298
  36.0 1.5 %collective-permute-done.12.refs_6_ = bf16[256,128]{1,0:T(8,128)(2,1)S(1)} collective-permute-done((bf16[256,128]{1,0:T(8,128)(2,1)S(1)}, bf16[256,128]{1,0:T(8,128)(2,1)S(1)}, u32[]{:S(2)}, u32[]{:S(2)}) %collective-permute-start.12) | collective-permute-done | bytes 65568 | tf_op jit(solution)/shard_map/ppermute | solution.py:298
  37.4 3.1 %collective-permute-done.13.refs_7_ = bf16[256,128]{1,0:T(8,128)(2,1)S(1)} collective-permute-done((bf16[256,128]{1,0:T(8,128)(2,1)S(1)}, bf16[256,128]{1,0:T(8,128)(2,1)S(1)}, u32[]{:S(2)}, u32[]{:S(2)}) %collective-permute-start.13) | collective-permute-done | bytes 65568 | tf_op jit(solution)/shard_map/ppermute | solution.py:298
  40.6 1.0 %shard_map.157 = (bf16[1,256,1024]{2,1,0:T(8,128)(2,1)S(1)}, bf16[256,1024]{1,0:T(8,128)(2,1)S(1)}) custom-call(bf16[256,1024]{1,0:T(8,128)(2,1)S(1)} %get-tuple-element.47.query_ref, f32[1,1024]{1,0:T(1,128)S(1)} %bitcast.14, bf16[2,1024,1024]{2,1,0:T(8,128)(2,1)S(1)} %get-tuple-element.48.weight_ref, bf16[256,128]{1,0:T(8,128)(2,1)S(1)} %get-tuple-element.60.refs_0_, ...), custom_call_target="tpu_custom_call" | custom-call | tf_op jit(solution)/shard_map/pallas_call | solution.py:387
  41.7 0.7 %shard_map.158 = f32[1,256,1024]{2,1,0:T(8,128)S(1)} custom-call(bf16[256,1024]{1,0:T(8,128)(2,1)S(1)} %get-tuple-element.71.mixed_ref, bf16[2,1024,1024]{2,1,0:T(8,128)(2,1)S(1)} %get-tuple-element.48.weight_ref), custom_call_target="tpu_custom_call" | custom-call | tf_op jit(solution)/shard_map/pallas_call | solution.py:400
  42.4 0.7 %shard_map.159 = bf16[1,256,1024]{2,1,0:T(8,128)(2,1)S(1)} custom-call(bf16[256,1024]{1,0:T(8,128)(2,1)S(1)} %get-tuple-element.71.mixed_ref, bf16[1,1024,1024]{2,1,0:T(8,128)(2,1)S(1)} %get-tuple-element.70.weight_ref), custom_call_target="tpu_custom_call" | custom-call | tf_op jit(solution)/shard_map/pallas_call | solution.py:400
  44.0 1.5 %collective-permute-start.17 = (bf16[1,256,512]{2,1,0:T(8,128)(2,1)S(1)}, bf16[1,256,512]{2,1,0:T(8,128)(2,1)S(1)}, u32[]{:S(2)}, u32[]{:S(2)}) collective-permute-start(bf16[1,256,512]{2,1,0:T(8,128)(2,1)S(1)} %get-tuple-element.74), channel_id=1, source_target_pairs={{0,2},{1,3},{2,0},{3,1},{4,6},{5,7},{6,4},{7,5},{8,10},{9,11},{10,... | collective-permute-start | bytes 786440 | tf_op jit(solution)/shard_map/ppermute | solution.py:385
  46.1 2.3 %shard_map.160 = f32[1,256,1024]{2,1,0:T(8,128)S(1)} custom-call(bf16[256,1024]{1,0:T(8,128)(2,1)S(1)} %get-tuple-element.71.mixed_ref, bf16[1024,4096]{1,0:T(8,128)(2,1)} %weight_hbm.5), custom_call_target="tpu_custom_call" | custom-call | tf_op jit(solution)/shard_map/pallas_call | solution.py:414
  48.4 4.8 %collective-permute-done.17 = bf16[1,256,512]{2,1,0:T(8,128)(2,1)S(1)} collective-permute-done((bf16[1,256,512]{2,1,0:T(8,128)(2,1)S(1)}, bf16[1,256,512]{2,1,0:T(8,128)(2,1)S(1)}, u32[]{:S(2)}, u32[]{:S(2)}) %collective-permute-start.17) | collective-permute-done | bytes 262176 | tf_op jit(solution)/shard_map/ppermute | solution.py:385
  53.2 0.9 %shard_map.161.refs_3_ = f32[1024,256]{1,0:T(8,128)} custom-call(f32[256,1024]{1,0:T(8,128)S(1)} %bitcast.8, bf16[256,1024]{1,0:T(8,128)(2,1)S(1)} %bitcast.10, bf16[256,512]{1,0:T(8,128)(2,1)S(1)} %bitcast.12), custom_call_target="tpu_custom_call" | custom-call | tf_op jit(solution)/shard_map/pallas_call | solution.py:435
  54.1 4.1 %collective-permute-done.16 = bf16[1,256,512]{2,1,0:T(8,128)(2,1)S(1)} collective-permute-done((bf16[1,256,512]{2,1,0:T(8,128)(2,1)S(1)}, bf16[1,256,512]{2,1,0:T(8,128)(2,1)S(1)}, u32[]{:S(2)}, u32[]{:S(2)}) %collective-permute-start.16) | collective-permute-done | bytes 262176 | tf_op jit(solution)/shard_map/ppermute | solution.py:385
  58.2 0.9 %shard_map.162 = f32[1024,256]{1,0:T(8,128)} custom-call(f32[256,1024]{1,0:T(8,128)S(1)} %bitcast.9, bf16[256,1024]{1,0:T(8,128)(2,1)S(1)} %bitcast.11, bf16[256,512]{1,0:T(8,128)(2,1)S(1)} %bitcast.13, f32[1024,256]{1,0:T(8,128)} %shard_map.161.refs_3_), custom_call_target="tpu_custom_call", output_to_operand_aliasing={{}: (3, {})} | custom-call | tf_op jit(solution)/shard_map/pallas_call | solution.py:435
  (33 shorter events, 2.9 us)
Async XLA Ops:
  0.0 16.7 %copy-start = (f32[64,1024]{1,0:T(8,128)S(1)}, f32[64,1024]{1,0:T(8,128)}, u32[]{:S(2)}) copy-start(f32[64,1024]{1,0:T(8,128)} %param.24) | copy-start | bytes 786436
  1.9 8.0 %collective-permute-start = (bf16[256,128]{1,0:T(8,128)(2,1)S(1)}, bf16[256,128]{1,0:T(8,128)(2,1)S(1)}, u32[]{:S(2)}, u32[]{:S(2)}) collective-permute-start(bf16[256,128]{1,0:T(8,128)(2,1)S(1)} %get-tuple-element.53.refs_9_), channel_id=1, source_target_pairs={{0,8},{4,12},{8,0},{12,4},{16,24},{20,28},{24,16},{28,20},{1,9},{5... | collective-permute-start | bytes 196616 | tf_op jit(solution)/shard_map/ppermute | solution.py:298
  5.0 9.4 %collective-permute-start.1 = (bf16[256,128]{1,0:T(8,128)(2,1)S(1)}, bf16[256,128]{1,0:T(8,128)(2,1)S(1)}, u32[]{:S(2)}, u32[]{:S(2)}) collective-permute-start(bf16[256,128]{1,0:T(8,128)(2,1)S(1)} %get-tuple-element.54.refs_10_), channel_id=1, source_target_pairs={{0,16},{4,20},{8,24},{12,28},{16,0},{20,4},{24,8},{28,12},{1,17},{... | collective-permute-start | bytes 196616 | tf_op jit(solution)/shard_map/ppermute | solution.py:298
  7.6 14.3 %collective-permute-start.2 = (bf16[256,128]{1,0:T(8,128)(2,1)S(1)}, bf16[256,128]{1,0:T(8,128)(2,1)S(1)}, u32[]{:S(2)}, u32[]{:S(2)}) collective-permute-start(bf16[256,128]{1,0:T(8,128)(2,1)S(1)} %get-tuple-element.55.refs_11_), channel_id=1, source_target_pairs={{0,24},{4,28},{8,16},{12,20},{16,8},{20,12},{24,0},{28,4},{1,25},{... | collective-permute-start | bytes 196616 | tf_op jit(solution)/shard_map/ppermute | solution.py:298
  7.6 14.3 %collective-permute-start.3 = (bf16[256,128]{1,0:T(8,128)(2,1)S(1)}, bf16[256,128]{1,0:T(8,128)(2,1)S(1)}, u32[]{:S(2)}, u32[]{:S(2)}) collective-permute-start(bf16[256,128]{1,0:T(8,128)(2,1)S(1)} %get-tuple-element.56.refs_12_), channel_id=1, source_target_pairs={{0,4},{4,0},{8,12},{12,8},{16,20},{20,16},{24,28},{28,24},{1,5},{5... | collective-permute-start | bytes 196616 | tf_op jit(solution)/shard_map/ppermute | solution.py:298
  9.3 12.6 %collective-permute-start.4 = (bf16[256,128]{1,0:T(8,128)(2,1)S(1)}, bf16[256,128]{1,0:T(8,128)(2,1)S(1)}, u32[]{:S(2)}, u32[]{:S(2)}) collective-permute-start(bf16[256,128]{1,0:T(8,128)(2,1)S(1)} %get-tuple-element.57.refs_13_), channel_id=1, source_target_pairs={{0,12},{4,8},{8,4},{12,0},{16,28},{20,24},{24,20},{28,16},{1,13},{... | collective-permute-start | bytes 196616 | tf_op jit(solution)/shard_map/ppermute | solution.py:298
  9.9 11.9 %collective-permute-start.5 = (bf16[256,128]{1,0:T(8,128)(2,1)S(1)}, bf16[256,128]{1,0:T(8,128)(2,1)S(1)}, u32[]{:S(2)}, u32[]{:S(2)}) collective-permute-start(bf16[256,128]{1,0:T(8,128)(2,1)S(1)} %get-tuple-element.58.refs_14_), channel_id=1, source_target_pairs={{0,20},{4,16},{8,28},{12,24},{16,4},{20,0},{24,12},{28,8},{1,21},{... | collective-permute-start | bytes 196616 | tf_op jit(solution)/shard_map/ppermute | solution.py:298
  14.3 7.5 %collective-permute-start.6 = (bf16[256,128]{1,0:T(8,128)(2,1)S(1)}, bf16[256,128]{1,0:T(8,128)(2,1)S(1)}, u32[]{:S(2)}, u32[]{:S(2)}) collective-permute-start(bf16[256,128]{1,0:T(8,128)(2,1)S(1)} %get-tuple-element.59.refs_15_), channel_id=1, source_target_pairs={{0,28},{4,24},{8,20},{12,16},{16,12},{20,8},{24,4},{28,0},{1,29},{... | collective-permute-start | bytes 196616 | tf_op jit(solution)/shard_map/ppermute | solution.py:298
  16.7 5.2 %copy-start.1 = (bf16[256,512]{1,0:T(8,128)(2,1)S(1)}, bf16[256,512]{1,0:T(8,128)(2,1)}, u32[]{:S(2)}) copy-start(bf16[256,512]{1,0:T(8,128)(2,1)} %constant.26.inverse_ref) | copy-start | bytes 786436
  16.7 5.2 %copy-start.2 = (bf16[512,256]{1,0:T(8,128)(2,1)S(1)}, bf16[512,256]{1,0:T(8,128)(2,1)}, u32[]{:S(2)}) copy-start(bf16[512,256]{1,0:T(8,128)(2,1)} %constant.25.table_ref) | copy-start | bytes 786436
  16.7 5.1 %copy-start.4 = (s32[16]{0:T(128)S(1)}, s32[16]{0:T(128)}, u32[]{:S(2)}) copy-start(s32[16]{0:T(128)} %order_ref.1) | copy-start | bytes 196
  21.9 18.7 %copy-start.3 = (f32[1024]{0:T(1024)S(1)}, f32[1024]{0:T(1024)}, u32[]{:S(2)}) copy-start(f32[1024]{0:T(1024)} %param.26) | copy-start | bytes 12292
  24.8 6.6 %collective-permute-start.7 = (bf16[256,128]{1,0:T(8,128)(2,1)S(1)}, bf16[256,128]{1,0:T(8,128)(2,1)S(1)}, u32[]{:S(2)}, u32[]{:S(2)}) collective-permute-start(bf16[256,128]{1,0:T(8,128)(2,1)S(1)} %get-tuple-element.61), channel_id=1, source_target_pairs={{0,8},{4,12},{8,0},{12,4},{16,24},{20,28},{24,16},{28,20},{1,9},{5... | collective-permute-start | bytes 196616 | tf_op jit(solution)/shard_map/ppermute | solution.py:298
  24.8 8.8 %collective-permute-start.8 = (bf16[256,128]{1,0:T(8,128)(2,1)S(1)}, bf16[256,128]{1,0:T(8,128)(2,1)S(1)}, u32[]{:S(2)}, u32[]{:S(2)}) collective-permute-start(bf16[256,128]{1,0:T(8,128)(2,1)S(1)} %get-tuple-element.62), channel_id=1, source_target_pairs={{0,16},{4,20},{8,24},{12,28},{16,0},{20,4},{24,8},{28,12},{1,17},{... | collective-permute-start | bytes 196616 | tf_op jit(solution)/shard_map/ppermute | solution.py:298
  26.8 9.2 %collective-permute-start.9 = (bf16[256,128]{1,0:T(8,128)(2,1)S(1)}, bf16[256,128]{1,0:T(8,128)(2,1)S(1)}, u32[]{:S(2)}, u32[]{:S(2)}) collective-permute-start(bf16[256,128]{1,0:T(8,128)(2,1)S(1)} %get-tuple-element.63), channel_id=1, source_target_pairs={{0,24},{4,28},{8,16},{12,20},{16,8},{20,12},{24,0},{28,4},{1,25},{... | collective-permute-start | bytes 196616 | tf_op jit(solution)/shard_map/ppermute | solution.py:298
  29.2 6.8 %collective-permute-start.10 = (bf16[256,128]{1,0:T(8,128)(2,1)S(1)}, bf16[256,128]{1,0:T(8,128)(2,1)S(1)}, u32[]{:S(2)}, u32[]{:S(2)}) collective-permute-start(bf16[256,128]{1,0:T(8,128)(2,1)S(1)} %get-tuple-element.64), channel_id=1, source_target_pairs={{0,4},{4,0},{8,12},{12,8},{16,20},{20,16},{24,28},{28,24},{1,5},{5... | collective-permute-start | bytes 196616 | tf_op jit(solution)/shard_map/ppermute | solution.py:298
  29.6 6.4 %collective-permute-start.11 = (bf16[256,128]{1,0:T(8,128)(2,1)S(1)}, bf16[256,128]{1,0:T(8,128)(2,1)S(1)}, u32[]{:S(2)}, u32[]{:S(2)}) collective-permute-start(bf16[256,128]{1,0:T(8,128)(2,1)S(1)} %get-tuple-element.65), channel_id=1, source_target_pairs={{0,12},{4,8},{8,4},{12,0},{16,28},{20,24},{24,20},{28,16},{1,13},{... | collective-permute-start | bytes 196616 | tf_op jit(solution)/shard_map/ppermute | solution.py:298
  31.4 6.1 %collective-permute-start.12 = (bf16[256,128]{1,0:T(8,128)(2,1)S(1)}, bf16[256,128]{1,0:T(8,128)(2,1)S(1)}, u32[]{:S(2)}, u32[]{:S(2)}) collective-permute-start(bf16[256,128]{1,0:T(8,128)(2,1)S(1)} %get-tuple-element.66), channel_id=1, source_target_pairs={{0,20},{4,16},{8,28},{12,24},{16,4},{20,0},{24,12},{28,8},{1,21},{... | collective-permute-start | bytes 196616 | tf_op jit(solution)/shard_map/ppermute | solution.py:298
  33.6 7.0 %collective-permute-start.13 = (bf16[256,128]{1,0:T(8,128)(2,1)S(1)}, bf16[256,128]{1,0:T(8,128)(2,1)S(1)}, u32[]{:S(2)}, u32[]{:S(2)}) collective-permute-start(bf16[256,128]{1,0:T(8,128)(2,1)S(1)} %get-tuple-element.67), channel_id=1, source_target_pairs={{0,28},{4,24},{8,20},{12,16},{16,12},{20,8},{24,4},{28,0},{1,29},{... | collective-permute-start | bytes 196616 | tf_op jit(solution)/shard_map/ppermute | solution.py:298
  41.6 2.0 %collective-permute-start.14 = (bf16[1,256,1024]{2,1,0:T(8,128)(2,1)S(1)}, bf16[1,256,1024]{2,1,0:T(8,128)(2,1)S(1)}, u32[]{:S(2)}, u32[]{:S(2)}) collective-permute-start(bf16[1,256,1024]{2,1,0:T(8,128)(2,1)S(1)} %get-tuple-element.69), channel_id=1, source_target_pairs={{0,1},{1,0},{2,3},{3,2},{4,5},{5,4},{6,7},{7,6},{8,9},{9,8},{10,11... | collective-permute-start | bytes 1572872 | tf_op jit(solution)/shard_map/ppermute | solution.py:385
  43.8 9.3 %collective-permute-start.15 = (bf16[1,256,1024]{2,1,0:T(8,128)(2,1)S(1)}, bf16[1,256,1024]{2,1,0:T(8,128)(2,1)S(1)}, u32[]{:S(2)}, u32[]{:S(2)}) collective-permute-start(bf16[1,256,1024]{2,1,0:T(8,128)(2,1)S(1)} %shard_map.159), channel_id=1, source_target_pairs={{0,1},{1,0},{2,3},{3,2},{4,5},{5,4},{6,7},{7,6},{8,9},{9,8},{10,11... | collective-permute-start | bytes 1572872 | tf_op jit(solution)/shard_map/ppermute | solution.py:385
  44.0 9.1 %collective-permute-start.17 = (bf16[1,256,512]{2,1,0:T(8,128)(2,1)S(1)}, bf16[1,256,512]{2,1,0:T(8,128)(2,1)S(1)}, u32[]{:S(2)}, u32[]{:S(2)}) collective-permute-start(bf16[1,256,512]{2,1,0:T(8,128)(2,1)S(1)} %get-tuple-element.74), channel_id=1, source_target_pairs={{0,2},{1,3},{2,0},{3,1},{4,6},{5,7},{6,4},{7,5},{8,10},{9,11},{10,... | collective-permute-start | bytes 786440 | tf_op jit(solution)/shard_map/ppermute | solution.py:385
  45.5 12.7 %collective-permute-start.16 = (bf16[1,256,512]{2,1,0:T(8,128)(2,1)S(1)}, bf16[1,256,512]{2,1,0:T(8,128)(2,1)S(1)}, u32[]{:S(2)}, u32[]{:S(2)}) collective-permute-start(bf16[1,256,512]{2,1,0:T(8,128)(2,1)S(1)} %get-tuple-element.73), channel_id=1, source_target_pairs={{0,2},{1,3},{2,0},{3,1},{4,6},{5,7},{6,4},{7,5},{8,10},{9,11},{10,... | collective-permute-start | bytes 786440 | tf_op jit(solution)/shard_map/ppermute | solution.py:385

commit v11 on v9

--- a/solution.py
+++ b/solution.py
@@ -89,9 +89,9 @@
 
 
 def filter_kernel(block, blocks_first, relative, out_w_ref, *refs):
-    smalls, (weight_hbm, query_hbm), refs = refs[:7], refs[7:9], refs[9:]
-    (real_ref, imag_ref, edge_ref, weight_out, query_out), refs = refs[:5], refs[5:]
-    near, (w1, w2, hid, filt, near_sem, weight_sem, query_sem) = refs[:7], refs[7:]
+    smalls, weight_hbm, refs = refs[:7], refs[7], refs[8:]
+    (real_ref, imag_ref, edge_ref, weight_out), refs = refs[:4], refs[4:]
+    near, (w1, w2, hid, filt, near_sem, weight_sem) = refs[:7], refs[7:]
     feat_ref, emb_w_ref, emb_b_ref, mid_w_ref, mid_b_ref, decay_all, table_ref = near
     fetches = [pltpu.make_async_copy(s, t, near_sem.at[i]) for i, (s, t) in enumerate(zip(smalls, near))]
     for fetch in fetches:
@@ -99,7 +99,6 @@
     for fetch in fetches[:-1]:
         fetch.wait()
     copies = weight_copies(blocks_first, weight_hbm, weight_out, weight_sem)
-    copies.append(pltpu.make_async_copy(query_hbm, query_out, query_sem.at[0]))
     for copy in copies:
         copy.start()
     emb, order = emb_w_ref.shape
@@ -209,6 +208,15 @@
         copy.wait()
 
 
+def copy_kernel(blocks_next, after_ref, weight_hbm, query_hbm, weight_out, query_out, weight_sem, query_sem):
+    copies = weight_copies(blocks_next, weight_hbm, weight_out, weight_sem)
+    copies.append(pltpu.make_async_copy(query_hbm, query_out, query_sem.at[0]))
+    for copy in copies:
+        copy.start()
+    for copy in copies:
+        copy.wait()
+
+
 def mix_kernel(arrival, query_ref, gain_ref, weight_ref, *refs):
     *refs, out_ref, mixed_ref = refs
     pieces = len(refs) // 2
@@ -330,21 +338,20 @@
     quarter = chan_count // 4
     odd = range(1, chan_count, 2)
     far_odd, near_odd = [j for j in odd if j & 2], [j for j in odd if not j & 2]
-    blocks_first, blocks_next, blocks_last = far_odd + [j ^ 1 for j in far_odd], near_odd, [j ^ 1 for j in near_odd]
+    blocks_kept, blocks_last = [j ^ 1 for j in far_odd], [j ^ 1 for j in near_odd]
     smalls = (
         features, emb_weight, emb_bias[None, :], mid_weight, mid_bias[None, :], decay, head_tail,
     )
-    real, imag, edge, weights_first, query_near = pl.pallas_call(
-        functools.partial(filter_kernel, block, blocks_first, pieces > 1),
+    real, imag, edge, weights_away = pl.pallas_call(
+        functools.partial(filter_kernel, block, far_odd, pieces > 1),
         out_shape=(
             jax.ShapeDtypeStruct((blocks, block, LANES), F32),
             jax.ShapeDtypeStruct((blocks, block, LANES), F32),
             jax.ShapeDtypeStruct((blocks, 16, LANES), F32),
-            jax.ShapeDtypeStruct((2 * quarter, chan_width, out_width), BF16),
-            jax.ShapeDtypeStruct(query.shape, BF16),
+            jax.ShapeDtypeStruct((quarter, chan_width, out_width), BF16),
         ),
-        in_specs=[in_vmem] + [in_hbm] * 9,
-        out_specs=[in_vmem] * 5,
+        in_specs=[in_vmem] + [in_hbm] * 8,
+        out_specs=[in_vmem] * 4,
         scratch_shapes=[
             *[pltpu.VMEM(small.shape, small.dtype) for small in smalls],
             pltpu.VMEM((feat_rows, order), F32),
@@ -352,14 +359,13 @@
             pltpu.VMEM((order + 8, length), F32),
             pltpu.VMEM((length + block, LANES), BF16),
             pltpu.SemaphoreType.DMA((len(smalls),)),
-            pltpu.SemaphoreType.DMA((2 * quarter,)),
-            pltpu.SemaphoreType.DMA((1,)),
+            pltpu.SemaphoreType.DMA((quarter,)),
         ],
         compiler_params=limit,
-    )(my_filter, *map(far, (*smalls, out_weight, query)))
-
-    *convolved, weights_next = pl.pallas_call(
-        functools.partial(conv_kernel, block, blocks_next, arrival, pieces > 1),
+    )(my_filter, *map(far, (*smalls, out_weight)))
+
+    *convolved, weights_kept = pl.pallas_call(
+        functools.partial(conv_kernel, block, blocks_kept, arrival, pieces > 1),
         out_shape=[
             *[jax.ShapeDtypeStruct((rows, LANES), BF16)] * seq_count,
             jax.ShapeDtypeStruct((quarter, chan_width, out_width), BF16),
@@ -376,6 +382,17 @@
         ],
         compiler_params=limit,
     )(group_order, real, imag, edge, head, inverse, far(out_weight), *[spread[k] for k in arrival])
+    weights_next, query_near = pl.pallas_call(
+        functools.partial(copy_kernel, near_odd),
+        out_shape=(
+            jax.ShapeDtypeStruct((quarter, chan_width, out_width), BF16),
+            jax.ShapeDtypeStruct(query.shape, BF16),
+        ),
+        in_specs=[in_vmem] + [in_hbm] * 2,
+        out_specs=[in_vmem] * 2,
+        scratch_shapes=[pltpu.SemaphoreType.DMA((quarter,)), pltpu.SemaphoreType.DMA((1,))],
+        compiler_params=limit,
+    )(convolved[0], far(out_weight), far(query))
     if pieces > 1:
         backs = swap(convolved)
     else:
@@ -394,7 +411,7 @@
         in_specs=[in_vmem] * (3 + 2 * pieces),
         out_specs=[in_vmem] * 2,
         compiler_params=limit,
-    )(query_near, skip_gain[None, :], weights_first, *[array[k] for array in (backs, signal) for k in (arrival if pieces > 1 else [0])])
+    )(query_near, skip_gain[None, :], weights_away, *[array[k] for array in (backs, signal) for k in (arrival if pieces > 1 else [0])])
     far_terms = exchange(far_away, 1)
 
     def products(first, weights, dtype):
@@ -406,7 +423,7 @@
             compiler_params=limit,
         )(mixed, weights)
 
-    far_kept, near_away = products(quarter, weights_first, F32), products(0, weights_next, BF16)
+    far_kept, near_away = products(0, weights_kept, F32), products(0, weights_next, BF16)
     spans = [(0, out_width // 2), (out_width // 2, out_width)]
     send = [(far_kept[:, :, a:b] + far_terms[:, :, a:b].astype(F32)).astype(BF16) for a, b in spans]
     send, near_away, mixed = lax.optimization_barrier((send, near_away, mixed))

time: 58.5 us -> 58.3 us (level)
  waiting for transfers between devices: 15.4 us -> 13.6 us
  Pallas kernels: 15.6 us -> 17 us
    ppermute x14, waiting for transfers between devices: 6.05 us -> 4.24 us  [swap(): lax.ppermute(arrays[k], 'seq', [(d, d ^ k) for d in range(seq_count)])]
    pallas_call x2 -> x3, Pallas kernels: 7.48 us -> 8.95 us  [the longest x1 4.31 us: local(): pl.pallas_call(functools.partial(filter_kernel, block, far_odd, pieces >...]
  transfers between devices with their start and end apart: 18 -> 18, of which waited for: 6 -> 6; matrix products, arithmetic and copies ran while one was open for 0% -> 0% of each run, Pallas kernels for 16% -> 19%
where the time goes in v11:
time: 58.3 us; the launch traced here: 58.1 us
  starting transfers between devices  27.1 us (46%)
  Pallas kernels  17 us (29%)
  waiting for transfers between devices  13.6 us (23%)
    ppermute x14, starting transfers between devices, swap(): lax.ppermute(arrays[k], 'seq', [(d, d ^ k) for d in range(seq_count)])  24.8 us
    ppermute x4, waiting for transfers between devices, exchange(): lax.ppermute(terms, 'chan', [(d, d ^ bit) for d in range(chan_count)])  9.36 us
    pallas_call x1, Pallas kernels, local(): pl.pallas_call(functools.partial(filter_kernel, block, far_odd, pieces >...  4.31 us
    ppermute x14, waiting for transfers between devices, swap(): lax.ppermute(arrays[k], 'seq', [(d, d ^ k) for d in range(seq_count)])  4.24 us
    pallas_call x1, Pallas kernels, local(): pl.pallas_call(functools.partial(conv_kernel, block, blocks_kept, arrival...  2.85 us
    ppermute x4, starting transfers between devices, exchange(): lax.ppermute(terms, 'chan', [(d, d ^ bit) for d in range(chan_count)])  2.31 us
    pallas_call x1, Pallas kernels, local(): pl.pallas_call(functools.partial(last_kernel, blocks_last), out_shape=jax...  2.31 us
    pallas_call x2, Pallas kernels, local(): pl.pallas_call(functools.partial(finish_kernel, span, len(terms)), out_sh...  1.87 us
  transfers between devices with their start and end apart: 18, of which 6 were waited for; matrix products, arithmetic and copies ran while one was open for 0% of the time, Pallas kernels for 19%

profile of v11, /device:TPU:0, one launch (start us, length us, event | category | flops | bytes accessed | tf_op | source)
XLA Modules:
  0.0 58.1 jit_solution(11792805473260299842)
XLA Ops:
  0.0 1.5 %shard_map.155 = (bf16[256,128]{1,0:T(8,128)(2,1)S(1)}, bf16[256,128]{1,0:T(8,128)(2,1)S(1)}, bf16[256,128]{1,0:T(8,128)(2,1)S(1)}, bf16[256,128]{1,0:T(8,128)(2...) custom-call(bf16[256,1024]{1,0:T(8,128)(2,1)} %key_hbm.1, ...), custom_call_target="tpu_custom_call" | custom-call | tf_op jit(solution)/shard_map/pallas_call | solution.py:312
  1.5 3.1 %collective-permute-start = (bf16[256,128]{1,0:T(8,128)(2,1)S(1)}, bf16[256,128]{1,0:T(8,128)(2,1)S(1)}, u32[]{:S(2)}, u32[]{:S(2)}) collective-permute-start(bf16[256,128]{1,0:T(8,128)(2,1)S(1)} %get-tuple-element.38.refs_9_), channel_id=1, source_target_pairs={{0,8},{4,12},{8,0},{12,4},{16,24},{20,28},{24,16},{28,20},{1,9},{5... | collective-permute-start | bytes 196616 | tf_op jit(solution)/shard_map/ppermute | solution.py:309
  4.6 2.6 %collective-permute-start.1 = (bf16[256,128]{1,0:T(8,128)(2,1)S(1)}, bf16[256,128]{1,0:T(8,128)(2,1)S(1)}, u32[]{:S(2)}, u32[]{:S(2)}) collective-permute-start(bf16[256,128]{1,0:T(8,128)(2,1)S(1)} %get-tuple-element.39.refs_10_), channel_id=1, source_target_pairs={{0,16},{4,20},{8,24},{12,28},{16,0},{20,4},{24,8},{28,12},{1,17},{... | collective-permute-start | bytes 196616 | tf_op jit(solution)/shard_map/ppermute | solution.py:309
  7.2 1.7 %collective-permute-start.3 = (bf16[256,128]{1,0:T(8,128)(2,1)S(1)}, bf16[256,128]{1,0:T(8,128)(2,1)S(1)}, u32[]{:S(2)}, u32[]{:S(2)}) collective-permute-start(bf16[256,128]{1,0:T(8,128)(2,1)S(1)} %get-tuple-element.41.refs_12_), channel_id=1, source_target_pairs={{0,4},{4,0},{8,12},{12,8},{16,20},{20,16},{24,28},{28,24},{1,5},{5... | collective-permute-start | bytes 196616 | tf_op jit(solution)/shard_map/ppermute | solution.py:309
  9.5 4.4 %collective-permute-start.5 = (bf16[256,128]{1,0:T(8,128)(2,1)S(1)}, bf16[256,128]{1,0:T(8,128)(2,1)S(1)}, u32[]{:S(2)}, u32[]{:S(2)}) collective-permute-start(bf16[256,128]{1,0:T(8,128)(2,1)S(1)} %get-tuple-element.43.refs_14_), channel_id=1, source_target_pairs={{0,20},{4,16},{8,28},{12,24},{16,4},{20,0},{24,12},{28,8},{1,21},{... | collective-permute-start | bytes 196616 | tf_op jit(solution)/shard_map/ppermute | solution.py:309
  13.9 2.4 %collective-permute-start.6 = (bf16[256,128]{1,0:T(8,128)(2,1)S(1)}, bf16[256,128]{1,0:T(8,128)(2,1)S(1)}, u32[]{:S(2)}, u32[]{:S(2)}) collective-permute-start(bf16[256,128]{1,0:T(8,128)(2,1)S(1)} %get-tuple-element.44.refs_15_), channel_id=1, source_target_pairs={{0,28},{4,24},{8,20},{12,16},{16,12},{20,8},{24,4},{28,0},{1,29},{... | collective-permute-start | bytes 196616 | tf_op jit(solution)/shard_map/ppermute | solution.py:309
  16.4 4.3 %shard_map.154 = (f32[8,256,128]{2,1,0:T(8,128)S(1)}, f32[8,256,128]{2,1,0:T(8,128)S(1)}, f32[8,16,128]{2,1,0:T(8,128)S(1)}, bf16[1,1024,1024]{2,1,0:T(8,128)(2,1)S(1)}) custom-call(f32[64,128]{1,0:T(8,128)S(1)} %constant_dynamic-slice_fusion.out_w_ref, f32[40,2048]{1,0:T(8,128)} %constant.23.clone.refs_0_, f32[33,64]{1,0:T(8,128)} %refs_1_.1, ...), custom_call_target="tpu_custom_call" | custom-call | tf_op jit(solution)/shard_map/pallas_call | solution.py:345
  20.9 2.8 %shard_map.156 = (bf16[256,128]{1,0:T(8,128)(2,1)S(1)}, bf16[256,128]{1,0:T(8,128)(2,1)S(1)}, bf16[256,128]{1,0:T(8,128)(2,1)S(1)}, bf16[256,128]{1,0:T(8,128)(2...) custom-call(s32[16]{0:T(128)S(1)} %copy-done.4, ...), custom_call_target="tpu_custom_call" | custom-call | tf_op jit(solution)/shard_map/pallas_call | solution.py:367
  23.8 1.9 %collective-permute-start.8 = (bf16[256,128]{1,0:T(8,128)(2,1)S(1)}, bf16[256,128]{1,0:T(8,128)(2,1)S(1)}, u32[]{:S(2)}, u32[]{:S(2)}) collective-permute-start(bf16[256,128]{1,0:T(8,128)(2,1)S(1)} %get-tuple-element.49), channel_id=1, source_target_pairs={{0,16},{4,20},{8,24},{12,28},{16,0},{20,4},{24,8},{28,12},{1,17},{... | collective-permute-start | bytes 196616 | tf_op jit(solution)/shard_map/ppermute | solution.py:309
  25.7 2.5 %collective-permute-start.9 = (bf16[256,128]{1,0:T(8,128)(2,1)S(1)}, bf16[256,128]{1,0:T(8,128)(2,1)S(1)}, u32[]{:S(2)}, u32[]{:S(2)}) collective-permute-start(bf16[256,128]{1,0:T(8,128)(2,1)S(1)} %get-tuple-element.50), channel_id=1, source_target_pairs={{0,24},{4,28},{8,16},{12,20},{16,8},{20,12},{24,0},{28,4},{1,25},{... | collective-permute-start | bytes 196616 | tf_op jit(solution)/shard_map/ppermute | solution.py:309
  28.9 1.3 %collective-permute-done.7.refs_1_ = bf16[256,128]{1,0:T(8,128)(2,1)S(1)} collective-permute-done((bf16[256,128]{1,0:T(8,128)(2,1)S(1)}, bf16[256,128]{1,0:T(8,128)(2,1)S(1)}, u32[]{:S(2)}, u32[]{:S(2)}) %collective-permute-start.7) | collective-permute-done | bytes 65568 | tf_op jit(solution)/shard_map/ppermute | solution.py:309
  30.1 2.5 %collective-permute-start.12 = (bf16[256,128]{1,0:T(8,128)(2,1)S(1)}, bf16[256,128]{1,0:T(8,128)(2,1)S(1)}, u32[]{:S(2)}, u32[]{:S(2)}) collective-permute-start(bf16[256,128]{1,0:T(8,128)(2,1)S(1)} %get-tuple-element.53), channel_id=1, source_target_pairs={{0,20},{4,16},{8,28},{12,24},{16,4},{20,0},{24,12},{28,8},{1,21},{... | collective-permute-start | bytes 196616 | tf_op jit(solution)/shard_map/ppermute | solution.py:309
  32.6 2.4 %collective-permute-start.13 = (bf16[256,128]{1,0:T(8,128)(2,1)S(1)}, bf16[256,128]{1,0:T(8,128)(2,1)S(1)}, u32[]{:S(2)}, u32[]{:S(2)}) collective-permute-start(bf16[256,128]{1,0:T(8,128)(2,1)S(1)} %get-tuple-element.54), channel_id=1, source_target_pairs={{0,28},{4,24},{8,20},{12,16},{16,12},{20,8},{24,4},{28,0},{1,29},{... | collective-permute-start | bytes 196616 | tf_op jit(solution)/shard_map/ppermute | solution.py:309
  35.0 1.8 %shard_map.157 = (bf16[1,1024,1024]{2,1,0:T(8,128)(2,1)S(1)}, bf16[256,1024]{1,0:T(8,128)(2,1)S(1)}) custom-call(bf16[256,128]{1,0:T(8,128)(2,1)S(1)} %get-tuple-element.45.after_ref.refs_0_, bf16[1024,4096]{1,0:T(8,128)(2,1)} %weight_hbm.5, bf16[256,1024]{1,0:T(8,128)(2,1)} %query_hbm.1), custom_call_target="tpu_custom_call" | custom-call | tf_op jit(solution)/shard_map/pallas_call | solution.py:385
  36.8 2.8 %collective-permute-done.13.refs_7_ = bf16[256,128]{1,0:T(8,128)(2,1)S(1)} collective-permute-done((bf16[256,128]{1,0:T(8,128)(2,1)S(1)}, bf16[256,128]{1,0:T(8,128)(2,1)S(1)}, u32[]{:S(2)}, u32[]{:S(2)}) %collective-permute-start.13) | collective-permute-done | bytes 65568 | tf_op jit(solution)/shard_map/ppermute | solution.py:309
  39.6 1.0 %shard_map.158 = (bf16[1,256,1024]{2,1,0:T(8,128)(2,1)S(1)}, bf16[256,1024]{1,0:T(8,128)(2,1)S(1)}) custom-call(bf16[256,1024]{1,0:T(8,128)(2,1)S(1)} %get-tuple-element.46.query_ref, f32[1,1024]{1,0:T(1,128)S(1)} %bitcast.14, bf16[1,1024,1024]{2,1,0:T(8,128)(2,1)S(1)} %get-tuple-element.47.weight_ref, ...), custom_call_target="tpu_custom_call" | custom-call | tf_op jit(solution)/shard_map/pallas_call | solution.py:405
  40.7 0.7 %shard_map.160 = bf16[1,256,1024]{2,1,0:T(8,128)(2,1)S(1)} custom-call(bf16[256,1024]{1,0:T(8,128)(2,1)S(1)} %get-tuple-element.59.mixed_ref, bf16[1,1024,1024]{2,1,0:T(8,128)(2,1)S(1)} %get-tuple-element.58.weight_ref), custom_call_target="tpu_custom_call" | custom-call | tf_op jit(solution)/shard_map/pallas_call | solution.py:418
  41.4 0.7 %shard_map.159 = f32[1,256,1024]{2,1,0:T(8,128)S(1)} custom-call(bf16[256,1024]{1,0:T(8,128)(2,1)S(1)} %get-tuple-element.59.mixed_ref, bf16[1,1024,1024]{2,1,0:T(8,128)(2,1)S(1)} %get-tuple-element.56.weight_ref), custom_call_target="tpu_custom_call" | custom-call | tf_op jit(solution)/shard_map/pallas_call | solution.py:418
  43.0 1.5 %collective-permute-start.17 = (bf16[1,256,512]{2,1,0:T(8,128)(2,1)S(1)}, bf16[1,256,512]{2,1,0:T(8,128)(2,1)S(1)}, u32[]{:S(2)}, u32[]{:S(2)}) collective-permute-start(bf16[1,256,512]{2,1,0:T(8,128)(2,1)S(1)} %get-tuple-element.62), channel_id=1, source_target_pairs={{0,2},{1,3},{2,0},{3,1},{4,6},{5,7},{6,4},{7,5},{8,10},{9,11},{10,... | collective-permute-start | bytes 786440 | tf_op jit(solution)/shard_map/ppermute | solution.py:403
  45.0 2.3 %shard_map.161 = f32[1,256,1024]{2,1,0:T(8,128)S(1)} custom-call(bf16[256,1024]{1,0:T(8,128)(2,1)S(1)} %get-tuple-element.59.mixed_ref, bf16[1024,4096]{1,0:T(8,128)(2,1)} %weight_hbm.5), custom_call_target="tpu_custom_call" | custom-call | tf_op jit(solution)/shard_map/pallas_call | solution.py:432
  47.3 4.8 %collective-permute-done.17 = bf16[1,256,512]{2,1,0:T(8,128)(2,1)S(1)} collective-permute-done((bf16[1,256,512]{2,1,0:T(8,128)(2,1)S(1)}, bf16[1,256,512]{2,1,0:T(8,128)(2,1)S(1)}, u32[]{:S(2)}, u32[]{:S(2)}) %collective-permute-start.17) | collective-permute-done | bytes 262176 | tf_op jit(solution)/shard_map/ppermute | solution.py:403
  52.1 0.9 %shard_map.162.refs_3_ = f32[1024,256]{1,0:T(8,128)} custom-call(f32[256,1024]{1,0:T(8,128)S(1)} %bitcast.8, bf16[256,1024]{1,0:T(8,128)(2,1)S(1)} %bitcast.10, bf16[256,512]{1,0:T(8,128)(2,1)S(1)} %bitcast.12), custom_call_target="tpu_custom_call" | custom-call | tf_op jit(solution)/shard_map/pallas_call | solution.py:453
  53.1 4.1 %collective-permute-done.16 = bf16[1,256,512]{2,1,0:T(8,128)(2,1)S(1)} collective-permute-done((bf16[1,256,512]{2,1,0:T(8,128)(2,1)S(1)}, bf16[1,256,512]{2,1,0:T(8,128)(2,1)S(1)}, u32[]{:S(2)}, u32[]{:S(2)}) %collective-permute-start.16) | collective-permute-done | bytes 262176 | tf_op jit(solution)/shard_map/ppermute | solution.py:403
  57.2 0.9 %shard_map.163 = f32[1024,256]{1,0:T(8,128)} custom-call(f32[256,1024]{1,0:T(8,128)S(1)} %bitcast.9, bf16[256,1024]{1,0:T(8,128)(2,1)S(1)} %bitcast.11, bf16[256,512]{1,0:T(8,128)(2,1)S(1)} %bitcast.13, f32[1024,256]{1,0:T(8,128)} %shard_map.162.refs_3_), custom_call_target="tpu_custom_call", output_to_operand_aliasing={{}: (3, {})} | custom-call | tf_op jit(solution)/shard_map/pallas_call | solution.py:453
  (34 shorter events, 3.0 us)
Async XLA Ops:
  0.0 16.3 %copy-start = (f32[64,1024]{1,0:T(8,128)S(1)}, f32[64,1024]{1,0:T(8,128)}, u32[]{:S(2)}) copy-start(f32[64,1024]{1,0:T(8,128)} %param.24) | copy-start | bytes 786436
  1.5 8.0 %collective-permute-start = (bf16[256,128]{1,0:T(8,128)(2,1)S(1)}, bf16[256,128]{1,0:T(8,128)(2,1)S(1)}, u32[]{:S(2)}, u32[]{:S(2)}) collective-permute-start(bf16[256,128]{1,0:T(8,128)(2,1)S(1)} %get-tuple-element.38.refs_9_), channel_id=1, source_target_pairs={{0,8},{4,12},{8,0},{12,4},{16,24},{20,28},{24,16},{28,20},{1,9},{5... | collective-permute-start | bytes 196616 | tf_op jit(solution)/shard_map/ppermute | solution.py:309
  4.6 9.4 %collective-permute-start.1 = (bf16[256,128]{1,0:T(8,128)(2,1)S(1)}, bf16[256,128]{1,0:T(8,128)(2,1)S(1)}, u32[]{:S(2)}, u32[]{:S(2)}) collective-permute-start(bf16[256,128]{1,0:T(8,128)(2,1)S(1)} %get-tuple-element.39.refs_10_), channel_id=1, source_target_pairs={{0,16},{4,20},{8,24},{12,28},{16,0},{20,4},{24,8},{28,12},{1,17},{... | collective-permute-start | bytes 196616 | tf_op jit(solution)/shard_map/ppermute | solution.py:309
  7.1 13.5 %collective-permute-start.2 = (bf16[256,128]{1,0:T(8,128)(2,1)S(1)}, bf16[256,128]{1,0:T(8,128)(2,1)S(1)}, u32[]{:S(2)}, u32[]{:S(2)}) collective-permute-start(bf16[256,128]{1,0:T(8,128)(2,1)S(1)} %get-tuple-element.40.refs_11_), channel_id=1, source_target_pairs={{0,24},{4,28},{8,16},{12,20},{16,8},{20,12},{24,0},{28,4},{1,25},{... | collective-permute-start | bytes 196616 | tf_op jit(solution)/shard_map/ppermute | solution.py:309
  7.2 13.5 %collective-permute-start.3 = (bf16[256,128]{1,0:T(8,128)(2,1)S(1)}, bf16[256,128]{1,0:T(8,128)(2,1)S(1)}, u32[]{:S(2)}, u32[]{:S(2)}) collective-permute-start(bf16[256,128]{1,0:T(8,128)(2,1)S(1)} %get-tuple-element.41.refs_12_), channel_id=1, source_target_pairs={{0,4},{4,0},{8,12},{12,8},{16,20},{20,16},{24,28},{28,24},{1,5},{5... | collective-permute-start | bytes 196616 | tf_op jit(solution)/shard_map/ppermute | solution.py:309
  8.9 11.8 %collective-permute-start.4 = (bf16[256,128]{1,0:T(8,128)(2,1)S(1)}, bf16[256,128]{1,0:T(8,128)(2,1)S(1)}, u32[]{:S(2)}, u32[]{:S(2)}) collective-permute-start(bf16[256,128]{1,0:T(8,128)(2,1)S(1)} %get-tuple-element.42.refs_13_), channel_id=1, source_target_pairs={{0,12},{4,8},{8,4},{12,0},{16,28},{20,24},{24,20},{28,16},{1,13},{... | collective-permute-start | bytes 196616 | tf_op jit(solution)/shard_map/ppermute | solution.py:309
  9.5 11.2 %collective-permute-start.5 = (bf16[256,128]{1,0:T(8,128)(2,1)S(1)}, bf16[256,128]{1,0:T(8,128)(2,1)S(1)}, u32[]{:S(2)}, u32[]{:S(2)}) collective-permute-start(bf16[256,128]{1,0:T(8,128)(2,1)S(1)} %get-tuple-element.43.refs_14_), channel_id=1, source_target_pairs={{0,20},{4,16},{8,28},{12,24},{16,4},{20,0},{24,12},{28,8},{1,21},{... | collective-permute-start | bytes 196616 | tf_op jit(solution)/shard_map/ppermute | solution.py:309
  13.9 7.0 %collective-permute-start.6 = (bf16[256,128]{1,0:T(8,128)(2,1)S(1)}, bf16[256,128]{1,0:T(8,128)(2,1)S(1)}, u32[]{:S(2)}, u32[]{:S(2)}) collective-permute-start(bf16[256,128]{1,0:T(8,128)(2,1)S(1)} %get-tuple-element.44.refs_15_), channel_id=1, source_target_pairs={{0,28},{4,24},{8,20},{12,16},{16,12},{20,8},{24,4},{28,0},{1,29},{... | collective-permute-start | bytes 196616 | tf_op jit(solution)/shard_map/ppermute | solution.py:309
  16.3 4.6 %copy-start.1 = (bf16[256,512]{1,0:T(8,128)(2,1)S(1)}, bf16[256,512]{1,0:T(8,128)(2,1)}, u32[]{:S(2)}) copy-start(bf16[256,512]{1,0:T(8,128)(2,1)} %constant.26.inverse_ref) | copy-start | bytes 786436
  16.3 4.6 %copy-start.2 = (bf16[512,256]{1,0:T(8,128)(2,1)S(1)}, bf16[512,256]{1,0:T(8,128)(2,1)}, u32[]{:S(2)}) copy-start(bf16[512,256]{1,0:T(8,128)(2,1)} %constant.25.table_ref) | copy-start | bytes 786436
  16.3 4.6 %copy-start.4 = (s32[16]{0:T(128)S(1)}, s32[16]{0:T(128)}, u32[]{:S(2)}) copy-start(s32[16]{0:T(128)} %order_ref.1) | copy-start | bytes 196
  23.8 6.4 %collective-permute-start.7 = (bf16[256,128]{1,0:T(8,128)(2,1)S(1)}, bf16[256,128]{1,0:T(8,128)(2,1)S(1)}, u32[]{:S(2)}, u32[]{:S(2)}) collective-permute-start(bf16[256,128]{1,0:T(8,128)(2,1)S(1)} %get-tuple-element.48), channel_id=1, source_target_pairs={{0,8},{4,12},{8,0},{12,4},{16,24},{20,28},{24,16},{28,20},{1,9},{5... | collective-permute-start | bytes 196616 | tf_op jit(solution)/shard_map/ppermute | solution.py:309
  23.8 8.8 %collective-permute-start.8 = (bf16[256,128]{1,0:T(8,128)(2,1)S(1)}, bf16[256,128]{1,0:T(8,128)(2,1)S(1)}, u32[]{:S(2)}, u32[]{:S(2)}) collective-permute-start(bf16[256,128]{1,0:T(8,128)(2,1)S(1)} %get-tuple-element.49), channel_id=1, source_target_pairs={{0,16},{4,20},{8,24},{12,28},{16,0},{20,4},{24,8},{28,12},{1,17},{... | collective-permute-start | bytes 196616 | tf_op jit(solution)/shard_map/ppermute | solution.py:309
  25.7 11.0 %collective-permute-start.9 = (bf16[256,128]{1,0:T(8,128)(2,1)S(1)}, bf16[256,128]{1,0:T(8,128)(2,1)S(1)}, u32[]{:S(2)}, u32[]{:S(2)}) collective-permute-start(bf16[256,128]{1,0:T(8,128)(2,1)S(1)} %get-tuple-element.50), channel_id=1, source_target_pairs={{0,24},{4,28},{8,16},{12,20},{16,8},{20,12},{24,0},{28,4},{1,25},{... | collective-permute-start | bytes 196616 | tf_op jit(solution)/shard_map/ppermute | solution.py:309
  28.2 8.6 %collective-permute-start.10 = (bf16[256,128]{1,0:T(8,128)(2,1)S(1)}, bf16[256,128]{1,0:T(8,128)(2,1)S(1)}, u32[]{:S(2)}, u32[]{:S(2)}) collective-permute-start(bf16[256,128]{1,0:T(8,128)(2,1)S(1)} %get-tuple-element.51), channel_id=1, source_target_pairs={{0,4},{4,0},{8,12},{12,8},{16,20},{20,16},{24,28},{28,24},{1,5},{5... | collective-permute-start | bytes 196616 | tf_op jit(solution)/shard_map/ppermute | solution.py:309
  28.8 8.1 %collective-permute-start.11 = (bf16[256,128]{1,0:T(8,128)(2,1)S(1)}, bf16[256,128]{1,0:T(8,128)(2,1)S(1)}, u32[]{:S(2)}, u32[]{:S(2)}) collective-permute-start(bf16[256,128]{1,0:T(8,128)(2,1)S(1)} %get-tuple-element.52), channel_id=1, source_target_pairs={{0,12},{4,8},{8,4},{12,0},{16,28},{20,24},{24,20},{28,16},{1,13},{... | collective-permute-start | bytes 196616 | tf_op jit(solution)/shard_map/ppermute | solution.py:309
  30.1 6.7 %collective-permute-start.12 = (bf16[256,128]{1,0:T(8,128)(2,1)S(1)}, bf16[256,128]{1,0:T(8,128)(2,1)S(1)}, u32[]{:S(2)}, u32[]{:S(2)}) collective-permute-start(bf16[256,128]{1,0:T(8,128)(2,1)S(1)} %get-tuple-element.53), channel_id=1, source_target_pairs={{0,20},{4,16},{8,28},{12,24},{16,4},{20,0},{24,12},{28,8},{1,21},{... | collective-permute-start | bytes 196616 | tf_op jit(solution)/shard_map/ppermute | solution.py:309
  32.6 7.0 %collective-permute-start.13 = (bf16[256,128]{1,0:T(8,128)(2,1)S(1)}, bf16[256,128]{1,0:T(8,128)(2,1)S(1)}, u32[]{:S(2)}, u32[]{:S(2)}) collective-permute-start(bf16[256,128]{1,0:T(8,128)(2,1)S(1)} %get-tuple-element.54), channel_id=1, source_target_pairs={{0,28},{4,24},{8,20},{12,16},{16,12},{20,8},{24,4},{28,0},{1,29},{... | collective-permute-start | bytes 196616 | tf_op jit(solution)/shard_map/ppermute | solution.py:309
  35.0 4.6 %copy-start.3 = (f32[1024]{0:T(1024)S(1)}, f32[1024]{0:T(1024)}, u32[]{:S(2)}) copy-start(f32[1024]{0:T(1024)} %param.26) | copy-start | bytes 12292
  40.6 2.0 %collective-permute-start.14 = (bf16[1,256,1024]{2,1,0:T(8,128)(2,1)S(1)}, bf16[1,256,1024]{2,1,0:T(8,128)(2,1)S(1)}, u32[]{:S(2)}, u32[]{:S(2)}) collective-permute-start(bf16[1,256,1024]{2,1,0:T(8,128)(2,1)S(1)} %get-tuple-element.57), channel_id=1, source_target_pairs={{0,1},{1,0},{2,3},{3,2},{4,5},{5,4},{6,7},{7,6},{8,9},{9,8},{10,11... | collective-permute-start | bytes 1572872 | tf_op jit(solution)/shard_map/ppermute | solution.py:403
  42.8 9.3 %collective-permute-start.15 = (bf16[1,256,1024]{2,1,0:T(8,128)(2,1)S(1)}, bf16[1,256,1024]{2,1,0:T(8,128)(2,1)S(1)}, u32[]{:S(2)}, u32[]{:S(2)}) collective-permute-start(bf16[1,256,1024]{2,1,0:T(8,128)(2,1)S(1)} %shard_map.160), channel_id=1, source_target_pairs={{0,1},{1,0},{2,3},{3,2},{4,5},{5,4},{6,7},{7,6},{8,9},{9,8},{10,11... | collective-permute-start | bytes 1572872 | tf_op jit(solution)/shard_map/ppermute | solution.py:403
  43.0 9.1 %collective-permute-start.17 = (bf16[1,256,512]{2,1,0:T(8,128)(2,1)S(1)}, bf16[1,256,512]{2,1,0:T(8,128)(2,1)S(1)}, u32[]{:S(2)}, u32[]{:S(2)}) collective-permute-start(bf16[1,256,512]{2,1,0:T(8,128)(2,1)S(1)} %get-tuple-element.62), channel_id=1, source_target_pairs={{0,2},{1,3},{2,0},{3,1},{4,6},{5,7},{6,4},{7,5},{8,10},{9,11},{10,... | collective-permute-start | bytes 786440 | tf_op jit(solution)/shard_map/ppermute | solution.py:403
  44.5 12.7 %collective-permute-start.16 = (bf16[1,256,512]{2,1,0:T(8,128)(2,1)S(1)}, bf16[1,256,512]{2,1,0:T(8,128)(2,1)S(1)}, u32[]{:S(2)}, u32[]{:S(2)}) collective-permute-start(bf16[1,256,512]{2,1,0:T(8,128)(2,1)S(1)} %get-tuple-element.61), channel_id=1, source_target_pairs={{0,2},{1,3},{2,0},{3,1},{4,6},{5,7},{6,4},{7,5},{8,10},{9,11},{10,... | collective-permute-start | bytes 786440 | tf_op jit(solution)/shard_map/ppermute | solution.py:403

commit v12 on v11

--- a/solution.py
+++ b/solution.py
@@ -208,23 +208,29 @@
         copy.wait()
 
 
-def copy_kernel(blocks_next, after_ref, weight_hbm, query_hbm, weight_out, query_out, weight_sem, query_sem):
-    copies = weight_copies(blocks_next, weight_hbm, weight_out, weight_sem)
-    copies.append(pltpu.make_async_copy(query_hbm, query_out, query_sem.at[0]))
+def copy_kernel(blocks_next, after_ref, gain_ref, weight_hbm, query_hbm, *refs):
+    *sig_refs, weight_out, query_out, skip_out, weight_sem, query_sem = refs
+    pieces = len(sig_refs)
+    unit = sig_refs[0].shape[1]
+    columns = [pl.ds(pl.multiple_of((first_piece(pieces) ^ k) * unit, LANES), unit) for k in range(pieces)]
+    copies = [
+        pltpu.make_async_copy(query_hbm.at[:, cols], query_out.at[k], query_sem.at[k]) for k, cols in enumerate(columns)
+    ]
+    copies += weight_copies(blocks_next, weight_hbm, weight_out, weight_sem)
     for copy in copies:
         copy.start()
+    for k, (cols, sig_ref) in enumerate(zip(columns, sig_refs)):
+        skip_out[k] = gain_ref[:, cols] * sig_ref[...].astype(F32)
     for copy in copies:
         copy.wait()
 
 
-def mix_kernel(arrival, query_ref, gain_ref, weight_ref, *refs):
-    *refs, out_ref, mixed_ref = refs
-    pieces = len(refs) // 2
-    unit = refs[0].shape[1]
-    for k, back_ref, sig_ref in zip(arrival, refs[:pieces], refs[pieces:]):
+def mix_kernel(arrival, query_ref, skip_ref, weight_ref, *refs):
+    *back_refs, out_ref, mixed_ref = refs
+    pieces, _, unit = query_ref.shape
+    for k, back_ref in zip(arrival, back_refs):
         cols = pl.ds(pl.multiple_of((first_piece(pieces) ^ k) * unit, LANES), unit)
-        inner = back_ref[...].astype(F32) + gain_ref[:, cols] * sig_ref[...].astype(F32)
-        mixed_ref[:, cols] = (query_ref[:, cols].astype(F32) * inner).astype(BF16)
+        mixed_ref[:, cols] = (query_ref[k].astype(F32) * (back_ref[...].astype(F32) + skip_ref[k])).astype(BF16)
     project_kernel(0, mixed_ref, weight_ref, out_ref)
 
 
@@ -382,17 +388,18 @@
         ],
         compiler_params=limit,
     )(group_order, real, imag, edge, head, inverse, far(out_weight), *[spread[k] for k in arrival])
-    weights_next, query_near = pl.pallas_call(
+    weights_next, query_near, skip = pl.pallas_call(
         functools.partial(copy_kernel, near_odd),
         out_shape=(
             jax.ShapeDtypeStruct((quarter, chan_width, out_width), BF16),
-            jax.ShapeDtypeStruct(query.shape, BF16),
+            jax.ShapeDtypeStruct((pieces, rows, unit), BF16),
+            jax.ShapeDtypeStruct((pieces, rows, unit), F32),
         ),
-        in_specs=[in_vmem] + [in_hbm] * 2,
-        out_specs=[in_vmem] * 2,
-        scratch_shapes=[pltpu.SemaphoreType.DMA((quarter,)), pltpu.SemaphoreType.DMA((1,))],
-        compiler_params=limit,
-    )(convolved[0], far(out_weight), far(query))
+        in_specs=[in_vmem] * 2 + [in_hbm] * 2 + [in_vmem] * pieces,
+        out_specs=[in_vmem] * 3,
+        scratch_shapes=[pltpu.SemaphoreType.DMA((quarter,)), pltpu.SemaphoreType.DMA((pieces,))],
+        compiler_params=limit,
+    )(convolved[0], skip_gain[None, :], far(out_weight), far(query), *signal)
     if pieces > 1:
         backs = swap(convolved)
     else:
@@ -408,10 +415,10 @@
             jax.ShapeDtypeStruct((quarter, rows, out_width), BF16),
             jax.ShapeDtypeStruct((rows, chan_width), BF16),
         ),
-        in_specs=[in_vmem] * (3 + 2 * pieces),
+        in_specs=[in_vmem] * (3 + pieces),
         out_specs=[in_vmem] * 2,
         compiler_params=limit,
-    )(query_near, skip_gain[None, :], weights_away, *[array[k] for array in (backs, signal) for k in (arrival if pieces > 1 else [0])])
+    )(query_near, skip, weights_away, *[backs[k] for k in (arrival if pieces > 1 else [0])])
     far_terms = exchange(far_away, 1)
 
     def products(first, weights, dtype):

time: 58.3 us -> 58.3 us (level)
  no operation moved by 1% of the time
where the time goes in v12:
time: 58.3 us; the launch traced here: 58 us
  starting transfers between devices  27.1 us (46%)
  Pallas kernels  17.2 us (30%)
  waiting for transfers between devices  13.4 us (23%)
    ppermute x14, starting transfers between devices, swap(): lax.ppermute(arrays[k], 'seq', [(d, d ^ k) for d in range(seq_count)])  24.8 us
    ppermute x4, waiting for transfers between devices, exchange(): lax.ppermute(terms, 'chan', [(d, d ^ bit) for d in range(chan_count)])  9.37 us
    pallas_call x1, Pallas kernels, local(): pl.pallas_call(functools.partial(filter_kernel, block, far_odd, pieces >...  4.31 us
    ppermute x14, waiting for transfers between devices, swap(): lax.ppermute(arrays[k], 'seq', [(d, d ^ k) for d in range(seq_count)])  4.04 us
    pallas_call x1, Pallas kernels, local(): pl.pallas_call(functools.partial(conv_kernel, block, blocks_kept, arrival...  2.85 us
    ppermute x4, starting transfers between devices, exchange(): lax.ppermute(terms, 'chan', [(d, d ^ bit) for d in range(chan_count)])  2.31 us
    pallas_call x1, Pallas kernels, local(): pl.pallas_call(functools.partial(last_kernel, blocks_last), out_shape=jax...  2.31 us
    pallas_call x1, Pallas kernels, local(): pl.pallas_call(functools.partial(copy_kernel, near_odd), out_shape=(jax.S...  1.99 us
  transfers between devices with their start and end apart: 18, of which 6 were waited for; matrix products, arithmetic and copies ran while one was open for 0% of the time, Pallas kernels for 19%

profile of v12, /device:TPU:0, one launch (start us, length us, event | category | flops | bytes accessed | tf_op | source)
XLA Modules:
  0.0 58.0 jit_solution(15312688504076707503)
XLA Ops:
  0.0 1.5 %shard_map.155 = (bf16[256,128]{1,0:T(8,128)(2,1)S(1)}, bf16[256,128]{1,0:T(8,128)(2,1)S(1)}, bf16[256,128]{1,0:T(8,128)(2,1)S(1)}, bf16[256,128]{1,0:T(8,128)(2...) custom-call(bf16[256,1024]{1,0:T(8,128)(2,1)} %key_hbm.1, ...), custom_call_target="tpu_custom_call" | custom-call | tf_op jit(solution)/shard_map/pallas_call | solution.py:318
  1.5 3.1 %collective-permute-start = (bf16[256,128]{1,0:T(8,128)(2,1)S(1)}, bf16[256,128]{1,0:T(8,128)(2,1)S(1)}, u32[]{:S(2)}, u32[]{:S(2)}) collective-permute-start(bf16[256,128]{1,0:T(8,128)(2,1)S(1)} %get-tuple-element.39.refs_2_), channel_id=1, source_target_pairs={{0,8},{4,12},{8,0},{12,4},{16,24},{20,28},{24,16},{28,20},{1,9},{5... | collective-permute-start | bytes 196616 | tf_op jit(solution)/shard_map/ppermute | solution.py:315
  4.6 2.6 %collective-permute-start.1 = (bf16[256,128]{1,0:T(8,128)(2,1)S(1)}, bf16[256,128]{1,0:T(8,128)(2,1)S(1)}, u32[]{:S(2)}, u32[]{:S(2)}) collective-permute-start(bf16[256,128]{1,0:T(8,128)(2,1)S(1)} %get-tuple-element.40.refs_4_), channel_id=1, source_target_pairs={{0,16},{4,20},{8,24},{12,28},{16,0},{20,4},{24,8},{28,12},{1,17},{... | collective-permute-start | bytes 196616 | tf_op jit(solution)/shard_map/ppermute | solution.py:315
  7.2 1.7 %collective-permute-start.3 = (bf16[256,128]{1,0:T(8,128)(2,1)S(1)}, bf16[256,128]{1,0:T(8,128)(2,1)S(1)}, u32[]{:S(2)}, u32[]{:S(2)}) collective-permute-start(bf16[256,128]{1,0:T(8,128)(2,1)S(1)} %get-tuple-element.42.refs_1_), channel_id=1, source_target_pairs={{0,4},{4,0},{8,12},{12,8},{16,20},{20,16},{24,28},{28,24},{1,5},{5... | collective-permute-start | bytes 196616 | tf_op jit(solution)/shard_map/ppermute | solution.py:315
  9.5 4.4 %collective-permute-start.5 = (bf16[256,128]{1,0:T(8,128)(2,1)S(1)}, bf16[256,128]{1,0:T(8,128)(2,1)S(1)}, u32[]{:S(2)}, u32[]{:S(2)}) collective-permute-start(bf16[256,128]{1,0:T(8,128)(2,1)S(1)} %get-tuple-element.44.refs_5_), channel_id=1, source_target_pairs={{0,20},{4,16},{8,28},{12,24},{16,4},{20,0},{24,12},{28,8},{1,21},{... | collective-permute-start | bytes 196616 | tf_op jit(solution)/shard_map/ppermute | solution.py:315
  13.9 2.4 %collective-permute-start.6 = (bf16[256,128]{1,0:T(8,128)(2,1)S(1)}, bf16[256,128]{1,0:T(8,128)(2,1)S(1)}, u32[]{:S(2)}, u32[]{:S(2)}) collective-permute-start(bf16[256,128]{1,0:T(8,128)(2,1)S(1)} %get-tuple-element.45.refs_7_), channel_id=1, source_target_pairs={{0,28},{4,24},{8,20},{12,16},{16,12},{20,8},{24,4},{28,0},{1,29},{... | collective-permute-start | bytes 196616 | tf_op jit(solution)/shard_map/ppermute | solution.py:315
  16.4 4.3 %shard_map.154 = (f32[8,256,128]{2,1,0:T(8,128)S(1)}, f32[8,256,128]{2,1,0:T(8,128)S(1)}, f32[8,16,128]{2,1,0:T(8,128)S(1)}, bf16[1,1024,1024]{2,1,0:T(8,128)(2,1)S(1)}) custom-call(f32[64,128]{1,0:T(8,128)S(1)} %constant_dynamic-slice_fusion.out_w_ref, f32[40,2048]{1,0:T(8,128)} %constant.23.clone.refs_0_, f32[33,64]{1,0:T(8,128)} %refs_1_.1, ...), custom_call_target="tpu_custom_call" | custom-call | tf_op jit(solution)/shard_map/pallas_call | solution.py:351
  20.9 2.9 %shard_map.156 = (bf16[256,128]{1,0:T(8,128)(2,1)S(1)}, bf16[256,128]{1,0:T(8,128)(2,1)S(1)}, bf16[256,128]{1,0:T(8,128)(2,1)S(1)}, bf16[256,128]{1,0:T(8,128)(2...) custom-call(s32[16]{0:T(128)S(1)} %copy-done.4, ...), custom_call_target="tpu_custom_call" | custom-call | tf_op jit(solution)/shard_map/pallas_call | solution.py:373
  23.9 1.9 %collective-permute-start.8 = (bf16[256,128]{1,0:T(8,128)(2,1)S(1)}, bf16[256,128]{1,0:T(8,128)(2,1)S(1)}, u32[]{:S(2)}, u32[]{:S(2)}) collective-permute-start(bf16[256,128]{1,0:T(8,128)(2,1)S(1)} %get-tuple-element.51), channel_id=1, source_target_pairs={{0,16},{4,20},{8,24},{12,28},{16,0},{20,4},{24,8},{28,12},{1,17},{... | collective-permute-start | bytes 196616 | tf_op jit(solution)/shard_map/ppermute | solution.py:315
  25.8 2.5 %collective-permute-start.9 = (bf16[256,128]{1,0:T(8,128)(2,1)S(1)}, bf16[256,128]{1,0:T(8,128)(2,1)S(1)}, u32[]{:S(2)}, u32[]{:S(2)}) collective-permute-start(bf16[256,128]{1,0:T(8,128)(2,1)S(1)} %get-tuple-element.52), channel_id=1, source_target_pairs={{0,24},{4,28},{8,16},{12,20},{16,8},{20,12},{24,0},{28,4},{1,25},{... | collective-permute-start | bytes 196616 | tf_op jit(solution)/shard_map/ppermute | solution.py:315
  28.9 1.3 %collective-permute-done.7.refs_1_ = bf16[256,128]{1,0:T(8,128)(2,1)S(1)} collective-permute-done((bf16[256,128]{1,0:T(8,128)(2,1)S(1)}, bf16[256,128]{1,0:T(8,128)(2,1)S(1)}, u32[]{:S(2)}, u32[]{:S(2)}) %collective-permute-start.7) | collective-permute-done | bytes 65568 | tf_op jit(solution)/shard_map/ppermute | solution.py:315
  30.1 2.5 %collective-permute-start.12 = (bf16[256,128]{1,0:T(8,128)(2,1)S(1)}, bf16[256,128]{1,0:T(8,128)(2,1)S(1)}, u32[]{:S(2)}, u32[]{:S(2)}) collective-permute-start(bf16[256,128]{1,0:T(8,128)(2,1)S(1)} %get-tuple-element.55), channel_id=1, source_target_pairs={{0,20},{4,16},{8,28},{12,24},{16,4},{20,0},{24,12},{28,8},{1,21},{... | collective-permute-start | bytes 196616 | tf_op jit(solution)/shard_map/ppermute | solution.py:315
  32.6 2.4 %collective-permute-start.13 = (bf16[256,128]{1,0:T(8,128)(2,1)S(1)}, bf16[256,128]{1,0:T(8,128)(2,1)S(1)}, u32[]{:S(2)}, u32[]{:S(2)}) collective-permute-start(bf16[256,128]{1,0:T(8,128)(2,1)S(1)} %get-tuple-element.56), channel_id=1, source_target_pairs={{0,28},{4,24},{8,20},{12,16},{16,12},{20,8},{24,4},{28,0},{1,29},{... | collective-permute-start | bytes 196616 | tf_op jit(solution)/shard_map/ppermute | solution.py:315
  35.0 2.0 %shard_map.157 = (bf16[1,1024,1024]{2,1,0:T(8,128)(2,1)S(1)}, bf16[8,256,128]{2,1,0:T(8,128)(2,1)S(1)}, f32[8,256,128]{2,1,0:T(8,128)S(1)}) custom-call(bf16[256,128]{1,0:T(8,128)(2,1)S(1)} %get-tuple-element.46.after_ref.refs_0_, f32[1,1024]{1,0:T(1,128)S(1)} %bitcast.14, bf16[1024,4096]{1,0:T(8,128)(2,1)} %weight_hbm.5, bf16[256,1024]{1,0:T(8,128)(2,1)} %query_hbm.1, ...), custom_call_target="tpu_custom_call" | custom-call | tf_op jit(solution)/shard_map/pallas_call | solution.py:391
  37.0 2.6 %collective-permute-done.13.refs_7_ = bf16[256,128]{1,0:T(8,128)(2,1)S(1)} collective-permute-done((bf16[256,128]{1,0:T(8,128)(2,1)S(1)}, bf16[256,128]{1,0:T(8,128)(2,1)S(1)}, u32[]{:S(2)}, u32[]{:S(2)}) %collective-permute-start.13) | collective-permute-done | bytes 65568 | tf_op jit(solution)/shard_map/ppermute | solution.py:315
  39.6 1.0 %shard_map.158 = (bf16[1,256,1024]{2,1,0:T(8,128)(2,1)S(1)}, bf16[256,1024]{1,0:T(8,128)(2,1)S(1)}) custom-call(bf16[8,256,128]{2,1,0:T(8,128)(2,1)S(1)} %get-tuple-element.47.query_ref, f32[8,256,128]{2,1,0:T(8,128)S(1)} %get-tuple-element.48.skip_ref, bf16[1,1024,1024]{2,1,0:T(8,128)(2,1)S(1)} %get-tuple-element.49.weight_ref, ...), custom_call_target="tpu_custom_call" | custom-call | tf_op jit(solution)/shard_map/pallas_call | solution.py:412
  40.6 0.7 %shard_map.160 = bf16[1,256,1024]{2,1,0:T(8,128)(2,1)S(1)} custom-call(bf16[256,1024]{1,0:T(8,128)(2,1)S(1)} %get-tuple-element.61.mixed_ref, bf16[1,1024,1024]{2,1,0:T(8,128)(2,1)S(1)} %get-tuple-element.60.weight_ref), custom_call_target="tpu_custom_call" | custom-call | tf_op jit(solution)/shard_map/pallas_call | solution.py:425
  41.4 0.7 %shard_map.159 = f32[1,256,1024]{2,1,0:T(8,128)S(1)} custom-call(bf16[256,1024]{1,0:T(8,128)(2,1)S(1)} %get-tuple-element.61.mixed_ref, bf16[1,1024,1024]{2,1,0:T(8,128)(2,1)S(1)} %get-tuple-element.58.weight_ref), custom_call_target="tpu_custom_call" | custom-call | tf_op jit(solution)/shard_map/pallas_call | solution.py:425
  42.9 1.5 %collective-permute-start.17 = (bf16[1,256,512]{2,1,0:T(8,128)(2,1)S(1)}, bf16[1,256,512]{2,1,0:T(8,128)(2,1)S(1)}, u32[]{:S(2)}, u32[]{:S(2)}) collective-permute-start(bf16[1,256,512]{2,1,0:T(8,128)(2,1)S(1)} %get-tuple-element.64), channel_id=1, source_target_pairs={{0,2},{1,3},{2,0},{3,1},{4,6},{5,7},{6,4},{7,5},{8,10},{9,11},{10,... | collective-permute-start | bytes 786440 | tf_op jit(solution)/shard_map/ppermute | solution.py:410
  45.0 2.3 %shard_map.161 = f32[1,256,1024]{2,1,0:T(8,128)S(1)} custom-call(bf16[256,1024]{1,0:T(8,128)(2,1)S(1)} %get-tuple-element.61.mixed_ref, bf16[1024,4096]{1,0:T(8,128)(2,1)} %weight_hbm.5), custom_call_target="tpu_custom_call" | custom-call | tf_op jit(solution)/shard_map/pallas_call | solution.py:439
  47.3 4.8 %collective-permute-done.17 = bf16[1,256,512]{2,1,0:T(8,128)(2,1)S(1)} collective-permute-done((bf16[1,256,512]{2,1,0:T(8,128)(2,1)S(1)}, bf16[1,256,512]{2,1,0:T(8,128)(2,1)S(1)}, u32[]{:S(2)}, u32[]{:S(2)}) %collective-permute-start.17) | collective-permute-done | bytes 262176 | tf_op jit(solution)/shard_map/ppermute | solution.py:410
  52.1 0.9 %shard_map.162.refs_3_ = f32[1024,256]{1,0:T(8,128)} custom-call(f32[256,1024]{1,0:T(8,128)S(1)} %bitcast.8, bf16[256,1024]{1,0:T(8,128)(2,1)S(1)} %bitcast.10, bf16[256,512]{1,0:T(8,128)(2,1)S(1)} %bitcast.12), custom_call_target="tpu_custom_call" | custom-call | tf_op jit(solution)/shard_map/pallas_call | solution.py:460
  53.0 4.1 %collective-permute-done.16 = bf16[1,256,512]{2,1,0:T(8,128)(2,1)S(1)} collective-permute-done((bf16[1,256,512]{2,1,0:T(8,128)(2,1)S(1)}, bf16[1,256,512]{2,1,0:T(8,128)(2,1)S(1)}, u32[]{:S(2)}, u32[]{:S(2)}) %collective-permute-start.16) | collective-permute-done | bytes 262176 | tf_op jit(solution)/shard_map/ppermute | solution.py:410
  57.1 0.9 %shard_map.163 = f32[1024,256]{1,0:T(8,128)} custom-call(f32[256,1024]{1,0:T(8,128)S(1)} %bitcast.9, bf16[256,1024]{1,0:T(8,128)(2,1)S(1)} %bitcast.11, bf16[256,512]{1,0:T(8,128)(2,1)S(1)} %bitcast.13, f32[1024,256]{1,0:T(8,128)} %shard_map.162.refs_3_), custom_call_target="tpu_custom_call", output_to_operand_aliasing={{}: (3, {})} | custom-call | tf_op jit(solution)/shard_map/pallas_call | solution.py:460
  (34 shorter events, 3.0 us)
Async XLA Ops:
  0.0 16.3 %copy-start = (f32[64,1024]{1,0:T(8,128)S(1)}, f32[64,1024]{1,0:T(8,128)}, u32[]{:S(2)}) copy-start(f32[64,1024]{1,0:T(8,128)} %param.24) | copy-start | bytes 786436
  1.5 8.0 %collective-permute-start = (bf16[256,128]{1,0:T(8,128)(2,1)S(1)}, bf16[256,128]{1,0:T(8,128)(2,1)S(1)}, u32[]{:S(2)}, u32[]{:S(2)}) collective-permute-start(bf16[256,128]{1,0:T(8,128)(2,1)S(1)} %get-tuple-element.39.refs_2_), channel_id=1, source_target_pairs={{0,8},{4,12},{8,0},{12,4},{16,24},{20,28},{24,16},{28,20},{1,9},{5... | collective-permute-start | bytes 196616 | tf_op jit(solution)/shard_map/ppermute | solution.py:315
  4.6 9.4 %collective-permute-start.1 = (bf16[256,128]{1,0:T(8,128)(2,1)S(1)}, bf16[256,128]{1,0:T(8,128)(2,1)S(1)}, u32[]{:S(2)}, u32[]{:S(2)}) collective-permute-start(bf16[256,128]{1,0:T(8,128)(2,1)S(1)} %get-tuple-element.40.refs_4_), channel_id=1, source_target_pairs={{0,16},{4,20},{8,24},{12,28},{16,0},{20,4},{24,8},{28,12},{1,17},{... | collective-permute-start | bytes 196616 | tf_op jit(solution)/shard_map/ppermute | solution.py:315
  7.1 13.5 %collective-permute-start.2 = (bf16[256,128]{1,0:T(8,128)(2,1)S(1)}, bf16[256,128]{1,0:T(8,128)(2,1)S(1)}, u32[]{:S(2)}, u32[]{:S(2)}) collective-permute-start(bf16[256,128]{1,0:T(8,128)(2,1)S(1)} %get-tuple-element.41.refs_6_), channel_id=1, source_target_pairs={{0,24},{4,28},{8,16},{12,20},{16,8},{20,12},{24,0},{28,4},{1,25},{... | collective-permute-start | bytes 196616 | tf_op jit(solution)/shard_map/ppermute | solution.py:315
  7.2 13.5 %collective-permute-start.3 = (bf16[256,128]{1,0:T(8,128)(2,1)S(1)}, bf16[256,128]{1,0:T(8,128)(2,1)S(1)}, u32[]{:S(2)}, u32[]{:S(2)}) collective-permute-start(bf16[256,128]{1,0:T(8,128)(2,1)S(1)} %get-tuple-element.42.refs_1_), channel_id=1, source_target_pairs={{0,4},{4,0},{8,12},{12,8},{16,20},{20,16},{24,28},{28,24},{1,5},{5... | collective-permute-start | bytes 196616 | tf_op jit(solution)/shard_map/ppermute | solution.py:315
  8.9 11.8 %collective-permute-start.4 = (bf16[256,128]{1,0:T(8,128)(2,1)S(1)}, bf16[256,128]{1,0:T(8,128)(2,1)S(1)}, u32[]{:S(2)}, u32[]{:S(2)}) collective-permute-start(bf16[256,128]{1,0:T(8,128)(2,1)S(1)} %get-tuple-element.43.refs_3_), channel_id=1, source_target_pairs={{0,12},{4,8},{8,4},{12,0},{16,28},{20,24},{24,20},{28,16},{1,13},{... | collective-permute-start | bytes 196616 | tf_op jit(solution)/shard_map/ppermute | solution.py:315
  9.5 11.2 %collective-permute-start.5 = (bf16[256,128]{1,0:T(8,128)(2,1)S(1)}, bf16[256,128]{1,0:T(8,128)(2,1)S(1)}, u32[]{:S(2)}, u32[]{:S(2)}) collective-permute-start(bf16[256,128]{1,0:T(8,128)(2,1)S(1)} %get-tuple-element.44.refs_5_), channel_id=1, source_target_pairs={{0,20},{4,16},{8,28},{12,24},{16,4},{20,0},{24,12},{28,8},{1,21},{... | collective-permute-start | bytes 196616 | tf_op jit(solution)/shard_map/ppermute | solution.py:315
  13.9 7.0 %collective-permute-start.6 = (bf16[256,128]{1,0:T(8,128)(2,1)S(1)}, bf16[256,128]{1,0:T(8,128)(2,1)S(1)}, u32[]{:S(2)}, u32[]{:S(2)}) collective-permute-start(bf16[256,128]{1,0:T(8,128)(2,1)S(1)} %get-tuple-element.45.refs_7_), channel_id=1, source_target_pairs={{0,28},{4,24},{8,20},{12,16},{16,12},{20,8},{24,4},{28,0},{1,29},{... | collective-permute-start | bytes 196616 | tf_op jit(solution)/shard_map/ppermute | solution.py:315
  16.3 4.6 %copy-start.1 = (bf16[256,512]{1,0:T(8,128)(2,1)S(1)}, bf16[256,512]{1,0:T(8,128)(2,1)}, u32[]{:S(2)}) copy-start(bf16[256,512]{1,0:T(8,128)(2,1)} %constant.26.inverse_ref) | copy-start | bytes 786436
  16.3 4.6 %copy-start.2 = (bf16[512,256]{1,0:T(8,128)(2,1)S(1)}, bf16[512,256]{1,0:T(8,128)(2,1)}, u32[]{:S(2)}) copy-start(bf16[512,256]{1,0:T(8,128)(2,1)} %constant.25.table_ref) | copy-start | bytes 786436
  16.3 4.6 %copy-start.4 = (s32[16]{0:T(128)S(1)}, s32[16]{0:T(128)}, u32[]{:S(2)}) copy-start(s32[16]{0:T(128)} %order_ref.1) | copy-start | bytes 196
  20.9 14.1 %copy-start.3 = (f32[1024]{0:T(1024)S(1)}, f32[1024]{0:T(1024)}, u32[]{:S(2)}) copy-start(f32[1024]{0:T(1024)} %param.26) | copy-start | bytes 12292
  23.8 6.4 %collective-permute-start.7 = (bf16[256,128]{1,0:T(8,128)(2,1)S(1)}, bf16[256,128]{1,0:T(8,128)(2,1)S(1)}, u32[]{:S(2)}, u32[]{:S(2)}) collective-permute-start(bf16[256,128]{1,0:T(8,128)(2,1)S(1)} %get-tuple-element.50), channel_id=1, source_target_pairs={{0,8},{4,12},{8,0},{12,4},{16,24},{20,28},{24,16},{28,20},{1,9},{5... | collective-permute-start | bytes 196616 | tf_op jit(solution)/shard_map/ppermute | solution.py:315
  23.9 8.8 %collective-permute-start.8 = (bf16[256,128]{1,0:T(8,128)(2,1)S(1)}, bf16[256,128]{1,0:T(8,128)(2,1)S(1)}, u32[]{:S(2)}, u32[]{:S(2)}) collective-permute-start(bf16[256,128]{1,0:T(8,128)(2,1)S(1)} %get-tuple-element.51), channel_id=1, source_target_pairs={{0,16},{4,20},{8,24},{12,28},{16,0},{20,4},{24,8},{28,12},{1,17},{... | collective-permute-start | bytes 196616 | tf_op jit(solution)/shard_map/ppermute | solution.py:315
  25.8 11.2 %collective-permute-start.9 = (bf16[256,128]{1,0:T(8,128)(2,1)S(1)}, bf16[256,128]{1,0:T(8,128)(2,1)S(1)}, u32[]{:S(2)}, u32[]{:S(2)}) collective-permute-start(bf16[256,128]{1,0:T(8,128)(2,1)S(1)} %get-tuple-element.52), channel_id=1, source_target_pairs={{0,24},{4,28},{8,16},{12,20},{16,8},{20,12},{24,0},{28,4},{1,25},{... | collective-permute-start | bytes 196616 | tf_op jit(solution)/shard_map/ppermute | solution.py:315
  28.2 8.8 %collective-permute-start.10 = (bf16[256,128]{1,0:T(8,128)(2,1)S(1)}, bf16[256,128]{1,0:T(8,128)(2,1)S(1)}, u32[]{:S(2)}, u32[]{:S(2)}) collective-permute-start(bf16[256,128]{1,0:T(8,128)(2,1)S(1)} %get-tuple-element.53), channel_id=1, source_target_pairs={{0,4},{4,0},{8,12},{12,8},{16,20},{20,16},{24,28},{28,24},{1,5},{5... | collective-permute-start | bytes 196616 | tf_op jit(solution)/shard_map/ppermute | solution.py:315
  28.8 8.2 %collective-permute-start.11 = (bf16[256,128]{1,0:T(8,128)(2,1)S(1)}, bf16[256,128]{1,0:T(8,128)(2,1)S(1)}, u32[]{:S(2)}, u32[]{:S(2)}) collective-permute-start(bf16[256,128]{1,0:T(8,128)(2,1)S(1)} %get-tuple-element.54), channel_id=1, source_target_pairs={{0,12},{4,8},{8,4},{12,0},{16,28},{20,24},{24,20},{28,16},{1,13},{... | collective-permute-start | bytes 196616 | tf_op jit(solution)/shard_map/ppermute | solution.py:315
  30.1 6.9 %collective-permute-start.12 = (bf16[256,128]{1,0:T(8,128)(2,1)S(1)}, bf16[256,128]{1,0:T(8,128)(2,1)S(1)}, u32[]{:S(2)}, u32[]{:S(2)}) collective-permute-start(bf16[256,128]{1,0:T(8,128)(2,1)S(1)} %get-tuple-element.55), channel_id=1, source_target_pairs={{0,20},{4,16},{8,28},{12,24},{16,4},{20,0},{24,12},{28,8},{1,21},{... | collective-permute-start | bytes 196616 | tf_op jit(solution)/shard_map/ppermute | solution.py:315
  32.6 7.0 %collective-permute-start.13 = (bf16[256,128]{1,0:T(8,128)(2,1)S(1)}, bf16[256,128]{1,0:T(8,128)(2,1)S(1)}, u32[]{:S(2)}, u32[]{:S(2)}) collective-permute-start(bf16[256,128]{1,0:T(8,128)(2,1)S(1)} %get-tuple-element.56), channel_id=1, source_target_pairs={{0,28},{4,24},{8,20},{12,16},{16,12},{20,8},{24,4},{28,0},{1,29},{... | collective-permute-start | bytes 196616 | tf_op jit(solution)/shard_map/ppermute | solution.py:315
  40.6 2.0 %collective-permute-start.14 = (bf16[1,256,1024]{2,1,0:T(8,128)(2,1)S(1)}, bf16[1,256,1024]{2,1,0:T(8,128)(2,1)S(1)}, u32[]{:S(2)}, u32[]{:S(2)}) collective-permute-start(bf16[1,256,1024]{2,1,0:T(8,128)(2,1)S(1)} %get-tuple-element.59), channel_id=1, source_target_pairs={{0,1},{1,0},{2,3},{3,2},{4,5},{5,4},{6,7},{7,6},{8,9},{9,8},{10,11... | collective-permute-start | bytes 1572872 | tf_op jit(solution)/shard_map/ppermute | solution.py:410
  42.7 9.3 %collective-permute-start.15 = (bf16[1,256,1024]{2,1,0:T(8,128)(2,1)S(1)}, bf16[1,256,1024]{2,1,0:T(8,128)(2,1)S(1)}, u32[]{:S(2)}, u32[]{:S(2)}) collective-permute-start(bf16[1,256,1024]{2,1,0:T(8,128)(2,1)S(1)} %shard_map.160), channel_id=1, source_target_pairs={{0,1},{1,0},{2,3},{3,2},{4,5},{5,4},{6,7},{7,6},{8,9},{9,8},{10,11... | collective-permute-start | bytes 1572872 | tf_op jit(solution)/shard_map/ppermute | solution.py:410
  42.9 9.1 %collective-permute-start.17 = (bf16[1,256,512]{2,1,0:T(8,128)(2,1)S(1)}, bf16[1,256,512]{2,1,0:T(8,128)(2,1)S(1)}, u32[]{:S(2)}, u32[]{:S(2)}) collective-permute-start(bf16[1,256,512]{2,1,0:T(8,128)(2,1)S(1)} %get-tuple-element.64), channel_id=1, source_target_pairs={{0,2},{1,3},{2,0},{3,1},{4,6},{5,7},{6,4},{7,5},{8,10},{9,11},{10,... | collective-permute-start | bytes 786440 | tf_op jit(solution)/shard_map/ppermute | solution.py:410
  44.4 12.7 %collective-permute-start.16 = (bf16[1,256,512]{2,1,0:T(8,128)(2,1)S(1)}, bf16[1,256,512]{2,1,0:T(8,128)(2,1)S(1)}, u32[]{:S(2)}, u32[]{:S(2)}) collective-permute-start(bf16[1,256,512]{2,1,0:T(8,128)(2,1)S(1)} %get-tuple-element.63), channel_id=1, source_target_pairs={{0,2},{1,3},{2,0},{3,1},{4,6},{5,7},{6,4},{7,5},{8,10},{9,11},{10,... | collective-permute-start | bytes 786440 | tf_op jit(solution)/shard_map/ppermute | solution.py:410

commit v13 on v12

--- a/solution.py
+++ b/solution.py
@@ -308,7 +308,8 @@
     unit = width if width % LANES == 0 else chan_width
     pieces = chan_width // unit
 
-    arrival = sorted(range(seq_count), key=lambda k: (k & 1, k))
+    middle = seq_count // 2
+    arrival = [k for near in range(middle) for k in (near, near + middle)]
 
     def swap(arrays):
         return [arrays[0]] + [

time: 58.3 us -> 57 us (0.978)
  starting transfers between devices: 27.1 us -> 25.6 us
    ppermute x14, starting transfers between devices: 24.8 us -> 23.3 us  [swap(): lax.ppermute(arrays[k], 'seq', [(d, d ^ k) for d in range(seq_count)])]
  transfers between devices with their start and end apart: 18 -> 18, of which waited for: 6 -> 7; matrix products, arithmetic and copies ran while one was open for 0% -> 0% of each run, Pallas kernels for 19% -> 19%
where the time goes in v13:
time: 57 us; the launch traced here: 56.8 us
  starting transfers between devices  25.6 us (45%)
  Pallas kernels  17.2 us (30%)
  waiting for transfers between devices  13.7 us (24%)
    ppermute x14, starting transfers between devices, swap(): lax.ppermute(arrays[k], 'seq', [(d, d ^ k) for d in range(seq_count)])  23.3 us
    ppermute x4, waiting for transfers between devices, exchange(): lax.ppermute(terms, 'chan', [(d, d ^ bit) for d in range(chan_count)])  9.37 us
    ppermute x14, waiting for transfers between devices, swap(): lax.ppermute(arrays[k], 'seq', [(d, d ^ k) for d in range(seq_count)])  4.33 us
    pallas_call x1, Pallas kernels, local(): pl.pallas_call(functools.partial(filter_kernel, block, far_odd, pieces >...  4.31 us
    pallas_call x1, Pallas kernels, local(): pl.pallas_call(functools.partial(conv_kernel, block, blocks_kept, arrival...  2.85 us
    ppermute x4, starting transfers between devices, exchange(): lax.ppermute(terms, 'chan', [(d, d ^ bit) for d in range(chan_count)])  2.31 us
    pallas_call x1, Pallas kernels, local(): pl.pallas_call(functools.partial(last_kernel, blocks_last), out_shape=jax...  2.31 us
    pallas_call x1, Pallas kernels, local(): pl.pallas_call(functools.partial(copy_kernel, near_odd), out_shape=(jax.S...  1.99 us
  transfers between devices with their start and end apart: 18, of which 7 were waited for; matrix products, arithmetic and copies ran while one was open for 0% of the time, Pallas kernels for 19%

profile of v13, /device:TPU:0, one launch (start us, length us, event | category | flops | bytes accessed | tf_op | source)
XLA Modules:
  0.0 56.8 jit_solution(6903698721834249480)
XLA Ops:
  0.0 1.5 %shard_map.155 = (bf16[256,128]{1,0:T(8,128)(2,1)S(1)}, bf16[256,128]{1,0:T(8,128)(2,1)S(1)}, bf16[256,128]{1,0:T(8,128)(2,1)S(1)}, bf16[256,128]{1,0:T(8,128)(2...) custom-call(bf16[256,1024]{1,0:T(8,128)(2,1)} %key_hbm.1, ...), custom_call_target="tpu_custom_call" | custom-call | tf_op jit(solution)/shard_map/pallas_call | solution.py:319
  1.5 4.1 %collective-permute-start = (bf16[256,128]{1,0:T(8,128)(2,1)S(1)}, bf16[256,128]{1,0:T(8,128)(2,1)S(1)}, u32[]{:S(2)}, u32[]{:S(2)}) collective-permute-start(bf16[256,128]{1,0:T(8,128)(2,1)S(1)} %get-tuple-element.39.refs_4_), channel_id=1, source_target_pairs={{0,16},{4,20},{8,24},{12,28},{16,0},{20,4},{24,8},{28,12},{1,17},{... | collective-permute-start | bytes 196616 | tf_op jit(solution)/shard_map/ppermute | solution.py:316
  5.6 1.5 %collective-permute-start.1 = (bf16[256,128]{1,0:T(8,128)(2,1)S(1)}, bf16[256,128]{1,0:T(8,128)(2,1)S(1)}, u32[]{:S(2)}, u32[]{:S(2)}) collective-permute-start(bf16[256,128]{1,0:T(8,128)(2,1)S(1)} %get-tuple-element.40.refs_1_), channel_id=1, source_target_pairs={{0,4},{4,0},{8,12},{12,8},{16,20},{20,16},{24,28},{28,24},{1,5},{5... | collective-permute-start | bytes 196616 | tf_op jit(solution)/shard_map/ppermute | solution.py:316
  7.1 1.8 %collective-permute-start.3 = (bf16[256,128]{1,0:T(8,128)(2,1)S(1)}, bf16[256,128]{1,0:T(8,128)(2,1)S(1)}, u32[]{:S(2)}, u32[]{:S(2)}) collective-permute-start(bf16[256,128]{1,0:T(8,128)(2,1)S(1)} %get-tuple-element.42.refs_2_), channel_id=1, source_target_pairs={{0,8},{4,12},{8,0},{12,4},{16,24},{20,28},{24,16},{28,20},{1,9},{5... | collective-permute-start | bytes 196616 | tf_op jit(solution)/shard_map/ppermute | solution.py:316
  8.9 2.5 %collective-permute-start.4 = (bf16[256,128]{1,0:T(8,128)(2,1)S(1)}, bf16[256,128]{1,0:T(8,128)(2,1)S(1)}, u32[]{:S(2)}, u32[]{:S(2)}) collective-permute-start(bf16[256,128]{1,0:T(8,128)(2,1)S(1)} %get-tuple-element.43.refs_6_), channel_id=1, source_target_pairs={{0,24},{4,28},{8,16},{12,20},{16,8},{20,12},{24,0},{28,4},{1,25},{... | collective-permute-start | bytes 196616 | tf_op jit(solution)/shard_map/ppermute | solution.py:316
  11.4 1.6 %collective-permute-start.5 = (bf16[256,128]{1,0:T(8,128)(2,1)S(1)}, bf16[256,128]{1,0:T(8,128)(2,1)S(1)}, u32[]{:S(2)}, u32[]{:S(2)}) collective-permute-start(bf16[256,128]{1,0:T(8,128)(2,1)S(1)} %get-tuple-element.44.refs_3_), channel_id=1, source_target_pairs={{0,12},{4,8},{8,4},{12,0},{16,28},{20,24},{24,20},{28,16},{1,13},{... | collective-permute-start | bytes 196616 | tf_op jit(solution)/shard_map/ppermute | solution.py:316
  13.0 2.4 %collective-permute-start.6 = (bf16[256,128]{1,0:T(8,128)(2,1)S(1)}, bf16[256,128]{1,0:T(8,128)(2,1)S(1)}, u32[]{:S(2)}, u32[]{:S(2)}) collective-permute-start(bf16[256,128]{1,0:T(8,128)(2,1)S(1)} %get-tuple-element.45.refs_7_), channel_id=1, source_target_pairs={{0,28},{4,24},{8,20},{12,16},{16,12},{20,8},{24,4},{28,0},{1,29},{... | collective-permute-start | bytes 196616 | tf_op jit(solution)/shard_map/ppermute | solution.py:316
  15.4 4.3 %shard_map.154 = (f32[8,256,128]{2,1,0:T(8,128)S(1)}, f32[8,256,128]{2,1,0:T(8,128)S(1)}, f32[8,16,128]{2,1,0:T(8,128)S(1)}, bf16[1,1024,1024]{2,1,0:T(8,128)(2,1)S(1)}) custom-call(f32[64,128]{1,0:T(8,128)S(1)} %constant_dynamic-slice_fusion.out_w_ref, f32[40,2048]{1,0:T(8,128)} %constant.23.clone.refs_0_, f32[33,64]{1,0:T(8,128)} %refs_1_.1, ...), custom_call_target="tpu_custom_call" | custom-call | tf_op jit(solution)/shard_map/pallas_call | solution.py:352
  20.0 2.8 %shard_map.156 = (bf16[256,128]{1,0:T(8,128)(2,1)S(1)}, bf16[256,128]{1,0:T(8,128)(2,1)S(1)}, bf16[256,128]{1,0:T(8,128)(2,1)S(1)}, bf16[256,128]{1,0:T(8,128)(2...) custom-call(s32[16]{0:T(128)S(1)} %copy-done.4, ...), custom_call_target="tpu_custom_call" | custom-call | tf_op jit(solution)/shard_map/pallas_call | solution.py:374
  22.9 1.3 %collective-permute-start.7 = (bf16[256,128]{1,0:T(8,128)(2,1)S(1)}, bf16[256,128]{1,0:T(8,128)(2,1)S(1)}, u32[]{:S(2)}, u32[]{:S(2)}) collective-permute-start(bf16[256,128]{1,0:T(8,128)(2,1)S(1)} %get-tuple-element.50), channel_id=1, source_target_pairs={{0,16},{4,20},{8,24},{12,28},{16,0},{20,4},{24,8},{28,12},{1,17},{... | collective-permute-start | bytes 196616 | tf_op jit(solution)/shard_map/ppermute | solution.py:316
  24.2 1.1 %collective-permute-start.8 = (bf16[256,128]{1,0:T(8,128)(2,1)S(1)}, bf16[256,128]{1,0:T(8,128)(2,1)S(1)}, u32[]{:S(2)}, u32[]{:S(2)}) collective-permute-start(bf16[256,128]{1,0:T(8,128)(2,1)S(1)} %get-tuple-element.51), channel_id=1, source_target_pairs={{0,4},{4,0},{8,12},{12,8},{16,20},{20,16},{24,28},{28,24},{1,5},{5... | collective-permute-start | bytes 196616 | tf_op jit(solution)/shard_map/ppermute | solution.py:316
  25.3 2.0 %collective-permute-start.9 = (bf16[256,128]{1,0:T(8,128)(2,1)S(1)}, bf16[256,128]{1,0:T(8,128)(2,1)S(1)}, u32[]{:S(2)}, u32[]{:S(2)}) collective-permute-start(bf16[256,128]{1,0:T(8,128)(2,1)S(1)} %get-tuple-element.52), channel_id=1, source_target_pairs={{0,20},{4,16},{8,28},{12,24},{16,4},{20,0},{24,12},{28,8},{1,21},{... | collective-permute-start | bytes 196616 | tf_op jit(solution)/shard_map/ppermute | solution.py:316
  27.3 1.0 %collective-permute-start.10 = (bf16[256,128]{1,0:T(8,128)(2,1)S(1)}, bf16[256,128]{1,0:T(8,128)(2,1)S(1)}, u32[]{:S(2)}, u32[]{:S(2)}) collective-permute-start(bf16[256,128]{1,0:T(8,128)(2,1)S(1)} %get-tuple-element.53), channel_id=1, source_target_pairs={{0,8},{4,12},{8,0},{12,4},{16,24},{20,28},{24,16},{28,20},{1,9},{5... | collective-permute-start | bytes 196616 | tf_op jit(solution)/shard_map/ppermute | solution.py:316
  28.3 1.8 %collective-permute-start.11 = (bf16[256,128]{1,0:T(8,128)(2,1)S(1)}, bf16[256,128]{1,0:T(8,128)(2,1)S(1)}, u32[]{:S(2)}, u32[]{:S(2)}) collective-permute-start(bf16[256,128]{1,0:T(8,128)(2,1)S(1)} %get-tuple-element.54), channel_id=1, source_target_pairs={{0,24},{4,28},{8,16},{12,20},{16,8},{20,12},{24,0},{28,4},{1,25},{... | collective-permute-start | bytes 196616 | tf_op jit(solution)/shard_map/ppermute | solution.py:316
  30.1 1.3 %collective-permute-done.7.refs_1_ = bf16[256,128]{1,0:T(8,128)(2,1)S(1)} collective-permute-done((bf16[256,128]{1,0:T(8,128)(2,1)S(1)}, bf16[256,128]{1,0:T(8,128)(2,1)S(1)}, u32[]{:S(2)}, u32[]{:S(2)}) %collective-permute-start.7) | collective-permute-done | bytes 65568 | tf_op jit(solution)/shard_map/ppermute | solution.py:316
  31.4 2.1 %collective-permute-start.13 = (bf16[256,128]{1,0:T(8,128)(2,1)S(1)}, bf16[256,128]{1,0:T(8,128)(2,1)S(1)}, u32[]{:S(2)}, u32[]{:S(2)}) collective-permute-start(bf16[256,128]{1,0:T(8,128)(2,1)S(1)} %get-tuple-element.56), channel_id=1, source_target_pairs={{0,28},{4,24},{8,20},{12,16},{16,12},{20,8},{24,4},{28,0},{1,29},{... | collective-permute-start | bytes 196616 | tf_op jit(solution)/shard_map/ppermute | solution.py:316
  33.5 2.0 %shard_map.157 = (bf16[1,1024,1024]{2,1,0:T(8,128)(2,1)S(1)}, bf16[8,256,128]{2,1,0:T(8,128)(2,1)S(1)}, f32[8,256,128]{2,1,0:T(8,128)S(1)}) custom-call(bf16[256,128]{1,0:T(8,128)(2,1)S(1)} %get-tuple-element.46.after_ref.refs_0_, f32[1,1024]{1,0:T(1,128)S(1)} %bitcast.14, bf16[1024,4096]{1,0:T(8,128)(2,1)} %weight_hbm.5, bf16[256,1024]{1,0:T(8,128)(2,1)} %query_hbm.1, ...), custom_call_target="tpu_custom_call" | custom-call | tf_op jit(solution)/shard_map/pallas_call | solution.py:392
  35.6 1.0 %collective-permute-done.12.refs_6_ = bf16[256,128]{1,0:T(8,128)(2,1)S(1)} collective-permute-done((bf16[256,128]{1,0:T(8,128)(2,1)S(1)}, bf16[256,128]{1,0:T(8,128)(2,1)S(1)}, u32[]{:S(2)}, u32[]{:S(2)}) %collective-permute-start.12) | collective-permute-done | bytes 65568 | tf_op jit(solution)/shard_map/ppermute | solution.py:316
  36.6 1.8 %collective-permute-done.13.refs_7_ = bf16[256,128]{1,0:T(8,128)(2,1)S(1)} collective-permute-done((bf16[256,128]{1,0:T(8,128)(2,1)S(1)}, bf16[256,128]{1,0:T(8,128)(2,1)S(1)}, u32[]{:S(2)}, u32[]{:S(2)}) %collective-permute-start.13) | collective-permute-done | bytes 65568 | tf_op jit(solution)/shard_map/ppermute | solution.py:316
  38.4 1.0 %shard_map.158 = (bf16[1,256,1024]{2,1,0:T(8,128)(2,1)S(1)}, bf16[256,1024]{1,0:T(8,128)(2,1)S(1)}) custom-call(bf16[8,256,128]{2,1,0:T(8,128)(2,1)S(1)} %get-tuple-element.47.query_ref, f32[8,256,128]{2,1,0:T(8,128)S(1)} %get-tuple-element.48.skip_ref, bf16[1,1024,1024]{2,1,0:T(8,128)(2,1)S(1)} %get-tuple-element.49.weight_ref, ...), custom_call_target="tpu_custom_call" | custom-call | tf_op jit(solution)/shard_map/pallas_call | solution.py:413
  41.7 1.6 %collective-permute-start.17 = (bf16[1,256,512]{2,1,0:T(8,128)(2,1)S(1)}, bf16[1,256,512]{2,1,0:T(8,128)(2,1)S(1)}, u32[]{:S(2)}, u32[]{:S(2)}) collective-permute-start(bf16[1,256,512]{2,1,0:T(8,128)(2,1)S(1)} %get-tuple-element.64), channel_id=1, source_target_pairs={{0,2},{1,3},{2,0},{3,1},{4,6},{5,7},{6,4},{7,5},{8,10},{9,11},{10,... | collective-permute-start | bytes 786440 | tf_op jit(solution)/shard_map/ppermute | solution.py:411
  43.7 2.3 %shard_map.161 = f32[1,256,1024]{2,1,0:T(8,128)S(1)} custom-call(bf16[256,1024]{1,0:T(8,128)(2,1)S(1)} %get-tuple-element.61.mixed_ref, bf16[1024,4096]{1,0:T(8,128)(2,1)} %weight_hbm.5), custom_call_target="tpu_custom_call" | custom-call | tf_op jit(solution)/shard_map/pallas_call | solution.py:440
  46.0 4.8 %collective-permute-done.17 = bf16[1,256,512]{2,1,0:T(8,128)(2,1)S(1)} collective-permute-done((bf16[1,256,512]{2,1,0:T(8,128)(2,1)S(1)}, bf16[1,256,512]{2,1,0:T(8,128)(2,1)S(1)}, u32[]{:S(2)}, u32[]{:S(2)}) %collective-permute-start.17) | collective-permute-done | bytes 262176 | tf_op jit(solution)/shard_map/ppermute | solution.py:411
  51.8 4.1 %collective-permute-done.16 = bf16[1,256,512]{2,1,0:T(8,128)(2,1)S(1)} collective-permute-done((bf16[1,256,512]{2,1,0:T(8,128)(2,1)S(1)}, bf16[1,256,512]{2,1,0:T(8,128)(2,1)S(1)}, u32[]{:S(2)}, u32[]{:S(2)}) %collective-permute-start.16) | collective-permute-done | bytes 262176 | tf_op jit(solution)/shard_map/ppermute | solution.py:411
  (34 shorter events, 4.9 us)
Async XLA Ops:
  0.0 15.4 %copy-start = (f32[64,1024]{1,0:T(8,128)S(1)}, f32[64,1024]{1,0:T(8,128)}, u32[]{:S(2)}) copy-start(f32[64,1024]{1,0:T(8,128)} %param.24) | copy-start | bytes 786436
  1.5 10.0 %collective-permute-start = (bf16[256,128]{1,0:T(8,128)(2,1)S(1)}, bf16[256,128]{1,0:T(8,128)(2,1)S(1)}, u32[]{:S(2)}, u32[]{:S(2)}) collective-permute-start(bf16[256,128]{1,0:T(8,128)(2,1)S(1)} %get-tuple-element.39.refs_4_), channel_id=1, source_target_pairs={{0,16},{4,20},{8,24},{12,28},{16,0},{20,4},{24,8},{28,12},{1,17},{... | collective-permute-start | bytes 196616 | tf_op jit(solution)/shard_map/ppermute | solution.py:316
  5.6 7.5 %collective-permute-start.1 = (bf16[256,128]{1,0:T(8,128)(2,1)S(1)}, bf16[256,128]{1,0:T(8,128)(2,1)S(1)}, u32[]{:S(2)}, u32[]{:S(2)}) collective-permute-start(bf16[256,128]{1,0:T(8,128)(2,1)S(1)} %get-tuple-element.40.refs_1_), channel_id=1, source_target_pairs={{0,4},{4,0},{8,12},{12,8},{16,20},{20,16},{24,28},{28,24},{1,5},{5... | collective-permute-start | bytes 196616 | tf_op jit(solution)/shard_map/ppermute | solution.py:316
  7.1 12.7 %collective-permute-start.2 = (bf16[256,128]{1,0:T(8,128)(2,1)S(1)}, bf16[256,128]{1,0:T(8,128)(2,1)S(1)}, u32[]{:S(2)}, u32[]{:S(2)}) collective-permute-start(bf16[256,128]{1,0:T(8,128)(2,1)S(1)} %get-tuple-element.41.refs_5_), channel_id=1, source_target_pairs={{0,20},{4,16},{8,28},{12,24},{16,4},{20,0},{24,12},{28,8},{1,21},{... | collective-permute-start | bytes 196616 | tf_op jit(solution)/shard_map/ppermute | solution.py:316
  7.1 12.7 %collective-permute-start.3 = (bf16[256,128]{1,0:T(8,128)(2,1)S(1)}, bf16[256,128]{1,0:T(8,128)(2,1)S(1)}, u32[]{:S(2)}, u32[]{:S(2)}) collective-permute-start(bf16[256,128]{1,0:T(8,128)(2,1)S(1)} %get-tuple-element.42.refs_2_), channel_id=1, source_target_pairs={{0,8},{4,12},{8,0},{12,4},{16,24},{20,28},{24,16},{28,20},{1,9},{5... | collective-permute-start | bytes 196616 | tf_op jit(solution)/shard_map/ppermute | solution.py:316
  8.9 10.8 %collective-permute-start.4 = (bf16[256,128]{1,0:T(8,128)(2,1)S(1)}, bf16[256,128]{1,0:T(8,128)(2,1)S(1)}, u32[]{:S(2)}, u32[]{:S(2)}) collective-permute-start(bf16[256,128]{1,0:T(8,128)(2,1)S(1)} %get-tuple-element.43.refs_6_), channel_id=1, source_target_pairs={{0,24},{4,28},{8,16},{12,20},{16,8},{20,12},{24,0},{28,4},{1,25},{... | collective-permute-start | bytes 196616 | tf_op jit(solution)/shard_map/ppermute | solution.py:316
  11.4 8.4 %collective-permute-start.5 = (bf16[256,128]{1,0:T(8,128)(2,1)S(1)}, bf16[256,128]{1,0:T(8,128)(2,1)S(1)}, u32[]{:S(2)}, u32[]{:S(2)}) collective-permute-start(bf16[256,128]{1,0:T(8,128)(2,1)S(1)} %get-tuple-element.44.refs_3_), channel_id=1, source_target_pairs={{0,12},{4,8},{8,4},{12,0},{16,28},{20,24},{24,20},{28,16},{1,13},{... | collective-permute-start | bytes 196616 | tf_op jit(solution)/shard_map/ppermute | solution.py:316
  13.0 7.0 %collective-permute-start.6 = (bf16[256,128]{1,0:T(8,128)(2,1)S(1)}, bf16[256,128]{1,0:T(8,128)(2,1)S(1)}, u32[]{:S(2)}, u32[]{:S(2)}) collective-permute-start(bf16[256,128]{1,0:T(8,128)(2,1)S(1)} %get-tuple-element.45.refs_7_), channel_id=1, source_target_pairs={{0,28},{4,24},{8,20},{12,16},{16,12},{20,8},{24,4},{28,0},{1,29},{... | collective-permute-start | bytes 196616 | tf_op jit(solution)/shard_map/ppermute | solution.py:316
  15.4 4.6 %copy-start.1 = (bf16[256,512]{1,0:T(8,128)(2,1)S(1)}, bf16[256,512]{1,0:T(8,128)(2,1)}, u32[]{:S(2)}) copy-start(bf16[256,512]{1,0:T(8,128)(2,1)} %constant.26.inverse_ref) | copy-start | bytes 786436
  15.4 4.6 %copy-start.2 = (bf16[512,256]{1,0:T(8,128)(2,1)S(1)}, bf16[512,256]{1,0:T(8,128)(2,1)}, u32[]{:S(2)}) copy-start(bf16[512,256]{1,0:T(8,128)(2,1)} %constant.25.table_ref) | copy-start | bytes 786436
  15.4 4.6 %copy-start.4 = (s32[16]{0:T(128)S(1)}, s32[16]{0:T(128)}, u32[]{:S(2)}) copy-start(s32[16]{0:T(128)} %order_ref.1) | copy-start | bytes 196
  20.0 13.5 %copy-start.3 = (f32[1024]{0:T(1024)S(1)}, f32[1024]{0:T(1024)}, u32[]{:S(2)}) copy-start(f32[1024]{0:T(1024)} %param.26) | copy-start | bytes 12292
  22.9 8.5 %collective-permute-start.7 = (bf16[256,128]{1,0:T(8,128)(2,1)S(1)}, bf16[256,128]{1,0:T(8,128)(2,1)S(1)}, u32[]{:S(2)}, u32[]{:S(2)}) collective-permute-start(bf16[256,128]{1,0:T(8,128)(2,1)S(1)} %get-tuple-element.50), channel_id=1, source_target_pairs={{0,16},{4,20},{8,24},{12,28},{16,0},{20,4},{24,8},{28,12},{1,17},{... | collective-permute-start | bytes 196616 | tf_op jit(solution)/shard_map/ppermute | solution.py:316
  24.2 7.2 %collective-permute-start.8 = (bf16[256,128]{1,0:T(8,128)(2,1)S(1)}, bf16[256,128]{1,0:T(8,128)(2,1)S(1)}, u32[]{:S(2)}, u32[]{:S(2)}) collective-permute-start(bf16[256,128]{1,0:T(8,128)(2,1)S(1)} %get-tuple-element.51), channel_id=1, source_target_pairs={{0,4},{4,0},{8,12},{12,8},{16,20},{20,16},{24,28},{28,24},{1,5},{5... | collective-permute-start | bytes 196616 | tf_op jit(solution)/shard_map/ppermute | solution.py:316
  25.3 10.2 %collective-permute-start.9 = (bf16[256,128]{1,0:T(8,128)(2,1)S(1)}, bf16[256,128]{1,0:T(8,128)(2,1)S(1)}, u32[]{:S(2)}, u32[]{:S(2)}) collective-permute-start(bf16[256,128]{1,0:T(8,128)(2,1)S(1)} %get-tuple-element.52), channel_id=1, source_target_pairs={{0,20},{4,16},{8,28},{12,24},{16,4},{20,0},{24,12},{28,8},{1,21},{... | collective-permute-start | bytes 196616 | tf_op jit(solution)/shard_map/ppermute | solution.py:316
  27.3 8.2 %collective-permute-start.10 = (bf16[256,128]{1,0:T(8,128)(2,1)S(1)}, bf16[256,128]{1,0:T(8,128)(2,1)S(1)}, u32[]{:S(2)}, u32[]{:S(2)}) collective-permute-start(bf16[256,128]{1,0:T(8,128)(2,1)S(1)} %get-tuple-element.53), channel_id=1, source_target_pairs={{0,8},{4,12},{8,0},{12,4},{16,24},{20,28},{24,16},{28,20},{1,9},{5... | collective-permute-start | bytes 196616 | tf_op jit(solution)/shard_map/ppermute | solution.py:316
  28.3 7.3 %collective-permute-start.11 = (bf16[256,128]{1,0:T(8,128)(2,1)S(1)}, bf16[256,128]{1,0:T(8,128)(2,1)S(1)}, u32[]{:S(2)}, u32[]{:S(2)}) collective-permute-start(bf16[256,128]{1,0:T(8,128)(2,1)S(1)} %get-tuple-element.54), channel_id=1, source_target_pairs={{0,24},{4,28},{8,16},{12,20},{16,8},{20,12},{24,0},{28,4},{1,25},{... | collective-permute-start | bytes 196616 | tf_op jit(solution)/shard_map/ppermute | solution.py:316
  31.4 5.2 %collective-permute-start.12 = (bf16[256,128]{1,0:T(8,128)(2,1)S(1)}, bf16[256,128]{1,0:T(8,128)(2,1)S(1)}, u32[]{:S(2)}, u32[]{:S(2)}) collective-permute-start(bf16[256,128]{1,0:T(8,128)(2,1)S(1)} %get-tuple-element.55), channel_id=1, source_target_pairs={{0,12},{4,8},{8,4},{12,0},{16,28},{20,24},{24,20},{28,16},{1,13},{... | collective-permute-start | bytes 196616 | tf_op jit(solution)/shard_map/ppermute | solution.py:316
  31.4 7.0 %collective-permute-start.13 = (bf16[256,128]{1,0:T(8,128)(2,1)S(1)}, bf16[256,128]{1,0:T(8,128)(2,1)S(1)}, u32[]{:S(2)}, u32[]{:S(2)}) collective-permute-start(bf16[256,128]{1,0:T(8,128)(2,1)S(1)} %get-tuple-element.56), channel_id=1, source_target_pairs={{0,28},{4,24},{8,20},{12,16},{16,12},{20,8},{24,4},{28,0},{1,29},{... | collective-permute-start | bytes 196616 | tf_op jit(solution)/shard_map/ppermute | solution.py:316
  39.3 2.0 %collective-permute-start.14 = (bf16[1,256,1024]{2,1,0:T(8,128)(2,1)S(1)}, bf16[1,256,1024]{2,1,0:T(8,128)(2,1)S(1)}, u32[]{:S(2)}, u32[]{:S(2)}) collective-permute-start(bf16[1,256,1024]{2,1,0:T(8,128)(2,1)S(1)} %get-tuple-element.59), channel_id=1, source_target_pairs={{0,1},{1,0},{2,3},{3,2},{4,5},{5,4},{6,7},{7,6},{8,9},{9,8},{10,11... | collective-permute-start | bytes 1572872 | tf_op jit(solution)/shard_map/ppermute | solution.py:411
  41.5 9.3 %collective-permute-start.15 = (bf16[1,256,1024]{2,1,0:T(8,128)(2,1)S(1)}, bf16[1,256,1024]{2,1,0:T(8,128)(2,1)S(1)}, u32[]{:S(2)}, u32[]{:S(2)}) collective-permute-start(bf16[1,256,1024]{2,1,0:T(8,128)(2,1)S(1)} %shard_map.160), channel_id=1, source_target_pairs={{0,1},{1,0},{2,3},{3,2},{4,5},{5,4},{6,7},{7,6},{8,9},{9,8},{10,11... | collective-permute-start | bytes 1572872 | tf_op jit(solution)/shard_map/ppermute | solution.py:411
  41.7 9.1 %collective-permute-start.17 = (bf16[1,256,512]{2,1,0:T(8,128)(2,1)S(1)}, bf16[1,256,512]{2,1,0:T(8,128)(2,1)S(1)}, u32[]{:S(2)}, u32[]{:S(2)}) collective-permute-start(bf16[1,256,512]{2,1,0:T(8,128)(2,1)S(1)} %get-tuple-element.64), channel_id=1, source_target_pairs={{0,2},{1,3},{2,0},{3,1},{4,6},{5,7},{6,4},{7,5},{8,10},{9,11},{10,... | collective-permute-start | bytes 786440 | tf_op jit(solution)/shard_map/ppermute | solution.py:411
  43.3 12.6 %collective-permute-start.16 = (bf16[1,256,512]{2,1,0:T(8,128)(2,1)S(1)}, bf16[1,256,512]{2,1,0:T(8,128)(2,1)S(1)}, u32[]{:S(2)}, u32[]{:S(2)}) collective-permute-start(bf16[1,256,512]{2,1,0:T(8,128)(2,1)S(1)} %get-tuple-element.63), channel_id=1, source_target_pairs={{0,2},{1,3},{2,0},{3,1},{4,6},{5,7},{6,4},{7,5},{8,10},{9,11},{10,... | collective-permute-start | bytes 786440 | tf_op jit(solution)/shard_map/ppermute | solution.py:411

commit v14 on v13

--- a/solution.py
+++ b/solution.py
@@ -309,7 +309,7 @@
     pieces = chan_width // unit
 
     middle = seq_count // 2
-    arrival = [k for near in range(middle) for k in (near, near + middle)]
+    arrival = [k for near in range(middle) for k in (near, seq_count - 1 - near)]
 
     def swap(arrays):
         return [arrays[0]] + [

time: 57 us -> 55.8 us (0.979)
  waiting for transfers between devices: 13.7 us -> 10.2 us
  starting transfers between devices: 25.6 us -> 27.8 us
    ppermute x14, waiting for transfers between devices: 4.33 us -> 0.85 us  [swap(): lax.ppermute(arrays[k], 'seq', [(d, d ^ k) for d in range(seq_count)])]
    ppermute x14, starting transfers between devices: 23.3 us -> 25.5 us  [swap(): lax.ppermute(arrays[k], 'seq', [(d, d ^ k) for d in range(seq_count)])]
  transfers between devices with their start and end apart: 18 -> 18, of which waited for: 7 -> 5; matrix products, arithmetic and copies ran while one was open for 0% -> 0% of each run, Pallas kernels for 19% -> 20%
where the time goes in v14:
time: 55.8 us; the launch traced here: 55.6 us
  starting transfers between devices  27.8 us (50%)
  Pallas kernels  17.2 us (31%)
  waiting for transfers between devices  10.2 us (18%)
    ppermute x14, starting transfers between devices, swap(): lax.ppermute(arrays[k], 'seq', [(d, d ^ k) for d in range(seq_count)])  25.5 us
    ppermute x4, waiting for transfers between devices, exchange(): lax.ppermute(terms, 'chan', [(d, d ^ bit) for d in range(chan_count)])  9.37 us
    pallas_call x1, Pallas kernels, local(): pl.pallas_call(functools.partial(filter_kernel, block, far_odd, pieces >...  4.32 us
    pallas_call x1, Pallas kernels, local(): pl.pallas_call(functools.partial(conv_kernel, block, blocks_kept, arrival...  2.85 us
    ppermute x4, starting transfers between devices, exchange(): lax.ppermute(terms, 'chan', [(d, d ^ bit) for d in range(chan_count)])  2.31 us
    pallas_call x1, Pallas kernels, local(): pl.pallas_call(functools.partial(last_kernel, blocks_last), out_shape=jax...  2.3 us
    pallas_call x1, Pallas kernels, local(): pl.pallas_call(functools.partial(copy_kernel, near_odd), out_shape=(jax.S...  1.99 us
    pallas_call x2, Pallas kernels, local(): pl.pallas_call(functools.partial(finish_kernel, span, len(terms)), out_sh...  1.87 us
  transfers between devices with their start and end apart: 18, of which 5 were waited for; matrix products, arithmetic and copies ran while one was open for 0% of the time, Pallas kernels for 20%

profile of v14, /device:TPU:0, one launch (start us, length us, event | category | flops | bytes accessed | tf_op | source)
XLA Modules:
  0.0 55.6 jit_solution(12237191543301322238)
XLA Ops:
  0.0 1.5 %shard_map.155 = (bf16[256,128]{1,0:T(8,128)(2,1)S(1)}, bf16[256,128]{1,0:T(8,128)(2,1)S(1)}, bf16[256,128]{1,0:T(8,128)(2,1)S(1)}, bf16[256,128]{1,0:T(8,128)(2...) custom-call(bf16[256,1024]{1,0:T(8,128)(2,1)} %key_hbm.1, ...), custom_call_target="tpu_custom_call" | custom-call | tf_op jit(solution)/shard_map/pallas_call | solution.py:319
  1.5 6.0 %collective-permute-start = (bf16[256,128]{1,0:T(8,128)(2,1)S(1)}, bf16[256,128]{1,0:T(8,128)(2,1)S(1)}, u32[]{:S(2)}, u32[]{:S(2)}) collective-permute-start(bf16[256,128]{1,0:T(8,128)(2,1)S(1)} %get-tuple-element.39.refs_7_), channel_id=1, source_target_pairs={{0,28},{4,24},{8,20},{12,16},{16,12},{20,8},{24,4},{28,0},{1,29},{... | collective-permute-start | bytes 196616 | tf_op jit(solution)/shard_map/ppermute | solution.py:316
  7.5 0.5 collective-permute-start.1
  8.2 5.2 %collective-permute-start.4 = (bf16[256,128]{1,0:T(8,128)(2,1)S(1)}, bf16[256,128]{1,0:T(8,128)(2,1)S(1)}, u32[]{:S(2)}, u32[]{:S(2)}) collective-permute-start(bf16[256,128]{1,0:T(8,128)(2,1)S(1)} %get-tuple-element.43.refs_5_), channel_id=1, source_target_pairs={{0,20},{4,16},{8,28},{12,24},{16,4},{20,0},{24,12},{28,8},{1,21},{... | collective-permute-start | bytes 196616 | tf_op jit(solution)/shard_map/ppermute | solution.py:316
  13.4 2.4 %collective-permute-start.6 = (bf16[256,128]{1,0:T(8,128)(2,1)S(1)}, bf16[256,128]{1,0:T(8,128)(2,1)S(1)}, u32[]{:S(2)}, u32[]{:S(2)}) collective-permute-start(bf16[256,128]{1,0:T(8,128)(2,1)S(1)} %get-tuple-element.45.refs_4_), channel_id=1, source_target_pairs={{0,16},{4,20},{8,24},{12,28},{16,0},{20,4},{24,8},{28,12},{1,17},{... | collective-permute-start | bytes 196616 | tf_op jit(solution)/shard_map/ppermute | solution.py:316
  15.8 4.3 %shard_map.154 = (f32[8,256,128]{2,1,0:T(8,128)S(1)}, f32[8,256,128]{2,1,0:T(8,128)S(1)}, f32[8,16,128]{2,1,0:T(8,128)S(1)}, bf16[1,1024,1024]{2,1,0:T(8,128)(2,1)S(1)}) custom-call(f32[64,128]{1,0:T(8,128)S(1)} %constant_dynamic-slice_fusion.out_w_ref, f32[40,2048]{1,0:T(8,128)} %constant.23.clone.refs_0_, f32[33,64]{1,0:T(8,128)} %refs_1_.1, ...), custom_call_target="tpu_custom_call" | custom-call | tf_op jit(solution)/shard_map/pallas_call | solution.py:352
  20.2 2.8 %shard_map.156 = (bf16[256,128]{1,0:T(8,128)(2,1)S(1)}, bf16[256,128]{1,0:T(8,128)(2,1)S(1)}, bf16[256,128]{1,0:T(8,128)(2,1)S(1)}, bf16[256,128]{1,0:T(8,128)(2...) custom-call(s32[16]{0:T(128)S(1)} %copy-done.4, ...), custom_call_target="tpu_custom_call" | custom-call | tf_op jit(solution)/shard_map/pallas_call | solution.py:374
  23.1 3.0 %collective-permute-start.7 = (bf16[256,128]{1,0:T(8,128)(2,1)S(1)}, bf16[256,128]{1,0:T(8,128)(2,1)S(1)}, u32[]{:S(2)}, u32[]{:S(2)}) collective-permute-start(bf16[256,128]{1,0:T(8,128)(2,1)S(1)} %get-tuple-element.50), channel_id=1, source_target_pairs={{0,28},{4,24},{8,20},{12,16},{16,12},{20,8},{24,4},{28,0},{1,29},{... | collective-permute-start | bytes 196616 | tf_op jit(solution)/shard_map/ppermute | solution.py:316
  26.0 0.5 collective-permute-start.8
  26.6 1.8 %collective-permute-start.9 = (bf16[256,128]{1,0:T(8,128)(2,1)S(1)}, bf16[256,128]{1,0:T(8,128)(2,1)S(1)}, u32[]{:S(2)}, u32[]{:S(2)}) collective-permute-start(bf16[256,128]{1,0:T(8,128)(2,1)S(1)} %get-tuple-element.52), channel_id=1, source_target_pairs={{0,24},{4,28},{8,16},{12,20},{16,8},{20,12},{24,0},{28,4},{1,25},{... | collective-permute-start | bytes 196616 | tf_op jit(solution)/shard_map/ppermute | solution.py:316
  28.4 3.5 %collective-permute-start.11 = (bf16[256,128]{1,0:T(8,128)(2,1)S(1)}, bf16[256,128]{1,0:T(8,128)(2,1)S(1)}, u32[]{:S(2)}, u32[]{:S(2)}) collective-permute-start(bf16[256,128]{1,0:T(8,128)(2,1)S(1)} %get-tuple-element.54), channel_id=1, source_target_pairs={{0,20},{4,16},{8,28},{12,24},{16,4},{20,0},{24,12},{28,8},{1,21},{... | collective-permute-start | bytes 196616 | tf_op jit(solution)/shard_map/ppermute | solution.py:316
  31.9 2.4 %collective-permute-start.13 = (bf16[256,128]{1,0:T(8,128)(2,1)S(1)}, bf16[256,128]{1,0:T(8,128)(2,1)S(1)}, u32[]{:S(2)}, u32[]{:S(2)}) collective-permute-start(bf16[256,128]{1,0:T(8,128)(2,1)S(1)} %get-tuple-element.56), channel_id=1, source_target_pairs={{0,16},{4,20},{8,24},{12,28},{16,0},{20,4},{24,8},{28,12},{1,17},{... | collective-permute-start | bytes 196616 | tf_op jit(solution)/shard_map/ppermute | solution.py:316
  34.3 2.0 %shard_map.157 = (bf16[1,1024,1024]{2,1,0:T(8,128)(2,1)S(1)}, bf16[8,256,128]{2,1,0:T(8,128)(2,1)S(1)}, f32[8,256,128]{2,1,0:T(8,128)S(1)}) custom-call(bf16[256,128]{1,0:T(8,128)(2,1)S(1)} %get-tuple-element.46.after_ref.refs_0_, f32[1,1024]{1,0:T(1,128)S(1)} %bitcast.14, bf16[1024,4096]{1,0:T(8,128)(2,1)} %weight_hbm.5, bf16[256,1024]{1,0:T(8,128)(2,1)} %query_hbm.1, ...), custom_call_target="tpu_custom_call" | custom-call | tf_op jit(solution)/shard_map/pallas_call | solution.py:392
  36.3 0.7 %collective-permute-done.12.refs_6_ = bf16[256,128]{1,0:T(8,128)(2,1)S(1)} collective-permute-done((bf16[256,128]{1,0:T(8,128)(2,1)S(1)}, bf16[256,128]{1,0:T(8,128)(2,1)S(1)}, u32[]{:S(2)}, u32[]{:S(2)}) %collective-permute-start.12) | collective-permute-done | bytes 65568 | tf_op jit(solution)/shard_map/ppermute | solution.py:316
  37.1 1.0 %shard_map.158 = (bf16[1,256,1024]{2,1,0:T(8,128)(2,1)S(1)}, bf16[256,1024]{1,0:T(8,128)(2,1)S(1)}) custom-call(bf16[8,256,128]{2,1,0:T(8,128)(2,1)S(1)} %get-tuple-element.47.query_ref, f32[8,256,128]{2,1,0:T(8,128)S(1)} %get-tuple-element.48.skip_ref, bf16[1,1024,1024]{2,1,0:T(8,128)(2,1)S(1)} %get-tuple-element.49.weight_ref, ...), custom_call_target="tpu_custom_call" | custom-call | tf_op jit(solution)/shard_map/pallas_call | solution.py:413
  38.2 0.7 %shard_map.160 = bf16[1,256,1024]{2,1,0:T(8,128)(2,1)S(1)} custom-call(bf16[256,1024]{1,0:T(8,128)(2,1)S(1)} %get-tuple-element.61.mixed_ref, bf16[1,1024,1024]{2,1,0:T(8,128)(2,1)S(1)} %get-tuple-element.60.weight_ref), custom_call_target="tpu_custom_call" | custom-call | tf_op jit(solution)/shard_map/pallas_call | solution.py:426
  38.9 0.7 %shard_map.159 = f32[1,256,1024]{2,1,0:T(8,128)S(1)} custom-call(bf16[256,1024]{1,0:T(8,128)(2,1)S(1)} %get-tuple-element.61.mixed_ref, bf16[1,1024,1024]{2,1,0:T(8,128)(2,1)S(1)} %get-tuple-element.58.weight_ref), custom_call_target="tpu_custom_call" | custom-call | tf_op jit(solution)/shard_map/pallas_call | solution.py:426
  40.5 1.5 %collective-permute-start.17 = (bf16[1,256,512]{2,1,0:T(8,128)(2,1)S(1)}, bf16[1,256,512]{2,1,0:T(8,128)(2,1)S(1)}, u32[]{:S(2)}, u32[]{:S(2)}) collective-permute-start(bf16[1,256,512]{2,1,0:T(8,128)(2,1)S(1)} %get-tuple-element.64), channel_id=1, source_target_pairs={{0,2},{1,3},{2,0},{3,1},{4,6},{5,7},{6,4},{7,5},{8,10},{9,11},{10,... | collective-permute-start | bytes 786440 | tf_op jit(solution)/shard_map/ppermute | solution.py:411
  42.0 0.5 collective-permute-start.16
  42.5 2.3 %shard_map.161 = f32[1,256,1024]{2,1,0:T(8,128)S(1)} custom-call(bf16[256,1024]{1,0:T(8,128)(2,1)S(1)} %get-tuple-element.61.mixed_ref, bf16[1024,4096]{1,0:T(8,128)(2,1)} %weight_hbm.5), custom_call_target="tpu_custom_call" | custom-call | tf_op jit(solution)/shard_map/pallas_call | solution.py:440
  44.8 4.8 %collective-permute-done.17 = bf16[1,256,512]{2,1,0:T(8,128)(2,1)S(1)} collective-permute-done((bf16[1,256,512]{2,1,0:T(8,128)(2,1)S(1)}, bf16[1,256,512]{2,1,0:T(8,128)(2,1)S(1)}, u32[]{:S(2)}, u32[]{:S(2)}) %collective-permute-start.17) | collective-permute-done | bytes 262176 | tf_op jit(solution)/shard_map/ppermute | solution.py:411
  49.6 0.9 %shard_map.162.refs_3_ = f32[1024,256]{1,0:T(8,128)} custom-call(f32[256,1024]{1,0:T(8,128)S(1)} %bitcast.8, bf16[256,1024]{1,0:T(8,128)(2,1)S(1)} %bitcast.10, bf16[256,512]{1,0:T(8,128)(2,1)S(1)} %bitcast.12), custom_call_target="tpu_custom_call" | custom-call | tf_op jit(solution)/shard_map/pallas_call | solution.py:461
  50.6 4.1 %collective-permute-done.16 = bf16[1,256,512]{2,1,0:T(8,128)(2,1)S(1)} collective-permute-done((bf16[1,256,512]{2,1,0:T(8,128)(2,1)S(1)}, bf16[1,256,512]{2,1,0:T(8,128)(2,1)S(1)}, u32[]{:S(2)}, u32[]{:S(2)}) %collective-permute-start.16) | collective-permute-done | bytes 262176 | tf_op jit(solution)/shard_map/ppermute | solution.py:411
  54.7 0.9 %shard_map.163 = f32[1024,256]{1,0:T(8,128)} custom-call(f32[256,1024]{1,0:T(8,128)S(1)} %bitcast.9, bf16[256,1024]{1,0:T(8,128)(2,1)S(1)} %bitcast.11, bf16[256,512]{1,0:T(8,128)(2,1)S(1)} %bitcast.13, f32[1024,256]{1,0:T(8,128)} %shard_map.162.refs_3_), custom_call_target="tpu_custom_call", output_to_operand_aliasing={{}: (3, {})} | custom-call | tf_op jit(solution)/shard_map/pallas_call | solution.py:461
  (34 shorter events, 1.2 us)
Async XLA Ops:
  0.0 15.8 %copy-start = (f32[64,1024]{1,0:T(8,128)S(1)}, f32[64,1024]{1,0:T(8,128)}, u32[]{:S(2)}) copy-start(f32[64,1024]{1,0:T(8,128)} %param.24) | copy-start | bytes 786436
  1.5 11.9 %collective-permute-start = (bf16[256,128]{1,0:T(8,128)(2,1)S(1)}, bf16[256,128]{1,0:T(8,128)(2,1)S(1)}, u32[]{:S(2)}, u32[]{:S(2)}) collective-permute-start(bf16[256,128]{1,0:T(8,128)(2,1)S(1)} %get-tuple-element.39.refs_7_), channel_id=1, source_target_pairs={{0,28},{4,24},{8,20},{12,16},{16,12},{20,8},{24,4},{28,0},{1,29},{... | collective-permute-start | bytes 196616 | tf_op jit(solution)/shard_map/ppermute | solution.py:316
  7.5 5.9 %collective-permute-start.1 = (bf16[256,128]{1,0:T(8,128)(2,1)S(1)}, bf16[256,128]{1,0:T(8,128)(2,1)S(1)}, u32[]{:S(2)}, u32[]{:S(2)}) collective-permute-start(bf16[256,128]{1,0:T(8,128)(2,1)S(1)} %get-tuple-element.40.refs_1_), channel_id=1, source_target_pairs={{0,4},{4,0},{8,12},{12,8},{16,20},{20,16},{24,28},{28,24},{1,5},{5... | collective-permute-start | bytes 196616 | tf_op jit(solution)/shard_map/ppermute | solution.py:316
  8.0 12.1 %collective-permute-start.2 = (bf16[256,128]{1,0:T(8,128)(2,1)S(1)}, bf16[256,128]{1,0:T(8,128)(2,1)S(1)}, u32[]{:S(2)}, u32[]{:S(2)}) collective-permute-start(bf16[256,128]{1,0:T(8,128)(2,1)S(1)} %get-tuple-element.41.refs_6_), channel_id=1, source_target_pairs={{0,24},{4,28},{8,16},{12,20},{16,8},{20,12},{24,0},{28,4},{1,25},{... | collective-permute-start | bytes 196616 | tf_op jit(solution)/shard_map/ppermute | solution.py:316
  8.2 12.0 %collective-permute-start.3 = (bf16[256,128]{1,0:T(8,128)(2,1)S(1)}, bf16[256,128]{1,0:T(8,128)(2,1)S(1)}, u32[]{:S(2)}, u32[]{:S(2)}) collective-permute-start(bf16[256,128]{1,0:T(8,128)(2,1)S(1)} %get-tuple-element.42.refs_2_), channel_id=1, source_target_pairs={{0,8},{4,12},{8,0},{12,4},{16,24},{20,28},{24,16},{28,20},{1,9},{5... | collective-permute-start | bytes 196616 | tf_op jit(solution)/shard_map/ppermute | solution.py:316
  8.2 12.0 %collective-permute-start.4 = (bf16[256,128]{1,0:T(8,128)(2,1)S(1)}, bf16[256,128]{1,0:T(8,128)(2,1)S(1)}, u32[]{:S(2)}, u32[]{:S(2)}) collective-permute-start(bf16[256,128]{1,0:T(8,128)(2,1)S(1)} %get-tuple-element.43.refs_5_), channel_id=1, source_target_pairs={{0,20},{4,16},{8,28},{12,24},{16,4},{20,0},{24,12},{28,8},{1,21},{... | collective-permute-start | bytes 196616 | tf_op jit(solution)/shard_map/ppermute | solution.py:316
  13.4 6.8 %collective-permute-start.5 = (bf16[256,128]{1,0:T(8,128)(2,1)S(1)}, bf16[256,128]{1,0:T(8,128)(2,1)S(1)}, u32[]{:S(2)}, u32[]{:S(2)}) collective-permute-start(bf16[256,128]{1,0:T(8,128)(2,1)S(1)} %get-tuple-element.44.refs_3_), channel_id=1, source_target_pairs={{0,12},{4,8},{8,4},{12,0},{16,28},{20,24},{24,20},{28,16},{1,13},{... | collective-permute-start | bytes 196616 | tf_op jit(solution)/shard_map/ppermute | solution.py:316
  13.4 6.8 %collective-permute-start.6 = (bf16[256,128]{1,0:T(8,128)(2,1)S(1)}, bf16[256,128]{1,0:T(8,128)(2,1)S(1)}, u32[]{:S(2)}, u32[]{:S(2)}) collective-permute-start(bf16[256,128]{1,0:T(8,128)(2,1)S(1)} %get-tuple-element.45.refs_4_), channel_id=1, source_target_pairs={{0,16},{4,20},{8,24},{12,28},{16,0},{20,4},{24,8},{28,12},{1,17},{... | collective-permute-start | bytes 196616 | tf_op jit(solution)/shard_map/ppermute | solution.py:316
  15.8 4.4 %copy-start.1 = (bf16[256,512]{1,0:T(8,128)(2,1)S(1)}, bf16[256,512]{1,0:T(8,128)(2,1)}, u32[]{:S(2)}) copy-start(bf16[256,512]{1,0:T(8,128)(2,1)} %constant.26.inverse_ref) | copy-start | bytes 786436
  15.8 4.4 %copy-start.2 = (bf16[512,256]{1,0:T(8,128)(2,1)S(1)}, bf16[512,256]{1,0:T(8,128)(2,1)}, u32[]{:S(2)}) copy-start(bf16[512,256]{1,0:T(8,128)(2,1)} %constant.25.table_ref) | copy-start | bytes 786436
  15.8 4.4 %copy-start.4 = (s32[16]{0:T(128)S(1)}, s32[16]{0:T(128)}, u32[]{:S(2)}) copy-start(s32[16]{0:T(128)} %order_ref.1) | copy-start | bytes 196
  20.2 14.1 %copy-start.3 = (f32[1024]{0:T(1024)S(1)}, f32[1024]{0:T(1024)}, u32[]{:S(2)}) copy-start(f32[1024]{0:T(1024)} %param.26) | copy-start | bytes 12292
  23.1 8.8 %collective-permute-start.7 = (bf16[256,128]{1,0:T(8,128)(2,1)S(1)}, bf16[256,128]{1,0:T(8,128)(2,1)S(1)}, u32[]{:S(2)}, u32[]{:S(2)}) collective-permute-start(bf16[256,128]{1,0:T(8,128)(2,1)S(1)} %get-tuple-element.50), channel_id=1, source_target_pairs={{0,28},{4,24},{8,20},{12,16},{16,12},{20,8},{24,4},{28,0},{1,29},{... | collective-permute-start | bytes 196616 | tf_op jit(solution)/shard_map/ppermute | solution.py:316
  26.0 5.9 %collective-permute-start.8 = (bf16[256,128]{1,0:T(8,128)(2,1)S(1)}, bf16[256,128]{1,0:T(8,128)(2,1)S(1)}, u32[]{:S(2)}, u32[]{:S(2)}) collective-permute-start(bf16[256,128]{1,0:T(8,128)(2,1)S(1)} %get-tuple-element.51), channel_id=1, source_target_pairs={{0,4},{4,0},{8,12},{12,8},{16,20},{20,16},{24,28},{28,24},{1,5},{5... | collective-permute-start | bytes 196616 | tf_op jit(solution)/shard_map/ppermute | solution.py:316
  26.6 9.7 %collective-permute-start.9 = (bf16[256,128]{1,0:T(8,128)(2,1)S(1)}, bf16[256,128]{1,0:T(8,128)(2,1)S(1)}, u32[]{:S(2)}, u32[]{:S(2)}) collective-permute-start(bf16[256,128]{1,0:T(8,128)(2,1)S(1)} %get-tuple-element.52), channel_id=1, source_target_pairs={{0,24},{4,28},{8,16},{12,20},{16,8},{20,12},{24,0},{28,4},{1,25},{... | collective-permute-start | bytes 196616 | tf_op jit(solution)/shard_map/ppermute | solution.py:316
  28.4 7.9 %collective-permute-start.10 = (bf16[256,128]{1,0:T(8,128)(2,1)S(1)}, bf16[256,128]{1,0:T(8,128)(2,1)S(1)}, u32[]{:S(2)}, u32[]{:S(2)}) collective-permute-start(bf16[256,128]{1,0:T(8,128)(2,1)S(1)} %get-tuple-element.53), channel_id=1, source_target_pairs={{0,8},{4,12},{8,0},{12,4},{16,24},{20,28},{24,16},{28,20},{1,9},{5... | collective-permute-start | bytes 196616 | tf_op jit(solution)/shard_map/ppermute | solution.py:316
  28.4 7.9 %collective-permute-start.11 = (bf16[256,128]{1,0:T(8,128)(2,1)S(1)}, bf16[256,128]{1,0:T(8,128)(2,1)S(1)}, u32[]{:S(2)}, u32[]{:S(2)}) collective-permute-start(bf16[256,128]{1,0:T(8,128)(2,1)S(1)} %get-tuple-element.54), channel_id=1, source_target_pairs={{0,20},{4,16},{8,28},{12,24},{16,4},{20,0},{24,12},{28,8},{1,21},{... | collective-permute-start | bytes 196616 | tf_op jit(solution)/shard_map/ppermute | solution.py:316
  31.9 5.2 %collective-permute-start.12 = (bf16[256,128]{1,0:T(8,128)(2,1)S(1)}, bf16[256,128]{1,0:T(8,128)(2,1)S(1)}, u32[]{:S(2)}, u32[]{:S(2)}) collective-permute-start(bf16[256,128]{1,0:T(8,128)(2,1)S(1)} %get-tuple-element.55), channel_id=1, source_target_pairs={{0,12},{4,8},{8,4},{12,0},{16,28},{20,24},{24,20},{28,16},{1,13},{... | collective-permute-start | bytes 196616 | tf_op jit(solution)/shard_map/ppermute | solution.py:316
  31.9 5.2 %collective-permute-start.13 = (bf16[256,128]{1,0:T(8,128)(2,1)S(1)}, bf16[256,128]{1,0:T(8,128)(2,1)S(1)}, u32[]{:S(2)}, u32[]{:S(2)}) collective-permute-start(bf16[256,128]{1,0:T(8,128)(2,1)S(1)} %get-tuple-element.56), channel_id=1, source_target_pairs={{0,16},{4,20},{8,24},{12,28},{16,0},{20,4},{24,8},{28,12},{1,17},{... | collective-permute-start | bytes 196616 | tf_op jit(solution)/shard_map/ppermute | solution.py:316
  38.1 2.0 %collective-permute-start.14 = (bf16[1,256,1024]{2,1,0:T(8,128)(2,1)S(1)}, bf16[1,256,1024]{2,1,0:T(8,128)(2,1)S(1)}, u32[]{:S(2)}, u32[]{:S(2)}) collective-permute-start(bf16[1,256,1024]{2,1,0:T(8,128)(2,1)S(1)} %get-tuple-element.59), channel_id=1, source_target_pairs={{0,1},{1,0},{2,3},{3,2},{4,5},{5,4},{6,7},{7,6},{8,9},{9,8},{10,11... | collective-permute-start | bytes 1572872 | tf_op jit(solution)/shard_map/ppermute | solution.py:411
  40.3 9.3 %collective-permute-start.15 = (bf16[1,256,1024]{2,1,0:T(8,128)(2,1)S(1)}, bf16[1,256,1024]{2,1,0:T(8,128)(2,1)S(1)}, u32[]{:S(2)}, u32[]{:S(2)}) collective-permute-start(bf16[1,256,1024]{2,1,0:T(8,128)(2,1)S(1)} %shard_map.160), channel_id=1, source_target_pairs={{0,1},{1,0},{2,3},{3,2},{4,5},{5,4},{6,7},{7,6},{8,9},{9,8},{10,11... | collective-permute-start | bytes 1572872 | tf_op jit(solution)/shard_map/ppermute | solution.py:411
  40.5 9.1 %collective-permute-start.17 = (bf16[1,256,512]{2,1,0:T(8,128)(2,1)S(1)}, bf16[1,256,512]{2,1,0:T(8,128)(2,1)S(1)}, u32[]{:S(2)}, u32[]{:S(2)}) collective-permute-start(bf16[1,256,512]{2,1,0:T(8,128)(2,1)S(1)} %get-tuple-element.64), channel_id=1, source_target_pairs={{0,2},{1,3},{2,0},{3,1},{4,6},{5,7},{6,4},{7,5},{8,10},{9,11},{10,... | collective-permute-start | bytes 786440 | tf_op jit(solution)/shard_map/ppermute | solution.py:411
  42.0 12.7 %collective-permute-start.16 = (bf16[1,256,512]{2,1,0:T(8,128)(2,1)S(1)}, bf16[1,256,512]{2,1,0:T(8,128)(2,1)S(1)}, u32[]{:S(2)}, u32[]{:S(2)}) collective-permute-start(bf16[1,256,512]{2,1,0:T(8,128)(2,1)S(1)} %get-tuple-element.63), channel_id=1, source_target_pairs={{0,2},{1,3},{2,0},{3,1},{4,6},{5,7},{6,4},{7,5},{8,10},{9,11},{10,... | collective-permute-start | bytes 786440 | tf_op jit(solution)/shard_map/ppermute | solution.py:411
